TPU v7x, 32 devices: a whole 2x2x4 slice. The times are simulated.
32 devices in a mesh: dp: 16 (over z, y, x), tensor: 2 (over core).
Axes of the slice: x: 2, y: 2, z: 4, core: 2. Of those that a mesh axis runs over, the one named last changes fastest.
Arguments:
- inputs: bfloat16 [12288, 1536], P(('dp', 'tensor')), may hold values from -6 to 6
- cotangent: bfloat16 [12288, 1536], P(('dp', 'tensor')), may hold values from -12 to 12
- context: bfloat16 [16, 130, 768], P('dp'), may hold values from -6 to 6
- context_live: int32 [16, 130], P('dp'), may hold values from 0 to 1, as said below
- lengths: int32 [16], P('dp'), may hold values from 384 to 768, as said below
- threshold: float32 [1], replicated, may hold values from 5 to 8
- self_gain: bfloat16 [1536], P('dp'), may hold values from 0.5 to 1.5
- self_bias: bfloat16 [1536], P('dp'), may hold values from -1.75 to 1.75
- self_query: bfloat16 [1536, 1536], P('dp', 'tensor')
- self_key: bfloat16 [1536, 1536], P('dp', 'tensor'), may hold values from -0.15625 to 0.15625
- self_value: bfloat16 [1536, 1536], P('dp', 'tensor'), may hold values from -0.15625 to 0.15625
- self_output: bfloat16 [1536, 1536], P('tensor', 'dp'), may hold values from -0.875 to 0.875
- cross_gain: bfloat16 [1536], P('dp'), may hold values from 0.5 to 1.5
- cross_bias: bfloat16 [1536], P('dp'), may hold values from -1.75 to 1.75
- cross_query: bfloat16 [1536, 1536], P('dp', 'tensor')
- cross_key: bfloat16 [768, 1536], P('dp', 'tensor'), may hold values from -0.21875 to 0.21875
- cross_value: bfloat16 [768, 1536], P('dp', 'tensor'), may hold values from -0.21875 to 0.21875
- cross_output: bfloat16 [1536, 1536], P('tensor', 'dp'), may hold values from -0.4375 to 0.4375
- feed_gain: bfloat16 [1536], P('dp'), may hold values from 0.5 to 1.5
- feed_bias: bfloat16 [1536], P('dp'), may hold values from -1.75 to 1.75
- gate_weight: bfloat16 [1536, 6144], P('dp', 'tensor'), may hold values from -0.15625 to 0.15625
- up_weight: bfloat16 [1536, 6144], P('dp', 'tensor'), may hold values from -0.15625 to 0.15625
- down_weight: bfloat16 [6144, 1536], P('tensor', 'dp'), may hold values from -0.078125 to 0.078125
Outputs:
- result: bfloat16 [12288, 1536], P(('dp', 'tensor'))
- input_grad: float32 [12288, 1536], P(('dp', 'tensor'))
- grad_self_gain: float32 [1536], P('dp')
- grad_self_bias: float32 [1536], P('dp')
- grad_self_query: float32 [1536, 1536], P('dp', 'tensor')
- grad_self_key: float32 [1536, 1536], P('dp', 'tensor')
- grad_self_value: float32 [1536, 1536], P('dp', 'tensor')
- grad_self_output: float32 [1536, 1536], P('tensor', 'dp')
- grad_cross_gain: float32 [1536], P('dp')
- grad_cross_bias: float32 [1536], P('dp')
- grad_cross_query: float32 [1536, 1536], P('dp', 'tensor')
- grad_cross_key: float32 [768, 1536], P('dp', 'tensor')
- grad_cross_value: float32 [768, 1536], P('dp', 'tensor')
- grad_cross_output: float32 [1536, 1536], P('tensor', 'dp')
- grad_feed_gain: float32 [1536], P('dp')
- grad_feed_bias: float32 [1536], P('dp')
- grad_gate_weight: float32 [1536, 6144], P('dp', 'tensor')
- grad_up_weight: float32 [1536, 6144], P('dp', 'tensor')
- grad_down_weight: float32 [6144, 1536], P('tensor', 'dp')
- peaks: float32 [24], P('tensor')
- scaled_self_query: float32 [1536, 1536], P('dp', 'tensor')
- scaled_self_key: float32 [1536, 1536], P('dp', 'tensor')
- scaled_cross_query: float32 [1536, 1536], P('dp', 'tensor')
- scaled_cross_key: float32 [768, 1536], P('dp', 'tensor')
Inputs may be any that keep to these rules, and one draw needn't show every extreme that they name: lengths counts the valid latent tokens of a sequence; the first sequence is full. `context_live`: the first conditioning token of every sequence is live.
All inputs are finite; a program needn't handle non-finite values.
Results may differ from a plain program's by a relative error of at most 0.025.
The roundings to bfloat16 on the way count: a program that leaves them out, or rounds other values in their place, can miss the bound.
Values may be sent and summed in bfloat16 or wider, within the bound.
A program may use at most 256 MiB of HBM per device.

v0:
```python
import jax
import jax.numpy as jnp
from jax import lax
from jax.sharding import PartitionSpec as P

HEAD_DIM = 64
ROT_DIM = 32


EPSILON = 1e-05
NEGATIVE = -1e30


def norm_forward(stream, gain_vec, bias_vec):
    average = jnp.mean(stream, axis=-1, keepdims=True)
    centred = stream - average
    inverse = lax.rsqrt(jnp.mean(centred * centred, axis=-1, keepdims=True) + EPSILON)
    unit_rows = centred * inverse
    return (unit_rows * gain_vec + bias_vec, unit_rows, inverse)


def norm_backward(incoming, unit_rows, inverse, gain_vec):
    gain_grad = jnp.sum(incoming * unit_rows, axis=0)
    bias_grad = jnp.sum(incoming, axis=0)
    scaled = incoming * gain_vec
    stream_grad = inverse * (
        scaled
        - jnp.mean(scaled, axis=-1, keepdims=True)
        - unit_rows * jnp.mean(scaled * unit_rows, axis=-1, keepdims=True)
    )
    return (stream_grad, gain_grad, bias_grad)


def rotate(field, positions, direction):
    half_count = ROT_DIM // 2
    rates = 10000.0 ** (-jnp.arange(0, ROT_DIM, 2).astype(jnp.float32) / ROT_DIM)
    angles = positions[:, None] * rates[None, :]
    cosine = jnp.cos(angles)[:, None, :]
    sine = direction * jnp.sin(angles)[:, None, :]
    first = field[..., :half_count]
    second = field[..., half_count:ROT_DIM]
    return jnp.concatenate(
        [first * cosine - second * sine, second * cosine + first * sine, field[..., ROT_DIM:]],
        axis=-1,
    )


def attend_forward(query, keys, values, allowed):
    raw_scores = jnp.einsum("qhe,khe->hqk", query, keys, preferred_element_type=jnp.float32)
    scores = jnp.where(allowed[None, None, :], raw_scores * HEAD_DIM ** (-0.5), NEGATIVE)
    head_peak = jnp.max(scores, axis=(1, 2))
    row_top = jnp.max(scores, axis=-1, keepdims=True)
    log_total = jnp.log(jnp.sum(jnp.exp(scores - row_top), axis=-1, keepdims=True)) + row_top
    weighting = jnp.exp(scores - log_total).astype(jnp.bfloat16)
    mixed = jnp.einsum("hqk,khe->qhe", weighting, values, preferred_element_type=jnp.float32)
    return (mixed, log_total, head_peak)


def attend_backward(query, keys, values, allowed, log_total, grad_mixed):
    raw_scores = jnp.einsum("qhe,khe->hqk", query, keys, preferred_element_type=jnp.float32)
    scores = jnp.where(allowed[None, None, :], raw_scores * HEAD_DIM ** (-0.5), NEGATIVE)
    weighting = jnp.exp(scores - log_total)
    grad_weights = jnp.einsum(
        "qhe,khe->hqk", grad_mixed, values, preferred_element_type=jnp.float32
    )
    grad_values = jnp.einsum(
        "hqk,qhe->khe",
        weighting.astype(jnp.bfloat16),
        grad_mixed,
        preferred_element_type=jnp.float32,
    )
    grad_scores = weighting * (
        grad_weights - jnp.sum(grad_weights * weighting, axis=-1, keepdims=True)
    )
    grad_raw = (grad_scores * HEAD_DIM ** (-0.5)).astype(jnp.bfloat16)
    grad_query = jnp.einsum("hqk,khe->qhe", grad_raw, keys, preferred_element_type=jnp.float32)
    grad_keys = jnp.einsum("hqk,qhe->khe", grad_raw, query, preferred_element_type=jnp.float32)
    return (grad_query, grad_keys, grad_values)


def gather_rows(pieces):
    return lax.all_gather(pieces, "tensor", axis=0, tiled=True)


def spread_rows(partial_rows):
    return lax.psum_scatter(partial_rows, "tensor", scatter_dimension=0, tiled=True)


def matmul(left, right):
    return jnp.dot(left, right, preferred_element_type=jnp.float32)


def left_product(left, right):
    return jnp.einsum("td,tc->dc", left, right, preferred_element_type=jnp.float32)


def right_product(left, right):
    return jnp.einsum("tc,dc->td", left, right, preferred_element_type=jnp.float32)


def per_device(
    inputs,
    cotangent,
    context,
    context_live,
    lengths,
    threshold,
    self_gain,
    self_bias,
    self_query,
    self_key,
    self_value,
    self_output,
    cross_gain,
    cross_bias,
    cross_query,
    cross_key,
    cross_value,
    cross_output,
    feed_gain,
    feed_bias,
    gate_weight,
    up_weight,
    down_weight,
):
    whole = (
        lax.all_gather(self_gain, "dp", axis=0, tiled=True),
        lax.all_gather(self_bias, "dp", axis=0, tiled=True),
        lax.all_gather(self_query, "dp", axis=0, tiled=True),
        lax.all_gather(self_key, "dp", axis=0, tiled=True),
        lax.all_gather(self_value, "dp", axis=0, tiled=True),
        lax.all_gather(self_output, "dp", axis=1, tiled=True),
        lax.all_gather(cross_gain, "dp", axis=0, tiled=True),
        lax.all_gather(cross_bias, "dp", axis=0, tiled=True),
        lax.all_gather(cross_query, "dp", axis=0, tiled=True),
        lax.all_gather(cross_key, "dp", axis=0, tiled=True),
        lax.all_gather(cross_value, "dp", axis=0, tiled=True),
        lax.all_gather(cross_output, "dp", axis=1, tiled=True),
        lax.all_gather(feed_gain, "dp", axis=0, tiled=True),
        lax.all_gather(feed_bias, "dp", axis=0, tiled=True),
        lax.all_gather(gate_weight, "dp", axis=0, tiled=True),
        lax.all_gather(up_weight, "dp", axis=0, tiled=True),
        lax.all_gather(down_weight, "dp", axis=1, tiled=True),
    )
    (
        full_self_gain,
        full_self_bias,
        full_self_query,
        full_self_key,
        full_self_value,
        full_self_output,
        full_cross_gain,
        full_cross_bias,
        full_cross_query,
        full_cross_key,
        full_cross_value,
        full_cross_output,
        full_feed_gain,
        full_feed_bias,
        full_gate,
        full_upward,
        full_down,
    ) = whole
    seq_len = inputs.shape[0] * lax.axis_size("tensor")
    heads_here = self_query.shape[1] // HEAD_DIM
    positions = jnp.arange(seq_len).astype(jnp.float32)
    self_allowed = jnp.arange(seq_len) < lengths[0]
    cross_allowed = context_live[0] > 0
    memory = context[0]
    head_shape = (seq_len, heads_here, HEAD_DIM)
    memory_shape = (memory.shape[0], heads_here, HEAD_DIM)
    stream = inputs.astype(jnp.float32)
    normed, unit_self, inverse_self = norm_forward(
        stream, full_self_gain.astype(jnp.float32), full_self_bias.astype(jnp.float32)
    )
    normed_self = gather_rows(normed.astype(jnp.bfloat16))
    query_self = rotate(
        matmul(normed_self, full_self_query).reshape(head_shape), positions, 1.0
    ).astype(jnp.bfloat16)
    key_self = rotate(
        matmul(normed_self, full_self_key).reshape(head_shape), positions, 1.0
    ).astype(jnp.bfloat16)
    value_self = matmul(normed_self, full_self_value).astype(jnp.bfloat16).reshape(head_shape)
    mixed, total_self, peak_self = attend_forward(query_self, key_self, value_self, self_allowed)
    mixed_self = mixed.reshape(seq_len, -1).astype(jnp.bfloat16)
    stream_cross = stream + spread_rows(matmul(mixed_self, full_self_output))
    normed, unit_cross, inverse_cross = norm_forward(
        stream_cross, full_cross_gain.astype(jnp.float32), full_cross_bias.astype(jnp.float32)
    )
    normed_cross = gather_rows(normed.astype(jnp.bfloat16))
    query_cross = matmul(normed_cross, full_cross_query).astype(jnp.bfloat16).reshape(head_shape)
    key_cross = matmul(memory, full_cross_key).astype(jnp.bfloat16).reshape(memory_shape)
    value_cross = matmul(memory, full_cross_value).astype(jnp.bfloat16).reshape(memory_shape)
    mixed, total_cross, peak_cross = attend_forward(
        query_cross, key_cross, value_cross, cross_allowed
    )
    mixed_cross = mixed.reshape(seq_len, -1).astype(jnp.bfloat16)
    stream_feed = stream_cross + spread_rows(matmul(mixed_cross, full_cross_output))
    normed, unit_feed, inverse_feed = norm_forward(
        stream_feed, full_feed_gain.astype(jnp.float32), full_feed_bias.astype(jnp.float32)
    )
    normed_feed = gather_rows(normed.astype(jnp.bfloat16))
    gate_pre = matmul(normed_feed, full_gate)
    upward = matmul(normed_feed, full_upward)
    hidden = (jax.nn.silu(gate_pre) * upward).astype(jnp.bfloat16)
    result = (stream_feed + spread_rows(matmul(hidden, full_down))).astype(jnp.bfloat16)
    peaks = lax.pmax(jnp.maximum(peak_self, peak_cross), "dp")
    back = (
        lax.all_gather(self_gain, "dp", axis=0, tiled=True),
        lax.all_gather(self_bias, "dp", axis=0, tiled=True),
        lax.all_gather(self_query, "dp", axis=0, tiled=True),
        lax.all_gather(self_key, "dp", axis=0, tiled=True),
        lax.all_gather(self_value, "dp", axis=0, tiled=True),
        lax.all_gather(self_output, "dp", axis=1, tiled=True),
        lax.all_gather(cross_gain, "dp", axis=0, tiled=True),
        lax.all_gather(cross_bias, "dp", axis=0, tiled=True),
        lax.all_gather(cross_query, "dp", axis=0, tiled=True),
        lax.all_gather(cross_key, "dp", axis=0, tiled=True),
        lax.all_gather(cross_value, "dp", axis=0, tiled=True),
        lax.all_gather(cross_output, "dp", axis=1, tiled=True),
        lax.all_gather(feed_gain, "dp", axis=0, tiled=True),
        lax.all_gather(feed_bias, "dp", axis=0, tiled=True),
        lax.all_gather(gate_weight, "dp", axis=0, tiled=True),
        lax.all_gather(up_weight, "dp", axis=0, tiled=True),
        lax.all_gather(down_weight, "dp", axis=1, tiled=True),
    )
    (
        back_self_gain,
        back_self_bias,
        back_self_query,
        back_self_key,
        back_self_value,
        back_self_output,
        back_cross_gain,
        back_cross_bias,
        back_cross_query,
        back_cross_key,
        back_cross_value,
        back_cross_output,
        back_feed_gain,
        back_feed_bias,
        back_gate,
        back_upward,
        back_down,
    ) = back
    grad_stream = cotangent.astype(jnp.float32)
    grad_full = gather_rows(cotangent)
    grad_down_weight = left_product(hidden, grad_full)
    grad_hidden = right_product(grad_full, back_down)
    sigmoid_gate = jax.nn.sigmoid(gate_pre)
    grad_gate = (
        grad_hidden * upward * sigmoid_gate * (1.0 + gate_pre * (1.0 - sigmoid_gate))
    ).astype(jnp.bfloat16)
    grad_upward = (grad_hidden * gate_pre * sigmoid_gate).astype(jnp.bfloat16)
    grad_gate_weight = left_product(normed_feed, grad_gate)
    grad_up_weight = left_product(normed_feed, grad_upward)
    grad_normed = spread_rows(
        right_product(grad_gate, back_gate) + right_product(grad_upward, back_upward)
    )
    stream_part, grad_feed_gain, grad_feed_bias = norm_backward(
        grad_normed, unit_feed, inverse_feed, back_feed_gain.astype(jnp.float32)
    )
    grad_stream = grad_stream + stream_part
    grad_full = gather_rows(grad_stream.astype(jnp.bfloat16))
    grad_cross_output = left_product(mixed_cross, grad_full)
    grad_mixed = (
        right_product(grad_full, back_cross_output).astype(jnp.bfloat16).reshape(head_shape)
    )
    grad_query, grad_keys, grad_values = attend_backward(
        query_cross, key_cross, value_cross, cross_allowed, total_cross, grad_mixed
    )
    grad_query = grad_query.astype(jnp.bfloat16).reshape(seq_len, -1)
    grad_keys = grad_keys.astype(jnp.bfloat16).reshape(memory.shape[0], -1)
    grad_values = grad_values.astype(jnp.bfloat16).reshape(memory.shape[0], -1)
    grad_cross_query = left_product(normed_cross, grad_query)
    grad_cross_key = left_product(memory, grad_keys)
    grad_cross_value = left_product(memory, grad_values)
    grad_normed = spread_rows(right_product(grad_query, back_cross_query))
    stream_part, grad_cross_gain, grad_cross_bias = norm_backward(
        grad_normed, unit_cross, inverse_cross, back_cross_gain.astype(jnp.float32)
    )
    grad_stream = grad_stream + stream_part
    grad_full = gather_rows(grad_stream.astype(jnp.bfloat16))
    grad_self_output = left_product(mixed_self, grad_full)
    grad_mixed = right_product(grad_full, back_self_output).astype(jnp.bfloat16).reshape(head_shape)
    grad_query, grad_keys, grad_values = attend_backward(
        query_self, key_self, value_self, self_allowed, total_self, grad_mixed
    )
    grad_query = rotate(grad_query, positions, -1.0).astype(jnp.bfloat16).reshape(seq_len, -1)
    grad_keys = rotate(grad_keys, positions, -1.0).astype(jnp.bfloat16).reshape(seq_len, -1)
    grad_values = grad_values.astype(jnp.bfloat16).reshape(seq_len, -1)
    grad_self_query = left_product(normed_self, grad_query)
    grad_self_key = left_product(normed_self, grad_keys)
    grad_self_value = left_product(normed_self, grad_values)
    grad_normed = spread_rows(
        right_product(grad_query, back_self_query)
        + right_product(grad_keys, back_self_key)
        + right_product(grad_values, back_self_value)
    )
    stream_part, grad_self_gain, grad_self_bias = norm_backward(
        grad_normed, unit_self, inverse_self, back_self_gain.astype(jnp.float32)
    )
    grad_stream = grad_stream + stream_part
    summed = (
        lax.psum_scatter(grad_self_gain, "dp", scatter_dimension=0, tiled=True),
        lax.psum_scatter(grad_self_bias, "dp", scatter_dimension=0, tiled=True),
        lax.psum_scatter(grad_self_query, "dp", scatter_dimension=0, tiled=True),
        lax.psum_scatter(grad_self_key, "dp", scatter_dimension=0, tiled=True),
        lax.psum_scatter(grad_self_value, "dp", scatter_dimension=0, tiled=True),
        lax.psum_scatter(grad_self_output, "dp", scatter_dimension=1, tiled=True),
        lax.psum_scatter(grad_cross_gain, "dp", scatter_dimension=0, tiled=True),
        lax.psum_scatter(grad_cross_bias, "dp", scatter_dimension=0, tiled=True),
        lax.psum_scatter(grad_cross_query, "dp", scatter_dimension=0, tiled=True),
        lax.psum_scatter(grad_cross_key, "dp", scatter_dimension=0, tiled=True),
        lax.psum_scatter(grad_cross_value, "dp", scatter_dimension=0, tiled=True),
        lax.psum_scatter(grad_cross_output, "dp", scatter_dimension=1, tiled=True),
        lax.psum_scatter(grad_feed_gain, "dp", scatter_dimension=0, tiled=True),
        lax.psum_scatter(grad_feed_bias, "dp", scatter_dimension=0, tiled=True),
        lax.psum_scatter(grad_gate_weight, "dp", scatter_dimension=0, tiled=True),
        lax.psum_scatter(grad_up_weight, "dp", scatter_dimension=0, tiled=True),
        lax.psum_scatter(grad_down_weight, "dp", scatter_dimension=1, tiled=True),
    )
    gain_parts = lax.psum(
        (summed[0], summed[1], summed[6], summed[7], summed[12], summed[13]), "tensor"
    )
    factor = jnp.sqrt(threshold[0] / jnp.maximum(peaks, threshold[0]))
    columns = jnp.repeat(factor, HEAD_DIM)[None, :]
    return (
        result,
        grad_stream,
        gain_parts[0],
        gain_parts[1],
        summed[2],
        summed[3],
        summed[4],
        summed[5],
        gain_parts[2],
        gain_parts[3],
        summed[8],
        summed[9],
        summed[10],
        summed[11],
        gain_parts[4],
        gain_parts[5],
        summed[14],
        summed[15],
        summed[16],
        peaks,
        self_query.astype(jnp.float32) * columns,
        self_key.astype(jnp.float32) * columns,
        cross_query.astype(jnp.float32) * columns,
        cross_key.astype(jnp.float32) * columns,
    )


def solution(mesh):
    in_specs = (
        P(("dp", "tensor"), None),
        P(("dp", "tensor"), None),
        P("dp", None, None),
        P("dp", None),
        P("dp"),
        P(),
        P("dp"),
        P("dp"),
        P("dp", "tensor"),
        P("dp", "tensor"),
        P("dp", "tensor"),
        P("tensor", "dp"),
        P("dp"),
        P("dp"),
        P("dp", "tensor"),
        P("dp", "tensor"),
        P("dp", "tensor"),
        P("tensor", "dp"),
        P("dp"),
        P("dp"),
        P("dp", "tensor"),
        P("dp", "tensor"),
        P("tensor", "dp"),
    )
    out_specs = (
        P(("dp", "tensor"), None),
        P(("dp", "tensor"), None),
        P("dp"),
        P("dp"),
        P("dp", "tensor"),
        P("dp", "tensor"),
        P("dp", "tensor"),
        P("tensor", "dp"),
        P("dp"),
        P("dp"),
        P("dp", "tensor"),
        P("dp", "tensor"),
        P("dp", "tensor"),
        P("tensor", "dp"),
        P("dp"),
        P("dp"),
        P("dp", "tensor"),
        P("dp", "tensor"),
        P("tensor", "dp"),
        P("tensor"),
        P("dp", "tensor"),
        P("dp", "tensor"),
        P("dp", "tensor"),
        P("dp", "tensor"),
    )
    return jax.shard_map(
        per_device, mesh=mesh, in_specs=in_specs, out_specs=out_specs, check_vma=False
    )
```

profile of v0, /device:TPU:0, one launch (start us, length us, event | category | flops | bytes accessed | tf_op | source)
XLA Modules:
  0.0 3349.3 jit_solution(14346025301410265502)
XLA Ops:
  14.4 78.5 %all-reduce.14 = (bf16[1536]{0:T(1024)(128)(2,1)S(1)}, bf16[1536]{0:T(1024)(128)(2,1)S(1)}, bf16[1536]{0:T(1024)(128)(2,1)S(1)}, bf16[1536]{0:T(1024)(128)(2,1)S...) all-reduce(bf16[1536]{0:T(1024)(128)(2,1)S(1)} %dynamic-update-slic, ...), channel_id=1, replica_groups=mesh['dp'=16,'tensor'=2] {'dp'}, use_global_device_ids=true, to_apply=%add.1 | all-reduce | flops 9216 | bytes 36864
  105.2 66.3 %all-gather.24.cloned.1.call-done = bf16[1536,768]{1,0:T(8,128)(2,1)} async-done(((bf16[96,768]{1,0:T(8,128)(2,1)}), bf16[1536,768]{1,0:T(8,128)(2,1)}) %all-gather.24.cloned.1.call-update) | async-done | bytes 2359312 | tf_op jit(solution)/shard_map/all_gather | solution.py:130
  176.1 59.4 %all-gather.22.cloned.1.call-done = bf16[1536,768]{1,0:T(8,128)(2,1)} async-done(((bf16[96,768]{1,0:T(8,128)(2,1)}), bf16[1536,768]{1,0:T(8,128)(2,1)}) %all-gather.22.cloned.1.call-update) | async-done | bytes 2359312 | tf_op jit(solution)/shard_map/all_gather | solution.py:129
  252.8 13.0 fusion.82
  265.7 33.5 %all-gather.20.cloned.1.call-done = bf16[1536,768]{1,0:T(8,128)(2,1)} async-done(((bf16[96,768]{1,0:T(8,128)(2,1)}), bf16[1536,768]{1,0:T(8,128)(2,1)}) %all-gather.20.cloned.1.call-update) | async-done | bytes 2359312 | tf_op jit(solution)/shard_map/all_gather | solution.py:131
  316.5 46.6 %all-gather.26.cloned.1.call-done = bf16[768,1536]{0,1:T(8,128)(2,1)} async-done(((bf16[768,96]{0,1:T(8,128)(2,1)}), bf16[768,1536]{0,1:T(8,128)(2,1)}) %all-gather.26.cloned.1.call-update) | async-done | bytes 2359312 | tf_op jit(solution)/shard_map/all_gather | solution.py:132
  385.7 55.2 %all-gather.34.cloned.1.call-done = bf16[768,768]{1,0:T(8,128)(2,1)} async-done(((bf16[48,768]{1,0:T(8,128)(2,1)}), bf16[768,768]{1,0:T(8,128)(2,1)}) %all-gather.34.cloned.1.call-update) | async-done | bytes 1179664 | tf_op jit(solution)/shard_map/all_gather | solution.py:136
  442.8 56.4 %all-gather.28.cloned.1.call-done = bf16[768,768]{1,0:T(8,128)(2,1)} async-done(((bf16[48,768]{1,0:T(8,128)(2,1)}), bf16[768,768]{1,0:T(8,128)(2,1)}) %all-gather.28.cloned.1.call-update) | async-done | bytes 1179664 | tf_op jit(solution)/shard_map/all_gather | solution.py:137
  502.6 61.0 %all-gather.32.cloned.1.call-done = bf16[1536,768]{1,0:T(8,128)(2,1)} async-done(((bf16[96,768]{1,0:T(8,128)(2,1)}), bf16[1536,768]{1,0:T(8,128)(2,1)}) %all-gather.32.cloned.1.call-update) | async-done | bytes 2359312 | tf_op jit(solution)/shard_map/all_gather | solution.py:135
  585.5 56.6 %all-gather.36.cloned.1.call-done = bf16[768,1536]{0,1:T(8,128)(2,1)} async-done(((bf16[768,96]{0,1:T(8,128)(2,1)}), bf16[768,1536]{0,1:T(8,128)(2,1)}) %all-gather.36.cloned.1.call-update) | async-done | bytes 2359312 | tf_op jit(solution)/shard_map/all_gather | solution.py:138
  667.2 119.2 %all-gather.40.cloned.1.call-done = bf16[1536,3072]{1,0:T(8,128)(2,1)} async-done(((bf16[96,3072]{1,0:T(8,128)(2,1)}), bf16[1536,3072]{1,0:T(8,128)(2,1)}) %all-gather.40.cloned.1.call-update) | async-done | bytes 9437200 | tf_op jit(solution)/shard_map/all_gather | solution.py:141
  810.5 113.4 %all-gather.42.cloned.1.call-done = bf16[1536,3072]{1,0:T(8,128)(2,1)} async-done(((bf16[96,3072]{1,0:T(8,128)(2,1)}), bf16[1536,3072]{1,0:T(8,128)(2,1)}) %all-gather.42.cloned.1.call-update) | async-done | bytes 9437200 | tf_op jit(solution)/shard_map/all_gather | solution.py:142
  936.8 124.0 %all-gather.44.cloned.1.call-done = bf16[3072,1536]{0,1:T(8,128)(2,1)} async-done(((bf16[3072,96]{0,1:T(8,128)(2,1)}), bf16[3072,1536]{0,1:T(8,128)(2,1)}) %all-gather.44.cloned.1.call-update) | async-done | bytes 9437200 | tf_op jit(solution)/shard_map/all_gather | solution.py:143
  1060.7 21.1 multiply_convert_fusion.1
  1176.5 13.9 reduce-scatter.30.cloned.1.call-done
  1236.3 37.8 %fusion.50 = f32[768,12,64]{0,2,1:T(8,128)} fusion(f32[12,768,768]{1,2,0:T(8,128)} %fusion.101, f32[12,768,768]{1,2,0:T(8,128)} %get-tuple-element.163, f32[12,768]{1,0:T(8,128)S(1)} %copy-done.34, bf16[768,12,32]{0,2,1:T(8,128)(2,1)S(1)} %copy-done.27, bf16[768,12,16]{0,2,1:T(8,128)(2,1)} %copy-done.40, bf16[768,12,16]{0,2,1:T(8,128)(2,1)} %copy-done.39), kind=kOutput, calls=%fused_computation.67 | convolution fusion | flops 959063808 | bytes 60198912 | tf_op jit(solution)/shard_map/hqk,qhe->khe/dot_general | solution.py:77
  1274.1 44.6 %fusion.47 = f32[768,12,64]{0,2,1:T(8,128)} fusion(f32[12,768,768]{1,2,0:T(8,128)} %fusion.101, f32[12,768,768]{1,2,0:T(8,128)} %get-tuple-element.163, f32[12,768]{1,0:T(8,128)S(1)} %copy-done.34, bf16[768,12,32]{0,2,1:T(8,128)(2,1)S(1)} %copy-done.25, bf16[768,12,16]{0,2,1:T(8,128)(2,1)S(1)} %copy-done.36, bf16[768,12,16]{0,2,1:T(8,128)(2,1)S(1)} %copy-done.38), kind=kOutput, calls=%fused_computation.66 | convolution fusion | flops 959063808 | bytes 60198912 | tf_op jit(solution)/shard_map/hqk,khe->qhe/dot_general | solution.py:76
  1399.7 13.0 fusion.110
  1412.8 13.2 fusion.111
  1427.6 13.0 fusion.112
  1442.2 42.1 %pmax.7 = f32[12]{0:T(128)S(1)} all-reduce(f32[12]{0:T(128)S(1)} %max.9), channel_id=1, replica_groups=mesh['dp'=16,'tensor'=2] {'dp'}, use_global_device_ids=true, to_apply=%region_55.56 | all-reduce | flops 12 | bytes 96 | tf_op jit(solution)/shard_map/pmax | solution.py:207
  1488.9 72.1 %all-reduce.12 = (f32[1536]{0:T(1024)S(1)}, f32[1536]{0:T(1024)S(1)}, f32[1536]{0:T(1024)S(1)}, f32[1536]{0:T(1024)S(1)}, f32[1536]{0:T(1024)S(1)}, /*index=5*/f32[1536]{0:T(1024)S(1)}) all-reduce(f32[1536]{0:T(1024)S(1)} %get-tuple-element.104, f32[1536]{0:T(1024)S(1)} %get-tuple-element.111, ...), channel_id=8, replica_groups=mesh['dp'=16,'tensor'=2] {'dp'}, use_global_device_ids=true, to_apply=%region_25.26.clone | all-reduce | flops 9216 | bytes 73728
  1569.1 46.2 %reduce-scatter.52.cloned.1.call-done = f32[48,768]{1,0:T(8,128)} async-done(((f32[768,768]{1,0:T(8,128)}), f32[48,768]{1,0:T(8,128)}) %reduce-scatter.52.cloned.1.call-update) | async-done | bytes 147472
  1615.2 142.2 %reduce-scatter.44.cloned.1.call-done = f32[768,96]{0,1:T(8,128)} async-done(((f32[768,1536]{0,1:T(8,128)}), f32[768,96]{0,1:T(8,128)}) %reduce-scatter.44.cloned.1.call-update) | async-done | bytes 294928 | tf_op jit(solution)/shard_map/reduce_scatter | solution.py:316
  1757.4 142.7 %reduce-scatter.42.cloned.1.call-done = f32[96,768]{1,0:T(8,128)} async-done(((f32[1536,768]{1,0:T(8,128)}), f32[96,768]{1,0:T(8,128)}) %reduce-scatter.42.cloned.1.call-update) | async-done | bytes 294928 | tf_op jit(solution)/shard_map/reduce_scatter | solution.py:313
  1900.2 142.0 %reduce-scatter.38.cloned.1.call-done = f32[96,768]{1,0:T(8,128)} async-done(((f32[1536,768]{1,0:T(8,128)}), f32[96,768]{1,0:T(8,128)}) %reduce-scatter.38.cloned.1.call-update) | async-done | bytes 294928 | tf_op jit(solution)/shard_map/reduce_scatter | solution.py:309
  2042.2 142.5 %reduce-scatter.36.cloned.1.call-done = f32[96,768]{1,0:T(8,128)} async-done(((f32[1536,768]{1,0:T(8,128)}), f32[96,768]{1,0:T(8,128)}) %reduce-scatter.36.cloned.1.call-update) | async-done | bytes 294928 | tf_op jit(solution)/shard_map/reduce_scatter | solution.py:308
  2184.7 142.0 %reduce-scatter.40.cloned.1.call-done = f32[768,96]{0,1:T(8,128)} async-done(((f32[768,1536]{0,1:T(8,128)}), f32[768,96]{0,1:T(8,128)}) %reduce-scatter.40.cloned.1.call-update) | async-done | bytes 294928 | tf_op jit(solution)/shard_map/reduce_scatter | solution.py:310
  2326.6 143.0 %reduce-scatter.34.cloned.1.call-done = f32[96,768]{1,0:T(8,128)} async-done(((f32[1536,768]{1,0:T(8,128)}), f32[96,768]{1,0:T(8,128)}) %reduce-scatter.34.cloned.1.call-update) | async-done | bytes 294928 | tf_op jit(solution)/shard_map/reduce_scatter | solution.py:307
  2469.6 290.6 %reduce-scatter.46.cloned.1.call-done = f32[96,3072]{1,0:T(8,128)} async-done(((f32[1536,3072]{1,0:T(8,128)}), f32[96,3072]{1,0:T(8,128)}) %reduce-scatter.46.cloned.1.call-update) | async-done | bytes 1179664 | tf_op jit(solution)/shard_map/reduce_scatter | solution.py:319
  2760.2 291.0 %reduce-scatter.48.cloned.1.call-done = f32[96,3072]{1,0:T(8,128)} async-done(((f32[1536,3072]{1,0:T(8,128)}), f32[96,3072]{1,0:T(8,128)}) %reduce-scatter.48.cloned.1.call-update) | async-done | bytes 1179664 | tf_op jit(solution)/shard_map/reduce_scatter | solution.py:320
  3051.2 290.8 %reduce-scatter.50.cloned.1.call-done = f32[3072,96]{0,1:T(8,128)} async-done(((f32[3072,1536]{0,1:T(8,128)}), f32[3072,96]{0,1:T(8,128)}) %reduce-scatter.50.cloned.1.call-update) | async-done | bytes 1179664 | tf_op jit(solution)/shard_map/reduce_scatter | solution.py:321
  (321 shorter events, 403.9 us)
Async XLA Ops:
  7.2 98.0 %all-gather.18.cloned.1.call-start = ((), (), s32[]{:S(2)}) async-start(), calls=%async_computation.17 | async-start | bytes 3538944 | tf_op jit(solution)/shard_map/all_gather | solution.py:82
  98.2 73.3 %all-gather.24.cloned.1.call-start = ((), (), s32[]{:S(2)}) async-start(), calls=%async_computation.20 | async-start | bytes 2506752 | tf_op jit(solution)/shard_map/all_gather | solution.py:130
  99.0 136.5 %all-gather.22.cloned.1.call-start = ((), (), s32[]{:S(2)}) async-start(), calls=%async_computation.19 | async-start | bytes 2506752 | tf_op jit(solution)/shard_map/all_gather | solution.py:129
  99.7 199.5 %all-gather.20.cloned.1.call-start = ((), (), s32[]{:S(2)}) async-start(), calls=%async_computation.18 | async-start | bytes 2506752 | tf_op jit(solution)/shard_map/all_gather | solution.py:131
  100.3 262.8 %all-gather.26.cloned.1.call-start = ((), (), s32[]{:S(2)}) async-start(), calls=%async_computation.21 | async-start | bytes 2506752 | tf_op jit(solution)/shard_map/all_gather | solution.py:132
  100.9 279.6 %reduce-scatter.22.cloned.1.call-start = ((), (), s32[]{:S(2)}) async-start(), calls=%async_computation.22 | async-start | bytes 7077888 | tf_op jit(solution)/shard_map/reduce_scatter | solution.py:86
  368.9 72.1 %all-gather.34.cloned.1.call-start = ((), (), s32[]{:S(2)}) async-start(), calls=%async_computation.26 | async-start | bytes 1253376 | tf_op jit(solution)/shard_map/all_gather | solution.py:136
  369.6 129.5 %all-gather.28.cloned.1.call-start = ((), (), s32[]{:S(2)}) async-start(), calls=%async_computation.23 | async-start | bytes 1253376 | tf_op jit(solution)/shard_map/all_gather | solution.py:137
  370.4 193.2 %all-gather.32.cloned.1.call-start = ((), (), s32[]{:S(2)}) async-start(), calls=%async_computation.25 | async-start | bytes 2506752 | tf_op jit(solution)/shard_map/all_gather | solution.py:135
  371.1 204.3 %all-gather.30.cloned.1.call-start = ((), (), s32[]{:S(2)}) async-start(), calls=%async_computation.24 | async-start | bytes 3538944 | tf_op jit(solution)/shard_map/all_gather | solution.py:82
  384.7 257.4 %all-gather.36.cloned.1.call-start = ((), (), s32[]{:S(2)}) async-start(), calls=%async_computation.27 | async-start | bytes 2506752 | tf_op jit(solution)/shard_map/all_gather | solution.py:138
  385.4 274.5 %reduce-scatter.24.cloned.1.call-start = ((), (), s32[]{:S(2)}) async-start(), calls=%async_computation.28 | async-start | bytes 7077888 | tf_op jit(solution)/shard_map/reduce_scatter | solution.py:86
  648.4 138.0 %all-gather.40.cloned.1.call-start = ((), (), s32[]{:S(2)}) async-start(), calls=%async_computation.30 | async-start | bytes 10027008 | tf_op jit(solution)/shard_map/all_gather | solution.py:141
  649.1 148.4 %all-gather.38.cloned.1.call-start = ((), (), s32[]{:S(2)}) async-start(), calls=%async_computation.29 | async-start | bytes 3538944 | tf_op jit(solution)/shard_map/all_gather | solution.py:82
  665.0 258.9 %all-gather.42.cloned.1.call-start = ((), (), s32[]{:S(2)}) async-start(), calls=%async_computation.31 | async-start | bytes 10027008 | tf_op jit(solution)/shard_map/all_gather | solution.py:142
  665.6 271.2 %all-gather.46.cloned.1.call-start = ((), (), s32[]{:S(2)}) async-start(), calls=%async_computation.34 | async-start | bytes 3538944 | tf_op jit(solution)/shard_map/all_gather | solution.py:82
  666.1 394.6 %all-gather.44.cloned.1.call-start = ((), (), s32[]{:S(2)}) async-start(), calls=%async_computation.32 | async-start | bytes 10027008 | tf_op jit(solution)/shard_map/all_gather | solution.py:143
  666.7 451.7 %reduce-scatter.28.cloned.1.call-start = ((), (), s32[]{:S(2)}) async-start(), calls=%async_computation.35 | async-start | bytes 7077888 | tf_op jit(solution)/shard_map/reduce_scatter | solution.py:86
  1118.3 33.2 all-gather.48.cloned.1.call-start
  1139.2 51.2 %reduce-scatter.30.cloned.1.call-start = ((), (), s32[]{:S(2)}) async-start(), calls=%async_computation.37 | async-start | bytes 7077888 | tf_op jit(solution)/shard_map/reduce_scatter | solution.py:86
  1196.6 289.5 %reduce-scatter.32.cloned.1.call-start = ((), (), s32[]{:S(2)}) async-start(), calls=%async_computation.39 | async-start | bytes 7077888 | tf_op jit(solution)/shard_map/reduce_scatter | solution.py:86
  1334.2 234.8 %reduce-scatter.54.cloned.1.call-start = ((), (), s32[]{:S(2)}) async-start(), calls=%async_computation.50 | async-start | bytes 2506752
  1341.3 273.9 %reduce-scatter.52.cloned.1.call-start = ((), (), s32[]{:S(2)}) async-start(), calls=%async_computation.49 | async-start | bytes 2506752
  1354.8 402.6 %reduce-scatter.44.cloned.1.call-start = ((), (), s32[]{:S(2)}) async-start(), calls=%async_computation.45 | async-start | bytes 5013504 | tf_op jit(solution)/shard_map/reduce_scatter | solution.py:316
  1362.0 538.2 %reduce-scatter.42.cloned.1.call-start = ((), (), s32[]{:S(2)}) async-start(), calls=%async_computation.44 | async-start | bytes 5013504 | tf_op jit(solution)/shard_map/reduce_scatter | solution.py:313
  1369.2 673.0 %reduce-scatter.38.cloned.1.call-start = ((), (), s32[]{:S(2)}) async-start(), calls=%async_computation.42 | async-start | bytes 5013504 | tf_op jit(solution)/shard_map/reduce_scatter | solution.py:309
  1376.3 808.3 %reduce-scatter.36.cloned.1.call-start = ((), (), s32[]{:S(2)}) async-start(), calls=%async_computation.41 | async-start | bytes 5013504 | tf_op jit(solution)/shard_map/reduce_scatter | solution.py:308
  1383.6 943.0 %reduce-scatter.40.cloned.1.call-start = ((), (), s32[]{:S(2)}) async-start(), calls=%async_computation.43 | async-start | bytes 5013504 | tf_op jit(solution)/shard_map/reduce_scatter | solution.py:310
  1390.9 1078.7 %reduce-scatter.34.cloned.1.call-start = ((), (), s32[]{:S(2)}) async-start(), calls=%async_computation.40 | async-start | bytes 5013504 | tf_op jit(solution)/shard_map/reduce_scatter | solution.py:307
  1398.0 1362.2 %reduce-scatter.46.cloned.1.call-start = ((), (), s32[]{:S(2)}) async-start(), calls=%async_computation.46 | async-start | bytes 20054016 | tf_op jit(solution)/shard_map/reduce_scatter | solution.py:319
  1412.7 1638.5 %reduce-scatter.48.cloned.1.call-start = ((), (), s32[]{:S(2)}) async-start(), calls=%async_computation.47 | async-start | bytes 20054016 | tf_op jit(solution)/shard_map/reduce_scatter | solution.py:320
  1426.0 1916.1 %reduce-scatter.50.cloned.1.call-start = ((), (), s32[]{:S(2)}) async-start(), calls=%async_computation.48 | async-start | bytes 20054016 | tf_op jit(solution)/shard_map/reduce_scatter | solution.py:321
  (65 other events, 1736.7 us)
Sparse Core Ops, SparseCore 0:
  108.0 63.4 all-gather.23
  174.3 61.0 all-gather.21
  238.1 61.1 all-gather.19
  301.9 61.1 all-gather.25
  369.0 11.4 reduce-scatter.21
  383.7 57.2 all-gather.33
  444.1 54.9 all-gather.27
  502.4 61.1 all-gather.31
  565.6 9.7 all-gather.29
  578.6 63.4 all-gather.35
  648.5 11.4 reduce-scatter.23
  662.7 123.6 all-gather.39
  800.2 123.6 all-gather.41
  925.2 9.1 all-gather.45
  937.1 123.6 all-gather.43
  1105.4 10.7 reduce-scatter.27
  1118.7 13.7 reduce-scatter.25
  1139.3 12.1 all-gather.47
  1176.6 13.7 reduce-scatter.29
  1196.7 12.1 all-gather.49
  1334.3 13.7 reduce-scatter.31
  1353.5 128.8 reduce-scatter.53
  1488.6 126.5 reduce-scatter.51
  1620.8 136.5 reduce-scatter.43
  1763.8 136.2 reduce-scatter.41
  1905.9 136.2 reduce-scatter.37
  2048.7 135.8 reduce-scatter.35
  2190.3 136.3 reduce-scatter.39
  2333.2 136.3 reduce-scatter.33
  2475.9 284.2 reduce-scatter.45
  2766.4 284.7 reduce-scatter.47
  3057.6 284.4 reduce-scatter.49
  (2 shorter events, 15.9 us)
where the time goes:
time: 3360 us; the launch traced here: 3350 us
  waiting for transfers between devices  2670 us (79%)
  matrix products  375 us (11%)
  blocking collectives  196 us (6%)
  other arithmetic  56.7 us (2%)
  local copies, waits for them, and re-layouts  34.5 us (1%)
    reduce_scatter x1, waiting for transfers between devices, per_device(): lax.psum_scatter(grad_up_weight, 'dp', scatter_dimension=0, tiled=True)  291 us
    reduce_scatter x1, waiting for transfers between devices, per_device(): lax.psum_scatter(grad_down_weight, 'dp', scatter_dimension=1, tiled=True)  291 us
    reduce_scatter x1, waiting for transfers between devices, per_device(): lax.psum_scatter(grad_gate_weight, 'dp', scatter_dimension=0, tiled=True)  291 us
    unnamed x2, blocking collectives  151 us
    reduce_scatter x1, waiting for transfers between devices, per_device(): lax.psum_scatter(grad_self_query, 'dp', scatter_dimension=0, tiled=True)  143 us
    reduce_scatter x1, waiting for transfers between devices, per_device(): lax.psum_scatter(grad_cross_query, 'dp', scatter_dimension=0, tiled=True)  143 us
    reduce_scatter x1, waiting for transfers between devices, per_device(): lax.psum_scatter(grad_self_key, 'dp', scatter_dimension=0, tiled=True)  143 us
    reduce_scatter x1, waiting for transfers between devices, per_device(): lax.psum_scatter(grad_cross_output, 'dp', scatter_dimension=1, tiled=True)  142 us
  transfers between devices with their start and end apart: 34, of which 30 were waited for; matrix products, arithmetic and copies ran while one was open for 7% of the time, Pallas kernels for 0%

commit v1 on v0

v1 whole, which is shorter than its diff:
```python
import jax
import jax.numpy as jnp
from jax import lax
from jax.sharding import Mesh
from jax.sharding import PartitionSpec as P

HEAD_DIM = 64
ROT_DIM = 32
EPSILON = 1e-05
NEGATIVE = -1e30
BF = jnp.bfloat16
F32 = jnp.float32


def swap(value, axis):
    return lax.ppermute(value, axis, [(0, 1), (1, 0)])


def join(own, other, axis_name, dim):
    size = own.shape[dim]
    whole = own.shape[:dim] + (2 * size,) + own.shape[dim + 1 :]
    at = lax.axis_index(axis_name)
    out = jnp.zeros(whole, own.dtype)
    out = lax.dynamic_update_slice_in_dim(out, own, at * size, dim)
    return lax.dynamic_update_slice_in_dim(out, other, (1 - at) * size, dim)


def pick(value, index, dim):
    return lax.dynamic_index_in_dim(value, index, dim, keepdims=False)


def gather_weights(shard):
    held = lax.all_gather(shard, "z", axis=0, tiled=False)
    held = held[:, None]
    held = join(held, swap(held, "y"), "y", 1)
    held = held[:, :, None]
    held = join(held, swap(held, "x"), "x", 2)
    return held.reshape(-1, shard.shape[1])


def gather_pair_weights(held):
    held = lax.all_gather(held, "z", axis=0, tiled=False)
    held = held[:, None]
    held = join(held, swap(held, "y"), "y", 1)
    return held.reshape(-1, held.shape[-1])


def nn(left, right):
    return lax.dot_general(left, right, (((1,), (0,)), ((), ())), preferred_element_type=F32)


def nt(left, right):
    return lax.dot_general(left, right, (((1,), (1,)), ((), ())), preferred_element_type=F32)


def tn(left, right):
    return lax.dot_general(left, right, (((0,), (0,)), ((), ())), preferred_element_type=F32)


def columns_by(value, axis_name, zs):
    rows = value.shape[0]
    at = lax.axis_index(axis_name)
    if axis_name == "y":
        split = value.reshape(rows, zs, 2, -1)
        dim = 2
    else:
        split = value.reshape(rows, 2 * zs, 2, -1)
        dim = 2
    return (
        pick(split, at, dim).reshape(rows, -1),
        pick(split, 1 - at, dim).reshape(rows, -1),
    )


def reduce_full(left_keep, left_send, right, zs):
    got = swap(tn(left_send, right).astype(BF), "x")
    held = (tn(left_keep, right) + got.astype(F32)).astype(BF)
    held = held.reshape(zs, 2, -1, right.shape[1])
    at = lax.axis_index("y")
    got = swap(pick(held, 1 - at, 1), "y")
    held = (pick(held, at, 1).astype(F32) + got.astype(F32)).astype(BF)
    return lax.psum_scatter(held, "z", scatter_dimension=0, tiled=False)


def reduce_pair(left_keep, left_send, right, zs):
    got = swap(tn(left_send, right).astype(BF), "y")
    held = (tn(left_keep, right) + got.astype(F32)).astype(BF)
    held = held.reshape(zs, -1, right.shape[1])
    held = lax.psum_scatter(held, "z", scatter_dimension=0, tiled=False)
    held = held.reshape(2, -1, right.shape[1])
    at = lax.axis_index("x")
    got = swap(pick(held, 1 - at, 0), "x")
    return pick(held, at, 0), got


def norm_forward(stream, gain_vec, bias_vec):
    average = jnp.mean(stream, axis=-1, keepdims=True)
    centred = stream - average
    inverse = lax.rsqrt(jnp.mean(centred * centred, axis=-1, keepdims=True) + EPSILON)
    unit_rows = centred * inverse
    return (unit_rows * gain_vec + bias_vec, unit_rows, inverse)


def norm_backward(incoming, unit_rows, inverse, gain_vec):
    gain_grad = jnp.sum(incoming * unit_rows, axis=0)
    bias_grad = jnp.sum(incoming, axis=0)
    scaled = incoming * gain_vec
    stream_grad = inverse * (
        scaled
        - jnp.mean(scaled, axis=-1, keepdims=True)
        - unit_rows * jnp.mean(scaled * unit_rows, axis=-1, keepdims=True)
    )
    return (stream_grad, gain_grad, bias_grad)


def rotate(field, positions, direction):
    half_count = ROT_DIM // 2
    rates = 10000.0 ** (-jnp.arange(0, ROT_DIM, 2).astype(F32) / ROT_DIM)
    angles = positions[:, None] * rates[None, :]
    cosine = jnp.cos(angles)[:, None, :]
    sine = direction * jnp.sin(angles)[:, None, :]
    first = field[..., :half_count]
    second = field[..., half_count:ROT_DIM]
    return jnp.concatenate(
        [first * cosine - second * sine, second * cosine + first * sine, field[..., ROT_DIM:]],
        axis=-1,
    )


def attend_forward(query, keys, values, allowed):
    raw_scores = jnp.einsum("qhe,khe->hqk", query, keys, preferred_element_type=F32)
    scores = jnp.where(allowed[None, None, :], raw_scores * HEAD_DIM ** (-0.5), NEGATIVE)
    head_peak = jnp.max(scores, axis=(1, 2))
    row_top = jnp.max(scores, axis=-1, keepdims=True)
    log_total = jnp.log(jnp.sum(jnp.exp(scores - row_top), axis=-1, keepdims=True)) + row_top
    weighting = jnp.exp(scores - log_total).astype(BF)
    mixed = jnp.einsum("hqk,khe->qhe", weighting, values, preferred_element_type=F32)
    return (mixed, log_total, head_peak)


def attend_backward(query, keys, values, allowed, log_total, grad_mixed):
    raw_scores = jnp.einsum("qhe,khe->hqk", query, keys, preferred_element_type=F32)
    scores = jnp.where(allowed[None, None, :], raw_scores * HEAD_DIM ** (-0.5), NEGATIVE)
    weighting = jnp.exp(scores - log_total)
    grad_weights = jnp.einsum("qhe,khe->hqk", grad_mixed, values, preferred_element_type=F32)
    grad_values = jnp.einsum(
        "hqk,qhe->khe", weighting.astype(BF), grad_mixed, preferred_element_type=F32
    )
    grad_scores = weighting * (
        grad_weights - jnp.sum(grad_weights * weighting, axis=-1, keepdims=True)
    )
    grad_raw = (grad_scores * HEAD_DIM ** (-0.5)).astype(BF)
    grad_query = jnp.einsum("hqk,khe->qhe", grad_raw, keys, preferred_element_type=F32)
    grad_keys = jnp.einsum("hqk,qhe->khe", grad_raw, query, preferred_element_type=F32)
    return (grad_query, grad_keys, grad_values)


def pair_rows(own):
    return jnp.concatenate([own, swap(own, "tensor")], axis=0)


def group_rows(own):
    both = jnp.stack([own, swap(own, "x")])
    other = swap(both, "tensor")
    return jnp.concatenate([both[0], other[0], both[1], other[1]], axis=0)


def spread_pair(left, right_t):
    rows = left.shape[0] // 2
    got = swap(nt(left[rows:], right_t), "tensor")
    return nt(left[:rows], right_t) + got


def spread_group(product):
    quarter = product.rows // 4
    far_send = product(3 * quarter, quarter)
    far = product(2 * quarter, quarter) + swap(far_send, "tensor")
    got_far = swap(far.astype(BF), "x")
    near = product(0, quarter) + swap(product(quarter, quarter), "tensor")
    return near + got_far.astype(F32)


class Product:
    def __init__(self, terms, transposed):
        self.terms = terms
        self.transposed = transposed
        self.rows = terms[0][0].shape[0]

    def __call__(self, first, count):
        total = None
        for left, right in self.terms:
            part = (nt if self.transposed else nn)(left[first : first + count], right)
            total = part if total is None else total + part
        return total


def per_device(
    inputs,
    cotangent,
    context,
    context_live,
    lengths,
    threshold,
    self_gain,
    self_bias,
    self_query,
    self_key,
    self_value,
    self_output,
    cross_gain,
    cross_bias,
    cross_query,
    cross_key,
    cross_value,
    cross_output,
    feed_gain,
    feed_bias,
    gate_weight,
    up_weight,
    down_weight,
):
    zs = lax.axis_size("z")
    x_at = lax.axis_index("x")
    t_at = lax.axis_index("tensor")
    width = inputs.shape[1]
    rows = inputs.shape[0]
    seq_len = 2 * rows
    inner = self_query.shape[1]
    heads_here = inner // HEAD_DIM
    ff_half = gate_weight.shape[1]
    ff = ff_half // 2
    shard_rows = self_query.shape[0]
    context_rows = cross_key.shape[0]

    vectors = jnp.stack(
        [self_gain, self_bias, cross_gain, cross_bias, feed_gain, feed_bias], axis=1
    )
    vectors = jnp.pad(vectors, ((0, 0), (0, 122)))
    first = gather_weights(
        jnp.concatenate([self_query, self_key, self_value, vectors], axis=1)
    )
    in_weight = first[:, : 3 * inner]
    norms = first[:, 3 * inner :].astype(F32).T
    second = gather_weights(
        jnp.concatenate(
            [
                self_output.T,
                cross_query,
                cross_output.T,
                jnp.concatenate([cross_key, cross_value], axis=0),
            ],
            axis=1,
        )
    )
    self_out_t = second[:, :inner]
    cross_in = second[:, inner : 2 * inner]
    cross_out_t = second[:, 2 * inner : 3 * inner]
    memory_weights = second[:, 3 * inner :].reshape(-1, 2, context_rows, inner)
    cross_keys_w = memory_weights[:, 0].reshape(-1, inner)
    cross_values_w = memory_weights[:, 1].reshape(-1, inner)

    feed = jnp.stack([gate_weight, up_weight, down_weight.T], axis=1)
    feed = feed.reshape(shard_rows, 3, 2, ff)
    kept = pick(feed, x_at, 2).reshape(shard_rows, 3 * ff)
    sent = pick(feed, 1 - x_at, 2).reshape(shard_rows, 3 * ff)
    feed = join(kept[None], swap(sent, "x")[None], "x", 0)
    gate_up = gather_pair_weights(feed[:, :, : 2 * ff])
    down_t = gather_pair_weights(feed[:, :, 2 * ff :])

    local = jnp.arange(rows)
    places = jnp.concatenate([t_at * rows + local, (1 - t_at) * rows + local])
    positions = places.astype(F32)
    self_allowed = places < lengths[0]
    cross_allowed = context_live[0] > 0
    memory = context[0]
    head_shape = (seq_len, heads_here, HEAD_DIM)
    memory_shape = (memory.shape[0], heads_here, HEAD_DIM)

    cot_group = group_rows(cotangent)
    all_inputs = pair_rows(inputs)
    stream = inputs.astype(F32)
    normed, _, _ = norm_forward(all_inputs.astype(F32), norms[0], norms[1])
    normed_self = normed.astype(BF)
    projected = nn(normed_self, in_weight)
    query_self = rotate(projected[:, :inner].reshape(head_shape), positions, 1.0).astype(BF)
    key_self = rotate(
        projected[:, inner : 2 * inner].reshape(head_shape), positions, 1.0
    ).astype(BF)
    value_self = projected[:, 2 * inner :].astype(BF).reshape(head_shape)
    mixed, total_self, peak_self = attend_forward(query_self, key_self, value_self, self_allowed)
    mixed_self = mixed.reshape(seq_len, -1).astype(BF)
    stream_cross = stream + spread_pair(mixed_self, self_out_t)
    normed, unit_cross, inverse_cross = norm_forward(stream_cross, norms[2], norms[3])
    normed_cross = pair_rows(normed.astype(BF))
    query_cross = nn(normed_cross, cross_in).astype(BF).reshape(head_shape)
    key_cross = nn(memory, cross_keys_w).astype(BF).reshape(memory_shape)
    value_cross = nn(memory, cross_values_w).astype(BF).reshape(memory_shape)
    mixed, total_cross, peak_cross = attend_forward(
        query_cross, key_cross, value_cross, cross_allowed
    )
    mixed_cross = mixed.reshape(seq_len, -1).astype(BF)
    stream_feed = stream_cross + spread_pair(mixed_cross, cross_out_t)
    normed, unit_feed, inverse_feed = norm_forward(stream_feed, norms[4], norms[5])
    normed_feed = group_rows(normed.astype(BF))
    gates = nn(normed_feed, gate_up)
    gate_pre = gates[:, :ff]
    upward = gates[:, ff:]
    sigmoid_gate = jax.nn.sigmoid(gate_pre)
    hidden = (gate_pre * sigmoid_gate * upward).astype(BF)
    result = (stream_feed + spread_group(Product([(hidden, down_t)], True))).astype(BF)
    peaks = lax.pmax(jnp.maximum(peak_self, peak_cross), ("z", "y", "x"))

    cot_keep, cot_send = columns_by(cot_group, "y", zs)
    down_keep, down_got = reduce_pair(cot_keep, cot_send, hidden, zs)
    grad_hidden = nn(cot_group, down_t)
    grad_gate = grad_hidden * upward * sigmoid_gate * (1.0 + gate_pre * (1.0 - sigmoid_gate))
    grad_upward = grad_hidden * gate_pre * sigmoid_gate
    grad_gates = jnp.concatenate([grad_gate.astype(BF), grad_upward.astype(BF)], axis=1)
    grad_normed = spread_group(Product([(grad_gates, gate_up)], True))
    feed_keep, feed_send = columns_by(normed_feed, "y", zs)
    gates_keep, gates_got = reduce_pair(feed_keep, feed_send, grad_gates, zs)
    stream_part, grad_feed_gain, grad_feed_bias = norm_backward(
        grad_normed, unit_feed, inverse_feed, norms[4]
    )
    grad_stream = cotangent.astype(F32) + stream_part
    grad_full = pair_rows(grad_stream.astype(BF))
    keep, send = columns_by(grad_full, "x", zs)
    sum_cross_output = reduce_full(keep, send, mixed_cross, zs)
    grad_mixed = nn(grad_full, cross_out_t).astype(BF).reshape(head_shape)
    grad_query, grad_keys, grad_values = attend_backward(
        query_cross, key_cross, value_cross, cross_allowed, total_cross, grad_mixed
    )
    grad_query = grad_query.astype(BF).reshape(seq_len, -1)
    grad_keys = grad_keys.astype(BF).reshape(memory.shape[0], -1)
    grad_values = grad_values.astype(BF).reshape(memory.shape[0], -1)
    grad_normed = spread_pair(grad_query, cross_in)
    keep, send = columns_by(normed_cross, "x", zs)
    sum_cross_query = reduce_full(keep, send, grad_query, zs)
    keep, send = columns_by(memory, "x", zs)
    sum_cross_memory = reduce_full(
        keep, send, jnp.concatenate([grad_keys, grad_values], axis=1), zs
    )
    stream_part, grad_cross_gain, grad_cross_bias = norm_backward(
        grad_normed, unit_cross, inverse_cross, norms[2]
    )
    grad_stream = grad_stream + stream_part
    grad_full = pair_rows(grad_stream.astype(BF))
    keep, send = columns_by(grad_full, "x", zs)
    sum_self_output = reduce_full(keep, send, mixed_self, zs)
    grad_mixed = nn(grad_full, self_out_t).astype(BF).reshape(head_shape)
    grad_query, grad_keys, grad_values = attend_backward(
        query_self, key_self, value_self, self_allowed, total_self, grad_mixed
    )
    grad_query = rotate(grad_query, positions, -1.0).astype(BF).reshape(seq_len, -1)
    grad_keys = rotate(grad_keys, positions, -1.0).astype(BF).reshape(seq_len, -1)
    grad_values = grad_values.astype(BF).reshape(seq_len, -1)
    grad_in = jnp.concatenate([grad_query, grad_keys, grad_values], axis=1)
    keep, send = columns_by(normed_self, "x", zs)
    sum_self_in = reduce_full(keep, send, grad_in, zs).astype(F32)
    grad_normed = spread_pair(grad_in, in_weight)
    _, unit_self, inverse_self = norm_forward(stream, norms[0], norms[1])
    stream_part, grad_self_gain, grad_self_bias = norm_backward(
        grad_normed, unit_self, inverse_self, norms[0]
    )
    grad_stream = grad_stream + stream_part

    vector_sums = jnp.stack(
        [
            grad_self_gain,
            grad_self_bias,
            grad_cross_gain,
            grad_cross_bias,
            grad_feed_gain,
            grad_feed_bias,
        ]
    ).reshape(6, zs, 2, 2, shard_rows)
    y_at = lax.axis_index("y")
    vector_sums = vector_sums + swap(vector_sums, "tensor")
    vector_sums = pick(vector_sums, x_at, 3) + swap(pick(vector_sums, 1 - x_at, 3), "x")
    vector_sums = pick(vector_sums, y_at, 2) + swap(pick(vector_sums, 1 - y_at, 2), "y")
    vector_sums = pick(lax.psum(vector_sums, "z"), lax.axis_index("z"), 1)

    factor = jnp.sqrt(threshold[0] / jnp.maximum(peaks, threshold[0]))
    columns = jnp.repeat(factor, HEAD_DIM)[None, :]
    down_sum = join(down_keep, down_got, "x", 1).T.astype(F32)
    gates_sum = join(
        gates_keep.reshape(-1, 2, 1, ff), gates_got.reshape(-1, 2, 1, ff), "x", 2
    ).astype(F32)
    return (
        result,
        grad_stream,
        vector_sums[0],
        vector_sums[1],
        sum_self_in[:, :inner],
        sum_self_in[:, inner : 2 * inner],
        sum_self_in[:, 2 * inner :],
        sum_self_output.T.astype(F32),
        vector_sums[2],
        vector_sums[3],
        sum_cross_query.astype(F32),
        sum_cross_memory[:, :inner].astype(F32),
        sum_cross_memory[:, inner:].astype(F32),
        sum_cross_output.T.astype(F32),
        vector_sums[4],
        vector_sums[5],
        gates_sum[:, 0].reshape(-1, ff_half),
        gates_sum[:, 1].reshape(-1, ff_half),
        down_sum,
        peaks,
        self_query.astype(F32) * columns,
        self_key.astype(F32) * columns,
        cross_query.astype(F32) * columns,
        cross_key.astype(F32) * columns,
    )


def solution(mesh):
    count = mesh.shape["dp"]
    mesh = Mesh(
        mesh.devices.reshape(count // 4, 2, 2, mesh.shape["tensor"]), ("z", "y", "x", "tensor")
    )
    dp = ("z", "y", "x")
    both = P(dp + ("tensor",), None)
    split = P(dp)
    row_major = P(dp, "tensor")
    column_major = P("tensor", dp)
    in_specs = (
        both,
        both,
        P(dp, None, None),
        P(dp, None),
        split,
        P(),
        split,
        split,
        row_major,
        row_major,
        row_major,
        column_major,
        split,
        split,
        row_major,
        row_major,
        row_major,
        column_major,
        split,
        split,
        row_major,
        row_major,
        column_major,
    )
    out_specs = (
        both,
        both,
        split,
        split,
        row_major,
        row_major,
        row_major,
        column_major,
        split,
        split,
        row_major,
        row_major,
        row_major,
        column_major,
        split,
        split,
        row_major,
        row_major,
        column_major,
        P("tensor"),
        row_major,
        row_major,
        row_major,
        row_major,
    )
    return jax.shard_map(
        per_device, mesh=mesh, in_specs=in_specs, out_specs=out_specs, check_vma=False
    )
```

time: 3360 us -> 1300 us (0.39)
  waiting for transfers between devices: 2670 us -> 489 us
  local copies, waits for them, and re-layouts: 34.5 us -> 195 us
  blocking collectives: 196 us -> 55.9 us
    reduce_scatter x15 -> x7, waiting for transfers between devices: 1770 us -> 0.05 us  [the longest x2 0.04 us: reduce_pair(): held = lax.psum_scatter(held, 'z', scatter_dimension=0, tiled=False)]
    all_gather x17 -> x4, waiting for transfers between devices: 841 us -> 49.6 us  [the longest x2 49.6 us: gather_weights(): held = lax.all_gather(shard, 'z', axis=0, tiled=False)]
    ppermute x0 -> x42, waiting for transfers between devices: none -> 440 us  [swap(): return lax.ppermute(value, axis, [(0, 1), (1, 0)])]
    unnamed x2 -> x0, blocking collectives: 151 us -> none
    unnamed x36 -> x11, waiting for transfers between devices: 54 us -> 0.18 us
    dynamic_update_slice x0 -> x18, local copies, waits for them, and re-layouts: none -> 50 us  [the longest x9 29.5 us: join(): return lax.dynamic_update_slice_in_dim(out, other, (1 - at) * size, dim)]
    slice x0 -> x19, local copies, waits for them, and re-layouts: none -> 37.8 us  [the longest x4 11.2 us: group_rows(): return jnp.concatenate([both[0], other[0], both[1], other[1]], axis=0)]
    ppermute x0 -> x42, starting transfers between devices: none -> 33.8 us  [swap(): return lax.ppermute(value, axis, [(0, 1), (1, 0)])]
  transfers between devices with their start and end apart: 34 -> 53, of which waited for: 30 -> 17; matrix products, arithmetic and copies ran while one was open for 7% -> 48% of each run, Pallas kernels for 0% -> 0%
where the time goes in v1:
time: 1300 us; the launch traced here: 1290 us
  waiting for transfers between devices  489 us (38%)
  matrix products  404 us (31%)
  local copies, waits for them, and re-layouts  195 us (15%)
  other arithmetic  88.9 us (7%)
  blocking collectives  55.9 us (4%)
  starting transfers between devices  35.1 us (3%)
  between operations  17.5 us (1%)
    ppermute x42, waiting for transfers between devices, swap(): return lax.ppermute(value, axis, [(0, 1), (1, 0)])  440 us
    dot_general x16, matrix products, nt(): lax.dot_general(left, right, (((1,), (1,)), ((), ())), preferred_element_...  102 us
    dot_general x8, matrix products, nn(): lax.dot_general(left, right, (((1,), (0,)), ((), ())), preferred_element_...  76 us
    dot_general x14, matrix products, tn(): lax.dot_general(left, right, (((0,), (0,)), ((), ())), preferred_element_...  72.2 us
    all_gather x2, waiting for transfers between devices, gather_weights(): held = lax.all_gather(shard, 'z', axis=0, tiled=False)  49.6 us
    dot_general x2, matrix products, attend_backward(): jnp.einsum('hqk,qhe->khe', grad_raw, query, preferred_element_type=F32)  48.8 us
    dot_general x2, matrix products, attend_backward(): jnp.einsum('hqk,khe->qhe', grad_raw, keys, preferred_element_type=F32)  48.4 us
    pmax x1, blocking collectives, per_device(): peaks = lax.pmax(jnp.maximum(peak_self, peak_cross), ('z', 'y', 'x'))  38.9 us
  transfers between devices with their start and end apart: 53, of which 17 were waited for; matrix products, arithmetic and copies ran while one was open for 48% of the time, Pallas kernels for 0%

profile of v1, /device:TPU:0, one launch (start us, length us, event | category | flops | bytes accessed | tf_op | source)
XLA Modules:
  0.0 1285.8 jit_solution(17216490874967101105)
XLA Ops:
  37.6 17.3 %all-gather.9.cloned.1.call-done = bf16[384,2432]{1,0:T(8,128)(2,1)} async-done(((bf16[96,2432]{1,0:T(8,128)(2,1)}), bf16[384,2432]{1,0:T(8,128)(2,1)}) %all-gather.9.cloned.1.call-update) | async-done | bytes 1867792 | tf_op jit(solution)/shard_map/all_gather | solution.py:33
  74.1 32.3 %all-gather.11.cloned.1.call-done = bf16[384,3072]{1,0:T(8,128)(2,1)} async-done(((bf16[96,3072]{1,0:T(8,128)(2,1)}), bf16[384,3072]{1,0:T(8,128)(2,1)}) %all-gather.11.cloned.1.call-update) | async-done | bytes 2359312 | tf_op jit(solution)/shard_map/all_gather | solution.py:33
  126.2 33.5 %collective-permute-done.3 = bf16[4,1,96,3072]{3,2,0,1:T(8,128)(2,1)} collective-permute-done((bf16[4,1,96,3072]{3,2,0,1:T(8,128)(2,1)}, bf16[4,1,96,3072]{3,2,0,1:T(8,128)(2,1)}, u32[]{:S(2)}, u32[]{:S(2)}) %collective-permute-start.3) | collective-permute-done | bytes 2359328 | tf_op jit(solution)/shard_map/ppermute | solution.py:16
  168.8 26.0 %collective-permute-done.2 = bf16[4,2,1,96,2432]{4,3,2,1,0:T(8,128)(2,1)} collective-permute-done((bf16[4,2,1,96,2432]{4,3,2,1,0:T(8,128)(2,1)}, bf16[4,2,1,96,2432]{4,3,2,1,0:T(8,128)(2,1)}, u32[]{:S(2)}, u32[]{:S(2)}) %collective-permute-start.2) | collective-permute-done | bytes 3735584 | tf_op jit(solution)/shard_map/ppermute | solution.py:16
  200.5 18.1 %fusion.21 = f32[768,2304]{1,0:T(8,128)} fusion(bf16[1536,2432]{1,0:T(8,128)(2,1)S(1)} %bitcast.297, f32[1536]{0:T(1024)S(1)} %get-tuple-element.44, f32[1536]{0:T(1024)S(1)} %get-tuple-element.45, f32[768]{0:T(1024)S(1)} %add_rsqrt_fusion, f32[768]{0:T(1024)S(1)} %broadcast_multiply_fusion.1, bf16[384,1536]{0,1:T(8,128)(2,1)S(1)} %collective-permute-done, ...), kind=kOutput, calls=%fused_computation.37 | convolution fusion | flops 5446434816 | bytes 16539648 | tf_op jit(solution)/shard_map/dot_general | solution.py:49
  232.8 12.1 fusion.208
  244.9 13.2 %fusion.195 = (f32[12]{0:T(128)}, f32[12,768]{1,0:T(8,128)}) fusion(f32[12,768,768]{1,2,0:T(8,128)} %get-tuple-element.125, f32[12,768]{1,0:T(8,128)S(1)} %get-tuple-element.124), kind=kLoop, calls=%fused_computation.358 | loop fusion | flops 21224436 | bytes 28385328 | tf_op jit(solution)/shard_map/reduce_max | solution.py:133
  261.5 11.6 fusion.136
  274.3 20.2 %collective-permute-done.4 = bf16[4,2,1,96,3072]{4,3,2,1,0:T(8,128)(2,1)} collective-permute-done((bf16[4,2,1,96,3072]{4,3,2,1,0:T(8,128)(2,1)}, bf16[4,2,1,96,3072]{4,3,2,1,0:T(8,128)(2,1)}, u32[]{:S(2)}, u32[]{:S(2)}) %collective-permute-start.4) | collective-permute-done | bytes 4718624 | tf_op jit(solution)/shard_map/ppermute | solution.py:16
  317.6 16.1 %collective-permute-done.16 = bf16[384,1536]{0,1:T(8,128)(2,1)} collective-permute-done((bf16[384,1536]{0,1:T(8,128)(2,1)}, bf16[384,1536]{0,1:T(8,128)(2,1)}, u32[]{:S(2)}, u32[]{:S(2)}) %collective-permute-start.16) | collective-permute-done | bytes 1179680 | tf_op jit(solution)/shard_map/ppermute | solution.py:16
  389.8 136.0 %collective-permute-done.12 = bf16[4,1,2,96,1536]{4,3,2,1,0:T(8,128)(2,1)S(1)} collective-permute-done((bf16[4,1,2,96,1536]{4,3,2,1,0:T(8,128)(2,1)}, bf16[4,1,2,96,1536]{4,3,2,1,0:T(8,128)(2,1)S(1)}, u32[]{:S(2)}, u32[]{:S(2)}) %collective-permute-start.12) | collective-permute-done | bytes 2359328 | tf_op jit(solution)/shard_map/ppermute | solution.py:16
  546.6 38.9 %pmax.7 = f32[12]{0:T(128)S(1)} all-reduce(f32[12]{0:T(128)S(1)} %max.9), channel_id=1, replica_groups=mesh['z'=4,'y'=2,'x'=2,'tensor'=2] {'z','y','x'}, use_global_device_ids=true, to_apply=%region_36.37 | all-reduce | flops 12 | bytes 96 | tf_op jit(solution)/shard_map/pmax | solution.py:311
  599.4 19.8 %fusion.29 = f32[1536,3072]{1,0:T(8,128)} fusion(bf16[1536,3072]{1,0:T(8,128)(2,1)} %bitcast.43, bf16[384,1536]{1,0:T(8,128)(2,1)S(1)} %get-tuple-element.73, bf16[384,1536]{1,0:T(8,128)(2,1)S(1)} %copy-done.41, bf16[384,1536]{1,0:T(8,128)(2,1)S(1)} %get-tuple-element.72, bf16[384,1536]{1,0:T(8,128)(2,1)S(1)} %add_convert_fusion.8), kind=kOutput, calls=%fused_computation.51 | convolution fusion | flops 14514388992 | bytes 33030144 | tf_op jit(solution)/shard_map/dot_general | solution.py:49
  619.2 21.4 %multiply_convert_fusion.1 = (bf16[1536,1536]{1,0:T(8,128)(2,1)}, bf16[1536,1536]{1,0:T(8,128)(2,1)}, bf16[1536,1536]{1,0:T(8,128)(2,1)}) fusion(f32[1536,3072]{1,0:T(8,128)} %fusion.29, bf16[1536,1536]{1,0:T(8,128)(2,1)} %bitcast.331, bf16[384,1536]{0,1:T(8,128)(2,1)} %get-tuple-element.69, bf16[384,1536]{0,1:T(8,128)(2,1)} %collective-permute-done.16, ...), kind=kOutput, calls=%fused_computation.20 | convolution fusion | flops 7304380416 | bytes 42467328 | tf_op jit(solution)/shard_map/dot_general | solution.py:49
  640.6 9.8 fusion.95
  659.6 9.7 fusion.90
  681.5 13.6 %fusion.23 = bf16[768,3072]{1,0:T(8,128)(2,1)} fusion(bf16[1536,768]{0,1:T(8,128)(2,1)S(1)} %bitcast.360, bf16[1536,1536]{1,0:T(8,128)(2,1)} %get-tuple-element.50, bf16[1536,1536]{1,0:T(8,128)(2,1)} %get-tuple-element.51), kind=kOutput, calls=%fused_computation.40 | convolution fusion | flops 7268990976 | bytes 16515072 | tf_op jit(solution)/shard_map/dot_general | solution.py:57
  695.1 14.2 %collective-permute-done.20 = bf16[384,1536]{1,0:T(8,128)(2,1)S(1)} collective-permute-done((bf16[384,1536]{1,0:T(8,128)(2,1)S(1)}, bf16[384,1536]{1,0:T(8,128)(2,1)S(1)}, u32[]{:S(2)}, u32[]{:S(2)}) %collective-permute-start.20) | collective-permute-done | bytes 1179680 | tf_op jit(solution)/shard_map/ppermute | solution.py:16
  709.3 10.3 multiply_reduce_fusion.2
  747.7 10.3 fusion.142
  768.5 10.4 fusion.124
  797.3 46.9 %collective-permute-done.35 = bf16[4,48,1536]{2,1,0:T(8,128)(2,1)S(1)} collective-permute-done((bf16[4,48,1536]{2,1,0:T(8,128)(2,1)S(1)}, bf16[4,48,1536]{2,1,0:T(8,128)(2,1)S(1)}, u32[]{:S(2)}, u32[]{:S(2)}) %collective-permute-start.35) | collective-permute-done | bytes 589856 | tf_op jit(solution)/shard_map/ppermute | solution.py:16
  864.3 13.5 %add_convert_fusion = bf16[768,3072]{1,0:T(8,128)(2,1)} fusion(bf16[768,3072]{1,0:T(8,128)(2,1)} %collective-permute-done.38, bf16[1536,768]{0,1:T(8,128)(2,1)S(1)} %bitcast.357, bf16[1536,1536]{1,0:T(8,128)(2,1)} %get-tuple-element.50, bf16[1536,1536]{1,0:T(8,128)(2,1)} %get-tuple-element.51), kind=kOutput, calls=%fused_computation.19 | convolution fusion | flops 7273709568 | bytes 21233664 | tf_op jit(solution)/shard_map/dot_general | solution.py:57
  914.1 11.2 fusion.213
  925.4 38.6 %fusion.121 = f32[768,12,64]{0,2,1:T(8,128)} fusion(f32[12,768,768]{1,2,0:T(8,128)} %fusion.213, f32[12,768,768]{1,2,0:T(8,128)} %get-tuple-element.125, f32[12,768]{1,0:T(8,128)} %copy-done.75, bf16[768,12,32]{0,2,1:T(8,128)(2,1)} %copy-done.73, bf16[768,12,16]{0,2,1:T(8,128)(2,1)} %copy-done.82, bf16[768,12,16]{0,2,1:T(8,128)(2,1)} %copy-done.81), kind=kOutput, calls=%fused_computation.172 | convolution fusion | flops 959063808 | bytes 60198912 | tf_op jit(solution)/shard_map/hqk,qhe->khe/dot_general | solution.py:154
  966.1 38.0 %fusion.118 = f32[768,12,64]{0,2,1:T(8,128)} fusion(f32[12,768,768]{1,2,0:T(8,128)} %fusion.213, f32[12,768,768]{1,2,0:T(8,128)} %get-tuple-element.125, f32[12,768]{1,0:T(8,128)} %copy-done.75, bf16[768,12,32]{0,2,1:T(8,128)(2,1)} %copy-done.72, bf16[768,12,16]{0,2,1:T(8,128)(2,1)} %copy-done.79, bf16[768,12,16]{0,2,1:T(8,128)(2,1)} %copy-done.80), kind=kOutput, calls=%fused_computation.171 | convolution fusion | flops 959063808 | bytes 60198912 | tf_op jit(solution)/shard_map/hqk,khe->qhe/dot_general | solution.py:153
  1007.8 12.5 fusion.139
  1041.6 90.9 %collective-permute-done.36 = bf16[768,768]{1,0:T(8,128)(2,1)} collective-permute-done((bf16[768,768]{1,0:T(8,128)(2,1)}, bf16[768,768]{1,0:T(8,128)(2,1)}, u32[]{:S(2)}, u32[]{:S(2)}) %collective-permute-start.36) | collective-permute-done | bytes 1179680 | tf_op jit(solution)/shard_map/ppermute | solution.py:16
  1141.0 15.7 %collective-permute-done.30 = bf16[768,768]{1,0:T(8,128)(2,1)S(1)} collective-permute-done((bf16[768,768]{1,0:T(8,128)(2,1)S(1)}, bf16[768,768]{1,0:T(8,128)(2,1)S(1)}, u32[]{:S(2)}, u32[]{:S(2)}) %collective-permute-start.30) | collective-permute-done | bytes 1179680 | tf_op jit(solution)/shard_map/ppermute | solution.py:16
  1179.1 9.7 fusion.84
  1190.2 22.3 %collective-permute-done.29 = bf16[4,96,2304]{2,1,0:T(8,128)(2,1)} collective-permute-done((bf16[4,96,2304]{2,1,0:T(8,128)(2,1)S(1)}, bf16[4,96,2304]{2,1,0:T(8,128)(2,1)}, u32[]{:S(2)}, u32[]{:S(2)}) %collective-permute-start.29) | collective-permute-done | bytes 1769504 | tf_op jit(solution)/shard_map/ppermute | solution.py:16
  1233.7 17.0 %psum.7 = f32[6,4,96]{2,1,0:T(4,128)S(1)} all-reduce(f32[6,4,96]{2,1,0:T(4,128)S(1)} %add.366), channel_id=1, replica_groups=mesh['z'=4,'y'=2,'x'=2,'tensor'=2] {'z'}, use_global_device_ids=true, to_apply=%region_26.27 | all-reduce | flops 2304 | bytes 18432 | tf_op jit(solution)/shard_map/psum | solution.py:381
  (580 shorter events, 457.2 us)
Async XLA Ops:
  7.2 47.7 %all-gather.9.cloned.1.call-start = ((), (), s32[]{:S(2)}) async-start(), calls=%async_computation.14 | async-start | bytes 2334720 | tf_op jit(solution)/shard_map/all_gather | solution.py:33
  10.1 96.3 %all-gather.11.cloned.1.call-start = ((), (), s32[]{:S(2)}) async-start(), calls=%async_computation.15 | async-start | bytes 2949120 | tf_op jit(solution)/shard_map/all_gather | solution.py:33
  12.2 359.1 %all-gather.13.cloned.1.call-start = ((), (), s32[]{:S(2)}) async-start(), calls=%async_computation.16 | async-start | bytes 5898240 | tf_op jit(solution)/shard_map/all_gather | solution.py:42
  13.0 104.1 %collective-permute-start = (bf16[384,1536]{0,1:T(8,128)(2,1)S(1)}, bf16[384,1536]{0,1:T(8,128)(2,1)S(1)}, u32[]{:S(2)}, u32[]{:S(2)}) collective-permute-start(bf16[384,1536]{0,1:T(8,128)(2,1)S(1)} %copy.162), channel_id=1, source_target_pairs={{0,1},{1,0},{2,3},{3,2},{4,5},{5,4},{6,7},{7,6},{8,9},{9,8},{10,11... | collective-permute-start | bytes 3538952 | tf_op jit(solution)/shard_map/ppermute | solution.py:16
  54.9 53.0 %collective-permute-start.1 = (bf16[4,1,96,2432]{3,2,0,1:T(8,128)(2,1)}, bf16[4,1,96,2432]{3,2,0,1:T(8,128)(2,1)}, u32[]{:S(2)}, u32[]{:S(2)}) collective-permute-start(bf16[4,1,96,2432]{3,2,0,1:T(8,128)(2,1)} %bitcast.368), channel_id=1, source_target_pairs={{0,4},{4,0},{1,5},{5,1},{2,6},{6,2},{3,7},{7,3},{8,12},{12,8},{9,1... | collective-permute-start | bytes 5603336 | tf_op jit(solution)/shard_map/ppermute | solution.py:16
  60.9 51.4 %collective-permute-start.10 = (bf16[96,4608]{1,0:T(8,128)(2,1)}, bf16[96,4608]{1,0:T(8,128)(2,1)}, u32[]{:S(2)}, u32[]{:S(2)}) collective-permute-start(bf16[96,4608]{1,0:T(8,128)(2,1)} %bitcast.169), channel_id=1, source_target_pairs={{0,2},{2,0},{1,3},{3,1},{4,6},{6,4},{5,7},{7,5},{8,10},{10,8},{9,1... | collective-permute-start | bytes 2654216 | tf_op jit(solution)/shard_map/ppermute | solution.py:16
  106.4 53.3 %collective-permute-start.3 = (bf16[4,1,96,3072]{3,2,0,1:T(8,128)(2,1)}, bf16[4,1,96,3072]{3,2,0,1:T(8,128)(2,1)}, u32[]{:S(2)}, u32[]{:S(2)}) collective-permute-start(bf16[4,1,96,3072]{3,2,0,1:T(8,128)(2,1)} %bitcast.363), channel_id=1, source_target_pairs={{0,4},{4,0},{1,5},{5,1},{2,6},{6,2},{3,7},{7,3},{8,12},{12,8},{9,1... | collective-permute-start | bytes 7077896 | tf_op jit(solution)/shard_map/ppermute | solution.py:16
  110.8 84.0 %collective-permute-start.2 = (bf16[4,2,1,96,2432]{4,3,2,1,0:T(8,128)(2,1)}, bf16[4,2,1,96,2432]{4,3,2,1,0:T(8,128)(2,1)}, u32[]{:S(2)}, u32[]{:S(2)}) collective-permute-start(bf16[4,2,1,96,2432]{4,3,2,1,0:T(8,128)(2,1)} %bitcast_dynamic-update-slice_fusion.1), channel_id=1, source_target_pairs={{0,2},{2,0},{1,3},{3,1},{4,6},{6,4},{5,7},{7,5},{8,10},{10,8},{9,1... | collective-permute-start | bytes 11206664 | tf_op jit(solution)/shard_map/ppermute | solution.py:16
  116.8 259.9 %all-gather.15.cloned.1.call-start = ((), (), s32[]{:S(2)}) async-start(), calls=%async_computation.17 | async-start | bytes 2949120 | tf_op jit(solution)/shard_map/all_gather | solution.py:42
  162.9 131.5 %collective-permute-start.4 = (bf16[4,2,1,96,3072]{4,3,2,1,0:T(8,128)(2,1)}, bf16[4,2,1,96,3072]{4,3,2,1,0:T(8,128)(2,1)}, u32[]{:S(2)}, u32[]{:S(2)}) collective-permute-start(bf16[4,2,1,96,3072]{4,3,2,1,0:T(8,128)(2,1)} %bitcast_dynamic-update-slice_fusion), channel_id=1, source_target_pairs={{0,2},{2,0},{1,3},{3,1},{4,6},{6,4},{5,7},{7,5},{8,10},{10,8},{9,1... | collective-permute-start | bytes 14155784 | tf_op jit(solution)/shard_map/ppermute | solution.py:16
  317.1 582.8 %reduce-scatter.20.cloned.1.call-start = ((), (), s32[]{:S(2)}) async-start(), calls=%async_computation.13 | async-start | bytes 2949120 | tf_op jit(solution)/shard_map/reduce_scatter | solution.py:89
  371.3 170.6 %collective-permute-start.11 = (bf16[4,1,2,96,3072]{4,3,2,1,0:T(8,128)(2,1)}, bf16[4,1,2,96,3072]{4,3,2,1,0:T(8,128)(2,1)}, u32[]{:S(2)}, u32[]{:S(2)}) collective-permute-start(bf16[4,1,2,96,3072]{4,3,2,1,0:T(8,128)(2,1)} %bitcast.327), channel_id=1, source_target_pairs={{0,4},{4,0},{1,5},{5,1},{2,6},{6,2},{3,7},{7,3},{8,12},{12,8},{9,1... | collective-permute-start | bytes 14155784 | tf_op jit(solution)/shard_map/ppermute | solution.py:16
  376.7 149.1 %collective-permute-start.12 = (bf16[4,1,2,96,1536]{4,3,2,1,0:T(8,128)(2,1)}, bf16[4,1,2,96,1536]{4,3,2,1,0:T(8,128)(2,1)S(1)}, u32[]{:S(2)}, u32[]{:S(2)}) collective-permute-start(bf16[4,1,2,96,1536]{4,3,2,1,0:T(8,128)(2,1)} %bitcast.365), channel_id=1, source_target_pairs={{0,4},{4,0},{1,5},{5,1},{2,6},{6,2},{3,7},{7,3},{8,12},{12,8},{9,1... | collective-permute-start | bytes 7077896 | tf_op jit(solution)/shard_map/ppermute | solution.py:16
  383.0 143.7 %collective-permute-start.8 = (bf16[384,1536]{1,0:T(8,128)(2,1)S(1)}, bf16[384,1536]{1,0:T(8,128)(2,1)S(1)}, u32[]{:S(2)}, u32[]{:S(2)}) collective-permute-start(bf16[384,1536]{1,0:T(8,128)(2,1)S(1)} %add_convert_fusion.8), channel_id=1, source_target_pairs={{0,2},{2,0},{1,3},{3,1},{4,6},{6,4},{5,7},{7,5},{8,10},{10,8},{9,1... | collective-permute-start | bytes 3538952 | tf_op jit(solution)/shard_map/ppermute | solution.py:16
  529.9 66.1 %collective-permute-start.9 = (bf16[2,384,1536]{2,1,0:T(8,128)(2,1)}, bf16[2,384,1536]{2,1,0:T(8,128)(2,1)}, u32[]{:S(2)}, u32[]{:S(2)}) collective-permute-start(bf16[2,384,1536]{2,1,0:T(8,128)(2,1)} %pad_maximum_fusion.12), channel_id=1, source_target_pairs={{0,1},{1,0},{2,3},{3,2},{4,5},{5,4},{6,7},{7,6},{8,9},{9,8},{10,11... | collective-permute-start | bytes 7077896 | tf_op jit(solution)/shard_map/ppermute | solution.py:16
  655.5 73.9 %collective-permute-start.40 = (bf16[768,1536]{1,0:T(8,128)(2,1)}, bf16[768,1536]{1,0:T(8,128)(2,1)}, u32[]{:S(2)}, u32[]{:S(2)}) collective-permute-start(bf16[768,1536]{1,0:T(8,128)(2,1)} %convolution_convert_fusion.1), channel_id=1, source_target_pairs={{0,4},{4,0},{1,5},{5,1},{2,6},{6,2},{3,7},{7,3},{8,12},{12,8},{9,1... | collective-permute-start | bytes 7077896 | tf_op jit(solution)/shard_map/ppermute | solution.py:16
  726.8 137.5 %collective-permute-start.38 = (bf16[768,3072]{1,0:T(8,128)(2,1)}, bf16[768,3072]{1,0:T(8,128)(2,1)}, u32[]{:S(2)}, u32[]{:S(2)}) collective-permute-start(bf16[768,3072]{1,0:T(8,128)(2,1)} %fusion.23), channel_id=1, source_target_pairs={{0,4},{4,0},{1,5},{5,1},{2,6},{6,2},{3,7},{7,3},{8,12},{12,8},{9,1... | collective-permute-start | bytes 14155784 | tf_op jit(solution)/shard_map/ppermute | solution.py:16
  728.8 63.0 %collective-permute-start.14 = (f32[384,1536]{1,0:T(8,128)}, f32[384,1536]{1,0:T(8,128)}, u32[]{:S(2)}, u32[]{:S(2)}) collective-permute-start(f32[384,1536]{1,0:T(8,128)} %fusion.145), channel_id=1, source_target_pairs={{0,1},{1,0},{2,3},{3,2},{4,5},{5,4},{6,7},{7,6},{8,9},{9,8},{10,11... | collective-permute-start | bytes 7077896 | tf_op jit(solution)/shard_map/ppermute | solution.py:16
  735.8 437.7 %reduce-scatter.14.cloned.1.call-start = ((), (), s32[]{:S(2)}) async-start(), calls=%async_computation.10 | async-start | bytes 737280 | tf_op jit(solution)/shard_map/reduce_scatter | solution.py:82
  768.5 118.9 %collective-permute-start.13 = (f32[384,1536]{1,0:T(8,128)}, f32[384,1536]{1,0:T(8,128)}, u32[]{:S(2)}, u32[]{:S(2)}) collective-permute-start(f32[384,1536]{1,0:T(8,128)} %fusion.148), channel_id=1, source_target_pairs={{0,1},{1,0},{2,3},{3,2},{4,5},{5,4},{6,7},{7,6},{8,9},{9,8},{10,11... | collective-permute-start | bytes 7077896 | tf_op jit(solution)/shard_map/ppermute | solution.py:16
  782.6 62.7 %collective-permute-start.32 = (bf16[768,768]{1,0:T(8,128)(2,1)}, bf16[768,768]{1,0:T(8,128)(2,1)}, u32[]{:S(2)}, u32[]{:S(2)}) collective-permute-start(bf16[768,768]{1,0:T(8,128)(2,1)} %convolution_convert_fusion.5), channel_id=1, source_target_pairs={{0,2},{2,0},{1,3},{3,1},{4,6},{6,4},{5,7},{7,5},{8,10},{10,8},{9,1... | collective-permute-start | bytes 3538952 | tf_op jit(solution)/shard_map/ppermute | solution.py:16
  791.7 52.5 %collective-permute-start.35 = (bf16[4,48,1536]{2,1,0:T(8,128)(2,1)S(1)}, bf16[4,48,1536]{2,1,0:T(8,128)(2,1)S(1)}, u32[]{:S(2)}, u32[]{:S(2)}) collective-permute-start(bf16[4,48,1536]{2,1,0:T(8,128)(2,1)S(1)} %dynamic-slice_bitcast_fusion.3), channel_id=1, source_target_pairs={{0,4},{4,0},{1,5},{5,1},{2,6},{6,2},{3,7},{7,3},{8,12},{12,8},{9,1... | collective-permute-start | bytes 1769480 | tf_op jit(solution)/shard_map/ppermute | solution.py:16
  797.2 90.2 %collective-permute-start.15 = (bf16[384,1536]{1,0:T(8,128)(2,1)}, bf16[384,1536]{1,0:T(8,128)(2,1)}, u32[]{:S(2)}, u32[]{:S(2)}) collective-permute-start(bf16[384,1536]{1,0:T(8,128)(2,1)} %fusion.73), channel_id=1, source_target_pairs={{0,2},{2,0},{1,3},{3,1},{4,6},{6,4},{5,7},{7,5},{8,10},{10,8},{9,1... | collective-permute-start | bytes 3538952 | tf_op jit(solution)/shard_map/ppermute | solution.py:16
  845.2 330.0 %reduce-scatter.12.cloned.1.call-start = ((), (), s32[]{:S(2)}) async-start(), calls=%async_computation.9 | async-start | bytes 737280 | tf_op jit(solution)/shard_map/reduce_scatter | solution.py:82
  864.2 366.6 %reduce-scatter.18.cloned.1.call-start = ((), (), s32[]{:S(2)}) async-start(), calls=%async_computation.12 | async-start | bytes 5898240 | tf_op jit(solution)/shard_map/reduce_scatter | solution.py:89
  877.9 373.4 %reduce-scatter.16.cloned.1.call-start = ((), (), s32[]{:S(2)}) async-start(), calls=%async_computation.11 | async-start | bytes 737280 | tf_op jit(solution)/shard_map/reduce_scatter | solution.py:82
  901.7 133.4 %collective-permute-start.41 = (bf16[96,1536]{1,0:T(8,128)(2,1)}, bf16[96,1536]{1,0:T(8,128)(2,1)}, u32[]{:S(2)}, u32[]{:S(2)}) collective-permute-start(bf16[96,1536]{1,0:T(8,128)(2,1)} %dynamic-slice_bitcast_fusion.6), channel_id=1, source_target_pairs={{0,2},{2,0},{1,3},{3,1},{4,6},{6,4},{5,7},{7,5},{8,10},{10,8},{9,1... | collective-permute-start | bytes 884744 | tf_op jit(solution)/shard_map/ppermute | solution.py:16
  1027.5 135.0 %collective-permute-start.28 = (bf16[768,2304]{1,0:T(8,128)(2,1)}, bf16[768,2304]{1,0:T(8,128)(2,1)}, u32[]{:S(2)}, u32[]{:S(2)}) collective-permute-start(bf16[768,2304]{1,0:T(8,128)(2,1)} %convolution_convert_fusion), channel_id=1, source_target_pairs={{0,2},{2,0},{1,3},{3,1},{4,6},{6,4},{5,7},{7,5},{8,10},{10,8},{9,1... | collective-permute-start | bytes 10616840 | tf_op jit(solution)/shard_map/ppermute | solution.py:16
  1033.2 99.3 %collective-permute-start.36 = (bf16[768,768]{1,0:T(8,128)(2,1)}, bf16[768,768]{1,0:T(8,128)(2,1)}, u32[]{:S(2)}, u32[]{:S(2)}) collective-permute-start(bf16[768,768]{1,0:T(8,128)(2,1)} %convolution_convert_fusion.4), channel_id=1, source_target_pairs={{0,2},{2,0},{1,3},{3,1},{4,6},{6,4},{5,7},{7,5},{8,10},{10,8},{9,1... | collective-permute-start | bytes 3538952 | tf_op jit(solution)/shard_map/ppermute | solution.py:16
  1039.4 117.3 %collective-permute-start.30 = (bf16[768,768]{1,0:T(8,128)(2,1)S(1)}, bf16[768,768]{1,0:T(8,128)(2,1)S(1)}, u32[]{:S(2)}, u32[]{:S(2)}) collective-permute-start(bf16[768,768]{1,0:T(8,128)(2,1)S(1)} %convolution_convert_fusion.6), channel_id=1, source_target_pairs={{0,2},{2,0},{1,3},{3,1},{4,6},{6,4},{5,7},{7,5},{8,10},{10,8},{9,1... | collective-permute-start | bytes 3538952 | tf_op jit(solution)/shard_map/ppermute | solution.py:16
  1162.5 90.4 %reduce-scatter.10.cloned.1.call-start = ((), (), s32[]{:S(2)}) async-start(), calls=%async_computation.8 | async-start | bytes 737280 | tf_op jit(solution)/shard_map/reduce_scatter | solution.py:82
  1179.0 97.8 %reduce-scatter.8.cloned.1.call-start = ((), (), s32[]{:S(2)}) async-start(), calls=%async_computation.7 | async-start | bytes 2211840 | tf_op jit(solution)/shard_map/reduce_scatter | solution.py:82
  (150 other events, 3206.9 us)
Sparse Core Ops, SparseCore 0:
  10.2 44.6 all-gather.8
  57.0 49.3 all-gather.10
  117.0 86.4 all-gather.12
  317.2 48.6 all-gather.14
  735.9 44.0 reduce-scatter.19
  845.3 19.6 reduce-scatter.13
  867.3 20.4 reduce-scatter.11
  890.1 83.6 reduce-scatter.17
  1162.6 19.4 reduce-scatter.15
  1184.8 20.2 reduce-scatter.9
  1216.5 37.2 reduce-scatter.7

commit v2 on v1

--- a/solution.py
+++ b/solution.py
@@ -1,6 +1,10 @@
+import functools
+
 import jax
 import jax.numpy as jnp
 from jax import lax
+from jax.experimental import pallas as pl
+from jax.experimental.pallas import tpu as pltpu
 from jax.sharding import Mesh
 from jax.sharding import PartitionSpec as P
 
@@ -29,20 +33,489 @@
     return lax.dynamic_index_in_dim(value, index, dim, keepdims=False)
 
 
-def gather_weights(shard):
-    held = lax.all_gather(shard, "z", axis=0, tiled=False)
-    held = held[:, None]
-    held = join(held, swap(held, "y"), "y", 1)
-    held = held[:, :, None]
-    held = join(held, swap(held, "x"), "x", 2)
-    return held.reshape(-1, shard.shape[1])
-
-
-def gather_pair_weights(held):
-    held = lax.all_gather(held, "z", axis=0, tiled=False)
-    held = held[:, None]
-    held = join(held, swap(held, "y"), "y", 1)
-    return held.reshape(-1, held.shape[-1])
+class Lanes:
+    def __init__(self, send_sems, recv_sems, local_sems, zs):
+        self.send_sems, self.recv_sems, self.local_sems = send_sems, recv_sems, local_sems
+        self.used = self.used_local = 0
+        self.z = lax.axis_index("z")
+        self.y = lax.axis_index("y")
+        self.x = lax.axis_index("x")
+        self.zs = zs
+
+    def local(self):
+        self.used_local += 1
+        return self.local_sems.at[self.used_local - 1]
+
+    def copy(self, source, target, device):
+        return self.copies([source], target, device)[0]
+
+    def copies(self, sources, target, device):
+        slot = self.used
+        self.used += 1
+        return [
+            pltpu.make_async_remote_copy(
+                src_ref=source,
+                dst_ref=target,
+                send_sem=self.send_sems.at[slot],
+                recv_sem=self.recv_sems.at[slot],
+                device_id=device,
+                device_id_type=pl.DeviceIdType.MESH,
+            )
+            for source in sources
+        ]
+
+
+def guarded(condition, action):
+    if condition is None:
+        action()
+    else:
+        pl.when(condition)(action)
+
+
+class Move:
+    def __init__(self, copy, sends, receives):
+        self.copy_, self.sends, self.receives = copy, sends, receives
+
+    def start(self):
+        guarded(self.sends, self.copy_.start)
+
+    def arrived(self):
+        guarded(self.receives, self.copy_.wait_recv)
+
+    def sent(self):
+        guarded(self.sends, self.copy_.wait_send)
+
+
+class Gather:
+    def __init__(self, lanes, own, whole):
+        zs, z, y, x = lanes.zs, lanes.z, lanes.y, lanes.x
+        self.lanes, self.own, self.whole = lanes, own, whole
+
+        def block(zz, yy):
+            return whole.at[zz, yy, x]
+
+        def along(source, target, axis, to, sends=None, receives=None):
+            return Move(lanes.copy(source, target, {axis: to}), sends, receives)
+
+        self.first = [
+            along(own, block(z, y), "y", 1 - y),
+            along(own, block(z, y), "x", 1 - x),
+        ]
+        self.far = [[along(block(z, 1 - y), block(z, 1 - y), "x", 1 - x)]]
+        self.steps = []
+        for k in range(zs - 1):
+            right, left = jnp.maximum(z - k, 0), jnp.minimum(z + k, zs - 1)
+            step = []
+            for zz, to, sends, receives, got in (
+                (right, z + 1, (z >= k) & (z < zs - 1), z >= k + 1, jnp.maximum(z - 1 - k, 0)),
+                (left, z - 1, (z + k < zs) & (z > 0), z + k + 1 < zs, jnp.minimum(z + 1 + k, zs - 1)),
+            ):
+                source = own if k == 0 else block(zz, y)
+                move = along(source, block(zz, y), "z", to, sends, receives)
+                follow = [
+                    along(block(got, y), block(got, y), "y", 1 - y, receives, receives),
+                    along(block(got, y), block(got, y), "x", 1 - x, receives, receives),
+                    along(block(got, 1 - y), block(got, 1 - y), "x", 1 - x, receives, receives),
+                ]
+                step.append((move, follow))
+            self.steps.append(step)
+
+    def begin(self):
+        for move, _ in self.steps[0]:
+            move.start()
+        for move in self.first:
+            move.start()
+
+    def step(self, k):
+        for side in range(2):
+            move, follow = self.steps[k][side]
+            move.arrived()
+            if k + 1 < len(self.steps):
+                self.steps[k + 1][side][0].start()
+            follow[0].start()
+            follow[1].start()
+
+    def far_first(self):
+        self.first[0].arrived()
+        self.far[0][0].start()
+
+    def far_step(self, k):
+        for side in range(2):
+            _, follow = self.steps[k][side]
+            follow[0].arrived()
+            follow[2].start()
+
+    def finish(self):
+        self.first[1].arrived()
+        self.far[0][0].arrived()
+        for step in self.steps:
+            for _, follow in step:
+                follow[1].arrived()
+                follow[2].arrived()
+        for move in self.first + self.far[0]:
+            move.sent()
+        for step in self.steps:
+            for move, follow in step:
+                move.sent()
+                for other in follow:
+                    other.sent()
+
+
+class PairGather:
+    def __init__(self, lanes, kept, sent, whole, y_first):
+        zs, z, y, x = lanes.zs, lanes.z, lanes.y, lanes.x
+        self.y_first = y_first
+
+        def along(piece, axis, to, sends=None, receives=None):
+            return Move(lanes.copy(piece, piece, {axis: to}), sends, receives)
+
+        self.swap = Move(lanes.copy(sent, whole.at[z, y, x], {"x": 1 - x}), None, None)
+        self.local = pltpu.make_async_copy(kept, whole.at[z, y, x], lanes.local())
+        self.own_y = along(whole.at[z, y], "y", 1 - y)
+        self.steps = []
+        for k in range(zs - 1):
+            step = []
+            for zz, to, sends, receives, got in (
+                (jnp.maximum(z - k, 0), z + 1, (z >= k) & (z < zs - 1), z >= k + 1, jnp.maximum(z - 1 - k, 0)),
+                (jnp.minimum(z + k, zs - 1), z - 1, (z + k < zs) & (z > 0), z + k + 1 < zs, jnp.minimum(z + 1 + k, zs - 1)),
+            ):
+                piece = whole.at[zz] if y_first else whole.at[zz, y]
+                move = along(piece, "z", to, sends, receives)
+                follow = [] if y_first else [along(whole.at[got, y], "y", 1 - y, receives, receives)]
+                step.append((move, follow))
+            self.steps.append(step)
+
+    def begin(self):
+        self.swap.start()
+        self.local.start()
+
+    def swapped(self):
+        self.swap.arrived()
+        self.local.wait()
+        self.own_y.start()
+        if not self.y_first:
+            for move, _ in self.steps[0]:
+                move.start()
+
+    def own_y_arrived(self):
+        self.own_y.arrived()
+        if self.y_first:
+            for move, _ in self.steps[0]:
+                move.start()
+
+    def step(self, k):
+        for side in range(2):
+            move, follow = self.steps[k][side]
+            move.arrived()
+            if k + 1 < len(self.steps):
+                self.steps[k + 1][side][0].start()
+            for other in follow:
+                other.start()
+
+    def finish(self):
+        if not self.y_first:
+            self.own_y.arrived()
+        for step in self.steps:
+            for move, follow in step:
+                for other in follow:
+                    other.arrived()
+        self.swap.sent()
+        self.own_y.sent()
+        for step in self.steps:
+            for move, follow in step:
+                move.sent()
+                for other in follow:
+                    other.sent()
+
+
+def greet(zs):
+    z, y, x = lax.axis_index("z"), lax.axis_index("y"), lax.axis_index("x")
+    barrier = pltpu.get_barrier_semaphore()
+
+    def signal(device):
+        pl.semaphore_signal(barrier, inc=1, device_id=device, device_id_type=pl.DeviceIdType.MESH)
+
+    signal({"x": 1 - x})
+    signal({"y": 1 - y})
+    pl.when(z > 0)(lambda: signal({"z": z - 1}))
+    pl.when(z < zs - 1)(lambda: signal({"z": z + 1}))
+    peers = 2 + (z > 0).astype(jnp.int32) + (z < zs - 1).astype(jnp.int32)
+    pl.semaphore_wait(barrier, peers)
+
+
+def gather_kernel(zs, groups, pairs, *refs):
+    owns = refs[:groups]
+    pair_in = refs[groups : groups + 2 * pairs]
+    outs = refs[groups + 2 * pairs : 2 * groups + 3 * pairs]
+    send_sems, recv_sems, local_sems = refs[2 * groups + 3 * pairs :]
+    lanes = Lanes(send_sems, recv_sems, local_sems, zs)
+    greet(zs)
+    gathers = [Gather(lanes, own, whole) for own, whole in zip(owns, outs)]
+    quarters = [
+        PairGather(lanes, pair_in[2 * i], pair_in[2 * i + 1], outs[groups + i], i == 0)
+        for i in range(pairs)
+    ]
+    locals_ = [
+        pltpu.make_async_copy(own, whole.at[lanes.z, lanes.y, lanes.x], lanes.local())
+        for own, whole in zip(owns, outs)
+    ]
+    for quarter in quarters:
+        quarter.begin()
+    for copy, gather in zip(locals_, gathers):
+        copy.start()
+        gather.begin()
+    for quarter in quarters:
+        quarter.swapped()
+    for gather in gathers:
+        gather.far_first()
+    for k in range(zs - 1):
+        for gather in gathers:
+            gather.step(k)
+        for quarter in quarters:
+            if quarter.y_first:
+                if k == 0:
+                    quarter.own_y_arrived()
+            else:
+                quarter.step(k)
+        for gather in gathers:
+            gather.far_step(k)
+        for quarter in quarters:
+            if quarter.y_first:
+                quarter.step(k)
+    for copy in locals_:
+        copy.wait()
+    for gather in gathers:
+        gather.finish()
+    for quarter in quarters:
+        quarter.finish()
+
+
+def gather_all(shards, quarters, zs):
+    groups, pairs = len(shards), len(quarters)
+    flat = list(shards) + [array for pair in quarters for array in pair]
+    outs = [
+        jax.ShapeDtypeStruct((zs, 2, 2) + array.shape, array.dtype)
+        for array in list(shards) + [kept for kept, _ in quarters]
+    ]
+    moves = groups * (3 + 8 * (zs - 1)) + pairs * (2 + 4 * (zs - 1))
+    hbm = pl.BlockSpec(memory_space=pltpu.HBM)
+    return pl.pallas_call(
+        functools.partial(gather_kernel, zs, groups, pairs),
+        out_shape=outs,
+        in_specs=[hbm] * len(flat),
+        out_specs=[hbm] * len(outs),
+        scratch_shapes=[
+            pltpu.SemaphoreType.DMA((moves,)),
+            pltpu.SemaphoreType.DMA((moves,)),
+            pltpu.SemaphoreType.DMA((groups + pairs,)),
+        ],
+        compiler_params=pltpu.CompilerParams(collective_id=1, has_side_effects=True),
+    )(*flat)
+
+
+def plus(*terms):
+    total = terms[0].astype(F32)
+    for term in terms[1:]:
+        total = total + term.astype(F32)
+    return total
+
+
+def ends_first(zs):
+    order = []
+    for i in range(zs // 2):
+        order += [zs - 1 - i, i]
+    return order
+
+
+class Line:
+    def __init__(self, lanes, part, from_left, from_right):
+        zs, z = lanes.zs, lanes.z
+        self.zs, self.z, self.part = zs, z, part
+        self.from_left, self.from_right = from_left, from_right
+        self.right, self.left = {}, {}
+        for d in ends_first(zs):
+            after, before = jnp.minimum(z + 1, zs - 1), jnp.maximum(z - 1, 0)
+            self.right[d] = lanes.copies(
+                (part.at[d], from_left.at[d]), from_left.at[d], {"z": after}
+            )
+            self.left[d] = lanes.copies(
+                (part.at[d], from_right.at[d]), from_right.at[d], {"z": before}
+            )
+
+    def pass_on(self, d):
+        for moves, inbox, sends, edge in (
+            (self.right[d], self.from_left, self.z < d, self.z == 0),
+            (self.left[d], self.from_right, self.z > d, self.z == self.zs - 1),
+        ):
+
+            @pl.when(sends & edge)
+            def _():
+                moves[0].start()
+
+            @pl.when(sends & jnp.logical_not(edge))
+            def _():
+                moves[1].wait_recv()
+                inbox[d] = plus(self.part[d], inbox[d]).astype(inbox.dtype)
+                moves[1].start()
+
+    def total(self, sink):
+        for d in range(self.zs):
+
+            @pl.when(self.z == d)
+            def _():
+                terms = [self.part[d]]
+                if d > 0:
+                    self.right[d][0].wait_recv()
+                    terms.append(self.from_left[d])
+                if d < self.zs - 1:
+                    self.left[d][0].wait_recv()
+                    terms.append(self.from_right[d])
+                sink[...] = plus(*terms).astype(sink.dtype)
+
+    def finish(self):
+        for d in ends_first(self.zs):
+            pl.when(self.z < d)(self.right[d][0].wait_send)
+            pl.when(self.z > d)(self.left[d][0].wait_send)
+
+
+class Scatter:
+    def __init__(self, lanes, part, held, out, first):
+        zs, z, y, x = lanes.zs, lanes.z, lanes.y, lanes.x
+        got, near, from_left, from_right, ready = held
+        second = "y" if first == "x" else "x"
+        self.lanes, self.part, self.got, self.near, self.ready, self.out = (
+            lanes, part, got, near, ready, out,
+        )
+        f, s = (x, y) if first == "x" else (y, x)
+        self.f, self.s = f, s
+
+        def block(zz, a, b):
+            return part.at[zz, b, a] if first == "x" else part.at[zz, a, b]
+
+        self.block = block
+        self.one, self.two = {}, {}
+        for zz in ends_first(zs):
+            for j, b in enumerate((1 - s, s)):
+                self.one[zz, j] = Move(
+                    lanes.copy(block(zz, 1 - f, b), got.at[zz, j], {first: 1 - f}), None, None
+                )
+        for zz in ends_first(zs):
+            self.two[zz] = Move(
+                lanes.copy(got.at[zz, 0], near.at[zz], {second: 1 - s}), None, None
+            )
+        self.line = Line(lanes, ready, from_left, from_right)
+
+    def begin(self):
+        for zz in ends_first(self.lanes.zs):
+            for j in range(2):
+                self.one[zz, j].start()
+
+    def second(self, zz):
+        self.one[zz, 0].arrived()
+        mine, got = self.block(zz, self.f, 1 - self.s), self.got
+        got[zz, 0] = plus(mine[...], got[zz, 0]).astype(got.dtype)
+        self.two[zz].start()
+
+    def third(self, zz):
+        self.one[zz, 1].arrived()
+        self.two[zz].arrived()
+        mine = self.block(zz, self.f, self.s)
+        self.ready[zz] = plus(mine[...], self.got[zz, 1], self.near[zz]).astype(self.ready.dtype)
+        self.line.pass_on(zz)
+
+    def finish(self):
+        self.line.total(self.out)
+        self.line.finish()
+        for move in list(self.one.values()) + list(self.two.values()):
+            move.sent()
+
+
+class ScatterZ:
+    def __init__(self, lanes, part, held, out):
+        y, x = lanes.y, lanes.x
+        from_left, from_right, held_z, near, last = held
+        self.lanes, self.sum_z, self.near, self.last, self.out = lanes, held_z, near, last, out
+        self.line = Line(lanes, part, from_left, from_right)
+        self.two = Move(lanes.copy(held_z.at[1 - y], near, {"y": 1 - y}), None, None)
+        self.three = Move(lanes.copy(near.at[1 - x], last, {"x": 1 - x}), None, None)
+
+    def pass_on(self, d):
+        self.line.pass_on(d)
+
+    def total(self):
+        self.line.total(self.sum_z)
+        self.two.start()
+
+    def after(self):
+        self.two.arrived()
+        self.near[...] = plus(self.sum_z[self.lanes.y], self.near[...]).astype(self.near.dtype)
+        self.three.start()
+
+    def finish(self):
+        self.three.arrived()
+        self.out[...] = plus(self.near[self.lanes.x], self.last[...]).astype(self.out.dtype)
+        self.line.finish()
+        self.two.sent()
+        self.three.sent()
+
+
+def scatter_kernel(zs, orders, *refs):
+    count = len(orders)
+    parts, outs, rest = refs[:count], refs[count : 2 * count], list(refs[2 * count :])
+    send_sems, recv_sems = rest[:2]
+    rest = rest[2:]
+    lanes = Lanes(send_sems, recv_sems, None, zs)
+    greet(zs)
+    full, zfirst = [], []
+    for i, order in enumerate(orders):
+        held, rest = rest[:5], rest[5:]
+        if order == "z":
+            zfirst.append(ScatterZ(lanes, parts[i], held, outs[i]))
+        else:
+            full.append(Scatter(lanes, parts[i], held, outs[i], order))
+    for item in full:
+        item.begin()
+    for d in ends_first(zs):
+        for item in zfirst:
+            item.pass_on(d)
+        for item in full:
+            item.second(d)
+    for item in zfirst:
+        item.total()
+    for d in ends_first(zs):
+        for item in full:
+            item.third(d)
+    for item in zfirst:
+        item.after()
+    for item in full:
+        item.finish()
+    for item in zfirst:
+        item.finish()
+
+
+def scatter_all(parts, orders, zs):
+    scratch, moves = [], 0
+    for part, order in zip(parts, orders):
+        block = part.shape[3:]
+        if order == "z":
+            shapes = [(zs, 2, 2) + block] * 2 + [(2, 2) + block, (2,) + block, block]
+            moves += 2 * zs + 2
+        else:
+            shapes = [(zs, 2) + block] + [(zs,) + block] * 4
+            moves += 5 * zs
+        scratch += [pltpu.VMEM(shape, part.dtype) for shape in shapes]
+    vmem = pl.BlockSpec(memory_space=pltpu.VMEM)
+    return pl.pallas_call(
+        functools.partial(scatter_kernel, zs, orders),
+        out_shape=[jax.ShapeDtypeStruct(part.shape[3:], F32) for part in parts],
+        in_specs=[vmem] * len(parts),
+        out_specs=[vmem] * len(parts),
+        scratch_shapes=[pltpu.SemaphoreType.DMA((moves,)), pltpu.SemaphoreType.DMA((moves,))]
+        + scratch,
+        compiler_params=pltpu.CompilerParams(
+            collective_id=2, has_side_effects=True, vmem_limit_bytes=56 * 2**20
+        ),
+    )(*parts)
 
 
 def nn(left, right):
@@ -70,16 +543,6 @@
         pick(split, at, dim).reshape(rows, -1),
         pick(split, 1 - at, dim).reshape(rows, -1),
     )
-
-
-def reduce_full(left_keep, left_send, right, zs):
-    got = swap(tn(left_send, right).astype(BF), "x")
-    held = (tn(left_keep, right) + got.astype(F32)).astype(BF)
-    held = held.reshape(zs, 2, -1, right.shape[1])
-    at = lax.axis_index("y")
-    got = swap(pick(held, 1 - at, 1), "y")
-    held = (pick(held, at, 1).astype(F32) + got.astype(F32)).astype(BF)
-    return lax.psum_scatter(held, "z", scatter_dimension=0, tiled=False)
 
 
 def reduce_pair(left_keep, left_send, right, zs):
@@ -233,39 +696,39 @@
     context_rows = cross_key.shape[0]
 
     vectors = jnp.stack(
-        [self_gain, self_bias, cross_gain, cross_bias, feed_gain, feed_bias], axis=1
-    )
-    vectors = jnp.pad(vectors, ((0, 0), (0, 122)))
-    first = gather_weights(
-        jnp.concatenate([self_query, self_key, self_value, vectors], axis=1)
-    )
-    in_weight = first[:, : 3 * inner]
-    norms = first[:, 3 * inner :].astype(F32).T
-    second = gather_weights(
-        jnp.concatenate(
-            [
-                self_output.T,
-                cross_query,
-                cross_output.T,
-                jnp.concatenate([cross_key, cross_value], axis=0),
-            ],
-            axis=1,
-        )
-    )
+        [self_gain, self_bias, cross_gain, cross_bias, feed_gain, feed_bias]
+    ).astype(F32)
+    vectors = jnp.pad(vectors, ((0, 2), (0, 128 - shard_rows)))
+    feed = jnp.stack([gate_weight, up_weight, down_weight.T]).reshape(3, shard_rows, 2, ff)
+    kept = pick(feed, x_at, 2)
+    sent = pick(feed, 1 - x_at, 2)
+    norms, in_weight, second, gate_full, up_full, down_t = gather_all(
+        [
+            vectors,
+            jnp.concatenate([self_query, self_key, self_value], axis=1),
+            jnp.concatenate(
+                [
+                    self_output.T,
+                    cross_query,
+                    cross_output.T,
+                    jnp.concatenate([cross_key, cross_value], axis=0),
+                ],
+                axis=1,
+            ),
+        ],
+        [(kept[i], sent[i]) for i in range(3)],
+        zs,
+    )
+    norms = norms.reshape(-1, 8, 128)[:, :6, :shard_rows].transpose(1, 0, 2).reshape(6, width)
+    in_weight = in_weight.reshape(width, -1)
+    second = second.reshape(width, -1)
+    gate_full, up_full, down_t = (w.reshape(width, ff) for w in (gate_full, up_full, down_t))
     self_out_t = second[:, :inner]
     cross_in = second[:, inner : 2 * inner]
     cross_out_t = second[:, 2 * inner : 3 * inner]
     memory_weights = second[:, 3 * inner :].reshape(-1, 2, context_rows, inner)
     cross_keys_w = memory_weights[:, 0].reshape(-1, inner)
     cross_values_w = memory_weights[:, 1].reshape(-1, inner)
-
-    feed = jnp.stack([gate_weight, up_weight, down_weight.T], axis=1)
-    feed = feed.reshape(shard_rows, 3, 2, ff)
-    kept = pick(feed, x_at, 2).reshape(shard_rows, 3 * ff)
-    sent = pick(feed, 1 - x_at, 2).reshape(shard_rows, 3 * ff)
-    feed = join(kept[None], swap(sent, "x")[None], "x", 0)
-    gate_up = gather_pair_weights(feed[:, :, : 2 * ff])
-    down_t = gather_pair_weights(feed[:, :, 2 * ff :])
 
     local = jnp.arange(rows)
     places = jnp.concatenate([t_at * rows + local, (1 - t_at) * rows + local])
@@ -302,9 +765,8 @@
     stream_feed = stream_cross + spread_pair(mixed_cross, cross_out_t)
     normed, unit_feed, inverse_feed = norm_forward(stream_feed, norms[4], norms[5])
     normed_feed = group_rows(normed.astype(BF))
-    gates = nn(normed_feed, gate_up)
-    gate_pre = gates[:, :ff]
-    upward = gates[:, ff:]
+    gate_pre = nn(normed_feed, gate_full)
+    upward = nn(normed_feed, up_full)
     sigmoid_gate = jax.nn.sigmoid(gate_pre)
     hidden = (gate_pre * sigmoid_gate * upward).astype(BF)
     result = (stream_feed + spread_group(Product([(hidden, down_t)], True))).astype(BF)
@@ -315,8 +777,10 @@
     grad_hidden = nn(cot_group, down_t)
     grad_gate = grad_hidden * upward * sigmoid_gate * (1.0 + gate_pre * (1.0 - sigmoid_gate))
     grad_upward = grad_hidden * gate_pre * sigmoid_gate
-    grad_gates = jnp.concatenate([grad_gate.astype(BF), grad_upward.astype(BF)], axis=1)
-    grad_normed = spread_group(Product([(grad_gates, gate_up)], True))
+    grad_gate = grad_gate.astype(BF)
+    grad_upward = grad_upward.astype(BF)
+    grad_gates = jnp.concatenate([grad_gate, grad_upward], axis=1)
+    grad_normed = spread_group(Product([(grad_gate, gate_full), (grad_upward, up_full)], True))
     feed_keep, feed_send = columns_by(normed_feed, "y", zs)
     gates_keep, gates_got = reduce_pair(feed_keep, feed_send, grad_gates, zs)
     stream_part, grad_feed_gain, grad_feed_bias = norm_backward(
@@ -324,8 +788,7 @@
     )
     grad_stream = cotangent.astype(F32) + stream_part
     grad_full = pair_rows(grad_stream.astype(BF))
-    keep, send = columns_by(grad_full, "x", zs)
-    sum_cross_output = reduce_full(keep, send, mixed_cross, zs)
+    part_cross_output = tn(grad_full, mixed_cross)
     grad_mixed = nn(grad_full, cross_out_t).astype(BF).reshape(head_shape)
     grad_query, grad_keys, grad_values = attend_backward(
         query_cross, key_cross, value_cross, cross_allowed, total_cross, grad_mixed
@@ -334,19 +797,14 @@
     grad_keys = grad_keys.astype(BF).reshape(memory.shape[0], -1)
     grad_values = grad_values.astype(BF).reshape(memory.shape[0], -1)
     grad_normed = spread_pair(grad_query, cross_in)
-    keep, send = columns_by(normed_cross, "x", zs)
-    sum_cross_query = reduce_full(keep, send, grad_query, zs)
-    keep, send = columns_by(memory, "x", zs)
-    sum_cross_memory = reduce_full(
-        keep, send, jnp.concatenate([grad_keys, grad_values], axis=1), zs
-    )
+    part_cross_query = tn(normed_cross, grad_query)
+    part_memory = tn(memory, jnp.concatenate([grad_keys, grad_values], axis=1))
     stream_part, grad_cross_gain, grad_cross_bias = norm_backward(
         grad_normed, unit_cross, inverse_cross, norms[2]
     )
     grad_stream = grad_stream + stream_part
     grad_full = pair_rows(grad_stream.astype(BF))
-    keep, send = columns_by(grad_full, "x", zs)
-    sum_self_output = reduce_full(keep, send, mixed_self, zs)
+    part_self_output = tn(grad_full, mixed_self)
     grad_mixed = nn(grad_full, self_out_t).astype(BF).reshape(head_shape)
     grad_query, grad_keys, grad_values = attend_backward(
         query_self, key_self, value_self, self_allowed, total_self, grad_mixed
@@ -355,8 +813,7 @@
     grad_keys = rotate(grad_keys, positions, -1.0).astype(BF).reshape(seq_len, -1)
     grad_values = grad_values.astype(BF).reshape(seq_len, -1)
     grad_in = jnp.concatenate([grad_query, grad_keys, grad_values], axis=1)
-    keep, send = columns_by(normed_self, "x", zs)
-    sum_self_in = reduce_full(keep, send, grad_in, zs).astype(F32)
+    part_self_in = tn(normed_self, grad_in)
     grad_normed = spread_pair(grad_in, in_weight)
     _, unit_self, inverse_self = norm_forward(stream, norms[0], norms[1])
     stream_part, grad_self_gain, grad_self_bias = norm_backward(
@@ -373,13 +830,30 @@
             grad_feed_gain,
             grad_feed_bias,
         ]
-    ).reshape(6, zs, 2, 2, shard_rows)
-    y_at = lax.axis_index("y")
+    ).reshape(6, -1, shard_rows)
     vector_sums = vector_sums + swap(vector_sums, "tensor")
-    vector_sums = pick(vector_sums, x_at, 3) + swap(pick(vector_sums, 1 - x_at, 3), "x")
-    vector_sums = pick(vector_sums, y_at, 2) + swap(pick(vector_sums, 1 - y_at, 2), "y")
-    vector_sums = pick(lax.psum(vector_sums, "z"), lax.axis_index("z"), 1)
-
+    vector_sums = jnp.pad(
+        vector_sums.transpose(1, 0, 2), ((0, 0), (0, 2), (0, 128 - shard_rows))
+    ).reshape(zs, 2, 2, 8, 128)
+
+    def blocks(part):
+        return part.astype(BF).reshape(zs, 2, 2, -1, part.shape[1])
+
+    vector_sums, sum_self_in, sum_self_output, sum_cross_query, sum_cross_output, sum_memory = (
+        scatter_all(
+            [
+                vector_sums,
+                blocks(part_self_in),
+                blocks(part_self_output),
+                blocks(part_cross_query),
+                blocks(part_cross_output),
+                blocks(part_memory),
+            ],
+            ["x", "x", "y", "y", "y", "z"],
+            zs,
+        )
+    )
+    vector_sums = vector_sums[:, :shard_rows]
     factor = jnp.sqrt(threshold[0] / jnp.maximum(peaks, threshold[0]))
     columns = jnp.repeat(factor, HEAD_DIM)[None, :]
     down_sum = join(down_keep, down_got, "x", 1).T.astype(F32)
@@ -394,13 +868,13 @@
         sum_self_in[:, :inner],
         sum_self_in[:, inner : 2 * inner],
         sum_self_in[:, 2 * inner :],
-        sum_self_output.T.astype(F32),
+        sum_self_output.T,
         vector_sums[2],
         vector_sums[3],
-        sum_cross_query.astype(F32),
-        sum_cross_memory[:, :inner].astype(F32),
-        sum_cross_memory[:, inner:].astype(F32),
-        sum_cross_output.T.astype(F32),
+        sum_cross_query,
+        sum_memory[:, :inner],
+        sum_memory[:, inner:],
+        sum_cross_output.T,
         vector_sums[4],
         vector_sums[5],
         gates_sum[:, 0].reshape(-1, ff_half),

time: 1300 us -> 1120 us (0.86)
  waiting for transfers between devices: 489 us -> 96.8 us
  Pallas kernels: 0 us -> 388 us
  local copies, waits for them, and re-layouts: 195 us -> 94.4 us
  other arithmetic: 88.9 us -> 52.6 us
  starting transfers between devices: 35.1 us -> 9.96 us
  blocking collectives: 55.9 us -> 40.8 us
    pallas_call x0 -> x2, Pallas kernels: none -> 388 us  [the longest x1 226 us: gather_all(): pl.pallas_call(functools.partial(gather_kernel, zs, groups, pairs), out_s...]
    ppermute x42 -> x23, waiting for transfers between devices: 440 us -> 96.7 us  [swap(): return lax.ppermute(value, axis, [(0, 1), (1, 0)])]
    all_gather x4 -> x0, waiting for transfers between devices: 49.6 us -> none  [the longest x2 49.6 us: gather_weights(): held = lax.all_gather(shard, 'z', axis=0, tiled=False)]
    ppermute x42 -> x23, starting transfers between devices: 33.8 us -> 9.88 us  [swap(): return lax.ppermute(value, axis, [(0, 1), (1, 0)])]
    another operation x9 -> x4, local copies, waits for them, and re-layouts: 27.2 us -> 5.79 us  [per_device(): jnp.stack([gate_weight, up_weight, down_weight.T])]
    dynamic_update_slice x9 -> x2, local copies, waits for them, and re-layouts: 29.5 us -> 9.01 us  [join(): return lax.dynamic_update_slice_in_dim(out, other, (1 - at) * size, dim)]
    convert_element_type x11 -> x0, other arithmetic: 18.2 us -> none  [the longest x5 8.85 us: reduce_full(): held = (pick(held, at, 1).astype(F32) + got.astype(F32)).astype(BF)]
    psum x1 -> x0, blocking collectives: 17 us -> none  [per_device(): vector_sums = pick(lax.psum(vector_sums, 'z'), lax.axis_index('z'), 1)]
  transfers between devices with their start and end apart: 53 -> 25, of which waited for: 17 -> 7; matrix products, arithmetic and copies ran while one was open for 48% -> 33% of each run, Pallas kernels for 0% -> 35%
where the time goes in v2:
time: 1120 us; the launch traced here: 1100 us
  matrix products  399 us (36%)
  Pallas kernels  388 us (35%)
  waiting for transfers between devices  96.8 us (9%)
  local copies, waits for them, and re-layouts  94.4 us (8%)
  other arithmetic  52.6 us (5%)
  blocking collectives  40.8 us (4%)
  between operations  17.6 us (2%)
    pallas_call x1, Pallas kernels, gather_all(): pl.pallas_call(functools.partial(gather_kernel, zs, groups, pairs), out_s...  226 us
    pallas_call x1, Pallas kernels, scatter_all(): pl.pallas_call(functools.partial(scatter_kernel, zs, orders), out_shape=[...  161 us
    dot_general x20, matrix products, nt(): lax.dot_general(left, right, (((1,), (1,)), ((), ())), preferred_element_...  103 us
    ppermute x23, waiting for transfers between devices, swap(): return lax.ppermute(value, axis, [(0, 1), (1, 0)])  96.7 us
    dot_general x9, matrix products, nn(): lax.dot_general(left, right, (((1,), (0,)), ((), ())), preferred_element_...  74.6 us
    dot_general x9, matrix products, tn(): lax.dot_general(left, right, (((0,), (0,)), ((), ())), preferred_element_...  68.8 us
    dot_general x2, matrix products, attend_backward(): jnp.einsum('hqk,qhe->khe', grad_raw, query, preferred_element_type=F32)  48.6 us
    dot_general x2, matrix products, attend_backward(): jnp.einsum('hqk,khe->qhe', grad_raw, keys, preferred_element_type=F32)  48 us
  transfers between devices with their start and end apart: 25, of which 7 were waited for; matrix products, arithmetic and copies ran while one was open for 33% of the time, Pallas kernels for 35%

profile of v2, /device:TPU:0, one launch (start us, length us, event | category | flops | bytes accessed | tf_op | source)
XLA Modules:
  0.0 1099.0 jit_solution(4559938483301769310)
XLA Ops:
  20.1 226.4 %shard_map.406 = (f32[4,2,2,8,128]{4,3,2,1,0:T(8,128)}, bf16[4,2,2,96,2304]{4,3,2,1,0:T(8,128)(2,1)}, bf16[4,2,2,96,3072]{4,3,2,1,0:T(8,128)(2,1)}, bf16[4,2,2,9...) custom-call(f32[8,128]{1,0:T(8,128)} %pad_convert_fusion.refs_0_, ...), custom_call_target="tpu_custom_call" | custom-call | tf_op jit(solution)/shard_map/pallas_call | solution.py:302
  250.5 9.0 fusion.171
  272.5 12.0 %fusion.187 = (f32[12,768]{1,0:T(8,128)S(1)}, f32[12,768,768]{1,2,0:T(8,128)}) fusion(bf16[768,12,32]{0,2,1:T(8,128)(2,1)S(1)} %slice.482, bf16[768,12,16]{0,2,1:T(8,128)(2,1)S(1)} %get-tuple-element.124, bf16[768,12,16]{0,2,1:T(8,128)(2,1)S(1)} %get-tuple-element.125, bf16[768,12,32]{0,2,1:T(8,128)(2,1)S(1)} %slice.483, ...), kind=kOutput, calls=%fused_computation.302 | convolution fusion | flops 934272000 | bytes 30708480 | tf_op jit(solution)/shard_map/qhe,khe->hqk/dot_general | solution.py:594
  284.5 12.5 %fusion.173 = (f32[12]{0:T(128)S(1)}, f32[12,768]{1,0:T(8,128)S(1)}) fusion(f32[12,768,768]{1,2,0:T(8,128)} %get-tuple-element.139, f32[12,768]{1,0:T(8,128)S(1)} %get-tuple-element.138), kind=kLoop, calls=%fused_computation.288 | loop fusion | flops 21224436 | bytes 28385328 | tf_op jit(solution)/shard_map/reduce_max | solution.py:596
  297.7 12.4 %fusion.106 = bf16[12,64,768]{2,1,0:T(8,128)(2,1)S(1)} fusion(bf16[768,12,64]{0,2,1:T(8,128)(2,1)S(1)} %bitcast.201, f32[12,768,768]{1,2,0:T(8,128)} %get-tuple-element.139, f32[12,768]{1,0:T(8,128)S(1)} %log_add_fusion.1), kind=kOutput, calls=%fused_computation.143 | convolution fusion | flops 920715264 | bytes 30707712 | tf_op jit(solution)/shard_map/hqk,khe->qhe/dot_general | solution.py:600
  352.5 26.7 %collective-permute-done.9 = bf16[384,1536]{0,1:T(8,128)(2,1)} collective-permute-done((bf16[384,1536]{0,1:T(8,128)(2,1)}, bf16[384,1536]{0,1:T(8,128)(2,1)}, u32[]{:S(2)}, u32[]{:S(2)}) %collective-permute-start.9) | collective-permute-done | bytes 1179680 | tf_op jit(solution)/shard_map/ppermute | solution.py:20
  392.2 23.9 %collective-permute-done.4 = bf16[384,1536]{1,0:T(8,128)(2,1)} collective-permute-done((bf16[384,1536]{1,0:T(8,128)(2,1)S(1)}, bf16[384,1536]{1,0:T(8,128)(2,1)}, u32[]{:S(2)}, u32[]{:S(2)}) %collective-permute-start.4) | collective-permute-done | bytes 1179680 | tf_op jit(solution)/shard_map/ppermute | solution.py:20
  427.9 40.8 %pmax.7 = f32[12]{0:T(128)S(1)} all-reduce(f32[12]{0:T(128)S(1)} %max.9), channel_id=1, replica_groups=mesh['z'=4,'y'=2,'x'=2,'tensor'=2] {'z','y','x'}, use_global_device_ids=true, to_apply=%region_30.31 | all-reduce | flops 12 | bytes 96 | tf_op jit(solution)/shard_map/pmax | solution.py:773
  477.1 15.5 %fusion.135 = f32[1536,1536]{0,1:T(8,128)} fusion(bf16[1536,1536]{1,0:T(8,128)(2,1)} %bitcast.301, bf16[384,1536]{1,0:T(8,128)(2,1)S(1)} %get-tuple-element.97, bf16[384,1536]{1,0:T(8,128)(2,1)} %collective-permute-done.4, bf16[384,1536]{1,0:T(8,128)(2,1)S(1)} %get-tuple-element.96, bf16[384,1536]{1,0:T(8,128)(2,1)S(1)} %copy-done.24), kind=kOutput, calls=%fused_computation.178 | convolution fusion | flops 7266631680 | bytes 18874368 | tf_op jit(solution)/shard_map/dot_general | solution.py:522
  492.5 13.2 %fusion.136 = f32[1536,1536]{0,1:T(8,128)} fusion(bf16[1536,1536]{1,0:T(8,128)(2,1)S(1)} %bitcast.314, bf16[384,1536]{1,0:T(8,128)(2,1)S(1)} %get-tuple-element.97, bf16[384,1536]{1,0:T(8,128)(2,1)} %collective-permute-done.4, bf16[384,1536]{1,0:T(8,128)(2,1)S(1)} %get-tuple-element.96, bf16[384,1536]{1,0:T(8,128)(2,1)S(1)} %copy-done.24), kind=kOutput, calls=%fused_computation.179 | convolution fusion | flops 7266631680 | bytes 18874368 | tf_op jit(solution)/shard_map/dot_general | solution.py:522
  505.7 20.6 %multiply_convert_fusion.1 = (bf16[1536,1536]{0,1:T(8,128)(2,1)}, bf16[1536,1536]{0,1:T(8,128)(2,1)}, bf16[1536,1536]{0,1:T(8,128)(2,1)}) fusion(f32[1536,1536]{0,1:T(8,128)} %fusion.136, f32[1536,1536]{0,1:T(8,128)} %fusion.135, bf16[1536,1536]{1,0:T(8,128)(2,1)} %bitcast.292, bf16[384,1536]{0,1:T(8,128)(2,1)} %get-tuple-element.93, ...), kind=kOutput, calls=%fused_computation.13 | convolution fusion | flops 7304380416 | bytes 42467328 | tf_op jit(solution)/shard_map/dot_general | solution.py:522
  556.8 13.7 %fusion.17 = bf16[768,3072]{1,0:T(8,128)(2,1)} fusion(bf16[1536,768]{0,1:T(8,128)(2,1)S(1)} %bitcast.252, bf16[1536,1536]{0,1:T(8,128)(2,1)} %get-tuple-element.74, bf16[1536,1536]{0,1:T(8,128)(2,1)} %get-tuple-element.75), kind=kOutput, calls=%fused_computation.25 | convolution fusion | flops 7268990976 | bytes 16515072 | tf_op jit(solution)/shard_map/dot_general | solution.py:530
  602.0 6.4 add_convert_fusion.1
  608.5 6.7 fusion.57
  617.2 14.0 %collective-permute-done.13 = bf16[384,1536]{1,0:T(8,128)(2,1)} collective-permute-done((bf16[384,1536]{1,0:T(8,128)(2,1)}, bf16[384,1536]{1,0:T(8,128)(2,1)}, u32[]{:S(2)}, u32[]{:S(2)}) %collective-permute-start.13) | collective-permute-done | bytes 1179680 | tf_op jit(solution)/shard_map/ppermute | solution.py:20
  631.2 6.8 multiply_reduce_fusion.2
  643.8 7.3 collective-permute-done.8
  651.1 7.0 fusion.56
  665.7 9.4 fusion.94
  679.7 15.7 %collective-permute-done.19 = bf16[768,3072]{1,0:T(8,128)(2,1)} collective-permute-done((bf16[768,3072]{1,0:T(8,128)(2,1)}, bf16[768,3072]{1,0:T(8,128)(2,1)}, u32[]{:S(2)}, u32[]{:S(2)}) %collective-permute-start.19) | collective-permute-done | bytes 4718624 | tf_op jit(solution)/shard_map/ppermute | solution.py:20
  695.4 14.8 %add_convert_fusion = bf16[768,3072]{1,0:T(8,128)(2,1)} fusion(bf16[768,3072]{1,0:T(8,128)(2,1)} %collective-permute-done.19, bf16[1536,768]{0,1:T(8,128)(2,1)S(1)} %bitcast.249, bf16[1536,1536]{0,1:T(8,128)(2,1)} %get-tuple-element.74, bf16[1536,1536]{0,1:T(8,128)(2,1)} %get-tuple-element.75), kind=kOutput, calls=%fused_computation.12 | convolution fusion | flops 7273709568 | bytes 21233664 | tf_op jit(solution)/shard_map/dot_general | solution.py:530
  711.0 10.9 fusion.112
  754.6 11.7 %fusion.192 = f32[12,768,768]{1,2,0:T(8,128)} fusion(bf16[768,12,64]{0,2,1:T(8,128)(2,1)S(1)} %bitcast.205, bf16[768,12,64]{0,2,1:T(8,128)(2,1)S(1)} %bitcast.202), kind=kOutput, calls=%fused_computation.307 | convolution fusion | flops 905969664 | bytes 30670848 | tf_op jit(solution)/shard_map/qhe,khe->hqk/dot_general | solution.py:608
  766.3 38.6 %fusion.88 = f32[768,12,64]{0,2,1:T(8,128)} fusion(f32[12,768,768]{1,2,0:T(8,128)} %fusion.192, f32[12,768,768]{1,2,0:T(8,128)} %get-tuple-element.139, f32[12,768]{1,0:T(8,128)S(1)} %copy-done.52, bf16[768,12,32]{0,2,1:T(8,128)(2,1)S(1)} %copy-done.44, bf16[768,12,16]{0,2,1:T(8,128)(2,1)} %copy-done.60, bf16[768,12,16]{0,2,1:T(8,128)(2,1)} %copy-done.61), kind=kOutput, calls=%fused_computation.136 | convolution fusion | flops 959063808 | bytes 60198912 | tf_op jit(solution)/shard_map/hqk,khe->qhe/dot_general | solution.py:616
  806.3 37.7 %fusion.91 = f32[768,12,64]{0,2,1:T(8,128)} fusion(f32[12,768,768]{1,2,0:T(8,128)} %fusion.192, f32[12,768,768]{1,2,0:T(8,128)} %get-tuple-element.139, f32[12,768]{1,0:T(8,128)S(1)} %copy-done.52, bf16[768,12,32]{0,2,1:T(8,128)(2,1)S(1)} %copy-done.42, bf16[768,12,16]{0,2,1:T(8,128)(2,1)} %copy-done.59, bf16[768,12,16]{0,2,1:T(8,128)(2,1)S(1)} %copy-done.58), kind=kOutput, calls=%fused_computation.137 | convolution fusion | flops 959063808 | bytes 60198912 | tf_op jit(solution)/shard_map/hqk,qhe->khe/dot_general | solution.py:617
  847.5 11.6 %fusion.109 = bf16[12,64,768]{2,1,0:T(8,128)(2,1)S(1)} fusion(bf16[768,12,64]{0,2,1:T(8,128)(2,1)S(1)} %bitcast.206, f32[12,768,768]{1,2,0:T(8,128)} %get-tuple-element.139, f32[12,768]{1,0:T(8,128)S(1)} %copy-done.52), kind=kOutput, calls=%fused_computation.144 | convolution fusion | flops 920715264 | bytes 30707712 | tf_op jit(solution)/shard_map/hqk,qhe->khe/dot_general | solution.py:609
  859.7 7.4 fusion.85
  875.0 11.1 %convolution_convert_fusion = bf16[1536,2304]{1,0:T(8,128)(2,1)} fusion(f32[1536]{0:T(1024)S(1)} %copy-done.88, f32[1536]{0:T(1024)S(1)} %copy-done.78, f32[768]{0:T(1024)S(1)} %copy-done.93, f32[768]{0:T(1024)S(1)} %copy-done.86, bf16[384,1536]{1,0:T(8,128)(2,1)S(1)} %copy-done.21, bf16[384,1536]{1,0:T(8,128)(2,1)S(1)} %copy-done.8, ...), kind=kOutput, calls=%fused_computation.10 | convolution fusion | flops 5460590592 | bytes 12994560 | tf_op jit(solution)/shard_map/dot_general | solution.py:530
  886.1 8.7 fusion.68
  900.5 161.3 %shard_map.407 = (f32[8,128]{1,0:T(8,128)}, f32[96,2304]{1,0:T(8,128)}, f32[96,768]{1,0:T(8,128)}, f32[96,768]{1,0:T(8,128)}, f32[96,768]{1,0:T(8,128)}, /*index=5*/f32[48,1536]{1,0:T(8,128)}) custom-call(f32[4,2,2,8,128]{4,3,2,1,0:T(8,128)} %bitcast.279, bf16[4,2,2,96,2304]{4,3,2,1,0:T(8,128)(2,1)} %bitcast.213, bf16[4,2,2,96,768]{4,3,2,1,0:T(8,128)(2,1)} %bitcast.257, ...), custom_call_target="tpu_custom_call" | custom-call | tf_op jit(solution)/shard_map/pallas_call | solution.py:508
  1067.5 7.8 dynamic_update_slice.12
  1078.5 7.8 dynamic_update_slice.13
  (444 shorter events, 252.1 us)
Async XLA Ops:
  7.2 322.8 %copy-start = (bf16[1,130,768]{2,1,0:T(8,128)(2,1)S(1)}, bf16[1,130,768]{2,1,0:T(8,128)(2,1)}, u32[]{:S(2)}) copy-start(bf16[1,130,768]{2,1,0:T(8,128)(2,1)} %param.25) | copy-start | bytes 599044
  7.2 738.6 %reduce-scatter.5.cloned.1.call-start = ((), (), s32[]{:S(2)}) async-start(), calls=%async_computation.3 | async-start | bytes 2949120 | tf_op jit(solution)/shard_map/reduce_scatter | solution.py:552
  7.3 242.0 %collective-permute-start = (bf16[384,1536]{1,0:T(8,128)(2,1)}, bf16[384,1536]{1,0:T(8,128)(2,1)S(1)}, u32[]{:S(2)}, u32[]{:S(2)}) collective-permute-start(bf16[384,1536]{1,0:T(8,128)(2,1)} %param.23), channel_id=1, source_target_pairs={{0,1},{1,0},{2,3},{3,2},{4,5},{5,4},{6,7},{7,6},{8,9},{9,8},{10,11... | collective-permute-start | bytes 3538952 | tf_op jit(solution)/shard_map/ppermute | solution.py:20
  19.5 229.8 %copy-start.6 = (bf16[384,1536]{1,0:T(8,128)(2,1)S(1)}, bf16[384,1536]{1,0:T(8,128)(2,1)}, u32[]{:S(2)}) copy-start(bf16[384,1536]{1,0:T(8,128)(2,1)} %param.23) | copy-start | bytes 3538948
  314.8 4.7 collective-permute-start.1
  324.9 57.6 %copy-start.2 = (f32[384,1536]{1,0:T(8,128)}, f32[384,1536]{1,0:T(8,128)S(1)}, u32[]{:S(2)}) copy-start(f32[384,1536]{1,0:T(8,128)S(1)} %get-tuple-element.141) | copy-start | bytes 7077892
  326.9 7.2 collective-permute-start.2
  347.9 34.7 %collective-permute-start.3 = (f32[384,1536]{1,0:T(8,128)}, f32[384,1536]{1,0:T(8,128)}, u32[]{:S(2)}, u32[]{:S(2)}) collective-permute-start(f32[384,1536]{1,0:T(8,128)} %fusion.72), channel_id=1, source_target_pairs={{0,1},{1,0},{2,3},{3,2},{4,5},{5,4},{6,7},{7,6},{8,9},{9,8},{10,11... | collective-permute-start | bytes 7077896 | tf_op jit(solution)/shard_map/ppermute | solution.py:20
  350.8 28.4 %collective-permute-start.9 = (bf16[384,1536]{0,1:T(8,128)(2,1)}, bf16[384,1536]{0,1:T(8,128)(2,1)}, u32[]{:S(2)}, u32[]{:S(2)}) collective-permute-start(bf16[384,1536]{0,1:T(8,128)(2,1)} %copy.74), channel_id=1, source_target_pairs={{0,2},{2,0},{1,3},{3,1},{4,6},{6,4},{5,7},{7,5},{8,10},{10,8},{9,1... | collective-permute-start | bytes 3538952 | tf_op jit(solution)/shard_map/ppermute | solution.py:20
  382.5 37.6 %collective-permute-start.10 = (bf16[2,384,1536]{1,2,0:T(8,128)(2,1)}, bf16[2,384,1536]{1,2,0:T(8,128)(2,1)}, u32[]{:S(2)}, u32[]{:S(2)}) collective-permute-start(bf16[2,384,1536]{1,2,0:T(8,128)(2,1)} %pad_maximum_fusion.14), channel_id=1, source_target_pairs={{0,1},{1,0},{2,3},{3,2},{4,5},{5,4},{6,7},{7,6},{8,9},{9,8},{10,11... | collective-permute-start | bytes 7077896 | tf_op jit(solution)/shard_map/ppermute | solution.py:20
  387.7 28.5 %collective-permute-start.4 = (bf16[384,1536]{1,0:T(8,128)(2,1)S(1)}, bf16[384,1536]{1,0:T(8,128)(2,1)}, u32[]{:S(2)}, u32[]{:S(2)}) collective-permute-start(bf16[384,1536]{1,0:T(8,128)(2,1)S(1)} %add_convert_fusion.2), channel_id=1, source_target_pairs={{0,2},{2,0},{1,3},{3,1},{4,6},{6,4},{5,7},{7,5},{8,10},{10,8},{9,1... | collective-permute-start | bytes 3538952 | tf_op jit(solution)/shard_map/ppermute | solution.py:20
  419.1 54.4 %collective-permute-start.5 = (bf16[2,384,1536]{2,1,0:T(8,128)(2,1)}, bf16[2,384,1536]{2,1,0:T(8,128)(2,1)}, u32[]{:S(2)}, u32[]{:S(2)}) collective-permute-start(bf16[2,384,1536]{2,1,0:T(8,128)(2,1)} %pad_maximum_fusion.13), channel_id=1, source_target_pairs={{0,1},{1,0},{2,3},{3,2},{4,5},{5,4},{6,7},{7,6},{8,9},{9,8},{10,11... | collective-permute-start | bytes 7077896 | tf_op jit(solution)/shard_map/ppermute | solution.py:20
  547.5 54.5 %collective-permute-start.21 = (bf16[768,1536]{1,0:T(8,128)(2,1)}, bf16[768,1536]{1,0:T(8,128)(2,1)}, u32[]{:S(2)}, u32[]{:S(2)}) collective-permute-start(bf16[768,1536]{1,0:T(8,128)(2,1)} %convolution_convert_fusion.1), channel_id=1, source_target_pairs={{0,4},{4,0},{1,5},{5,1},{2,6},{6,2},{3,7},{7,3},{8,12},{12,8},{9,1... | collective-permute-start | bytes 7077896 | tf_op jit(solution)/shard_map/ppermute | solution.py:20
  570.5 124.9 %collective-permute-start.19 = (bf16[768,3072]{1,0:T(8,128)(2,1)}, bf16[768,3072]{1,0:T(8,128)(2,1)}, u32[]{:S(2)}, u32[]{:S(2)}) collective-permute-start(bf16[768,3072]{1,0:T(8,128)(2,1)} %fusion.17), channel_id=1, source_target_pairs={{0,4},{4,0},{1,5},{5,1},{2,6},{6,2},{3,7},{7,3},{8,12},{12,8},{9,1... | collective-permute-start | bytes 14155784 | tf_op jit(solution)/shard_map/ppermute | solution.py:20
  575.9 18.0 %collective-permute-start.12 = (f32[384,1536]{1,0:T(8,128)S(1)}, f32[384,1536]{1,0:T(8,128)S(1)}, u32[]{:S(2)}, u32[]{:S(2)}) collective-permute-start(f32[384,1536]{1,0:T(8,128)S(1)} %convolution_add_fusion.3), channel_id=1, source_target_pairs={{0,1},{1,0},{2,3},{3,2},{4,5},{5,4},{6,7},{7,6},{8,9},{9,8},{10,11... | collective-permute-start | bytes 7077896 | tf_op jit(solution)/shard_map/ppermute | solution.py:20
  576.0 32.5 %collective-permute-start.7 = (f32[384,1536]{1,0:T(8,128)}, f32[384,1536]{1,0:T(8,128)}, u32[]{:S(2)}, u32[]{:S(2)}) collective-permute-start(f32[384,1536]{1,0:T(8,128)} %fusion.127), channel_id=1, source_target_pairs={{0,1},{1,0},{2,3},{3,2},{4,5},{5,4},{6,7},{7,6},{8,9},{9,8},{10,11... | collective-permute-start | bytes 7077896 | tf_op jit(solution)/shard_map/ppermute | solution.py:20
  590.3 26.9 %collective-permute-start.11 = (f32[384,1536]{1,0:T(8,128)}, f32[384,1536]{1,0:T(8,128)}, u32[]{:S(2)}, u32[]{:S(2)}) collective-permute-start(f32[384,1536]{1,0:T(8,128)} %convolution_add_fusion.5), channel_id=1, source_target_pairs={{0,1},{1,0},{2,3},{3,2},{4,5},{5,4},{6,7},{7,6},{8,9},{9,8},{10,11... | collective-permute-start | bytes 7077896 | tf_op jit(solution)/shard_map/ppermute | solution.py:20
  593.9 49.8 %collective-permute-start.6 = (f32[384,1536]{1,0:T(8,128)}, f32[384,1536]{1,0:T(8,128)}, u32[]{:S(2)}, u32[]{:S(2)}) collective-permute-start(f32[384,1536]{1,0:T(8,128)} %fusion.130), channel_id=1, source_target_pairs={{0,1},{1,0},{2,3},{3,2},{4,5},{5,4},{6,7},{7,6},{8,9},{9,8},{10,11... | collective-permute-start | bytes 7077896 | tf_op jit(solution)/shard_map/ppermute | solution.py:20
  602.0 29.2 %collective-permute-start.13 = (bf16[384,1536]{1,0:T(8,128)(2,1)}, bf16[384,1536]{1,0:T(8,128)(2,1)}, u32[]{:S(2)}, u32[]{:S(2)}) collective-permute-start(bf16[384,1536]{1,0:T(8,128)(2,1)} %fusion.55), channel_id=1, source_target_pairs={{0,2},{2,0},{1,3},{3,1},{4,6},{6,4},{5,7},{7,5},{8,10},{10,8},{9,1... | collective-permute-start | bytes 3538952 | tf_op jit(solution)/shard_map/ppermute | solution.py:20
  608.4 453.4 %reduce-scatter.3.cloned.1.call-start = ((), (), s32[]{:S(2)}) async-start(), calls=%async_computation.2 | async-start | bytes 5898240 | tf_op jit(solution)/shard_map/reduce_scatter | solution.py:552
  615.1 22.9 %copy-start.14 = (bf16[384,1536]{1,0:T(8,128)(2,1)S(1)}, bf16[384,1536]{1,0:T(8,128)(2,1)}, u32[]{:S(2)}) copy-start(bf16[384,1536]{1,0:T(8,128)(2,1)} %param.24) | copy-start | bytes 3538948
  615.1 36.0 %collective-permute-start.8 = (bf16[384,1536]{1,0:T(8,128)(2,1)}, bf16[384,1536]{1,0:T(8,128)(2,1)}, u32[]{:S(2)}, u32[]{:S(2)}) collective-permute-start(bf16[384,1536]{1,0:T(8,128)(2,1)} %fusion.57), channel_id=1, source_target_pairs={{0,2},{2,0},{1,3},{3,1},{4,6},{6,4},{5,7},{7,5},{8,10},{10,8},{9,1... | collective-permute-start | bytes 3538952 | tf_op jit(solution)/shard_map/ppermute | solution.py:20
  640.8 17.3 %collective-permute-start.14 = (bf16[384,1536]{1,0:T(8,128)(2,1)}, bf16[384,1536]{1,0:T(8,128)(2,1)}, u32[]{:S(2)}, u32[]{:S(2)}) collective-permute-start(bf16[384,1536]{1,0:T(8,128)(2,1)} %get-tuple-element.72), channel_id=1, source_target_pairs={{0,1},{1,0},{2,3},{3,2},{4,5},{5,4},{6,7},{7,6},{8,9},{9,8},{10,11... | collective-permute-start | bytes 3538952 | tf_op jit(solution)/shard_map/ppermute | solution.py:20
  679.7 51.1 %collective-permute-start.15 = (f32[384,1536]{1,0:T(8,128)}, f32[384,1536]{1,0:T(8,128)}, u32[]{:S(2)}, u32[]{:S(2)}) collective-permute-start(f32[384,1536]{1,0:T(8,128)} %fusion.75), channel_id=1, source_target_pairs={{0,1},{1,0},{2,3},{3,2},{4,5},{5,4},{6,7},{7,6},{8,9},{9,8},{10,11... | collective-permute-start | bytes 7077896 | tf_op jit(solution)/shard_map/ppermute | solution.py:20
  738.3 11.6 %collective-permute-start.16 = (bf16[384,1536]{1,0:T(8,128)(2,1)S(1)}, bf16[384,1536]{1,0:T(8,128)(2,1)}, u32[]{:S(2)}, u32[]{:S(2)}) collective-permute-start(bf16[384,1536]{1,0:T(8,128)(2,1)S(1)} %get-tuple-element.70), channel_id=1, source_target_pairs={{0,1},{1,0},{2,3},{3,2},{4,5},{5,4},{6,7},{7,6},{8,9},{9,8},{10,11... | collective-permute-start | bytes 3538952 | tf_op jit(solution)/shard_map/ppermute | solution.py:20
  747.5 120.1 %collective-permute-start.22 = (bf16[96,1536]{1,0:T(8,128)(2,1)}, bf16[96,1536]{1,0:T(8,128)(2,1)}, u32[]{:S(2)}, u32[]{:S(2)}) collective-permute-start(bf16[96,1536]{1,0:T(8,128)(2,1)} %dynamic-slice_bitcast_fusion.7), channel_id=1, source_target_pairs={{0,2},{2,0},{1,3},{3,1},{4,6},{6,4},{5,7},{7,5},{8,10},{10,8},{9,1... | collective-permute-start | bytes 884744 | tf_op jit(solution)/shard_map/ppermute | solution.py:20
  766.3 40.0 %copy-start.42 = (bf16[768,12,32]{0,2,1:T(8,128)(2,1)S(1)}, bf16[768,12,32]{0,2,1:T(8,128)(2,1)}, u32[]{:S(2)}) copy-start(bf16[768,12,32]{0,2,1:T(8,128)(2,1)} %copy-done.41) | copy-start | bytes 1769476
  766.3 40.0 %copy-start.58 = (bf16[768,12,16]{0,2,1:T(8,128)(2,1)S(1)}, bf16[768,12,16]{0,2,1:T(8,128)(2,1)}, u32[]{:S(2)}) copy-start(bf16[768,12,16]{0,2,1:T(8,128)(2,1)} %copy-done.57) | copy-start | bytes 884740
  806.3 39.0 %copy-start.50 = (f32[768,16]{0,1:T(8,128)S(1)}, f32[768,16]{0,1:T(8,128)}, u32[]{:S(2)}) copy-start(f32[768,16]{0,1:T(8,128)} %copy-done.49) | copy-start | bytes 147460
  867.1 19.0 %collective-permute-start.17 = (f32[384,1536]{1,0:T(8,128)}, f32[384,1536]{1,0:T(8,128)}, u32[]{:S(2)}, u32[]{:S(2)}) collective-permute-start(f32[384,1536]{1,0:T(8,128)} %fusion.85), channel_id=1, source_target_pairs={{0,1},{1,0},{2,3},{3,2},{4,5},{5,4},{6,7},{7,6},{8,9},{9,8},{10,11... | collective-permute-start | bytes 7077896 | tf_op jit(solution)/shard_map/ppermute | solution.py:20
  895.1 4.7 collective-permute-start.18
  1063.2 12.1 %collective-permute-start.20 = (bf16[96,3072]{1,0:T(8,128)(2,1)S(1)}, bf16[96,3072]{1,0:T(8,128)(2,1)}, u32[]{:S(2)}, u32[]{:S(2)}) collective-permute-start(bf16[96,3072]{1,0:T(8,128)(2,1)S(1)} %get-tuple-element.109), channel_id=1, source_target_pairs={{0,2},{2,0},{1,3},{3,1},{4,6},{6,4},{5,7},{7,5},{8,10},{10,8},{9,1... | collective-permute-start | bytes 1769480 | tf_op jit(solution)/shard_map/ppermute | solution.py:20
  (112 other events, 744.0 us)
Sparse Core Ops, SparseCore 0:
  608.5 45.8 reduce-scatter.4
  710.4 81.2 reduce-scatter.2

commit v3 on v2

--- a/solution.py
+++ b/solution.py
@@ -18,15 +18,6 @@
 
 def swap(value, axis):
     return lax.ppermute(value, axis, [(0, 1), (1, 0)])
-
-
-def join(own, other, axis_name, dim):
-    size = own.shape[dim]
-    whole = own.shape[:dim] + (2 * size,) + own.shape[dim + 1 :]
-    at = lax.axis_index(axis_name)
-    out = jnp.zeros(whole, own.dtype)
-    out = lax.dynamic_update_slice_in_dim(out, own, at * size, dim)
-    return lax.dynamic_update_slice_in_dim(out, other, (1 - at) * size, dim)
 
 
 def pick(value, index, dim):
@@ -87,9 +78,9 @@
 
 
 class Gather:
-    def __init__(self, lanes, own, whole):
+    def __init__(self, lanes, whole):
         zs, z, y, x = lanes.zs, lanes.z, lanes.y, lanes.x
-        self.lanes, self.own, self.whole = lanes, own, whole
+        own = whole.at[z, y, x]
 
         def block(zz, yy):
             return whole.at[zz, yy, x]
@@ -162,8 +153,11 @@
 
 
 class PairGather:
-    def __init__(self, lanes, kept, sent, whole, y_first):
+    def __init__(self, lanes, shard, whole, y_first):
         zs, z, y, x = lanes.zs, lanes.z, lanes.y, lanes.x
+        ff = whole.shape[-1]
+        kept = shard.at[:, pl.ds(pl.multiple_of(x * ff, ff), ff)]
+        sent = shard.at[:, pl.ds(pl.multiple_of((1 - x) * ff, ff), ff)]
         self.y_first = y_first
 
         def along(piece, axis, to, sends=None, receives=None):
@@ -244,25 +238,31 @@
 
 
 def gather_kernel(zs, groups, pairs, *refs):
-    owns = refs[:groups]
-    pair_in = refs[groups : groups + 2 * pairs]
-    outs = refs[groups + 2 * pairs : 2 * groups + 3 * pairs]
-    send_sems, recv_sems, local_sems = refs[2 * groups + 3 * pairs :]
-    lanes = Lanes(send_sems, recv_sems, local_sems, zs)
+    shards = sum(groups)
+    owns, pair_in = refs[:shards], refs[shards : shards + pairs]
+    refs = refs[shards + pairs :]
+    outs = refs[: len(groups) + pairs]
+    lanes = Lanes(*refs[len(groups) + pairs :], zs)
+    z, y, x = lanes.z, lanes.y, lanes.x
+    pieces, at = [], 0
+    for count, whole in zip(groups, outs):
+        width = whole.shape[-1] // count
+        for i in range(count):
+            target = whole.at[z, y, x, :, pl.ds(i * width, width)]
+            pieces.append(pltpu.make_async_copy(owns[at], target, lanes.local()))
+            at += 1
+    for piece in pieces:
+        piece.start()
     greet(zs)
-    gathers = [Gather(lanes, own, whole) for own, whole in zip(owns, outs)]
+    gathers = [Gather(lanes, whole) for whole in outs[: len(groups)]]
     quarters = [
-        PairGather(lanes, pair_in[2 * i], pair_in[2 * i + 1], outs[groups + i], i == 0)
-        for i in range(pairs)
-    ]
-    locals_ = [
-        pltpu.make_async_copy(own, whole.at[lanes.z, lanes.y, lanes.x], lanes.local())
-        for own, whole in zip(owns, outs)
+        PairGather(lanes, pair_in[i], outs[len(groups) + i], i == 0) for i in range(pairs)
     ]
     for quarter in quarters:
         quarter.begin()
-    for copy, gather in zip(locals_, gathers):
-        copy.start()
+    for piece in pieces:
+        piece.wait()
+    for gather in gathers:
         gather.begin()
     for quarter in quarters:
         quarter.swapped()
@@ -282,32 +282,36 @@
         for quarter in quarters:
             if quarter.y_first:
                 quarter.step(k)
-    for copy in locals_:
-        copy.wait()
     for gather in gathers:
         gather.finish()
     for quarter in quarters:
         quarter.finish()
 
 
-def gather_all(shards, quarters, zs):
-    groups, pairs = len(shards), len(quarters)
-    flat = list(shards) + [array for pair in quarters for array in pair]
-    outs = [
-        jax.ShapeDtypeStruct((zs, 2, 2) + array.shape, array.dtype)
-        for array in list(shards) + [kept for kept, _ in quarters]
-    ]
-    moves = groups * (3 + 8 * (zs - 1)) + pairs * (2 + 4 * (zs - 1))
+def gather_all(groups, quarters, zs):
+    flat = [shard for group in groups for shard in group] + list(quarters)
+    outs = []
+    for group in groups:
+        columns = sum(shard.shape[1] for shard in group)
+        outs.append(
+            jax.ShapeDtypeStruct((zs, 2, 2, group[0].shape[0], columns), group[0].dtype)
+        )
+    for shard in quarters:
+        outs.append(
+            jax.ShapeDtypeStruct((zs, 2, 2, shard.shape[0], shard.shape[1] // 2), shard.dtype)
+        )
+    count, pairs = len(groups), len(quarters)
+    moves = count * (3 + 8 * (zs - 1)) + pairs * (2 + 4 * (zs - 1))
     hbm = pl.BlockSpec(memory_space=pltpu.HBM)
     return pl.pallas_call(
-        functools.partial(gather_kernel, zs, groups, pairs),
+        functools.partial(gather_kernel, zs, tuple(len(group) for group in groups), pairs),
         out_shape=outs,
         in_specs=[hbm] * len(flat),
         out_specs=[hbm] * len(outs),
         scratch_shapes=[
             pltpu.SemaphoreType.DMA((moves,)),
             pltpu.SemaphoreType.DMA((moves,)),
-            pltpu.SemaphoreType.DMA((groups + pairs,)),
+            pltpu.SemaphoreType.DMA((len(flat),)),
         ],
         compiler_params=pltpu.CompilerParams(collective_id=1, has_side_effects=True),
     )(*flat)
@@ -459,9 +463,55 @@
         self.three.sent()
 
 
+class Crest:
+    def __init__(self, lanes, own, held, out):
+        zs, z, y, x = lanes.zs, lanes.z, lanes.y, lanes.x
+        near_x, near_y, mine_x, mine_y, right, left, inbox_r, inbox_l = (
+            held.at[i] for i in range(8)
+        )
+        self.zs, self.z, self.own, self.out = zs, z, own, out
+        self.near_x, self.near_y, self.mine_x, self.mine_y = near_x, near_y, mine_x, mine_y
+        self.ways = (
+            (right, inbox_r, z > 0, z < zs - 1),
+            (left, inbox_l, z < zs - 1, z > 0),
+        )
+        self.one = Move(lanes.copy(own, near_x, {"x": 1 - x}), None, None)
+        self.two = Move(lanes.copy(mine_x, near_y, {"y": 1 - y}), None, None)
+        self.moves = [
+            Move(lanes.copy(right, inbox_r, {"z": jnp.minimum(z + 1, zs - 1)}), z < zs - 1, z > 0),
+            Move(lanes.copy(left, inbox_l, {"z": jnp.maximum(z - 1, 0)}), z > 0, z < zs - 1),
+        ]
+
+    def second(self):
+        self.one.arrived()
+        self.mine_x[...] = jnp.maximum(self.own[...], self.near_x[...])
+        self.two.start()
+
+    def finish(self):
+        self.two.arrived()
+        self.mine_y[...] = jnp.maximum(self.mine_x[...], self.near_y[...])
+        self.out[...] = self.mine_y[...]
+        for move, (held, inbox, has_before, has_after) in zip(self.moves, self.ways):
+
+            @pl.when(has_before)
+            def _():
+                move.copy_.wait_recv()
+                self.out[...] = jnp.maximum(self.out[...], inbox[...])
+                held[...] = jnp.maximum(self.mine_y[...], inbox[...])
+
+            @pl.when(jnp.logical_not(has_before))
+            def _():
+                held[...] = self.mine_y[...]
+
+            move.start()
+        for move in [self.one, self.two] + self.moves:
+            move.sent()
+
+
 def scatter_kernel(zs, orders, *refs):
     count = len(orders)
-    parts, outs, rest = refs[:count], refs[count : 2 * count], list(refs[2 * count :])
+    parts, crest_in, refs = refs[:count], refs[count], refs[count + 1 :]
+    outs, crest_out, rest = refs[:count], refs[count], list(refs[count + 1 :])
     send_sems, recv_sems = rest[:2]
     rest = rest[2:]
     lanes = Lanes(send_sems, recv_sems, None, zs)
@@ -473,8 +523,11 @@
             zfirst.append(ScatterZ(lanes, parts[i], held, outs[i]))
         else:
             full.append(Scatter(lanes, parts[i], held, outs[i], order))
+    crest = Crest(lanes, crest_in, rest[0], crest_out)
+    crest.one.start()
     for item in full:
         item.begin()
+    crest.second()
     for d in ends_first(zs):
         for item in zfirst:
             item.pass_on(d)
@@ -482,6 +535,7 @@
             item.second(d)
     for item in zfirst:
         item.total()
+    crest.finish()
     for d in ends_first(zs):
         for item in full:
             item.third(d)
@@ -493,8 +547,8 @@
         item.finish()
 
 
-def scatter_all(parts, orders, zs):
-    scratch, moves = [], 0
+def scatter_all(parts, orders, crest, zs):
+    scratch, moves = [], 4
     for part, order in zip(parts, orders):
         block = part.shape[3:]
         if order == "z":
@@ -507,15 +561,17 @@
     vmem = pl.BlockSpec(memory_space=pltpu.VMEM)
     return pl.pallas_call(
         functools.partial(scatter_kernel, zs, orders),
-        out_shape=[jax.ShapeDtypeStruct(part.shape[3:], F32) for part in parts],
-        in_specs=[vmem] * len(parts),
-        out_specs=[vmem] * len(parts),
+        out_shape=[jax.ShapeDtypeStruct(part.shape[3:], F32) for part in parts]
+        + [jax.ShapeDtypeStruct(crest.shape, F32)],
+        in_specs=[vmem] * (len(parts) + 1),
+        out_specs=[vmem] * (len(parts) + 1),
         scratch_shapes=[pltpu.SemaphoreType.DMA((moves,)), pltpu.SemaphoreType.DMA((moves,))]
-        + scratch,
+        + scratch
+        + [pltpu.VMEM((8,) + crest.shape, F32)],
         compiler_params=pltpu.CompilerParams(
             collective_id=2, has_side_effects=True, vmem_limit_bytes=56 * 2**20
         ),
-    )(*parts)
+    )(*parts, crest)
 
 
 def nn(left, right):
@@ -576,46 +632,215 @@
     return (stream_grad, gain_grad, bias_grad)
 
 
-def rotate(field, positions, direction):
-    half_count = ROT_DIM // 2
+def turn_tables(positions):
     rates = 10000.0 ** (-jnp.arange(0, ROT_DIM, 2).astype(F32) / ROT_DIM)
     angles = positions[:, None] * rates[None, :]
-    cosine = jnp.cos(angles)[:, None, :]
-    sine = direction * jnp.sin(angles)[:, None, :]
-    first = field[..., :half_count]
-    second = field[..., half_count:ROT_DIM]
-    return jnp.concatenate(
-        [first * cosine - second * sine, second * cosine + first * sine, field[..., ROT_DIM:]],
-        axis=-1,
-    )
-
-
-def attend_forward(query, keys, values, allowed):
-    raw_scores = jnp.einsum("qhe,khe->hqk", query, keys, preferred_element_type=F32)
-    scores = jnp.where(allowed[None, None, :], raw_scores * HEAD_DIM ** (-0.5), NEGATIVE)
-    head_peak = jnp.max(scores, axis=(1, 2))
-    row_top = jnp.max(scores, axis=-1, keepdims=True)
-    log_total = jnp.log(jnp.sum(jnp.exp(scores - row_top), axis=-1, keepdims=True)) + row_top
-    weighting = jnp.exp(scores - log_total).astype(BF)
-    mixed = jnp.einsum("hqk,khe->qhe", weighting, values, preferred_element_type=F32)
-    return (mixed, log_total, head_peak)
-
-
-def attend_backward(query, keys, values, allowed, log_total, grad_mixed):
-    raw_scores = jnp.einsum("qhe,khe->hqk", query, keys, preferred_element_type=F32)
-    scores = jnp.where(allowed[None, None, :], raw_scores * HEAD_DIM ** (-0.5), NEGATIVE)
-    weighting = jnp.exp(scores - log_total)
-    grad_weights = jnp.einsum("qhe,khe->hqk", grad_mixed, values, preferred_element_type=F32)
-    grad_values = jnp.einsum(
-        "hqk,qhe->khe", weighting.astype(BF), grad_mixed, preferred_element_type=F32
-    )
-    grad_scores = weighting * (
-        grad_weights - jnp.sum(grad_weights * weighting, axis=-1, keepdims=True)
-    )
-    grad_raw = (grad_scores * HEAD_DIM ** (-0.5)).astype(BF)
-    grad_query = jnp.einsum("hqk,khe->qhe", grad_raw, keys, preferred_element_type=F32)
-    grad_keys = jnp.einsum("hqk,qhe->khe", grad_raw, query, preferred_element_type=F32)
-    return (grad_query, grad_keys, grad_values)
+    cosine, sine = jnp.cos(angles), jnp.sin(angles)
+    rest = jnp.ones((positions.shape[0], HEAD_DIM - ROT_DIM), F32)
+    zero, none = jnp.zeros_like(rest), jnp.zeros_like(sine)
+    return (
+        jnp.concatenate([cosine, cosine, rest] * 2, axis=1),
+        jnp.concatenate([-sine, none, zero] * 2, axis=1),
+        jnp.concatenate([none, sine, zero] * 2, axis=1),
+    )
+
+
+def turn(field, cosine, sine_a, sine_b, direction):
+    half = ROT_DIM // 2
+    width = field.shape[-1]
+    ahead = pltpu.roll(field, width - half, 1)
+    behind = pltpu.roll(field, half, 1)
+    return field * cosine + direction * (ahead * sine_a + behind * sine_b)
+
+
+def head_lanes(shape, which):
+    lanes = lax.broadcasted_iota(jnp.int32, shape, 1)
+    return (lanes >= which * HEAD_DIM) & (lanes < (which + 1) * HEAD_DIM)
+
+
+def attend_tile(query, keys, values, bias):
+    scores = nt(query, keys) + bias
+    top = jnp.max(scores, axis=-1, keepdims=True)
+    weights = jnp.exp(scores - top)
+    total = jnp.sum(weights, axis=-1, keepdims=True)
+    return nn(weights.astype(BF), values) / total, top
+
+
+def attend_kernel(q_ref, k_ref, v_ref, bias_ref, mixed_ref, peak_ref):
+    rows = q_ref.shape[0]
+    tile = rows // 3 if rows % 3 == 0 and (rows // 3) % 16 == 0 else rows
+    keys, values, bias = k_ref[...], v_ref[...], bias_ref[...]
+    peaks = [None, None]
+    for start in range(0, rows, tile):
+        query = q_ref[start : start + tile, :] * BF(HEAD_DIM ** (-0.5))
+        outs = []
+        for which in range(2):
+            one = jnp.where(head_lanes(query.shape, which), query, jnp.zeros_like(query))
+            out, top = attend_tile(one, keys, values, bias)
+            outs.append(out)
+            top = jnp.max(top, axis=0, keepdims=True)
+            peaks[which] = top if peaks[which] is None else jnp.maximum(peaks[which], top)
+        mixed = jnp.where(head_lanes(outs[0].shape, 0), outs[0], outs[1])
+        mixed_ref[start : start + tile, :] = mixed.astype(BF)
+    spot = head_lanes((8, 2 * HEAD_DIM), 0)
+    peak_ref[0] = jnp.where(
+        spot, jnp.broadcast_to(peaks[0], spot.shape), jnp.broadcast_to(peaks[1], spot.shape)
+    )
+
+
+def attend(query, keys, values, bias, offsets):
+    rows, tokens = query.shape[0], keys.shape[0]
+    pairs = bias.shape[0]
+    wide = 2 * HEAD_DIM
+    mixed, peak = pl.pallas_call(
+        attend_kernel,
+        grid=(pairs,),
+        out_shape=[
+            jax.ShapeDtypeStruct((rows, pairs * wide), BF),
+            jax.ShapeDtypeStruct((pairs, 8, wide), F32),
+        ],
+        in_specs=[
+            pl.BlockSpec((rows, wide), lambda j: (0, offsets[0] + j)),
+            pl.BlockSpec((tokens, wide), lambda j: (0, offsets[1] + j)),
+            pl.BlockSpec((tokens, wide), lambda j: (0, offsets[2] + j)),
+            pl.BlockSpec((1, tokens), lambda j: (0, 0)),
+        ],
+        out_specs=[
+            pl.BlockSpec((rows, wide), lambda j: (0, j)),
+            pl.BlockSpec((1, 8, wide), lambda j: (j, 0, 0)),
+        ],
+        compiler_params=pltpu.CompilerParams(vmem_limit_bytes=48 * 2**20),
+        cost_estimate=pl.CostEstimate(
+            flops=8 * rows * tokens * pairs * wide,
+            bytes_accessed=4 * (rows + tokens) * pairs * wide,
+            transcendentals=2 * pairs * rows * tokens,
+        ),
+    )(query, keys, values, bias[:1])
+    return mixed, peak[:, 0, ::HEAD_DIM].reshape(-1)
+
+
+def attend_back_kernel(turned, q_ref, k_ref, v_ref, g_ref, bias_ref, *refs):
+    if turned:
+        cos_ref, sa_ref, sb_ref = refs[:3]
+        refs = refs[3:]
+    dq_ref, dk_ref, dv_ref, dk_acc, dv_acc = refs
+    rows = q_ref.shape[0]
+    tile = rows // 3 if rows % 3 == 0 and (rows // 3) % 128 == 0 else rows
+    scale = BF(HEAD_DIM ** (-0.5))
+    keys, values, bias = k_ref[...], v_ref[...], bias_ref[...]
+    for start in range(0, rows, tile):
+        part = slice(start, start + tile)
+        query, grad = q_ref[part, :] * scale, g_ref[part, :]
+        dq = None
+        for which in range(2):
+            mine = head_lanes(query.shape, which)
+            one = jnp.where(mine, query, jnp.zeros_like(query))
+            out = jnp.where(mine, grad, jnp.zeros_like(grad))
+            scores = nt(keys, one) + bias
+            weights = jnp.exp(scores - jnp.max(scores, axis=0, keepdims=True))
+            weights = weights * (1.0 / jnp.sum(weights, axis=0, keepdims=True))
+            slope = nt(values, out)
+            slope = weights * (slope - jnp.sum(weights * slope, axis=0, keepdims=True))
+            slope = slope.astype(BF)
+            dv = nn(weights.astype(BF), out)
+            dk = nn(slope, one)
+            other = jnp.where(head_lanes(keys.shape, which), keys, jnp.zeros_like(keys))
+            piece = tn(slope, other * scale)
+            dq = piece if dq is None else dq + piece
+            if start == 0 and which == 0:
+                dv_acc[...] = dv
+                dk_acc[...] = dk
+            else:
+                dv_acc[...] += dv
+                dk_acc[...] += dk
+        if turned:
+            dq = turn(dq, cos_ref[part, :], sa_ref[part, :], sb_ref[part, :], -1.0)
+        dq_ref[part, :] = dq.astype(BF)
+    dk = dk_acc[...]
+    if turned:
+        dk = turn(dk, cos_ref[...], sa_ref[...], sb_ref[...], -1.0)
+    dk_ref[...] = dk.astype(BF)
+    dv_ref[...] = dv_acc[...].astype(BF)
+
+
+def attend_back(query, keys, values, grad, bias_column, offsets, turns):
+    rows, tokens = query.shape[0], keys.shape[0]
+    wide = 2 * HEAD_DIM
+    pairs = grad.shape[1] // wide
+    ins = [query, keys, values, grad, bias_column]
+    specs = [
+        pl.BlockSpec((rows, wide), lambda j: (0, offsets[0] + j)),
+        pl.BlockSpec((tokens, wide), lambda j: (0, offsets[1] + j)),
+        pl.BlockSpec((tokens, wide), lambda j: (0, offsets[2] + j)),
+        pl.BlockSpec((rows, wide), lambda j: (0, j)),
+        pl.BlockSpec((tokens, 1), lambda j: (0, 0)),
+    ]
+    if turns is not None:
+        ins += list(turns)
+        specs += [pl.BlockSpec((rows, wide), lambda j: (0, 0))] * 3
+    return pl.pallas_call(
+        functools.partial(attend_back_kernel, turns is not None),
+        grid=(pairs,),
+        out_shape=[
+            jax.ShapeDtypeStruct((rows, pairs * wide), BF),
+            jax.ShapeDtypeStruct((tokens, pairs * wide), BF),
+            jax.ShapeDtypeStruct((tokens, pairs * wide), BF),
+        ],
+        in_specs=specs,
+        out_specs=[
+            pl.BlockSpec((rows, wide), lambda j: (0, j)),
+            pl.BlockSpec((tokens, wide), lambda j: (0, j)),
+            pl.BlockSpec((tokens, wide), lambda j: (0, j)),
+        ],
+        scratch_shapes=[pltpu.VMEM((tokens, wide), F32), pltpu.VMEM((tokens, wide), F32)],
+        compiler_params=pltpu.CompilerParams(vmem_limit_bytes=48 * 2**20),
+        cost_estimate=pl.CostEstimate(
+            flops=20 * rows * tokens * pairs * wide,
+            bytes_accessed=8 * (rows + tokens) * pairs * wide,
+            transcendentals=2 * pairs * rows * tokens,
+        ),
+    )(*ins)
+
+
+def project_kernel(turned, x_ref, w_ref, cos_ref, sa_ref, sb_ref, out_ref):
+    wide = 2 * HEAD_DIM
+    made = nn(x_ref[...], w_ref[...])
+
+    @pl.when(pl.program_id(0) < turned)
+    def _():
+        for start in range(0, made.shape[1], wide):
+            piece = turn(made[:, start : start + wide], cos_ref[...], sa_ref[...], sb_ref[...], 1.0)
+            out_ref[:, start : start + wide] = piece.astype(BF)
+
+    @pl.when(pl.program_id(0) >= turned)
+    def _():
+        out_ref[...] = made.astype(BF)
+
+
+def project(rows, weight, turns, turned_columns):
+    count, depth = rows.shape
+    columns = weight.shape[1]
+    block = 2 * HEAD_DIM * (2 if turned_columns % (4 * HEAD_DIM) == 0 else 1)
+    table = pl.BlockSpec((count, 2 * HEAD_DIM), lambda j: (0, 0))
+    return pl.pallas_call(
+        functools.partial(project_kernel, turned_columns // block),
+        grid=(columns // block,),
+        out_shape=jax.ShapeDtypeStruct((count, columns), BF),
+        in_specs=[
+            pl.BlockSpec((count, depth), lambda j: (0, 0)),
+            pl.BlockSpec((depth, block), lambda j: (0, j)),
+            table,
+            table,
+            table,
+        ],
+        out_specs=pl.BlockSpec((count, block), lambda j: (0, j)),
+        compiler_params=pltpu.CompilerParams(vmem_limit_bytes=48 * 2**20),
+        cost_estimate=pl.CostEstimate(
+            flops=2 * count * depth * columns,
+            bytes_accessed=2 * (count * depth + depth * columns + count * columns),
+            transcendentals=0,
+        ),
+    )(rows, weight, *turns)
 
 
 def pair_rows(own):
@@ -690,78 +915,65 @@
     seq_len = 2 * rows
     inner = self_query.shape[1]
     heads_here = inner // HEAD_DIM
-    ff_half = gate_weight.shape[1]
-    ff = ff_half // 2
+    ff = gate_weight.shape[1] // 2
     shard_rows = self_query.shape[0]
-    context_rows = cross_key.shape[0]
 
     vectors = jnp.stack(
         [self_gain, self_bias, cross_gain, cross_bias, feed_gain, feed_bias]
     ).astype(F32)
     vectors = jnp.pad(vectors, ((0, 2), (0, 128 - shard_rows)))
-    feed = jnp.stack([gate_weight, up_weight, down_weight.T]).reshape(3, shard_rows, 2, ff)
-    kept = pick(feed, x_at, 2)
-    sent = pick(feed, 1 - x_at, 2)
-    norms, in_weight, second, gate_full, up_full, down_t = gather_all(
-        [
-            vectors,
-            jnp.concatenate([self_query, self_key, self_value], axis=1),
-            jnp.concatenate(
-                [
-                    self_output.T,
-                    cross_query,
-                    cross_output.T,
-                    jnp.concatenate([cross_key, cross_value], axis=0),
-                ],
-                axis=1,
-            ),
-        ],
-        [(kept[i], sent[i]) for i in range(3)],
-        zs,
+    (norms, in_weight, self_out_t, cross_in, memory_weight, cross_out_t, gate_full, up_full, down_t) = (
+        gather_all(
+            [
+                [vectors],
+                [self_query, self_key, self_value],
+                [self_output.T],
+                [cross_query],
+                [cross_key, cross_value],
+                [cross_output.T],
+            ],
+            [gate_weight, up_weight, down_weight.T],
+            zs,
+        )
     )
     norms = norms.reshape(-1, 8, 128)[:, :6, :shard_rows].transpose(1, 0, 2).reshape(6, width)
-    in_weight = in_weight.reshape(width, -1)
-    second = second.reshape(width, -1)
-    gate_full, up_full, down_t = (w.reshape(width, ff) for w in (gate_full, up_full, down_t))
-    self_out_t = second[:, :inner]
-    cross_in = second[:, inner : 2 * inner]
-    cross_out_t = second[:, 2 * inner : 3 * inner]
-    memory_weights = second[:, 3 * inner :].reshape(-1, 2, context_rows, inner)
-    cross_keys_w = memory_weights[:, 0].reshape(-1, inner)
-    cross_values_w = memory_weights[:, 1].reshape(-1, inner)
+    in_weight, self_out_t, cross_in, cross_out_t, gate_full, up_full, down_t = (
+        w.reshape(width, -1)
+        for w in (in_weight, self_out_t, cross_in, cross_out_t, gate_full, up_full, down_t)
+    )
+    memory_weight = memory_weight.reshape(-1, 2 * inner)
 
     local = jnp.arange(rows)
     places = jnp.concatenate([t_at * rows + local, (1 - t_at) * rows + local])
-    positions = places.astype(F32)
-    self_allowed = places < lengths[0]
-    cross_allowed = context_live[0] > 0
-    memory = context[0]
-    head_shape = (seq_len, heads_here, HEAD_DIM)
-    memory_shape = (memory.shape[0], heads_here, HEAD_DIM)
+    turns = turn_tables(places.astype(F32))
+    self_bias_row = jnp.where(places < lengths[0], 0.0, NEGATIVE).astype(F32)
+    tokens = context.shape[1]
+    token_rows = -(-tokens // 128) * 128
+    cross_bias_row = jnp.pad(
+        jnp.where(context_live[0] > 0, 0.0, NEGATIVE).astype(F32),
+        (0, token_rows - tokens),
+        constant_values=NEGATIVE,
+    )
+    memory = jnp.pad(context[0], ((0, token_rows - tokens), (0, 0)))
+    pairs = inner // (2 * HEAD_DIM)
 
     cot_group = group_rows(cotangent)
     all_inputs = pair_rows(inputs)
     stream = inputs.astype(F32)
     normed, _, _ = norm_forward(all_inputs.astype(F32), norms[0], norms[1])
     normed_self = normed.astype(BF)
-    projected = nn(normed_self, in_weight)
-    query_self = rotate(projected[:, :inner].reshape(head_shape), positions, 1.0).astype(BF)
-    key_self = rotate(
-        projected[:, inner : 2 * inner].reshape(head_shape), positions, 1.0
-    ).astype(BF)
-    value_self = projected[:, 2 * inner :].astype(BF).reshape(head_shape)
-    mixed, total_self, peak_self = attend_forward(query_self, key_self, value_self, self_allowed)
-    mixed_self = mixed.reshape(seq_len, -1).astype(BF)
+    taken = project(normed_self, in_weight, turns, 2 * inner)
+    self_bias_rows = jnp.broadcast_to(self_bias_row, (pairs, seq_len))
+    mixed_self, peak_self = attend(taken, taken, taken, self_bias_rows, (0, pairs, 2 * pairs))
     stream_cross = stream + spread_pair(mixed_self, self_out_t)
     normed, unit_cross, inverse_cross = norm_forward(stream_cross, norms[2], norms[3])
     normed_cross = pair_rows(normed.astype(BF))
-    query_cross = nn(normed_cross, cross_in).astype(BF).reshape(head_shape)
-    key_cross = nn(memory, cross_keys_w).astype(BF).reshape(memory_shape)
-    value_cross = nn(memory, cross_values_w).astype(BF).reshape(memory_shape)
-    mixed, total_cross, peak_cross = attend_forward(
-        query_cross, key_cross, value_cross, cross_allowed
-    )
-    mixed_cross = mixed.reshape(seq_len, -1).astype(BF)
+    query_cross = nn(normed_cross, cross_in).astype(BF)
+    taken_cross = nn(memory, memory_weight).astype(BF)
+    cross_bias_rows = jnp.broadcast_to(cross_bias_row, (pairs, token_rows))
+    mixed_cross, peak_cross = attend(
+        query_cross, taken_cross, taken_cross, cross_bias_rows, (0, 0, pairs)
+    )
     stream_feed = stream_cross + spread_pair(mixed_cross, cross_out_t)
     normed, unit_feed, inverse_feed = norm_forward(stream_feed, norms[4], norms[5])
     normed_feed = group_rows(normed.astype(BF))
@@ -770,7 +982,9 @@
     sigmoid_gate = jax.nn.sigmoid(gate_pre)
     hidden = (gate_pre * sigmoid_gate * upward).astype(BF)
     result = (stream_feed + spread_group(Product([(hidden, down_t)], True))).astype(BF)
-    peaks = lax.pmax(jnp.maximum(peak_self, peak_cross), ("z", "y", "x"))
+    crest = jnp.pad(
+        jnp.maximum(peak_self, peak_cross)[None], ((0, 7), (0, 128 - heads_here))
+    )
 
     cot_keep, cot_send = columns_by(cot_group, "y", zs)
     down_keep, down_got = reduce_pair(cot_keep, cot_send, hidden, zs)
@@ -789,13 +1003,10 @@
     grad_stream = cotangent.astype(F32) + stream_part
     grad_full = pair_rows(grad_stream.astype(BF))
     part_cross_output = tn(grad_full, mixed_cross)
-    grad_mixed = nn(grad_full, cross_out_t).astype(BF).reshape(head_shape)
-    grad_query, grad_keys, grad_values = attend_backward(
-        query_cross, key_cross, value_cross, cross_allowed, total_cross, grad_mixed
-    )
-    grad_query = grad_query.astype(BF).reshape(seq_len, -1)
-    grad_keys = grad_keys.astype(BF).reshape(memory.shape[0], -1)
-    grad_values = grad_values.astype(BF).reshape(memory.shape[0], -1)
+    grad_mixed = nn(grad_full, cross_out_t).astype(BF)
+    grad_query, grad_keys, grad_values = attend_back(
+        query_cross, taken_cross, taken_cross, grad_mixed, cross_bias_row[:, None], (0, 0, pairs), None
+    )
     grad_normed = spread_pair(grad_query, cross_in)
     part_cross_query = tn(normed_cross, grad_query)
     part_memory = tn(memory, jnp.concatenate([grad_keys, grad_values], axis=1))
@@ -805,14 +1016,13 @@
     grad_stream = grad_stream + stream_part
     grad_full = pair_rows(grad_stream.astype(BF))
     part_self_output = tn(grad_full, mixed_self)
-    grad_mixed = nn(grad_full, self_out_t).astype(BF).reshape(head_shape)
-    grad_query, grad_keys, grad_values = attend_backward(
-        query_self, key_self, value_self, self_allowed, total_self, grad_mixed
-    )
-    grad_query = rotate(grad_query, positions, -1.0).astype(BF).reshape(seq_len, -1)
-    grad_keys = rotate(grad_keys, positions, -1.0).astype(BF).reshape(seq_len, -1)
-    grad_values = grad_values.astype(BF).reshape(seq_len, -1)
-    grad_in = jnp.concatenate([grad_query, grad_keys, grad_values], axis=1)
+    grad_mixed = nn(grad_full, self_out_t).astype(BF)
+    grad_in = jnp.concatenate(
+        attend_back(
+            taken, taken, taken, grad_mixed, self_bias_row[:, None], (0, pairs, 2 * pairs), turns
+        ),
+        axis=1,
+    )
     part_self_in = tn(normed_self, grad_in)
     grad_normed = spread_pair(grad_in, in_weight)
     _, unit_self, inverse_self = norm_forward(stream, norms[0], norms[1])
@@ -839,7 +1049,7 @@
     def blocks(part):
         return part.astype(BF).reshape(zs, 2, 2, -1, part.shape[1])
 
-    vector_sums, sum_self_in, sum_self_output, sum_cross_query, sum_cross_output, sum_memory = (
+    (vector_sums, sum_self_in, sum_self_output, sum_cross_query, sum_cross_output, sum_memory, crest) = (
         scatter_all(
             [
                 vector_sums,
@@ -850,16 +1060,23 @@
                 blocks(part_memory),
             ],
             ["x", "x", "y", "y", "y", "z"],
+            crest,
             zs,
         )
     )
     vector_sums = vector_sums[:, :shard_rows]
+    peaks = crest[0, :heads_here]
     factor = jnp.sqrt(threshold[0] / jnp.maximum(peaks, threshold[0]))
     columns = jnp.repeat(factor, HEAD_DIM)[None, :]
-    down_sum = join(down_keep, down_got, "x", 1).T.astype(F32)
-    gates_sum = join(
-        gates_keep.reshape(-1, 2, 1, ff), gates_got.reshape(-1, 2, 1, ff), "x", 2
-    ).astype(F32)
+
+    def side_by_side(kept, got):
+        low = jnp.where(x_at == 0, kept, got).astype(F32)
+        high = jnp.where(x_at == 0, got, kept).astype(F32)
+        return jnp.concatenate([low, high], axis=1)
+
+    down_sum = side_by_side(down_keep, down_got).T
+    gate_sum = side_by_side(gates_keep[:, :ff], gates_got[:, :ff])
+    up_sum = side_by_side(gates_keep[:, ff:], gates_got[:, ff:])
     return (
         result,
         grad_stream,
@@ -877,8 +1094,8 @@
         sum_cross_output.T,
         vector_sums[4],
         vector_sums[5],
-        gates_sum[:, 0].reshape(-1, ff_half),
-        gates_sum[:, 1].reshape(-1, ff_half),
+        gate_sum,
+        up_sum,
         down_sum,
         peaks,
         self_query.astype(F32) * columns,

time: 1120 us -> 987 us (0.88); the launches traced: 1100 us -> 980 us
  matrix products: 399 us -> 212 us
  Pallas kernels: 388 us -> 532 us
  blocking collectives: 40.8 us -> 0 us
  local copies, waits for them, and re-layouts: 94.4 us -> 55.2 us
  waiting for transfers between devices: 96.8 us -> 111 us
  other arithmetic: 52.6 us -> 40.5 us
    dot_general x12 -> x0, matrix products: 153 us -> none  [the longest x2 48.6 us: attend_backward(): jnp.einsum('hqk,qhe->khe', grad_raw, query, preferred_element_type=F32)]
    pallas_call x1 -> x6, Pallas kernels: 226 us -> 348 us  [the longest x1 259 us: gather_all(): pl.pallas_call(functools.partial(gather_kernel, zs, tuple((len(group) for...]
    pmax x1 -> x0, blocking collectives: 40.8 us -> none  [per_device(): peaks = lax.pmax(jnp.maximum(peak_self, peak_cross), ('z', 'y', 'x'))]
    pallas_call x1, Pallas kernels: 161 us -> 184 us  [scatter_all(): pl.pallas_call(functools.partial(scatter_kernel, zs, orders), out_shape=[...]
    slice x15 -> x2, local copies, waits for them, and re-layouts: 18.6 us -> 0.18 us  [attend(): return (mixed, peak[:, 0, ::HEAD_DIM].reshape(-1))]
    dynamic_update_slice x4 -> x0, local copies, waits for them, and re-layouts: 17.8 us -> none  [the longest x2 9.01 us: join(): return lax.dynamic_update_slice_in_dim(out, other, (1 - at) * size, dim)]
    dot_general x9 -> x7, matrix products: 74.6 us -> 58.9 us  [nn(): lax.dot_general(left, right, (((1,), (0,)), ((), ())), preferred_element_...]
    dot_general x20, matrix products: 103 us -> 87.1 us  [nt(): lax.dot_general(left, right, (((1,), (1,)), ((), ())), preferred_element_...]
  transfers between devices with their start and end apart: 25 -> 25, of which waited for: 7 -> 9; matrix products, arithmetic and copies ran while one was open for 33% -> 21% of each run, Pallas kernels for 35% -> 51%
where the time goes in v3:
time: 987 us; the launch traced here: 980 us
  Pallas kernels  532 us (54%)
  matrix products  212 us (21%)
  waiting for transfers between devices  111 us (11%)
  local copies, waits for them, and re-layouts  55.2 us (6%)
  other arithmetic  40.5 us (4%)
  between operations  16.9 us (2%)
  starting transfers between devices  12.9 us (1%)
    pallas_call x1, Pallas kernels, gather_all(): pl.pallas_call(functools.partial(gather_kernel, zs, tuple((len(group) for...  259 us
    pallas_call x1, Pallas kernels, scatter_all(): pl.pallas_call(functools.partial(scatter_kernel, zs, orders), out_shape=[...  184 us
    ppermute x23, waiting for transfers between devices, swap(): return lax.ppermute(value, axis, [(0, 1), (1, 0)])  111 us
    dot_general x20, matrix products, nt(): lax.dot_general(left, right, (((1,), (1,)), ((), ())), preferred_element_...  87.1 us
    dot_general x9, matrix products, tn(): lax.dot_general(left, right, (((0,), (0,)), ((), ())), preferred_element_...  65.6 us
    dot_general x7, matrix products, nn(): lax.dot_general(left, right, (((1,), (0,)), ((), ())), preferred_element_...  58.9 us
    pallas_call x2, Pallas kernels, attend_back(): pl.pallas_call(functools.partial(attend_back_kernel, turns is not None),...  53.1 us
    pallas_call x2, Pallas kernels, attend(): pl.pallas_call(attend_kernel, grid=(pairs,), out_shape=[jax.ShapeDtypeStr...  23.5 us
  transfers between devices with their start and end apart: 25, of which 9 were waited for; matrix products, arithmetic and copies ran while one was open for 21% of the time, Pallas kernels for 51%

profile of v3, /device:TPU:0, one launch (start us, length us, event | category | flops | bytes accessed | tf_op | source)
XLA Modules:
  0.0 980.0 jit_solution(11790300320618122278)
XLA Ops:
  9.1 259.1 %shard_map.406 = (f32[4,2,2,8,128]{4,3,2,1,0:T(8,128)}, bf16[4,2,2,96,2304]{4,3,2,1,0:T(8,128)(2,1)}, bf16[4,2,2,96,768]{4,3,2,1,0:T(8,128)(2,1)}, bf16[4,2,2,96...) custom-call(f32[8,128]{1,0:T(8,128)} %pad_convert_fusion.refs_0_, ...), custom_call_target="tpu_custom_call" | custom-call | tf_op jit(solution)/shard_map/pallas_call | solution.py:306
  282.8 12.6 %shard_map.407.q_ref.k_ref.v_ref = bf16[768,2304]{1,0:T(8,128)(2,1)} custom-call(bf16[768,1536]{1,0:T(8,128)(2,1)S(1)} %fusion.8.x_ref, bf16[1536,2304]{1,0:T(8,128)(2,1)} %bitcast.179, f32[768,128]{1,0:T(8,128)S(1)} %concatenate.108.cos_ref.refs_0_, f32[768,128]{1,0:T(8,128)S(1)} %concatenate.109.sa_ref.refs_1_, f32[768,128]{1,0:T(8,128)S(1)} %concatenate.110.sb_ref.refs_2_), custom_call_target="tpu_custom_call" | custom-call | flops 5435817984 | bytes 12976128 | tf_op jit(solution)/shard_map/pallas_call | solution.py:825
  298.9 16.4 %shard_map.408 = (bf16[768,768]{1,0:T(8,128)(2,1)S(1)}, f32[6,8,128]{2,1,0:T(8,128)S(1)}) custom-call(bf16[768,2304]{1,0:T(8,128)(2,1)S(1)} %copy-done.14, bf16[768,2304]{1,0:T(8,128)(2,1)S(1)} %copy-done.14, bf16[768,2304]{1,0:T(8,128)(2,1)S(1)} %copy-done.14, f32[1,768]{1,0:T(1,128)S(1)} %compare_select_fusion.bias_ref), custom_call_target="tpu_custom_call" | custom-call | flops 3623878656 | bytes 4718592 | tf_op jit(solution)/shard_map/pallas_call | solution.py:695
  332.6 7.1 shard_map.409
  346.4 26.9 %collective-permute-done.9 = bf16[384,1536]{0,1:T(8,128)(2,1)} collective-permute-done((bf16[384,1536]{0,1:T(8,128)(2,1)}, bf16[384,1536]{0,1:T(8,128)(2,1)}, u32[]{:S(2)}, u32[]{:S(2)}) %collective-permute-start.9) | collective-permute-done | bytes 1179680 | tf_op jit(solution)/shard_map/ppermute | solution.py:20
  383.7 26.4 %collective-permute-done.4 = bf16[384,1536]{1,0:T(8,128)(2,1)S(1)} collective-permute-done((bf16[384,1536]{1,0:T(8,128)(2,1)S(1)}, bf16[384,1536]{1,0:T(8,128)(2,1)S(1)}, u32[]{:S(2)}, u32[]{:S(2)}) %collective-permute-start.4) | collective-permute-done | bytes 1179680 | tf_op jit(solution)/shard_map/ppermute | solution.py:20
  429.8 14.7 %fusion.58 = f32[1536,1536]{0,1:T(8,128)} fusion(bf16[1536,1536]{1,0:T(8,128)(2,1)} %bitcast.193, bf16[384,1536]{1,0:T(8,128)(2,1)S(1)} %get-tuple-element.113, bf16[384,1536]{1,0:T(8,128)(2,1)S(1)} %copy-done.33, bf16[384,1536]{1,0:T(8,128)(2,1)S(1)} %get-tuple-element.112, bf16[384,1536]{1,0:T(8,128)(2,1)S(1)} %copy-done.31), kind=kOutput, calls=%fused_computation.115 | convolution fusion | flops 7266631680 | bytes 18874368 | tf_op jit(solution)/shard_map/dot_general | solution.py:578
  444.5 12.3 %fusion.59 = f32[1536,1536]{0,1:T(8,128)} fusion(bf16[1536,1536]{1,0:T(8,128)(2,1)S(1)} %bitcast.204, bf16[384,1536]{1,0:T(8,128)(2,1)S(1)} %get-tuple-element.113, bf16[384,1536]{1,0:T(8,128)(2,1)S(1)} %copy-done.33, bf16[384,1536]{1,0:T(8,128)(2,1)S(1)} %get-tuple-element.112, bf16[384,1536]{1,0:T(8,128)(2,1)S(1)} %copy-done.31), kind=kOutput, calls=%fused_computation.116 | convolution fusion | flops 7266631680 | bytes 18874368 | tf_op jit(solution)/shard_map/dot_general | solution.py:578
  456.8 20.3 %multiply_convert_fusion = (bf16[1536,1536]{0,1:T(8,128)(2,1)}, bf16[1536,1536]{0,1:T(8,128)(2,1)}, bf16[1536,1536]{0,1:T(8,128)(2,1)}) fusion(f32[1536,1536]{0,1:T(8,128)} %fusion.59, f32[1536,1536]{0,1:T(8,128)} %fusion.58, bf16[1536,1536]{1,0:T(8,128)(2,1)} %bitcast.184, bf16[384,1536]{0,1:T(8,128)(2,1)} %get-tuple-element.109, ...), kind=kOutput, calls=%fused_computation.3 | convolution fusion | flops 7304380416 | bytes 42467328 | tf_op jit(solution)/shard_map/dot_general | solution.py:578
  477.1 6.3 fusion.47
  483.4 6.3 fusion.41
  489.7 5.2 convolution_convert_fusion.1
  506.0 13.8 %fusion.4 = bf16[768,3072]{1,0:T(8,128)(2,1)} fusion(bf16[1536,768]{0,1:T(8,128)(2,1)S(1)} %bitcast.155, bf16[1536,1536]{0,1:T(8,128)(2,1)} %get-tuple-element.100, bf16[1536,1536]{0,1:T(8,128)(2,1)} %get-tuple-element.101), kind=kOutput, calls=%fused_computation.13 | convolution fusion | flops 7268990976 | bytes 16515072 | tf_op jit(solution)/shard_map/dot_general | solution.py:586
  524.5 4.9 convolution_add_fusion.5
  548.8 6.5 add_convert_fusion.1
  555.6 15.1 %collective-permute-done.13 = bf16[384,1536]{1,0:T(8,128)(2,1)} collective-permute-done((bf16[384,1536]{1,0:T(8,128)(2,1)S(1)}, bf16[384,1536]{1,0:T(8,128)(2,1)}, u32[]{:S(2)}, u32[]{:S(2)}) %collective-permute-start.13) | collective-permute-done | bytes 1179680 | tf_op jit(solution)/shard_map/ppermute | solution.py:20
  570.7 8.1 multiply_reduce_fusion
  582.1 6.5 fusion.30
  595.9 16.8 %shard_map.410 = (bf16[768,768]{1,0:T(8,128)(2,1)S(1)}, bf16[256,768]{1,0:T(8,128)(2,1)S(1)}, bf16[256,768]{1,0:T(8,128)(2,1)S(1)}) custom-call(bf16[768,768]{1,0:T(8,128)(2,1)S(1)} %copy-done.16, bf16[256,1536]{1,0:T(8,128)(2,1)S(1)} %copy-done.13, bf16[256,1536]{1,0:T(8,128)(2,1)S(1)} %copy-done.13, bf16[768,768]{1,0:T(8,128)(2,1)S(1)} %convolution_convert_fusion.8.g_ref, ...), custom_call_target="tpu_custom_call" | custom-call | flops 3019898880 | bytes 6291456 | tf_op jit(solution)/shard_map/pallas_call | solution.py:781
  617.4 5.6 fusion.29
  623.0 28.4 %collective-permute-done.19 = bf16[768,3072]{1,0:T(8,128)(2,1)} collective-permute-done((bf16[768,3072]{1,0:T(8,128)(2,1)}, bf16[768,3072]{1,0:T(8,128)(2,1)}, u32[]{:S(2)}, u32[]{:S(2)}) %collective-permute-start.19) | collective-permute-done | bytes 4718624 | tf_op jit(solution)/shard_map/ppermute | solution.py:20
  651.4 14.8 %add_convert_fusion = bf16[768,3072]{1,0:T(8,128)(2,1)} fusion(bf16[768,3072]{1,0:T(8,128)(2,1)} %collective-permute-done.19, bf16[1536,768]{0,1:T(8,128)(2,1)S(1)} %bitcast.152, bf16[1536,1536]{0,1:T(8,128)(2,1)} %get-tuple-element.100, bf16[1536,1536]{0,1:T(8,128)(2,1)} %get-tuple-element.101), kind=kOutput, calls=%fused_computation.2 | convolution fusion | flops 7273709568 | bytes 21233664 | tf_op jit(solution)/shard_map/dot_general | solution.py:586
  667.5 5.2 convolution_convert_fusion.3
  681.8 4.9 convolution_convert_fusion.4
  692.2 4.7 convolution_convert_fusion.7.g_ref
  696.9 36.4 %shard_map.411 = (bf16[768,768]{1,0:T(8,128)(2,1)S(1)}, bf16[768,768]{1,0:T(8,128)(2,1)S(1)}, bf16[768,768]{1,0:T(8,128)(2,1)S(1)}) custom-call(bf16[768,2304]{1,0:T(8,128)(2,1)} %shard_map.407.q_ref.k_ref.v_ref, bf16[768,2304]{1,0:T(8,128)(2,1)} %shard_map.407.q_ref.k_ref.v_ref, bf16[768,2304]{1,0:T(8,128)(2,1)} %shard_map.407.q_ref.k_ref.v_ref, ...), custom_call_target="tpu_custom_call" | custom-call | flops 9059696640 | bytes 9437184 | tf_op jit(solution)/shard_map/pallas_call | solution.py:781
  733.6 5.5 fusion.37
  740.6 5.2 convolution_convert_fusion.5
  745.8 7.8 convolution_convert_fusion
  753.7 5.3 fusion.35
  769.4 183.9 %shard_map.412 = (f32[8,128]{1,0:T(8,128)}, f32[96,2304]{1,0:T(8,128)}, f32[96,768]{1,0:T(8,128)}, f32[96,768]{1,0:T(8,128)}, f32[96,768]{1,0:T(8,128)}, /*index=5*/f32[48,1536]{1,0:T(8,128)}, f32[8,128]{1,0:T(8,128)}) custom-call(f32[4,2,2,8,128]{4,3,2,1,0:T(8,128)} %bitcast.166, bf16[4,2,2,96,2304]{4,3,2,1,0:T(8,128)(2,1)} %bitcast.137, ...), custom_call_target="tpu_custom_call" | custom-call | tf_op jit(solution)/shard_map/pallas_call | solution.py:562
  962.7 5.7 collective-permute-done.20
  (366 shorter events, 164.4 us)
Async XLA Ops:
  7.2 672.2 %reduce-scatter.5.cloned.1.call-start = ((), (), s32[]{:S(2)}) async-start(), calls=%async_computation.3 | async-start | bytes 2949120 | tf_op jit(solution)/shard_map/reduce_scatter | solution.py:608
  7.2 269.4 %collective-permute-start = (bf16[384,1536]{1,0:T(8,128)(2,1)}, bf16[384,1536]{1,0:T(8,128)(2,1)}, u32[]{:S(2)}, u32[]{:S(2)}) collective-permute-start(bf16[384,1536]{1,0:T(8,128)(2,1)} %param.23), channel_id=1, source_target_pairs={{0,1},{1,0},{2,3},{3,2},{4,5},{5,4},{6,7},{7,6},{8,9},{9,8},{10,11... | collective-permute-start | bytes 3538952 | tf_op jit(solution)/shard_map/ppermute | solution.py:20
  317.8 4.9 collective-permute-start.1
  327.7 2.8 collective-permute-start.2
  339.7 37.1 %copy-start.10 = (bf16[768,768]{1,0:T(8,128)(2,1)}, bf16[768,768]{1,0:T(8,128)(2,1)S(1)}, u32[]{:S(2)}) copy-start(bf16[768,768]{1,0:T(8,128)(2,1)S(1)} %get-tuple-element.56) | copy-start | bytes 3538948
  342.2 34.6 %collective-permute-start.3 = (f32[384,1536]{1,0:T(8,128)}, f32[384,1536]{1,0:T(8,128)}, u32[]{:S(2)}, u32[]{:S(2)}) collective-permute-start(f32[384,1536]{1,0:T(8,128)} %fusion.66), channel_id=1, source_target_pairs={{0,1},{1,0},{2,3},{3,2},{4,5},{5,4},{6,7},{7,6},{8,9},{9,8},{10,11... | collective-permute-start | bytes 7077896 | tf_op jit(solution)/shard_map/ppermute | solution.py:20
  344.8 28.6 %collective-permute-start.9 = (bf16[384,1536]{0,1:T(8,128)(2,1)}, bf16[384,1536]{0,1:T(8,128)(2,1)}, u32[]{:S(2)}, u32[]{:S(2)}) collective-permute-start(bf16[384,1536]{0,1:T(8,128)(2,1)} %copy.72), channel_id=1, source_target_pairs={{0,2},{2,0},{1,3},{3,1},{4,6},{6,4},{5,7},{7,5},{8,10},{10,8},{9,1... | collective-permute-start | bytes 3538952 | tf_op jit(solution)/shard_map/ppermute | solution.py:20
  376.8 37.5 %collective-permute-start.10 = (bf16[2,384,1536]{1,2,0:T(8,128)(2,1)}, bf16[2,384,1536]{1,2,0:T(8,128)(2,1)}, u32[]{:S(2)}, u32[]{:S(2)}) collective-permute-start(bf16[2,384,1536]{1,2,0:T(8,128)(2,1)} %pad_maximum_fusion.13), channel_id=1, source_target_pairs={{0,1},{1,0},{2,3},{3,2},{4,5},{5,4},{6,7},{7,6},{8,9},{9,8},{10,11... | collective-permute-start | bytes 7077896 | tf_op jit(solution)/shard_map/ppermute | solution.py:20
  379.8 32.1 %copy-start.20 = (f32[384,1536]{1,0:T(8,128)}, f32[384,1536]{1,0:T(8,128)S(1)}, u32[]{:S(2)}) copy-start(f32[384,1536]{1,0:T(8,128)S(1)} %get-tuple-element.143) | copy-start | bytes 7077892
  381.7 28.4 %collective-permute-start.4 = (bf16[384,1536]{1,0:T(8,128)(2,1)S(1)}, bf16[384,1536]{1,0:T(8,128)(2,1)S(1)}, u32[]{:S(2)}, u32[]{:S(2)}) collective-permute-start(bf16[384,1536]{1,0:T(8,128)(2,1)S(1)} %add_convert_fusion.2), channel_id=1, source_target_pairs={{0,2},{2,0},{1,3},{3,1},{4,6},{6,4},{5,7},{7,5},{8,10},{10,8},{9,1... | collective-permute-start | bytes 3538952 | tf_op jit(solution)/shard_map/ppermute | solution.py:20
  411.9 14.4 %collective-permute-start.5 = (bf16[2,384,1536]{2,1,0:T(8,128)(2,1)}, bf16[2,384,1536]{2,1,0:T(8,128)(2,1)}, u32[]{:S(2)}, u32[]{:S(2)}) collective-permute-start(bf16[2,384,1536]{2,1,0:T(8,128)(2,1)} %pad_maximum_fusion.12), channel_id=1, source_target_pairs={{0,1},{1,0},{2,3},{3,2},{4,5},{5,4},{6,7},{7,6},{8,9},{9,8},{10,11... | collective-permute-start | bytes 7077896 | tf_op jit(solution)/shard_map/ppermute | solution.py:20
  494.8 54.0 %collective-permute-start.21 = (bf16[768,1536]{1,0:T(8,128)(2,1)}, bf16[768,1536]{1,0:T(8,128)(2,1)}, u32[]{:S(2)}, u32[]{:S(2)}) collective-permute-start(bf16[768,1536]{1,0:T(8,128)(2,1)} %convolution_convert_fusion.1), channel_id=1, source_target_pairs={{0,4},{4,0},{1,5},{5,1},{2,6},{6,2},{3,7},{7,3},{8,12},{12,8},{9,1... | collective-permute-start | bytes 7077896 | tf_op jit(solution)/shard_map/ppermute | solution.py:20
  524.2 14.8 %collective-permute-start.12 = (f32[384,1536]{1,0:T(8,128)S(1)}, f32[384,1536]{1,0:T(8,128)S(1)}, u32[]{:S(2)}, u32[]{:S(2)}) collective-permute-start(f32[384,1536]{1,0:T(8,128)S(1)} %convolution_add_fusion.3), channel_id=1, source_target_pairs={{0,1},{1,0},{2,3},{3,2},{4,5},{5,4},{6,7},{7,6},{8,9},{9,8},{10,11... | collective-permute-start | bytes 7077896 | tf_op jit(solution)/shard_map/ppermute | solution.py:20
  529.4 26.2 %collective-permute-start.11 = (f32[384,1536]{1,0:T(8,128)}, f32[384,1536]{1,0:T(8,128)}, u32[]{:S(2)}, u32[]{:S(2)}) collective-permute-start(f32[384,1536]{1,0:T(8,128)} %convolution_add_fusion.5), channel_id=1, source_target_pairs={{0,1},{1,0},{2,3},{3,2},{4,5},{5,4},{6,7},{7,6},{8,9},{9,8},{10,11... | collective-permute-start | bytes 7077896 | tf_op jit(solution)/shard_map/ppermute | solution.py:20
  542.4 28.3 %collective-permute-start.13 = (bf16[384,1536]{1,0:T(8,128)(2,1)S(1)}, bf16[384,1536]{1,0:T(8,128)(2,1)}, u32[]{:S(2)}, u32[]{:S(2)}) collective-permute-start(bf16[384,1536]{1,0:T(8,128)(2,1)S(1)} %fusion.28), channel_id=1, source_target_pairs={{0,2},{2,0},{1,3},{3,1},{4,6},{6,4},{5,7},{7,5},{8,10},{10,8},{9,1... | collective-permute-start | bytes 3538952 | tf_op jit(solution)/shard_map/ppermute | solution.py:20
  547.4 104.0 %collective-permute-start.19 = (bf16[768,3072]{1,0:T(8,128)(2,1)}, bf16[768,3072]{1,0:T(8,128)(2,1)}, u32[]{:S(2)}, u32[]{:S(2)}) collective-permute-start(bf16[768,3072]{1,0:T(8,128)(2,1)} %fusion.4), channel_id=1, source_target_pairs={{0,4},{4,0},{1,5},{5,1},{2,6},{6,2},{3,7},{7,3},{8,12},{12,8},{9,1... | collective-permute-start | bytes 14155784 | tf_op jit(solution)/shard_map/ppermute | solution.py:20
  547.8 34.3 %collective-permute-start.7 = (f32[384,1536]{1,0:T(8,128)}, f32[384,1536]{1,0:T(8,128)}, u32[]{:S(2)}, u32[]{:S(2)}) collective-permute-start(f32[384,1536]{1,0:T(8,128)} %fusion.52), channel_id=1, source_target_pairs={{0,1},{1,0},{2,3},{3,2},{4,5},{5,4},{6,7},{7,6},{8,9},{9,8},{10,11... | collective-permute-start | bytes 7077896 | tf_op jit(solution)/shard_map/ppermute | solution.py:20
  548.8 66.6 %collective-permute-start.6 = (f32[384,1536]{1,0:T(8,128)}, f32[384,1536]{1,0:T(8,128)}, u32[]{:S(2)}, u32[]{:S(2)}) collective-permute-start(f32[384,1536]{1,0:T(8,128)} %fusion.55), channel_id=1, source_target_pairs={{0,1},{1,0},{2,3},{3,2},{4,5},{5,4},{6,7},{7,6},{8,9},{9,8},{10,11... | collective-permute-start | bytes 7077896 | tf_op jit(solution)/shard_map/ppermute | solution.py:20
  555.3 23.5 %copy-start.28 = (bf16[384,1536]{1,0:T(8,128)(2,1)S(1)}, bf16[384,1536]{1,0:T(8,128)(2,1)}, u32[]{:S(2)}) copy-start(bf16[384,1536]{1,0:T(8,128)(2,1)} %param.24) | copy-start | bytes 3538948
  555.4 401.8 %reduce-scatter.3.cloned.1.call-start = ((), (), s32[]{:S(2)}) async-start(), calls=%async_computation.2 | async-start | bytes 5898240 | tf_op jit(solution)/shard_map/reduce_scatter | solution.py:608
  555.6 23.3 %copy-start.21 = (f32[384,1536]{1,0:T(8,128)S(1)}, f32[384,1536]{1,0:T(8,128)}, u32[]{:S(2)}) copy-start(f32[384,1536]{1,0:T(8,128)} %copy-done.20) | copy-start | bytes 7077892
  581.3 10.4 %collective-permute-start.14 = (bf16[384,1536]{1,0:T(8,128)(2,1)S(1)}, bf16[384,1536]{1,0:T(8,128)(2,1)}, u32[]{:S(2)}, u32[]{:S(2)}) collective-permute-start(bf16[384,1536]{1,0:T(8,128)(2,1)S(1)} %get-tuple-element.98), channel_id=1, source_target_pairs={{0,1},{1,0},{2,3},{3,2},{4,5},{5,4},{6,7},{7,6},{8,9},{9,8},{10,11... | collective-permute-start | bytes 3538952 | tf_op jit(solution)/shard_map/ppermute | solution.py:20
  588.7 28.7 %collective-permute-start.8 = (bf16[384,1536]{1,0:T(8,128)(2,1)}, bf16[384,1536]{1,0:T(8,128)(2,1)}, u32[]{:S(2)}, u32[]{:S(2)}) collective-permute-start(bf16[384,1536]{1,0:T(8,128)(2,1)} %fusion.30), channel_id=1, source_target_pairs={{0,2},{2,0},{1,3},{3,1},{4,6},{6,4},{5,7},{7,5},{8,10},{10,8},{9,1... | collective-permute-start | bytes 3538952 | tf_op jit(solution)/shard_map/ppermute | solution.py:20
  591.6 25.7 %slice-start.4 = ((s8[4718592]{0:T(1024)(128)(4,1)}), s8[4194304]{0:T(1024)(128)(4,1)S(1)}, s32[]{:S(2)}) async-start(s8[4718592]{0:T(1024)(128)(4,1)} %bitcast.190), calls=%async_computation.8 | async-start | bytes 8388608
  615.2 36.2 %copy-start.36 = (bf16[1536,4,1,192]{0,3,2,1:T(8,128)(2,1)S(1)}, bf16[1536,4,1,192]{0,3,2,1:T(8,128)(2,1)}, u32[]{:S(2)}) copy-start(bf16[1536,4,1,192]{0,3,2,1:T(8,128)(2,1)} %get-tuple-element.105) | copy-start | bytes 7077892
  615.2 57.5 %collective-permute-start.15 = (f32[384,1536]{1,0:T(8,128)}, f32[384,1536]{1,0:T(8,128)}, u32[]{:S(2)}, u32[]{:S(2)}) collective-permute-start(f32[384,1536]{1,0:T(8,128)} %fusion.63), channel_id=1, source_target_pairs={{0,1},{1,0},{2,3},{3,2},{4,5},{5,4},{6,7},{7,6},{8,9},{9,8},{10,11... | collective-permute-start | bytes 7077896 | tf_op jit(solution)/shard_map/ppermute | solution.py:20
  679.4 12.8 %collective-permute-start.16 = (bf16[384,1536]{1,0:T(8,128)(2,1)}, bf16[384,1536]{1,0:T(8,128)(2,1)}, u32[]{:S(2)}, u32[]{:S(2)}) collective-permute-start(bf16[384,1536]{1,0:T(8,128)(2,1)} %get-tuple-element.96), channel_id=1, source_target_pairs={{0,1},{1,0},{2,3},{3,2},{4,5},{5,4},{6,7},{7,6},{8,9},{9,8},{10,11... | collective-permute-start | bytes 3538952 | tf_op jit(solution)/shard_map/ppermute | solution.py:20
  681.1 9.9 %collective-permute-start.22 = (bf16[96,1536]{1,0:T(8,128)(2,1)}, bf16[96,1536]{1,0:T(8,128)(2,1)}, u32[]{:S(2)}, u32[]{:S(2)}) collective-permute-start(bf16[96,1536]{1,0:T(8,128)(2,1)} %dynamic-slice_bitcast_fusion.2), channel_id=1, source_target_pairs={{0,2},{2,0},{1,3},{3,1},{4,6},{6,4},{5,7},{7,5},{8,10},{10,8},{9,1... | collective-permute-start | bytes 884744 | tf_op jit(solution)/shard_map/ppermute | solution.py:20
  739.1 14.5 %collective-permute-start.17 = (f32[384,1536]{1,0:T(8,128)S(1)}, f32[384,1536]{1,0:T(8,128)S(1)}, u32[]{:S(2)}, u32[]{:S(2)}) collective-permute-start(f32[384,1536]{1,0:T(8,128)S(1)} %fusion.37), channel_id=1, source_target_pairs={{0,1},{1,0},{2,3},{3,2},{4,5},{5,4},{6,7},{7,6},{8,9},{9,8},{10,11... | collective-permute-start | bytes 7077896 | tf_op jit(solution)/shard_map/ppermute | solution.py:20
  763.2 5.5 collective-permute-start.18
  769.3 185.3 %copy-start.49 = (bf16[48,768]{1,0:T(8,128)(2,1)S(1)}, bf16[48,768]{1,0:T(8,128)(2,1)}, u32[]{:S(2)}) copy-start(bf16[48,768]{1,0:T(8,128)(2,1)} %refs_6_.1) | copy-start | bytes 221188
  958.5 9.9 %collective-permute-start.20 = (bf16[96,3072]{1,0:T(8,128)(2,1)S(1)}, bf16[96,3072]{1,0:T(8,128)(2,1)S(1)}, u32[]{:S(2)}, u32[]{:S(2)}) collective-permute-start(bf16[96,3072]{1,0:T(8,128)(2,1)S(1)} %get-tuple-element.120), channel_id=1, source_target_pairs={{0,2},{2,0},{1,3},{3,1},{4,6},{6,4},{5,7},{7,5},{8,10},{10,8},{9,1... | collective-permute-start | bytes 1769480 | tf_op jit(solution)/shard_map/ppermute | solution.py:20
  (87 other events, 542.0 us)
Sparse Core Ops, SparseCore 0:
  555.5 48.6 reduce-scatter.4
  666.3 83.8 reduce-scatter.2

commit v4 on v3

--- a/solution.py
+++ b/solution.py
@@ -136,13 +136,15 @@
             follow[0].arrived()
             follow[2].start()
 
-    def finish(self):
+    def landed(self):
         self.first[1].arrived()
         self.far[0][0].arrived()
         for step in self.steps:
             for _, follow in step:
                 follow[1].arrived()
                 follow[2].arrived()
+
+    def sent(self):
         for move in self.first + self.far[0]:
             move.sent()
         for step in self.steps:
@@ -206,13 +208,15 @@
             for other in follow:
                 other.start()
 
-    def finish(self):
+    def landed(self):
         if not self.y_first:
             self.own_y.arrived()
         for step in self.steps:
             for move, follow in step:
                 for other in follow:
                     other.arrived()
+
+    def sent(self):
         self.swap.sent()
         self.own_y.sent()
         for step in self.steps:
@@ -222,7 +226,7 @@
                     other.sent()
 
 
-def greet(zs):
+def greet(zs, mates=False):
     z, y, x = lax.axis_index("z"), lax.axis_index("y"), lax.axis_index("x")
     barrier = pltpu.get_barrier_semaphore()
 
@@ -233,7 +237,9 @@
     signal({"y": 1 - y})
     pl.when(z > 0)(lambda: signal({"z": z - 1}))
     pl.when(z < zs - 1)(lambda: signal({"z": z + 1}))
-    peers = 2 + (z > 0).astype(jnp.int32) + (z < zs - 1).astype(jnp.int32)
+    if mates:
+        signal({"tensor": 1 - lax.axis_index("tensor")})
+    peers = (3 if mates else 2) + (z > 0).astype(jnp.int32) + (z < zs - 1).astype(jnp.int32)
     pl.semaphore_wait(barrier, peers)
 
 
@@ -282,10 +288,9 @@
         for quarter in quarters:
             if quarter.y_first:
                 quarter.step(k)
-    for gather in gathers:
-        gather.finish()
-    for quarter in quarters:
-        quarter.finish()
+    for item in gathers + quarters:
+        item.landed()
+        item.sent()
 
 
 def gather_all(groups, quarters, zs):
@@ -535,10 +540,10 @@
             item.second(d)
     for item in zfirst:
         item.total()
-    crest.finish()
     for d in ends_first(zs):
         for item in full:
             item.third(d)
+    crest.finish()
     for item in zfirst:
         item.after()
     for item in full:
@@ -601,6 +606,16 @@
     )
 
 
+def reduce_full(left_keep, left_send, right, zs):
+    got = swap(tn(left_send, right).astype(BF), "x")
+    held = (tn(left_keep, right) + got.astype(F32)).astype(BF)
+    held = held.reshape(zs, 2, -1, right.shape[1])
+    at = lax.axis_index("y")
+    got = swap(pick(held, 1 - at, 1), "y")
+    held = (pick(held, at, 1).astype(F32) + got.astype(F32)).astype(BF)
+    return lax.psum_scatter(held, "z", scatter_dimension=0, tiled=False)
+
+
 def reduce_pair(left_keep, left_send, right, zs):
     got = swap(tn(left_send, right).astype(BF), "y")
     held = (tn(left_keep, right) + got.astype(F32)).astype(BF)
@@ -618,6 +633,11 @@
     inverse = lax.rsqrt(jnp.mean(centred * centred, axis=-1, keepdims=True) + EPSILON)
     unit_rows = centred * inverse
     return (unit_rows * gain_vec + bias_vec, unit_rows, inverse)
+
+
+def unit_rows_of(stream):
+    _, unit_rows, inverse = norm_forward(stream, 1.0, 0.0)
+    return unit_rows, inverse
 
 
 def norm_backward(incoming, unit_rows, inverse, gain_vec):
@@ -843,6 +863,356 @@
     )(rows, weight, *turns)
 
 
+def normalise(stream, gain_vec, bias_vec):
+    average = jnp.mean(stream, axis=-1, keepdims=True)
+    centred = stream - average
+    inverse = lax.rsqrt(jnp.mean(centred * centred, axis=-1, keepdims=True) + EPSILON)
+    return centred * inverse * gain_vec + bias_vec
+
+
+def attend_pair(query, keys, values, bias, tile):
+    outs_all, peaks = [], [None, None]
+    for start in range(0, tile[0], tile[1]):
+        rows = query(start, tile[1]) * BF(HEAD_DIM ** (-0.5))
+        outs = []
+        for which in range(2):
+            one = jnp.where(head_lanes(rows.shape, which), rows, jnp.zeros_like(rows))
+            out, top = attend_tile(one, keys, values, bias)
+            outs.append(out)
+            top = jnp.max(top, axis=0, keepdims=True)
+            peaks[which] = top if peaks[which] is None else jnp.maximum(peaks[which], top)
+        outs_all.append((start, jnp.where(head_lanes(outs[0].shape, 0), outs[0], outs[1])))
+    return outs_all, peaks
+
+
+def forward_kernel(zs, *refs):
+    refs = list(refs)
+
+    def take(count):
+        taken_refs = refs[:count]
+        del refs[:count]
+        return taken_refs
+
+    shards = take(9)
+    quarters_in = take(3)
+    inputs_hbm, cot_hbm, cos_ref, sa_ref, sb_ref, self_bias, cross_bias, memory = take(8)
+    wholes = take(6)
+    quarter_outs = take(3)
+    outs = take(10)
+    cot_out = take(1)[0]
+    peak_out = take(1)[0]
+    send_sems, recv_sems, local_sems = take(3)
+    w_vec, w_in, w_so, w_cq, w_kv, w_co = take(6)
+    (
+        x_all, normed_self, taken, mixed_self, stream_cross, normed_cross,
+        query_cross, taken_cross, mixed_cross, stream_feed, normed_feed,
+        part_send, part_got, part_send2, part_got2, vectors,
+    ) = take(16)
+    lanes = Lanes(send_sems, recv_sems, local_sems, zs)
+    z, y, x = lanes.z, lanes.y, lanes.x
+    t = lax.axis_index("tensor")
+    rows, width = inputs_hbm.shape
+    wide = 2 * HEAD_DIM
+
+    def local(source, target):
+        return pltpu.make_async_copy(source, target, lanes.local())
+
+    pieces, at = [], 0
+    for count, whole in zip((1, 3, 1, 1, 2, 1), wholes):
+        columns = whole.shape[-1] // count
+        for i in range(count):
+            target = whole.at[z, y, x, :, pl.ds(i * columns, columns)]
+            pieces.append(local(shards[at], target))
+            at += 1
+    own_inputs = local(inputs_hbm, x_all.at[0])
+    own_cot = local(cot_hbm, cot_out.at[0])
+    for piece in pieces + [own_inputs, own_cot]:
+        piece.start()
+    greet(zs, True)
+
+    def mate(source, target):
+        return Move(lanes.copy(source, target, {"tensor": 1 - t}), None, None)
+
+    def across(source, target):
+        return Move(lanes.copy(source, target, {"x": 1 - x}), None, None)
+
+    mate_inputs = mate(inputs_hbm, x_all.at[1])
+    cot_moves = [
+        mate(cot_hbm, cot_out.at[1]),
+        across(cot_hbm, cot_out.at[2]),
+        mate(cot_out.at[2], cot_out.at[3]),
+    ]
+    feed_moves = [
+        mate(normed_feed.at[0], normed_feed.at[1]),
+        across(normed_feed.at[0], normed_feed.at[2]),
+        mate(normed_feed.at[2], normed_feed.at[3]),
+    ]
+    mate_self = mate(part_send, part_got)
+    mate_normed = mate(normed_cross.at[0], normed_cross.at[1])
+    mate_cross = mate(part_send2, part_got2)
+    gathers = [Gather(lanes, whole) for whole in wholes]
+    quarters = [
+        PairGather(lanes, quarters_in[i], quarter_outs[i], i == 0) for i in range(3)
+    ]
+    loads = [
+        local(whole, held)
+        for whole, held in zip(wholes, (w_vec, w_in, w_so, w_cq, w_kv, w_co))
+    ]
+    results = (
+        normed_self, taken, mixed_self, stream_cross, normed_cross,
+        query_cross, taken_cross, mixed_cross, stream_feed, normed_feed,
+    )
+    saves = [local(held, out) for held, out in zip(results, outs)]
+
+    mate_inputs.start()
+    cot_moves[0].start()
+    for piece in pieces:
+        piece.wait()
+    early, late = gathers[:2], gathers[2:]
+    for gather in early:
+        gather.begin()
+    for quarter in quarters:
+        quarter.begin()
+
+    news = []
+
+    def every(items, name, *args):
+        for item in items:
+            news.append(functools.partial(getattr(item, name), *args))
+
+    every(early, "far_first")
+    every(early, "step", 0)
+    every(quarters, "swapped")
+    every(late, "begin")
+    every(early, "far_step", 0)
+    for k in range(1, zs - 1):
+        every(early, "step", k)
+        every(early, "far_step", k)
+    news.append(cot_moves[1].start)
+    every(early, "landed")
+    until_in = len(news)
+    every(late, "far_first")
+    for k in range(zs - 1):
+        every(late, "step", k)
+        every(quarters[1:], "step", k)
+        if k == 0:
+            every(quarters[:1], "own_y_arrived")
+        every(late, "far_step", k)
+        every(quarters[:1], "step", k)
+        if k == 0:
+            news.append(cot_moves[1].arrived)
+            news.append(cot_moves[2].start)
+    until_late = {}
+    for i, gather in enumerate(late):
+        every([gather], "landed")
+        news.append(loads[2 + i].start)
+        until_late[i] = len(news)
+    done = [0]
+
+    def hear(upto):
+        while done[0] < min(upto, len(news)):
+            news[done[0]]()
+            done[0] += 1
+
+    def hear_some(count):
+        hear(done[0] + count)
+
+    hear(until_in)
+    loads[0].start()
+    loads[1].start()
+    own_inputs.wait()
+    mate_inputs.arrived()
+    loads[0].wait()
+    vectors[...] = jnp.transpose(w_vec[...].reshape(width, w_vec.shape[-1]))
+
+    def vec(i):
+        return vectors[i : i + 1, :]
+
+    tile = 128 if rows % 128 == 0 else rows
+    for side in range(2):
+        for start in range(0, rows, tile):
+            part = slice(start, start + tile)
+            made = normalise(x_all[side, part, :].astype(F32), vec(0), vec(1))
+            normed_self[side * rows + start : side * rows + start + tile, :] = made.astype(BF)
+    saves[0].start()
+    hear_some(2)
+    loads[1].wait()
+    columns = w_in.shape[-1]
+    block = 2 * wide
+    for start in range(0, columns, block):
+        made = nn(normed_self[...], w_in[..., start : start + block].reshape(width, block))
+        for at in range(0, block, wide):
+            piece = made[:, at : at + wide]
+            if start + at < columns * 2 // 3:
+                piece = turn(piece, cos_ref[...], sa_ref[...], sb_ref[...], 1.0)
+            taken[:, start + at : start + at + wide] = piece.astype(BF)
+        hear_some(2)
+    saves[1].start()
+    inner = columns // 3
+    pairs = inner // wide
+    tops = []
+
+    def attend_all(query_ref, keys_at, values_at, kv_ref, bias_ref, mixed_ref):
+        total = 2 * rows
+        step = total // 3 if total % 3 == 0 and (total // 3) % 16 == 0 else total
+        for j in range(pairs):
+            lanes_at = j * wide
+            bits, peaks = attend_pair(
+                lambda start, count: query_ref[start : start + count, lanes_at : lanes_at + wide],
+                kv_ref[:, keys_at + lanes_at : keys_at + lanes_at + wide],
+                kv_ref[:, values_at + lanes_at : values_at + lanes_at + wide],
+                bias_ref[...],
+                (total, step),
+            )
+            for start, bit in bits:
+                mixed_ref[start : start + step, lanes_at : lanes_at + wide] = bit.astype(BF)
+            tops.append(peaks)
+            hear_some(2)
+
+    def out_rows(mixed_ref, first, weight, zz):
+        columns_here = weight[zz].reshape(-1, inner)
+        return nt(mixed_ref[first : first + rows, :], columns_here)
+
+    def out_project(mixed_ref, weight, move, send, got, base, target):
+        chunk = width // zs
+        for zz in range(zs):
+            send[:, zz * chunk : (zz + 1) * chunk] = out_rows(mixed_ref, rows, weight, zz)
+        move.start()
+        for zz in range(zs):
+            part = slice(zz * chunk, (zz + 1) * chunk)
+            target[:, part] = out_rows(mixed_ref, 0, weight, zz) + base(part)
+            hear_some(1)
+        move.arrived()
+        for start in range(0, rows, tile):
+            part = slice(start, start + tile)
+            target[part, :] = target[part, :] + got[part, :]
+
+    attend_all(taken, inner, 2 * inner, taken, self_bias, mixed_self)
+    saves[2].start()
+    hear(until_late[0])
+    loads[2].wait()
+    out_project(
+        mixed_self, w_so, mate_self, part_send, part_got,
+        lambda part: x_all[0, :, part].astype(F32), stream_cross,
+    )
+    saves[3].start()
+    for start in range(0, rows, tile):
+        part = slice(start, start + tile)
+        normed_cross[0, part, :] = normalise(stream_cross[part, :], vec(2), vec(3)).astype(BF)
+    mate_normed.start()
+    hear(until_late[2])
+    loads[4].wait()
+    depth = memory.shape[1]
+    for start in range(0, 2 * inner, block):
+        weight = w_kv[..., start : start + block].reshape(depth, block)
+        taken_cross[:, start : start + block] = nn(memory[...], weight).astype(BF)
+    saves[6].start()
+    loads[3].wait()
+    for side in range(2):
+        if side == 1:
+            mate_normed.arrived()
+            saves[4].start()
+        for start in range(0, inner, block):
+            weight = w_cq[..., start : start + block].reshape(width, block)
+            made = nn(normed_cross[side], weight).astype(BF)
+            query_cross[side * rows : (side + 1) * rows, start : start + block] = made
+        hear_some(1)
+    saves[5].start()
+    attend_all(query_cross, 0, inner, taken_cross, cross_bias, mixed_cross)
+    saves[7].start()
+    hear(until_late[3])
+    loads[5].wait()
+    out_project(
+        mixed_cross, w_co, mate_cross, part_send2, part_got2,
+        lambda part: stream_cross[:, part], stream_feed,
+    )
+    saves[8].start()
+    for start in range(0, rows, tile):
+        part = slice(start, start + tile)
+        normed_feed[0, part, :] = normalise(stream_feed[part, :], vec(4), vec(5)).astype(BF)
+    feed_moves[1].start()
+    feed_moves[0].start()
+    lane = lax.broadcasted_iota(jnp.int32, peak_out.shape, 1)
+    crest = jnp.full(peak_out.shape, NEGATIVE, F32)
+    for i, peaks in enumerate(tops):
+        for which in range(2):
+            head = (i % pairs) * 2 + which
+            crest = jnp.where(lane == head, jnp.maximum(crest, peaks[which]), crest)
+    peak_out[...] = crest
+    hear(len(news))
+    feed_moves[1].arrived()
+    feed_moves[2].start()
+    for quarter in quarters:
+        quarter.landed()
+    feed_moves[0].arrived()
+    feed_moves[2].arrived()
+    saves[9].start()
+    cot_moves[0].arrived()
+    cot_moves[2].arrived()
+    own_cot.wait()
+    for item in gathers + quarters:
+        item.sent()
+    for move in [mate_inputs, mate_self, mate_normed, mate_cross] + cot_moves + feed_moves:
+        move.sent()
+    for save in saves:
+        save.wait()
+
+
+def forward(shards, quarters, inputs, cotangent, turns, self_bias, cross_bias, memory, zs):
+    rows, width = inputs.shape
+    seq_len, inner = 2 * rows, shards[1].shape[1]
+    tokens = memory.shape[0]
+    spread = []
+    groups = ([shards[0]], shards[1:4], [shards[4]], [shards[5]], shards[6:8], [shards[8]])
+    for group in groups:
+        columns = sum(shard.shape[1] for shard in group)
+        spread.append(jax.ShapeDtypeStruct((zs, 2, 2, group[0].shape[0], columns), group[0].dtype))
+    for shard in quarters:
+        spread.append(
+            jax.ShapeDtypeStruct((zs, 2, 2, shard.shape[0], shard.shape[1] // 2), shard.dtype)
+        )
+    results = [
+        jax.ShapeDtypeStruct((seq_len, width), BF),
+        jax.ShapeDtypeStruct((seq_len, 3 * inner), BF),
+        jax.ShapeDtypeStruct((seq_len, inner), BF),
+        jax.ShapeDtypeStruct((rows, width), F32),
+        jax.ShapeDtypeStruct((2, rows, width), BF),
+        jax.ShapeDtypeStruct((seq_len, inner), BF),
+        jax.ShapeDtypeStruct((tokens, 2 * inner), BF),
+        jax.ShapeDtypeStruct((seq_len, inner), BF),
+        jax.ShapeDtypeStruct((rows, width), F32),
+        jax.ShapeDtypeStruct((4, rows, width), BF),
+    ]
+    cot_out = jax.ShapeDtypeStruct((4, rows, width), BF)
+    peak = jax.ShapeDtypeStruct((8, 2 * HEAD_DIM), F32)
+    moves = 6 * (3 + 8 * (zs - 1)) + 3 * (2 + 4 * (zs - 1)) + 10
+    hbm = pl.BlockSpec(memory_space=pltpu.HBM)
+    vmem = pl.BlockSpec(memory_space=pltpu.VMEM)
+    held = [pltpu.VMEM(shape.shape, shape.dtype) for shape in spread[:6]]
+    held += [pltpu.VMEM((2, rows, width), BF)]
+    held += [pltpu.VMEM(shape.shape, shape.dtype) for shape in results]
+    held += [pltpu.VMEM((rows, width), F32)] * 4
+    held += [pltpu.VMEM((shards[0].shape[1], width), F32)]
+    flops = 2 * seq_len * inner * (7 * width + 4 * seq_len) // 1
+    made = pl.pallas_call(
+        functools.partial(forward_kernel, zs),
+        out_shape=spread + results + [cot_out, peak],
+        in_specs=[hbm] * 14 + [vmem] * 6,
+        out_specs=[hbm] * 20 + [vmem],
+        scratch_shapes=[
+            pltpu.SemaphoreType.DMA((moves,)),
+            pltpu.SemaphoreType.DMA((moves,)),
+            pltpu.SemaphoreType.DMA((9 + 2 + 3 + 6 + 10,)),
+        ]
+        + held,
+        compiler_params=pltpu.CompilerParams(
+            collective_id=1, has_side_effects=True, vmem_limit_bytes=62 * 2**20
+        ),
+        cost_estimate=pl.CostEstimate(flops=flops, bytes_accessed=10**8, transcendentals=10**7),
+    )(*shards, *quarters, inputs, cotangent, *turns, self_bias, cross_bias, memory)
+    return made[:9], made[9:19], made[19], made[20]
+
+
 def pair_rows(own):
     return jnp.concatenate([own, swap(own, "tensor")], axis=0)
 
@@ -918,31 +1288,9 @@
     ff = gate_weight.shape[1] // 2
     shard_rows = self_query.shape[0]
 
-    vectors = jnp.stack(
-        [self_gain, self_bias, cross_gain, cross_bias, feed_gain, feed_bias]
-    ).astype(F32)
-    vectors = jnp.pad(vectors, ((0, 2), (0, 128 - shard_rows)))
-    (norms, in_weight, self_out_t, cross_in, memory_weight, cross_out_t, gate_full, up_full, down_t) = (
-        gather_all(
-            [
-                [vectors],
-                [self_query, self_key, self_value],
-                [self_output.T],
-                [cross_query],
-                [cross_key, cross_value],
-                [cross_output.T],
-            ],
-            [gate_weight, up_weight, down_weight.T],
-            zs,
-        )
-    )
-    norms = norms.reshape(-1, 8, 128)[:, :6, :shard_rows].transpose(1, 0, 2).reshape(6, width)
-    in_weight, self_out_t, cross_in, cross_out_t, gate_full, up_full, down_t = (
-        w.reshape(width, -1)
-        for w in (in_weight, self_out_t, cross_in, cross_out_t, gate_full, up_full, down_t)
-    )
-    memory_weight = memory_weight.reshape(-1, 2 * inner)
-
+    quarters = [gate_weight, up_weight, down_weight.T]
+    vector_list = [self_gain, self_bias, cross_gain, cross_bias, feed_gain, feed_bias]
+    stream = inputs.astype(F32)
     local = jnp.arange(rows)
     places = jnp.concatenate([t_at * rows + local, (1 - t_at) * rows + local])
     turns = turn_tables(places.astype(F32))
@@ -957,34 +1305,102 @@
     memory = jnp.pad(context[0], ((0, token_rows - tokens), (0, 0)))
     pairs = inner // (2 * HEAD_DIM)
 
-    cot_group = group_rows(cotangent)
-    all_inputs = pair_rows(inputs)
-    stream = inputs.astype(F32)
-    normed, _, _ = norm_forward(all_inputs.astype(F32), norms[0], norms[1])
-    normed_self = normed.astype(BF)
-    taken = project(normed_self, in_weight, turns, 2 * inner)
-    self_bias_rows = jnp.broadcast_to(self_bias_row, (pairs, seq_len))
-    mixed_self, peak_self = attend(taken, taken, taken, self_bias_rows, (0, pairs, 2 * pairs))
-    stream_cross = stream + spread_pair(mixed_self, self_out_t)
-    normed, unit_cross, inverse_cross = norm_forward(stream_cross, norms[2], norms[3])
-    normed_cross = pair_rows(normed.astype(BF))
-    query_cross = nn(normed_cross, cross_in).astype(BF)
-    taken_cross = nn(memory, memory_weight).astype(BF)
-    cross_bias_rows = jnp.broadcast_to(cross_bias_row, (pairs, token_rows))
-    mixed_cross, peak_cross = attend(
-        query_cross, taken_cross, taken_cross, cross_bias_rows, (0, 0, pairs)
-    )
-    stream_feed = stream_cross + spread_pair(mixed_cross, cross_out_t)
-    normed, unit_feed, inverse_feed = norm_forward(stream_feed, norms[4], norms[5])
-    normed_feed = group_rows(normed.astype(BF))
+    if shard_rows % 32 == 0:
+        vectors = jnp.pad(jnp.stack(vector_list, axis=1).astype(F32), ((0, 0), (0, 122)))
+        spread, made, cot_group, crest = forward(
+            [
+                vectors,
+                self_query,
+                self_key,
+                self_value,
+                self_output.T,
+                cross_query,
+                cross_key,
+                cross_value,
+                cross_output.T,
+            ],
+            quarters,
+            inputs,
+            cotangent,
+            turns,
+            self_bias_row[None],
+            cross_bias_row[None],
+            memory,
+            zs,
+        )
+        norms, in_weight, self_out_t, cross_in, memory_weight, cross_out_t = spread[:6]
+        norms = norms.reshape(width, -1).T
+        (
+            normed_self,
+            taken,
+            mixed_self,
+            stream_cross,
+            normed_cross,
+            query_cross,
+            taken_cross,
+            mixed_cross,
+            stream_feed,
+            normed_feed,
+        ) = made
+        gate_full, up_full, down_t = spread[6:]
+        normed_cross = normed_cross.reshape(seq_len, width)
+        normed_feed, cot_group = (v.reshape(-1, width) for v in (normed_feed, cot_group))
+    else:
+        vectors = jnp.stack(vector_list).astype(F32)
+        vectors = jnp.pad(vectors, ((0, 2), (0, 128 - shard_rows)))
+        (norms, in_weight, self_out_t, cross_in, memory_weight, cross_out_t, gate_full, up_full, down_t) = (
+            gather_all(
+                [
+                    [vectors],
+                    [self_query, self_key, self_value],
+                    [self_output.T],
+                    [cross_query],
+                    [cross_key, cross_value],
+                    [cross_output.T],
+                ],
+                quarters,
+                zs,
+            )
+        )
+        norms = norms.reshape(-1, 8, 128)[:, :6, :shard_rows].transpose(1, 0, 2).reshape(6, width)
+        in_weight, memory_weight = in_weight.reshape(width, -1), memory_weight.reshape(-1, 2 * inner)
+        self_out_t, cross_in, cross_out_t, gate_full, up_full, down_t = (
+            w.reshape(width, -1)
+            for w in (self_out_t, cross_in, cross_out_t, gate_full, up_full, down_t)
+        )
+        cot_group = group_rows(cotangent)
+        all_inputs = pair_rows(inputs)
+        normed, _, _ = norm_forward(all_inputs.astype(F32), norms[0], norms[1])
+        normed_self = normed.astype(BF)
+        taken = project(normed_self, in_weight, turns, 2 * inner)
+        self_bias_rows = jnp.broadcast_to(self_bias_row, (pairs, seq_len))
+        mixed_self, peak_self = attend(taken, taken, taken, self_bias_rows, (0, pairs, 2 * pairs))
+        stream_cross = stream + spread_pair(mixed_self, self_out_t)
+        normed, _, _ = norm_forward(stream_cross, norms[2], norms[3])
+        normed_cross = pair_rows(normed.astype(BF))
+        query_cross = nn(normed_cross, cross_in).astype(BF)
+        taken_cross = nn(memory, memory_weight).astype(BF)
+        cross_bias_rows = jnp.broadcast_to(cross_bias_row, (pairs, token_rows))
+        mixed_cross, peak_cross = attend(
+            query_cross, taken_cross, taken_cross, cross_bias_rows, (0, 0, pairs)
+        )
+        stream_feed = stream_cross + spread_pair(mixed_cross, cross_out_t)
+        normed, _, _ = norm_forward(stream_feed, norms[4], norms[5])
+        normed_feed = group_rows(normed.astype(BF))
+        crest = jnp.pad(
+            jnp.maximum(peak_self, peak_cross)[None], ((0, 7), (0, 128 - heads_here))
+        )
+    in_weight, self_out_t, cross_in, cross_out_t, gate_full, up_full, down_t = (
+        w.reshape(width, -1)
+        for w in (in_weight, self_out_t, cross_in, cross_out_t, gate_full, up_full, down_t)
+    )
+    unit_cross, inverse_cross = unit_rows_of(stream_cross)
+    unit_feed, inverse_feed = unit_rows_of(stream_feed)
     gate_pre = nn(normed_feed, gate_full)
     upward = nn(normed_feed, up_full)
     sigmoid_gate = jax.nn.sigmoid(gate_pre)
     hidden = (gate_pre * sigmoid_gate * upward).astype(BF)
     result = (stream_feed + spread_group(Product([(hidden, down_t)], True))).astype(BF)
-    crest = jnp.pad(
-        jnp.maximum(peak_self, peak_cross)[None], ((0, 7), (0, 128 - heads_here))
-    )
 
     cot_keep, cot_send = columns_by(cot_group, "y", zs)
     down_keep, down_got = reduce_pair(cot_keep, cot_send, hidden, zs)
@@ -1002,13 +1418,15 @@
     )
     grad_stream = cotangent.astype(F32) + stream_part
     grad_full = pair_rows(grad_stream.astype(BF))
-    part_cross_output = tn(grad_full, mixed_cross)
+    keep, send = columns_by(grad_full, "x", zs)
+    sum_cross_output = reduce_full(keep, send, mixed_cross, zs).astype(F32)
     grad_mixed = nn(grad_full, cross_out_t).astype(BF)
     grad_query, grad_keys, grad_values = attend_back(
         query_cross, taken_cross, taken_cross, grad_mixed, cross_bias_row[:, None], (0, 0, pairs), None
     )
     grad_normed = spread_pair(grad_query, cross_in)
-    part_cross_query = tn(normed_cross, grad_query)
+    keep, send = columns_by(normed_cross, "x", zs)
+    sum_cross_query = reduce_full(keep, send, grad_query, zs).astype(F32)
     part_memory = tn(memory, jnp.concatenate([grad_keys, grad_values], axis=1))
     stream_part, grad_cross_gain, grad_cross_bias = norm_backward(
         grad_normed, unit_cross, inverse_cross, norms[2]
@@ -1017,15 +1435,13 @@
     grad_full = pair_rows(grad_stream.astype(BF))
     part_self_output = tn(grad_full, mixed_self)
     grad_mixed = nn(grad_full, self_out_t).astype(BF)
-    grad_in = jnp.concatenate(
-        attend_back(
-            taken, taken, taken, grad_mixed, self_bias_row[:, None], (0, pairs, 2 * pairs), turns
-        ),
-        axis=1,
-    )
-    part_self_in = tn(normed_self, grad_in)
+    grad_parts = attend_back(
+        taken, taken, taken, grad_mixed, self_bias_row[:, None], (0, pairs, 2 * pairs), turns
+    )
+    grad_in = jnp.concatenate(grad_parts, axis=1)
+    part_query, part_key, part_value = (tn(normed_self, part) for part in grad_parts)
     grad_normed = spread_pair(grad_in, in_weight)
-    _, unit_self, inverse_self = norm_forward(stream, norms[0], norms[1])
+    unit_self, inverse_self = unit_rows_of(stream)
     stream_part, grad_self_gain, grad_self_bias = norm_backward(
         grad_normed, unit_self, inverse_self, norms[0]
     )
@@ -1049,17 +1465,17 @@
     def blocks(part):
         return part.astype(BF).reshape(zs, 2, 2, -1, part.shape[1])
 
-    (vector_sums, sum_self_in, sum_self_output, sum_cross_query, sum_cross_output, sum_memory, crest) = (
+    (vector_sums, sum_query, sum_key, sum_value, sum_self_output, sum_memory, crest) = (
         scatter_all(
             [
                 vector_sums,
-                blocks(part_self_in),
+                blocks(part_query),
+                blocks(part_key),
+                blocks(part_value),
                 blocks(part_self_output),
-                blocks(part_cross_query),
-                blocks(part_cross_output),
                 blocks(part_memory),
             ],
-            ["x", "x", "y", "y", "y", "z"],
+            ["x", "x", "y", "x", "y", "z"],
             crest,
             zs,
         )
@@ -1082,9 +1498,9 @@
         grad_stream,
         vector_sums[0],
         vector_sums[1],
-        sum_self_in[:, :inner],
-        sum_self_in[:, inner : 2 * inner],
-        sum_self_in[:, 2 * inner :],
+        sum_query,
+        sum_key,
+        sum_value,
         sum_self_output.T,
         vector_sums[2],
         vector_sums[3],

time: 987 us -> 959 us (0.972)
  waiting for transfers between devices: 111 us -> 33.6 us
  Pallas kernels: 532 us -> 566 us
  local copies, waits for them, and re-layouts: 55.2 us -> 82 us
    pallas_call x4 -> x1, Pallas kernels: 295 us -> 375 us  [forward(): pl.pallas_call(functools.partial(forward_kernel, zs), out_shape=spread +...]
    ppermute x23 -> x19, waiting for transfers between devices: 111 us -> 33.5 us  [swap(): return lax.ppermute(value, axis, [(0, 1), (1, 0)])]
    pallas_call x1, Pallas kernels: 184 us -> 138 us  [scatter_all(): pl.pallas_call(functools.partial(scatter_kernel, zs, orders), out_shape=[...]
    pallas_call x0 -> x3, local copies, waits for them, and re-layouts: none -> 23.9 us  [forward(): pl.pallas_call(functools.partial(forward_kernel, zs), out_shape=spread +...]
    another operation x1 -> x5, local copies, waits for them, and re-layouts: 0.76 us -> 24.2 us  [the longest x2 17.6 us: columns_by(): split = value.reshape(rows, zs, 2, -1)]
    slice x8 -> x1, local copies, waits for them, and re-layouts: 13.3 us -> 0.63 us  [per_device(): norms[0]]
    dot_general x7 -> x5, matrix products: 58.9 us -> 53.7 us  [nn(): lax.dot_general(left, right, (((1,), (0,)), ((), ())), preferred_element_...]
    dot_general x20 -> x16, matrix products: 87.1 us -> 83 us  [nt(): lax.dot_general(left, right, (((1,), (1,)), ((), ())), preferred_element_...]
  transfers between devices with their start and end apart: 25 -> 23, of which waited for: 9 -> 6; matrix products, arithmetic and copies ran while one was open for 21% -> 24% of each run, Pallas kernels for 51% -> 20%
where the time goes in v4:
time: 959 us; the launch traced here: 954 us
  Pallas kernels  566 us (59%)
  matrix products  206 us (21%)
  local copies, waits for them, and re-layouts  82 us (9%)
  other arithmetic  34.5 us (4%)
  waiting for transfers between devices  33.6 us (4%)
  between operations  16.4 us (2%)
  starting transfers between devices  16 us (2%)
    pallas_call x1, Pallas kernels, forward(): pl.pallas_call(functools.partial(forward_kernel, zs), out_shape=spread +...  375 us
    pallas_call x1, Pallas kernels, scatter_all(): pl.pallas_call(functools.partial(scatter_kernel, zs, orders), out_shape=[...  138 us
    dot_general x16, matrix products, nt(): lax.dot_general(left, right, (((1,), (1,)), ((), ())), preferred_element_...  83 us
    dot_general x13, matrix products, tn(): lax.dot_general(left, right, (((0,), (0,)), ((), ())), preferred_element_...  69.2 us
    dot_general x5, matrix products, nn(): lax.dot_general(left, right, (((1,), (0,)), ((), ())), preferred_element_...  53.7 us
    pallas_call x2, Pallas kernels, attend_back(): pl.pallas_call(functools.partial(attend_back_kernel, turns is not None),...  53 us
    ppermute x19, waiting for transfers between devices, swap(): return lax.ppermute(value, axis, [(0, 1), (1, 0)])  33.5 us
    pallas_call x3, local copies, waits for them, and re-layouts, forward(): pl.pallas_call(functools.partial(forward_kernel, zs), out_shape=spread +...  23.9 us
  transfers between devices with their start and end apart: 23, of which 6 were waited for; matrix products, arithmetic and copies ran while one was open for 24% of the time, Pallas kernels for 20%

profile of v4, /device:TPU:0, one launch (start us, length us, event | category | flops | bytes accessed | tf_op | source)
XLA Modules:
  0.0 954.2 jit_solution(8512985723130339658)
XLA Ops:
  16.9 374.9 %shard_map.406 = (f32[4,2,2,96,128]{4,3,2,1,0:T(8,128)}, bf16[4,2,2,96,2304]{4,3,2,1,0:T(8,128)(2,1)}, bf16[4,2,2,96,768]{4,3,2,1,0:T(8,128)(2,1)}, bf16[4,2,2,9...) custom-call(f32[96,128]{1,0:T(8,128)} %pad_convert_fusion.refs_0_, ...), custom_call_target="tpu_custom_call" | custom-call | flops 16307453952 | bytes 100000000 | tf_op jit(solution)/shard_map/pallas_call | solution.py:1197
  391.9 13.5 %fusion.63 = f32[1536,1536]{0,1:T(8,128)} fusion(bf16[1536,1536]{1,0:T(8,128)(2,1)} %bitcast.155, bf16[1536,1536]{1,0:T(8,128)(2,1)} %bitcast.213), kind=kOutput, calls=%fused_computation.175 | convolution fusion | flops 7247757312 | bytes 18874368 | tf_op jit(solution)/shard_map/dot_general | solution.py:583
  405.4 10.3 %fusion.62 = f32[1536,1536]{0,1:T(8,128)} fusion(bf16[1536,1536]{1,0:T(8,128)(2,1)S(1)} %bitcast.156, bf16[1536,1536]{1,0:T(8,128)(2,1)S(1)} %bitcast.225), kind=kOutput, calls=%fused_computation.174 | convolution fusion | flops 7247757312 | bytes 18874368 | tf_op jit(solution)/shard_map/dot_general | solution.py:583
  415.7 8.5 copy.92
  424.2 8.8 reshape_reshape.11
  437.2 22.1 %multiply_convert_fusion = (bf16[1536,1536]{0,1:T(8,128)(2,1)}, bf16[1536,1536]{0,1:T(8,128)(2,1)}, bf16[1536,1536]{0,1:T(8,128)(2,1)}) fusion(f32[1536,1536]{0,1:T(8,128)} %fusion.62, f32[1536,1536]{0,1:T(8,128)} %fusion.63, bf16[1536,1536]{1,0:T(8,128)(2,1)} %bitcast.157, bf16[1536,1536]{1,0:T(8,128)(2,1)} %bitcast.202), kind=kOutput, calls=%fused_computation.2 | convolution fusion | flops 7285506048 | bytes 42467328 | tf_op jit(solution)/shard_map/dot_general | solution.py:583
  459.2 7.4 convolution_convert_fusion
  469.1 8.5 copy.91
  477.6 8.9 reshape_reshape.10
  490.8 13.5 %fusion.2 = bf16[768,3072]{1,0:T(8,128)(2,1)} fusion(bf16[1536,768]{0,1:T(8,128)(2,1)S(1)} %bitcast.161, bf16[1536,1536]{0,1:T(8,128)(2,1)} %get-tuple-element.111, bf16[1536,1536]{0,1:T(8,128)(2,1)} %get-tuple-element.112), kind=kOutput, calls=%fused_computation.8 | convolution fusion | flops 7268990976 | bytes 16515072 | tf_op jit(solution)/shard_map/dot_general | solution.py:591
  504.4 4.9 fusion.32
  517.9 5.2 convolution_add_fusion.1
  523.4 4.9 fusion.37
  528.6 6.3 fusion.35
  535.0 4.9 fusion.29
  545.4 5.7 fusion.13
  554.1 6.8 copy.87
  561.0 6.4 reshape_reshape.9
  570.0 9.0 add_convert_fusion.1
  579.7 7.5 multiply_reduce_fusion
  610.7 16.3 %shard_map.407 = (bf16[768,768]{1,0:T(8,128)(2,1)S(1)}, bf16[256,768]{1,0:T(8,128)(2,1)S(1)}, bf16[256,768]{1,0:T(8,128)(2,1)S(1)}) custom-call(bf16[768,768]{1,0:T(8,128)(2,1)S(1)} %copy-done.4, bf16[256,1536]{1,0:T(8,128)(2,1)S(1)} %copy-done.5, bf16[256,1536]{1,0:T(8,128)(2,1)S(1)} %copy-done.5, bf16[768,768]{1,0:T(8,128)(2,1)S(1)} %convolution_convert_fusion.9.g_ref, ...), custom_call_target="tpu_custom_call" | custom-call | flops 3019898880 | bytes 6291456 | tf_op jit(solution)/shard_map/pallas_call | solution.py:801
  639.9 9.5 collective-permute-done.14
  650.5 7.8 collective-permute-done.11
  662.9 6.6 fusion.15
  671.0 5.1 collective-permute-done.12
  677.1 14.4 %add_convert_fusion = bf16[768,3072]{1,0:T(8,128)(2,1)} fusion(bf16[768,3072]{1,0:T(8,128)(2,1)} %collective-permute-done.15, bf16[1536,768]{0,1:T(8,128)(2,1)} %bitcast.158, bf16[1536,1536]{0,1:T(8,128)(2,1)} %get-tuple-element.111, bf16[1536,1536]{0,1:T(8,128)(2,1)} %get-tuple-element.112), kind=kOutput, calls=%fused_computation.1 | convolution fusion | flops 7273709568 | bytes 21233664 | tf_op jit(solution)/shard_map/dot_general | solution.py:591
  701.3 6.2 fusion.14
  717.8 36.7 %shard_map.408 = (bf16[768,768]{1,0:T(8,128)(2,1)S(1)}, bf16[768,768]{1,0:T(8,128)(2,1)S(1)}, bf16[768,768]{1,0:T(8,128)(2,1)S(1)}) custom-call(bf16[768,2304]{1,0:T(8,128)(2,1)} %get-tuple-element.70.q_ref.k_ref.v_ref, bf16[768,2304]{1,0:T(8,128)(2,1)} %get-tuple-element.70.q_ref.k_ref.v_ref, bf16[768,2304]{1,0:T(8,128)(2,1)} %get-tuple-element.70.q_ref.k_ref.v_ref, ...), custom_call_target="tpu_custom_call" | custom-call | flops 9059696640 | bytes 9437184 | tf_op jit(solution)/shard_map/pallas_call | solution.py:801
  762.4 5.6 convolution_convert_fusion.2
  778.7 6.1 fusion.20
  790.9 137.9 %shard_map.409 = (f32[8,128]{1,0:T(8,128)}, f32[96,768]{1,0:T(8,128)}, f32[96,768]{1,0:T(8,128)}, f32[96,768]{1,0:T(8,128)}, f32[96,768]{1,0:T(8,128)}, /*index=5*/f32[48,1536]{1,0:T(8,128)}, f32[8,128]{1,0:T(8,128)}) custom-call(f32[4,2,2,8,128]{4,3,2,1,0:T(8,128)} %bitcast.183, bf16[4,2,2,96,768]{4,3,2,1,0:T(8,128)(2,1)} %bitcast.166, ...), custom_call_target="tpu_custom_call" | custom-call | tf_op jit(solution)/shard_map/pallas_call | solution.py:567
  934.6 7.6 collective-permute-done.16
  (300 shorter events, 140.0 us)
Async XLA Ops:
  7.2 684.4 %reduce-scatter.11.cloned.1.call-start = ((), (), s32[]{:S(2)}) async-start(), calls=%async_computation.7 | async-start | bytes 2949120 | tf_op jit(solution)/shard_map/reduce_scatter | solution.py:623
  391.9 13.5 %copy-start.13 = (bf16[4,384,1536]{2,1,0:T(8,128)(2,1)S(1)}, bf16[4,384,1536]{2,1,0:T(8,128)(2,1)}, u32[]{:S(2)}) copy-start(bf16[4,384,1536]{2,1,0:T(8,128)(2,1)} %get-tuple-element.58) | copy-start | bytes 14155780
  391.9 13.5 %copy-start.48 = (bf16[4,2,2,96,1536]{4,3,2,1,0:T(8,128)(2,1)S(1)}, bf16[4,2,2,96,1536]{4,3,2,1,0:T(8,128)(2,1)}, u32[]{:S(2)}) copy-start(bf16[4,2,2,96,1536]{4,3,2,1,0:T(8,128)(2,1)} %get-tuple-element.59) | copy-start | bytes 14155780
  466.6 103.2 %collective-permute-start.17 = (bf16[768,1536]{1,0:T(8,128)(2,1)}, bf16[768,1536]{1,0:T(8,128)(2,1)}, u32[]{:S(2)}, u32[]{:S(2)}) collective-permute-start(bf16[768,1536]{1,0:T(8,128)(2,1)} %convolution_convert_fusion), channel_id=1, source_target_pairs={{0,4},{4,0},{1,5},{5,1},{2,6},{6,2},{3,7},{7,3},{8,12},{12,8},{9,1... | collective-permute-start | bytes 7077896 | tf_op jit(solution)/shard_map/ppermute | solution.py:20
  486.5 22.7 %slice-start.10 = ((s8[4718592]{0:T(1024)(128)(4,1)}), s8[4194304]{0:T(1024)(128)(4,1)S(1)}, s32[]{:S(2)}) async-start(s8[4718592]{0:T(1024)(128)(4,1)} %bitcast.215), calls=%async_computation.18 | async-start | bytes 8388608
  490.8 18.5 %slice-start.11 = ((s8[4718592]{0:T(1024)(128)(4,1)}), s8[524288]{0:T(1024)(128)(4,1)S(1)}, s32[]{:S(2)}) async-start(s8[4718592]{0:T(1024)(128)(4,1)} %bitcast.215), calls=%async_computation.19 | async-start | bytes 1048576
  504.4 172.8 %collective-permute-start.15 = (bf16[768,3072]{1,0:T(8,128)(2,1)}, bf16[768,3072]{1,0:T(8,128)(2,1)}, u32[]{:S(2)}, u32[]{:S(2)}) collective-permute-start(bf16[768,3072]{1,0:T(8,128)(2,1)} %fusion.2), channel_id=1, source_target_pairs={{0,4},{4,0},{1,5},{5,1},{2,6},{6,2},{3,7},{7,3},{8,12},{12,8},{9,1... | collective-permute-start | bytes 14155784 | tf_op jit(solution)/shard_map/ppermute | solution.py:20
  514.2 65.0 %collective-permute-start.3 = (f32[384,1536]{1,0:T(8,128)}, f32[384,1536]{1,0:T(8,128)}, u32[]{:S(2)}, u32[]{:S(2)}) collective-permute-start(f32[384,1536]{1,0:T(8,128)} %convolution_add_fusion.3), channel_id=1, source_target_pairs={{0,1},{1,0},{2,3},{3,2},{4,5},{5,4},{6,7},{7,6},{8,9},{9,8},{10,11... | collective-permute-start | bytes 7077896 | tf_op jit(solution)/shard_map/ppermute | solution.py:20
  523.0 22.3 %collective-permute-start.4 = (f32[384,1536]{1,0:T(8,128)}, f32[384,1536]{1,0:T(8,128)}, u32[]{:S(2)}, u32[]{:S(2)}) collective-permute-start(f32[384,1536]{1,0:T(8,128)} %convolution_add_fusion.1), channel_id=1, source_target_pairs={{0,1},{1,0},{2,3},{3,2},{4,5},{5,4},{6,7},{7,6},{8,9},{9,8},{10,11... | collective-permute-start | bytes 7077896 | tf_op jit(solution)/shard_map/ppermute | solution.py:20
  528.3 134.6 %collective-permute-start.1 = (f32[384,1536]{1,0:T(8,128)}, f32[384,1536]{1,0:T(8,128)}, u32[]{:S(2)}, u32[]{:S(2)}) collective-permute-start(f32[384,1536]{1,0:T(8,128)} %fusion.37), channel_id=1, source_target_pairs={{0,1},{1,0},{2,3},{3,2},{4,5},{5,4},{6,7},{7,6},{8,9},{9,8},{10,11... | collective-permute-start | bytes 7077896 | tf_op jit(solution)/shard_map/ppermute | solution.py:20
  551.1 28.6 %collective-permute-start.5 = (bf16[384,1536]{1,0:T(8,128)(2,1)}, bf16[384,1536]{1,0:T(8,128)(2,1)}, u32[]{:S(2)}, u32[]{:S(2)}) collective-permute-start(bf16[384,1536]{1,0:T(8,128)(2,1)} %fusion.13), channel_id=1, source_target_pairs={{0,2},{2,0},{1,3},{3,1},{4,6},{6,4},{5,7},{7,5},{8,10},{10,8},{9,1... | collective-permute-start | bytes 3538952 | tf_op jit(solution)/shard_map/ppermute | solution.py:20
  552.6 38.2 %copy-start.36 = (f32[384]{0:T(512)}, f32[384]{0:T(512)S(1)}, u32[]{:S(2)}) copy-start(f32[384]{0:T(512)S(1)} %broadcast_multiply_fusion.2) | copy-start | bytes 4612
  569.9 131.4 %collective-permute-start = (f32[384,1536]{1,0:T(8,128)}, f32[384,1536]{1,0:T(8,128)}, u32[]{:S(2)}, u32[]{:S(2)}) collective-permute-start(f32[384,1536]{1,0:T(8,128)} %fusion.40), channel_id=1, source_target_pairs={{0,1},{1,0},{2,3},{3,2},{4,5},{5,4},{6,7},{7,6},{8,9},{9,8},{10,11... | collective-permute-start | bytes 7077896 | tf_op jit(solution)/shard_map/ppermute | solution.py:20
  579.1 180.1 %reduce-scatter.7.cloned.1.call-start = ((), (), s32[]{:S(2)}) async-start(), calls=%async_computation.5 | async-start | bytes 737280 | tf_op jit(solution)/shard_map/reduce_scatter | solution.py:616
  589.9 5.3 collective-permute-start.6
  604.5 28.8 %collective-permute-start.13 = (bf16[768,768]{1,0:T(8,128)(2,1)S(1)}, bf16[768,768]{1,0:T(8,128)(2,1)S(1)}, u32[]{:S(2)}, u32[]{:S(2)}) collective-permute-start(bf16[768,768]{1,0:T(8,128)(2,1)S(1)} %convolution_convert_fusion.6), channel_id=1, source_target_pairs={{0,2},{2,0},{1,3},{3,1},{4,6},{6,4},{5,7},{7,5},{8,10},{10,8},{9,1... | collective-permute-start | bytes 3538952 | tf_op jit(solution)/shard_map/ppermute | solution.py:20
  629.1 29.2 %collective-permute-start.11 = (bf16[768,768]{1,0:T(8,128)(2,1)}, bf16[768,768]{1,0:T(8,128)(2,1)}, u32[]{:S(2)}, u32[]{:S(2)}) collective-permute-start(bf16[768,768]{1,0:T(8,128)(2,1)} %convolution_convert_fusion.7), channel_id=1, source_target_pairs={{0,2},{2,0},{1,3},{3,1},{4,6},{6,4},{5,7},{7,5},{8,10},{10,8},{9,1... | collective-permute-start | bytes 3538952 | tf_op jit(solution)/shard_map/ppermute | solution.py:20
  634.4 15.0 %collective-permute-start.14 = (bf16[4,96,768]{2,1,0:T(8,128)(2,1)S(1)}, bf16[4,96,768]{2,1,0:T(8,128)(2,1)S(1)}, u32[]{:S(2)}, u32[]{:S(2)}) collective-permute-start(bf16[4,96,768]{2,1,0:T(8,128)(2,1)S(1)} %dynamic-slice_bitcast_fusion.2), channel_id=1, source_target_pairs={{0,4},{4,0},{1,5},{5,1},{2,6},{6,2},{3,7},{7,3},{8,12},{12,8},{9,1... | collective-permute-start | bytes 1769480 | tf_op jit(solution)/shard_map/ppermute | solution.py:20
  639.9 18.4 %copy-start.15 = (bf16[768,8,1,96]{0,3,2,1:T(8,128)(2,1)S(1)}, bf16[768,8,1,96]{0,3,2,1:T(8,128)(2,1)}, u32[]{:S(2)}) copy-start(bf16[768,8,1,96]{0,3,2,1:T(8,128)(2,1)} %get-tuple-element.121) | copy-start | bytes 3538948
  649.5 44.7 %collective-permute-start.7 = (f32[384,1536]{1,0:T(8,128)}, f32[384,1536]{1,0:T(8,128)}, u32[]{:S(2)}, u32[]{:S(2)}) collective-permute-start(f32[384,1536]{1,0:T(8,128)} %fusion.48), channel_id=1, source_target_pairs={{0,1},{1,0},{2,3},{3,2},{4,5},{5,4},{6,7},{7,6},{8,9},{9,8},{10,11... | collective-permute-start | bytes 7077896 | tf_op jit(solution)/shard_map/ppermute | solution.py:20
  650.4 110.3 %reduce-scatter.5.cloned.1.call-start = ((), (), s32[]{:S(2)}) async-start(), calls=%async_computation.4 | async-start | bytes 737280 | tf_op jit(solution)/shard_map/reduce_scatter | solution.py:616
  660.7 15.4 %collective-permute-start.12 = (bf16[4,96,768]{2,1,0:T(8,128)(2,1)S(1)}, bf16[4,96,768]{2,1,0:T(8,128)(2,1)S(1)}, u32[]{:S(2)}, u32[]{:S(2)}) collective-permute-start(bf16[4,96,768]{2,1,0:T(8,128)(2,1)S(1)} %dynamic-slice_bitcast_fusion.3), channel_id=1, source_target_pairs={{0,4},{4,0},{1,5},{5,1},{2,6},{6,2},{3,7},{7,3},{8,12},{12,8},{9,1... | collective-permute-start | bytes 1769480 | tf_op jit(solution)/shard_map/ppermute | solution.py:20
  669.5 31.8 %collective-permute-start.2 = (bf16[384,1536]{1,0:T(8,128)(2,1)}, bf16[384,1536]{1,0:T(8,128)(2,1)}, u32[]{:S(2)}, u32[]{:S(2)}) collective-permute-start(bf16[384,1536]{1,0:T(8,128)(2,1)} %fusion.15), channel_id=1, source_target_pairs={{0,2},{2,0},{1,3},{3,1},{4,6},{6,4},{5,7},{7,5},{8,10},{10,8},{9,1... | collective-permute-start | bytes 3538952 | tf_op jit(solution)/shard_map/ppermute | solution.py:20
  677.1 253.9 %reduce-scatter.9.cloned.1.call-start = ((), (), s32[]{:S(2)}) async-start(), calls=%async_computation.6 | async-start | bytes 5898240 | tf_op jit(solution)/shard_map/reduce_scatter | solution.py:623
  692.6 18.6 %collective-permute-start.18 = (bf16[96,1536]{1,0:T(8,128)(2,1)S(1)}, bf16[96,1536]{1,0:T(8,128)(2,1)S(1)}, u32[]{:S(2)}, u32[]{:S(2)}) collective-permute-start(bf16[96,1536]{1,0:T(8,128)(2,1)S(1)} %dynamic-slice_bitcast_fusion.4), channel_id=1, source_target_pairs={{0,2},{2,0},{1,3},{3,1},{4,6},{6,4},{5,7},{7,5},{8,10},{10,8},{9,1... | collective-permute-start | bytes 884744 | tf_op jit(solution)/shard_map/ppermute | solution.py:20
  701.2 11.2 %collective-permute-start.8 = (bf16[384,1536]{1,0:T(8,128)(2,1)S(1)}, bf16[384,1536]{1,0:T(8,128)(2,1)}, u32[]{:S(2)}, u32[]{:S(2)}) collective-permute-start(bf16[384,1536]{1,0:T(8,128)(2,1)S(1)} %get-tuple-element.107), channel_id=1, source_target_pairs={{0,1},{1,0},{2,3},{3,2},{4,5},{5,4},{6,7},{7,6},{8,9},{9,8},{10,11... | collective-permute-start | bytes 3538952 | tf_op jit(solution)/shard_map/ppermute | solution.py:20
  713.3 41.4 %slice-start = ((s8[7077888]{0:T(1024)(128)(4,1)}), s8[4194304]{0:T(1024)(128)(4,1)S(1)}, s32[]{:S(2)}) async-start(s8[7077888]{0:T(1024)(128)(4,1)} %bitcast.196), calls=%async_computation.8 | async-start | bytes 8388608
  717.8 37.0 %slice-start.1 = ((s8[7077888]{0:T(1024)(128)(4,1)}), s8[2883584]{0:T(1024)(128)(4,1)S(1)}, s32[]{:S(2)}) async-start(s8[7077888]{0:T(1024)(128)(4,1)} %bitcast.196), calls=%async_computation.9 | async-start | bytes 5767168
  759.1 19.4 %collective-permute-start.9 = (f32[384,1536]{1,0:T(8,128)}, f32[384,1536]{1,0:T(8,128)}, u32[]{:S(2)}, u32[]{:S(2)}) collective-permute-start(f32[384,1536]{1,0:T(8,128)} %fusion.22), channel_id=1, source_target_pairs={{0,1},{1,0},{2,3},{3,2},{4,5},{5,4},{6,7},{7,6},{8,9},{9,8},{10,11... | collective-permute-start | bytes 7077896 | tf_op jit(solution)/shard_map/ppermute | solution.py:20
  785.1 5.2 collective-permute-start.10
  790.9 139.4 %copy-start.32 = (bf16[48,768]{1,0:T(8,128)(2,1)S(1)}, bf16[48,768]{1,0:T(8,128)(2,1)}, u32[]{:S(2)}) copy-start(bf16[48,768]{1,0:T(8,128)(2,1)} %refs_6_.1) | copy-start | bytes 221188
  932.3 9.9 %collective-permute-start.16 = (bf16[96,3072]{1,0:T(8,128)(2,1)S(1)}, bf16[96,3072]{1,0:T(8,128)(2,1)S(1)}, u32[]{:S(2)}, u32[]{:S(2)}) collective-permute-start(bf16[96,3072]{1,0:T(8,128)(2,1)S(1)} %get-tuple-element.127), channel_id=1, source_target_pairs={{0,2},{2,0},{1,3},{3,1},{4,6},{6,4},{5,7},{7,5},{8,10},{10,8},{9,1... | collective-permute-start | bytes 1769480 | tf_op jit(solution)/shard_map/ppermute | solution.py:20
  (61 other events, 290.6 us)
Sparse Core Ops, SparseCore 0:
  579.2 47.1 reduce-scatter.10
  650.6 21.8 reduce-scatter.6
  677.2 21.7 reduce-scatter.4
  701.1 83.6 reduce-scatter.8

commit v5 on v4

--- a/solution.py
+++ b/solution.py
@@ -117,24 +117,22 @@
         for move in self.first:
             move.start()
 
-    def step(self, k):
-        for side in range(2):
-            move, follow = self.steps[k][side]
-            move.arrived()
-            if k + 1 < len(self.steps):
-                self.steps[k + 1][side][0].start()
-            follow[0].start()
-            follow[1].start()
+    def step(self, k, side):
+        move, follow = self.steps[k][side]
+        move.arrived()
+        if k + 1 < len(self.steps):
+            self.steps[k + 1][side][0].start()
+        follow[0].start()
+        follow[1].start()
 
     def far_first(self):
         self.first[0].arrived()
         self.far[0][0].start()
 
-    def far_step(self, k):
-        for side in range(2):
-            _, follow = self.steps[k][side]
-            follow[0].arrived()
-            follow[2].start()
+    def far_step(self, k, side):
+        _, follow = self.steps[k][side]
+        follow[0].arrived()
+        follow[2].start()
 
     def landed(self):
         self.first[1].arrived()
@@ -185,7 +183,7 @@
         self.swap.start()
         self.local.start()
 
-    def swapped(self):
+    def far_first(self):
         self.swap.arrived()
         self.local.wait()
         self.own_y.start()
@@ -199,14 +197,13 @@
             for move, _ in self.steps[0]:
                 move.start()
 
-    def step(self, k):
-        for side in range(2):
-            move, follow = self.steps[k][side]
-            move.arrived()
-            if k + 1 < len(self.steps):
-                self.steps[k + 1][side][0].start()
-            for other in follow:
-                other.start()
+    def step(self, k, side):
+        move, follow = self.steps[k][side]
+        move.arrived()
+        if k + 1 < len(self.steps):
+            self.steps[k + 1][side][0].start()
+        for other in follow:
+            other.start()
 
     def landed(self):
         if not self.y_first:
@@ -271,23 +268,23 @@
     for gather in gathers:
         gather.begin()
     for quarter in quarters:
-        quarter.swapped()
+        quarter.far_first()
     for gather in gathers:
         gather.far_first()
-    for k in range(zs - 1):
+    for k, side in [(k, side) for k in range(zs - 1) for side in range(2)]:
         for gather in gathers:
-            gather.step(k)
+            gather.step(k, side)
         for quarter in quarters:
             if quarter.y_first:
-                if k == 0:
+                if k == 0 and side == 0:
                     quarter.own_y_arrived()
             else:
-                quarter.step(k)
+                quarter.step(k, side)
         for gather in gathers:
-            gather.far_step(k)
+            gather.far_step(k, side)
         for quarter in quarters:
             if quarter.y_first:
-                quarter.step(k)
+                quarter.step(k, side)
     for item in gathers + quarters:
         item.landed()
         item.sent()
@@ -414,10 +411,9 @@
             )
         self.line = Line(lanes, ready, from_left, from_right)
 
-    def begin(self):
-        for zz in ends_first(self.lanes.zs):
-            for j in range(2):
-                self.one[zz, j].start()
+    def begin(self, zz):
+        for j in range(2):
+            self.one[zz, j].start()
 
     def second(self, zz):
         self.one[zz, 0].arrived()
@@ -530,19 +526,25 @@
             full.append(Scatter(lanes, parts[i], held, outs[i], order))
     crest = Crest(lanes, crest_in, rest[0], crest_out)
     crest.one.start()
-    for item in full:
-        item.begin()
-    crest.second()
-    for d in ends_first(zs):
-        for item in zfirst:
-            item.pass_on(d)
+    order = ends_first(zs)
+    for i in range(zs + 3):
         for item in full:
-            item.second(d)
-    for item in zfirst:
-        item.total()
-    for d in ends_first(zs):
+            if i < zs:
+                item.begin(order[i])
+        if i == 1:
+            crest.second()
+        if i < zs:
+            for item in zfirst:
+                item.pass_on(order[i])
         for item in full:
-            item.third(d)
+            if 2 <= i < zs + 2:
+                item.second(order[i - 2])
+        if i == zs:
+            for item in zfirst:
+                item.total()
+        for item in full:
+            if 3 <= i:
+                item.third(order[i - 3])
     crest.finish()
     for item in zfirst:
         item.after()
@@ -591,24 +593,11 @@
     return lax.dot_general(left, right, (((0,), (0,)), ((), ())), preferred_element_type=F32)
 
 
-def columns_by(value, axis_name, zs):
-    rows = value.shape[0]
-    at = lax.axis_index(axis_name)
-    if axis_name == "y":
-        split = value.reshape(rows, zs, 2, -1)
-        dim = 2
-    else:
-        split = value.reshape(rows, 2 * zs, 2, -1)
-        dim = 2
-    return (
-        pick(split, at, dim).reshape(rows, -1),
-        pick(split, 1 - at, dim).reshape(rows, -1),
-    )
-
-
-def reduce_full(left_keep, left_send, right, zs):
-    got = swap(tn(left_send, right).astype(BF), "x")
-    held = (tn(left_keep, right) + got.astype(F32)).astype(BF)
+def reduce_full(left, right, zs):
+    held = tn(left, right).astype(BF).reshape(zs * 2, 2, -1, right.shape[1])
+    at = lax.axis_index("x")
+    got = swap(pick(held, 1 - at, 1), "x")
+    held = (pick(held, at, 1).astype(F32) + got.astype(F32)).astype(BF)
     held = held.reshape(zs, 2, -1, right.shape[1])
     at = lax.axis_index("y")
     got = swap(pick(held, 1 - at, 1), "y")
@@ -616,10 +605,11 @@
     return lax.psum_scatter(held, "z", scatter_dimension=0, tiled=False)
 
 
-def reduce_pair(left_keep, left_send, right, zs):
-    got = swap(tn(left_send, right).astype(BF), "y")
-    held = (tn(left_keep, right) + got.astype(F32)).astype(BF)
-    held = held.reshape(zs, -1, right.shape[1])
+def reduce_pair(left, right, zs):
+    held = tn(left, right).astype(BF).reshape(zs, 2, -1, right.shape[1])
+    at = lax.axis_index("y")
+    got = swap(pick(held, 1 - at, 1), "y")
+    held = (pick(held, at, 1).astype(F32) + got.astype(F32)).astype(BF)
     held = lax.psum_scatter(held, "z", scatter_dimension=0, tiled=False)
     held = held.reshape(2, -1, right.shape[1])
     at = lax.axis_index("x")
@@ -863,6 +853,20 @@
     )(rows, weight, *turns)
 
 
+PLAN = (
+    100, 700, 0, 1000, 2000, 2001, 800, 1100, 2100, 2101, 3000, 2010, 2011, 3001, 1700, 600,
+    2110, 2111, 3100, 2020, 2021, 1800, 3101, 3010, 3011, 2700, 2701, 200, 2120, 2121, 3020,
+    3021, 300, 400, 3110, 3111, 2710, 2711, 500, 2200, 2201, 1600, 5800, 2720, 2721, 2300, 2301,
+    2400, 2401, 2210, 2211, 3120, 3121, 2220, 2221, 2310, 2311, 2500, 2501, 2410, 2411, 1200,
+    4000, 2320, 2321, 2600, 2601, 2420, 2421, 1300, 1400, 3200, 3201, 4100, -1, 4700, -1, -1,
+    1500, 3300, 3301, -1, -1, 2800, 2801, -1, 3400, 3401, -1, -1, 2510, 2511, 3210, 3211, -1,
+    -1, 3220, 3221, -1, 3310, 3311, -1, -1, 2610, 2611, -1, 3410, 3411, 3320, 3321, -1, -1,
+    3420, 3421, 3500, 3501, 4200, -1, -1, 2810, 2811, -1, -1, -1, -1, 4300, 2620, 2621, 4400,
+    -1, -1, 2520, 2521, -1, -1, -1, -1, -1, -1, -1, -1, -1, 3510, 3511, -1, 4600, -1, -1, 3520,
+    3521, 4500, -1, -1, -1, -1, -1, 2820, 2821, -1,
+)
+
+
 def normalise(stream, gain_vec, bias_vec):
     average = jnp.mean(stream, axis=-1, keepdims=True)
     centred = stream - average
@@ -952,7 +956,7 @@
     mate_cross = mate(part_send2, part_got2)
     gathers = [Gather(lanes, whole) for whole in wholes]
     quarters = [
-        PairGather(lanes, quarters_in[i], quarter_outs[i], i == 0) for i in range(3)
+        PairGather(lanes, quarters_in[i], quarter_outs[i], i == 2) for i in range(3)
     ]
     loads = [
         local(whole, held)
@@ -968,93 +972,26 @@
     cot_moves[0].start()
     for piece in pieces:
         piece.wait()
-    early, late = gathers[:2], gathers[2:]
-    for gather in early:
-        gather.begin()
-    for quarter in quarters:
-        quarter.begin()
-
-    news = []
-
-    def every(items, name, *args):
-        for item in items:
-            news.append(functools.partial(getattr(item, name), *args))
-
-    every(early, "far_first")
-    every(early, "step", 0)
-    every(quarters, "swapped")
-    every(late, "begin")
-    every(early, "far_step", 0)
-    for k in range(1, zs - 1):
-        every(early, "step", k)
-        every(early, "far_step", k)
-    news.append(cot_moves[1].start)
-    every(early, "landed")
-    until_in = len(news)
-    every(late, "far_first")
-    for k in range(zs - 1):
-        every(late, "step", k)
-        every(quarters[1:], "step", k)
-        if k == 0:
-            every(quarters[:1], "own_y_arrived")
-        every(late, "far_step", k)
-        every(quarters[:1], "step", k)
-        if k == 0:
-            news.append(cot_moves[1].arrived)
-            news.append(cot_moves[2].start)
-    until_late = {}
-    for i, gather in enumerate(late):
-        every([gather], "landed")
-        news.append(loads[2 + i].start)
-        until_late[i] = len(news)
-    done = [0]
-
-    def hear(upto):
-        while done[0] < min(upto, len(news)):
-            news[done[0]]()
-            done[0] += 1
-
-    def hear_some(count):
-        hear(done[0] + count)
-
-    hear(until_in)
-    loads[0].start()
-    loads[1].start()
-    own_inputs.wait()
-    mate_inputs.arrived()
-    loads[0].wait()
-    vectors[...] = jnp.transpose(w_vec[...].reshape(width, w_vec.shape[-1]))
+    columns = w_in.shape[-1]
+    inner = columns // 3
+    pairs = inner // wide
+    block = 2 * wide
+    tile = 128 if rows % 128 == 0 else rows
+    chunk = width // zs
+    total = 2 * rows
+    step = total // 3 if total % 3 == 0 and (total // 3) % 16 == 0 else total
+    tops, ready = [], set()
 
     def vec(i):
         return vectors[i : i + 1, :]
 
-    tile = 128 if rows % 128 == 0 else rows
-    for side in range(2):
-        for start in range(0, rows, tile):
-            part = slice(start, start + tile)
-            made = normalise(x_all[side, part, :].astype(F32), vec(0), vec(1))
-            normed_self[side * rows + start : side * rows + start + tile, :] = made.astype(BF)
-    saves[0].start()
-    hear_some(2)
-    loads[1].wait()
-    columns = w_in.shape[-1]
-    block = 2 * wide
-    for start in range(0, columns, block):
-        made = nn(normed_self[...], w_in[..., start : start + block].reshape(width, block))
-        for at in range(0, block, wide):
-            piece = made[:, at : at + wide]
-            if start + at < columns * 2 // 3:
-                piece = turn(piece, cos_ref[...], sa_ref[...], sb_ref[...], 1.0)
-            taken[:, start + at : start + at + wide] = piece.astype(BF)
-        hear_some(2)
-    saves[1].start()
-    inner = columns // 3
-    pairs = inner // wide
-    tops = []
+    def need(*groups):
+        assert ready.issuperset(groups)
+
+    def tiles():
+        return [slice(start, start + tile) for start in range(0, rows, tile)]
 
     def attend_all(query_ref, keys_at, values_at, kv_ref, bias_ref, mixed_ref):
-        total = 2 * rows
-        step = total // 3 if total % 3 == 0 and (total // 3) % 16 == 0 else total
         for j in range(pairs):
             lanes_at = j * wide
             bits, peaks = attend_pair(
@@ -1067,71 +1004,118 @@
             for start, bit in bits:
                 mixed_ref[start : start + step, lanes_at : lanes_at + wide] = bit.astype(BF)
             tops.append(peaks)
-            hear_some(2)
+            yield
 
     def out_rows(mixed_ref, first, weight, zz):
         columns_here = weight[zz].reshape(-1, inner)
         return nt(mixed_ref[first : first + rows, :], columns_here)
 
     def out_project(mixed_ref, weight, move, send, got, base, target):
-        chunk = width // zs
         for zz in range(zs):
             send[:, zz * chunk : (zz + 1) * chunk] = out_rows(mixed_ref, rows, weight, zz)
         move.start()
+        yield
         for zz in range(zs):
             part = slice(zz * chunk, (zz + 1) * chunk)
             target[:, part] = out_rows(mixed_ref, 0, weight, zz) + base(part)
-            hear_some(1)
+            yield
         move.arrived()
-        for start in range(0, rows, tile):
-            part = slice(start, start + tile)
+        for part in tiles():
             target[part, :] = target[part, :] + got[part, :]
 
-    attend_all(taken, inner, 2 * inner, taken, self_bias, mixed_self)
-    saves[2].start()
-    hear(until_late[0])
-    loads[2].wait()
-    out_project(
-        mixed_self, w_so, mate_self, part_send, part_got,
-        lambda part: x_all[0, :, part].astype(F32), stream_cross,
-    )
-    saves[3].start()
-    for start in range(0, rows, tile):
-        part = slice(start, start + tile)
-        normed_cross[0, part, :] = normalise(stream_cross[part, :], vec(2), vec(3)).astype(BF)
-    mate_normed.start()
-    hear(until_late[2])
-    loads[4].wait()
-    depth = memory.shape[1]
-    for start in range(0, 2 * inner, block):
-        weight = w_kv[..., start : start + block].reshape(depth, block)
-        taken_cross[:, start : start + block] = nn(memory[...], weight).astype(BF)
-    saves[6].start()
-    loads[3].wait()
-    for side in range(2):
-        if side == 1:
-            mate_normed.arrived()
-            saves[4].start()
-        for start in range(0, inner, block):
-            weight = w_cq[..., start : start + block].reshape(width, block)
-            made = nn(normed_cross[side], weight).astype(BF)
-            query_cross[side * rows : (side + 1) * rows, start : start + block] = made
-        hear_some(1)
-    saves[5].start()
-    attend_all(query_cross, 0, inner, taken_cross, cross_bias, mixed_cross)
-    saves[7].start()
-    hear(until_late[3])
-    loads[5].wait()
-    out_project(
-        mixed_cross, w_co, mate_cross, part_send2, part_got2,
-        lambda part: stream_cross[:, part], stream_feed,
-    )
-    saves[8].start()
-    for start in range(0, rows, tile):
-        part = slice(start, start + tile)
-        normed_feed[0, part, :] = normalise(stream_feed[part, :], vec(4), vec(5)).astype(BF)
-    feed_moves[1].start()
-    feed_moves[0].start()
+    def compute():
+        need(0, 1)
+        own_inputs.wait()
+        mate_inputs.arrived()
+        loads[0].wait()
+        vectors[...] = jnp.transpose(w_vec[...].reshape(width, w_vec.shape[-1]))
+        for side in range(2):
+            for part in tiles():
+                made = normalise(x_all[side, part, :].astype(F32), vec(0), vec(1))
+                at = side * rows + part.start
+                normed_self[at : at + tile, :] = made.astype(BF)
+        saves[0].start()
+        loads[1].wait()
+        yield
+        for start in range(0, columns, block):
+            made = nn(normed_self[...], w_in[..., start : start + block].reshape(width, block))
+            for at in range(0, block, wide):
+                piece = made[:, at : at + wide]
+                if start + at < 2 * inner:
+                    piece = turn(piece, cos_ref[...], sa_ref[...], sb_ref[...], 1.0)
+                taken[:, start + at : start + at + wide] = piece.astype(BF)
+            yield
+        saves[1].start()
+        yield from attend_all(taken, inner, 2 * inner, taken, self_bias, mixed_self)
+        saves[2].start()
+        need(2)
+        loads[2].wait()
+        yield from out_project(
+            mixed_self, w_so, mate_self, part_send, part_got,
+            lambda part: x_all[0, :, part].astype(F32), stream_cross,
+        )
+        saves[3].start()
+        for part in tiles():
+            made = normalise(stream_cross[part, :], vec(2), vec(3))
+            normed_cross[0, part, :] = made.astype(BF)
+        mate_normed.start()
+        yield
+        need(4)
+        loads[4].wait()
+        depth = memory.shape[1]
+        for start in range(0, 2 * inner, block):
+            weight = w_kv[..., start : start + block].reshape(depth, block)
+            taken_cross[:, start : start + block] = nn(memory[...], weight).astype(BF)
+        saves[6].start()
+        yield
+        need(3)
+        loads[3].wait()
+        yield
+        for side in range(2):
+            if side == 1:
+                mate_normed.arrived()
+                saves[4].start()
+            for start in range(0, inner, block):
+                weight = w_cq[..., start : start + block].reshape(width, block)
+                made = nn(normed_cross[side], weight).astype(BF)
+                query_cross[side * rows : (side + 1) * rows, start : start + block] = made
+                yield
+        saves[5].start()
+        yield from attend_all(query_cross, 0, inner, taken_cross, cross_bias, mixed_cross)
+        saves[7].start()
+        need(5)
+        loads[5].wait()
+        yield from out_project(
+            mixed_cross, w_co, mate_cross, part_send2, part_got2,
+            lambda part: stream_cross[:, part], stream_feed,
+        )
+        saves[8].start()
+        for part in tiles():
+            made = normalise(stream_feed[part, :], vec(4), vec(5))
+            normed_feed[0, part, :] = made.astype(BF)
+        feed_moves[1].start()
+        feed_moves[0].start()
+
+    items = gathers + quarters
+    names = ("begin", "far_first", "step", "far_step", "landed", "own_y_arrived")
+    work = compute()
+    for entry in PLAN:
+        if entry < 0:
+            next(work, None)
+            continue
+        kind, which, k, side = entry // 1000, entry // 100 % 10, entry // 10 % 10, entry % 10
+        item = items[which]
+        getattr(item, names[kind])(*((k, side) if kind in (2, 3) else ()))
+        if kind == 0 and which == 4:
+            cot_moves[1].start()
+        if kind == 4:
+            ready.add(which)
+            if which < 6:
+                loads[which].start()
+    cot_moves[1].arrived()
+    cot_moves[2].start()
+    for _ in work:
+        pass
     lane = lax.broadcasted_iota(jnp.int32, peak_out.shape, 1)
     crest = jnp.full(peak_out.shape, NEGATIVE, F32)
     for i, peaks in enumerate(tops):
@@ -1139,11 +1123,11 @@
             head = (i % pairs) * 2 + which
             crest = jnp.where(lane == head, jnp.maximum(crest, peaks[which]), crest)
     peak_out[...] = crest
-    hear(len(news))
     feed_moves[1].arrived()
     feed_moves[2].start()
-    for quarter in quarters:
-        quarter.landed()
+    for i, item in enumerate(items):
+        if i not in ready:
+            item.landed()
     feed_moves[0].arrived()
     feed_moves[2].arrived()
     saves[9].start()
@@ -1402,31 +1386,27 @@
     hidden = (gate_pre * sigmoid_gate * upward).astype(BF)
     result = (stream_feed + spread_group(Product([(hidden, down_t)], True))).astype(BF)
 
-    cot_keep, cot_send = columns_by(cot_group, "y", zs)
-    down_keep, down_got = reduce_pair(cot_keep, cot_send, hidden, zs)
+    down_keep, down_got = reduce_pair(cot_group, hidden, zs)
     grad_hidden = nn(cot_group, down_t)
     grad_gate = grad_hidden * upward * sigmoid_gate * (1.0 + gate_pre * (1.0 - sigmoid_gate))
     grad_upward = grad_hidden * gate_pre * sigmoid_gate
     grad_gate = grad_gate.astype(BF)
     grad_upward = grad_upward.astype(BF)
-    grad_gates = jnp.concatenate([grad_gate, grad_upward], axis=1)
     grad_normed = spread_group(Product([(grad_gate, gate_full), (grad_upward, up_full)], True))
-    feed_keep, feed_send = columns_by(normed_feed, "y", zs)
-    gates_keep, gates_got = reduce_pair(feed_keep, feed_send, grad_gates, zs)
+    gate_keep, gate_got = reduce_pair(normed_feed, grad_gate, zs)
+    up_keep, up_got = reduce_pair(normed_feed, grad_upward, zs)
     stream_part, grad_feed_gain, grad_feed_bias = norm_backward(
         grad_normed, unit_feed, inverse_feed, norms[4]
     )
     grad_stream = cotangent.astype(F32) + stream_part
     grad_full = pair_rows(grad_stream.astype(BF))
-    keep, send = columns_by(grad_full, "x", zs)
-    sum_cross_output = reduce_full(keep, send, mixed_cross, zs).astype(F32)
+    sum_cross_output = reduce_full(grad_full, mixed_cross, zs).astype(F32)
     grad_mixed = nn(grad_full, cross_out_t).astype(BF)
     grad_query, grad_keys, grad_values = attend_back(
         query_cross, taken_cross, taken_cross, grad_mixed, cross_bias_row[:, None], (0, 0, pairs), None
     )
     grad_normed = spread_pair(grad_query, cross_in)
-    keep, send = columns_by(normed_cross, "x", zs)
-    sum_cross_query = reduce_full(keep, send, grad_query, zs).astype(F32)
+    sum_cross_query = reduce_full(normed_cross, grad_query, zs).astype(F32)
     part_memory = tn(memory, jnp.concatenate([grad_keys, grad_values], axis=1))
     stream_part, grad_cross_gain, grad_cross_bias = norm_backward(
         grad_normed, unit_cross, inverse_cross, norms[2]
@@ -1491,8 +1471,8 @@
         return jnp.concatenate([low, high], axis=1)
 
     down_sum = side_by_side(down_keep, down_got).T
-    gate_sum = side_by_side(gates_keep[:, :ff], gates_got[:, :ff])
-    up_sum = side_by_side(gates_keep[:, ff:], gates_got[:, ff:])
+    gate_sum = side_by_side(gate_keep, gate_got)
+    up_sum = side_by_side(up_keep, up_got)
     return (
         result,
         grad_stream,

time: 959 us -> 916 us (0.955)
  waiting for transfers between devices: 33.6 us -> 99.3 us
  Pallas kernels: 566 us -> 503 us
  local copies, waits for them, and re-layouts: 82 us -> 42.3 us
  matrix products: 206 us -> 193 us
  other arithmetic: 34.5 us -> 46.1 us
    ppermute x19 -> x21, waiting for transfers between devices: 33.5 us -> 99.2 us  [swap(): return lax.ppermute(value, axis, [(0, 1), (1, 0)])]
    pallas_call x1, Pallas kernels: 375 us -> 325 us  [forward(): pl.pallas_call(functools.partial(forward_kernel, zs), out_shape=spread +...]
    another operation x3 -> x0, local copies, waits for them, and re-layouts: 24.1 us -> none  [the longest x2 17.6 us: columns_by(): split = value.reshape(rows, zs, 2, -1)]
    pallas_call x3 -> x0, local copies, waits for them, and re-layouts: 23.9 us -> none  [forward(): pl.pallas_call(functools.partial(forward_kernel, zs), out_shape=spread +...]
    pallas_call x1, Pallas kernels: 138 us -> 125 us  [scatter_all(): pl.pallas_call(functools.partial(scatter_kernel, zs, orders), out_shape=[...]
    squeeze x4 -> x10, local copies, waits for them, and re-layouts: 2.4 us -> 14.9 us  [pick(): return lax.dynamic_index_in_dim(value, index, dim, keepdims=False)]
    dot_general x13 -> x10, matrix products: 69.2 us -> 58.7 us  [tn(): lax.dot_general(left, right, (((0,), (0,)), ((), ())), preferred_element_...]
    dynamic_slice x4 -> x0, local copies, waits for them, and re-layouts: 9.84 us -> none  [pick(): return lax.dynamic_index_in_dim(value, index, dim, keepdims=False)]
  transfers between devices with their start and end apart: 23 -> 26, of which waited for: 6 -> 7; matrix products, arithmetic and copies ran while one was open for 24% -> 22% of each run, Pallas kernels for 20% -> 6%
where the time goes in v5:
time: 916 us; the launch traced here: 912 us
  Pallas kernels  503 us (55%)
  matrix products  193 us (21%)
  waiting for transfers between devices  99.3 us (11%)
  other arithmetic  46.1 us (5%)
  local copies, waits for them, and re-layouts  42.3 us (5%)
  between operations  16.3 us (2%)
  starting transfers between devices  12 us (1%)
    pallas_call x1, Pallas kernels, forward(): pl.pallas_call(functools.partial(forward_kernel, zs), out_shape=spread +...  325 us
    pallas_call x1, Pallas kernels, scatter_all(): pl.pallas_call(functools.partial(scatter_kernel, zs, orders), out_shape=[...  125 us
    ppermute x21, waiting for transfers between devices, swap(): return lax.ppermute(value, axis, [(0, 1), (1, 0)])  99.2 us
    dot_general x16, matrix products, nt(): lax.dot_general(left, right, (((1,), (1,)), ((), ())), preferred_element_...  86.7 us
    dot_general x10, matrix products, tn(): lax.dot_general(left, right, (((0,), (0,)), ((), ())), preferred_element_...  58.7 us
    pallas_call x2, Pallas kernels, attend_back(): pl.pallas_call(functools.partial(attend_back_kernel, turns is not None),...  53 us
    dot_general x5, matrix products, nn(): lax.dot_general(left, right, (((1,), (0,)), ((), ())), preferred_element_...  48 us
  transfers between devices with their start and end apart: 26, of which 7 were waited for; matrix products, arithmetic and copies ran while one was open for 22% of the time, Pallas kernels for 6%

profile of v5, /device:TPU:0, one launch (start us, length us, event | category | flops | bytes accessed | tf_op | source)
XLA Modules:
  0.0 912.4 jit_solution(7487344358270125836)
XLA Ops:
  18.1 325.2 %shard_map.406 = (f32[4,2,2,96,128]{4,3,2,1,0:T(8,128)}, bf16[4,2,2,96,2304]{4,3,2,1,0:T(8,128)(2,1)}, bf16[4,2,2,96,768]{4,3,2,1,0:T(8,128)(2,1)}, bf16[4,2,2,9...) custom-call(f32[96,128]{1,0:T(8,128)} %pad_convert_fusion.refs_0_, ...), custom_call_target="tpu_custom_call" | custom-call | flops 16307453952 | bytes 100000000 | tf_op jit(solution)/shard_map/pallas_call | solution.py:1181
  343.3 13.3 %fusion.65 = f32[1536,1536]{1,0:T(8,128)} fusion(bf16[1536,1536]{1,0:T(8,128)(2,1)} %bitcast.248, bf16[1536,1536]{1,0:T(8,128)(2,1)} %bitcast.232), kind=kOutput, calls=%fused_computation.176 | convolution fusion | flops 7247757312 | bytes 18874368 | tf_op jit(solution)/shard_map/dot_general | solution.py:585
  356.7 10.5 %fusion.64 = f32[1536,1536]{1,0:T(8,128)} fusion(bf16[1536,1536]{1,0:T(8,128)(2,1)S(1)} %bitcast.251, bf16[1536,1536]{1,0:T(8,128)(2,1)S(1)} %bitcast.242), kind=kOutput, calls=%fused_computation.175 | convolution fusion | flops 7247757312 | bytes 18874368 | tf_op jit(solution)/shard_map/dot_general | solution.py:585
  367.2 19.1 %multiply_convert_fusion = (bf16[1536,1536]{1,0:T(8,128)(2,1)}, bf16[1536,1536]{1,0:T(8,128)(2,1)}, bf16[1536,1536]{1,0:T(8,128)(2,1)}) fusion(f32[1536,1536]{1,0:T(8,128)} %fusion.64, f32[1536,1536]{1,0:T(8,128)} %fusion.65, bf16[1536,1536]{1,0:T(8,128)(2,1)} %bitcast.246, bf16[1536,1536]{1,0:T(8,128)(2,1)S(1)} %bitcast.226), kind=kOutput, calls=%fused_computation | convolution fusion | flops 7285506048 | bytes 42467328 | tf_op jit(solution)/shard_map/dot_general | solution.py:585
  386.3 4.7 fusion.42
  391.0 4.7 fusion.39
  396.2 12.3 %convolution_convert_fusion.2 = bf16[1536,1536]{1,0:T(8,128)(2,1)} fusion(bf16[1536,1536]{1,0:T(8,128)(2,1)} %bitcast.249, bf16[1536,1536]{1,0:T(8,128)(2,1)} %get-tuple-element.112), kind=kOutput, calls=%fused_computation.6 | convolution fusion | flops 7250116608 | bytes 14155776 | tf_op jit(solution)/shard_map/dot_general | solution.py:593
  412.4 11.2 %convolution_convert_fusion.1 = bf16[1536,1536]{1,0:T(8,128)(2,1)S(1)} fusion(bf16[1536,1536]{1,0:T(8,128)(2,1)} %bitcast.250, bf16[1536,1536]{1,0:T(8,128)(2,1)} %get-tuple-element.111), kind=kOutput, calls=%fused_computation.5 | convolution fusion | flops 7250116608 | bytes 14155776 | tf_op jit(solution)/shard_map/dot_general | solution.py:593
  432.0 4.8 convolution_add_fusion.3
  436.8 4.9 fusion.28
  441.7 6.2 convolution_add_fusion.1
  447.9 18.4 %collective-permute-done.15 = bf16[4,192,1536]{2,1,0:T(8,128)(2,1)S(1)} collective-permute-done((bf16[4,192,1536]{2,1,0:T(8,128)(2,1)}, bf16[4,192,1536]{2,1,0:T(8,128)(2,1)S(1)}, u32[]{:S(2)}, u32[]{:S(2)}) %collective-permute-start.15) | collective-permute-done | bytes 2359328 | tf_op jit(solution)/shard_map/ppermute | solution.py:20
  468.4 12.8 %convolution_convert_fusion = bf16[1536,1536]{1,0:T(8,128)(2,1)} fusion(bf16[1536,1536]{1,0:T(8,128)(2,1)} %bitcast.247, bf16[1536,1536]{1,0:T(8,128)(2,1)} %get-tuple-element.113), kind=kOutput, calls=%fused_computation.4 | convolution fusion | flops 7250116608 | bytes 14155776 | tf_op jit(solution)/shard_map/dot_general | solution.py:593
  488.8 6.3 fusion.31
  495.0 20.9 %collective-permute-done.17 = bf16[4,192,1536]{2,1,0:T(8,128)(2,1)} collective-permute-done((bf16[4,192,1536]{2,1,0:T(8,128)(2,1)}, bf16[4,192,1536]{2,1,0:T(8,128)(2,1)}, u32[]{:S(2)}, u32[]{:S(2)}) %collective-permute-start.17) | collective-permute-done | bytes 2359328 | tf_op jit(solution)/shard_map/ppermute | solution.py:20
  520.7 7.3 fusion.13
  530.4 6.2 fusion.37
  537.7 17.4 %collective-permute-done.5 = bf16[384,1536]{1,0:T(8,128)(2,1)} collective-permute-done((bf16[384,1536]{1,0:T(8,128)(2,1)}, bf16[384,1536]{1,0:T(8,128)(2,1)}, u32[]{:S(2)}, u32[]{:S(2)}) %collective-permute-start.5) | collective-permute-done | bytes 1179680 | tf_op jit(solution)/shard_map/ppermute | solution.py:20
  555.1 8.0 multiply_reduce_fusion
  583.2 16.3 %shard_map.407 = (bf16[768,768]{1,0:T(8,128)(2,1)S(1)}, bf16[256,768]{1,0:T(8,128)(2,1)S(1)}, bf16[256,768]{1,0:T(8,128)(2,1)S(1)}) custom-call(bf16[768,768]{1,0:T(8,128)(2,1)S(1)} %copy-done.4, bf16[256,1536]{1,0:T(8,128)(2,1)S(1)} %copy-done.5, bf16[256,1536]{1,0:T(8,128)(2,1)S(1)} %copy-done.5, bf16[768,768]{1,0:T(8,128)(2,1)S(1)} %convolution_convert_fusion.11.g_ref, ...), custom_call_target="tpu_custom_call" | custom-call | flops 3019898880 | bytes 6291456 | tf_op jit(solution)/shard_map/pallas_call | solution.py:791
  603.7 5.1 fusion.15
  615.8 16.8 %collective-permute-done.11 = bf16[8,96,768]{2,1,0:T(8,128)(2,1)} collective-permute-done((bf16[8,96,768]{2,1,0:T(8,128)(2,1)S(1)}, bf16[8,96,768]{2,1,0:T(8,128)(2,1)}, u32[]{:S(2)}, u32[]{:S(2)}) %collective-permute-start.11) | collective-permute-done | bytes 1179680 | tf_op jit(solution)/shard_map/ppermute | solution.py:20
  638.2 18.1 %collective-permute-done.2 = bf16[384,1536]{1,0:T(8,128)(2,1)} collective-permute-done((bf16[384,1536]{1,0:T(8,128)(2,1)}, bf16[384,1536]{1,0:T(8,128)(2,1)}, u32[]{:S(2)}, u32[]{:S(2)}) %collective-permute-start.2) | collective-permute-done | bytes 1179680 | tf_op jit(solution)/shard_map/ppermute | solution.py:20
  656.3 7.5 fusion.14
  673.8 4.7 multiply_reduce_fusion.1
  689.7 4.5 collective-permute-done.20
  698.5 36.7 %shard_map.408 = (bf16[768,768]{1,0:T(8,128)(2,1)S(1)}, bf16[768,768]{1,0:T(8,128)(2,1)S(1)}, bf16[768,768]{1,0:T(8,128)(2,1)S(1)}) custom-call(bf16[768,2304]{1,0:T(8,128)(2,1)} %get-tuple-element.70.q_ref.k_ref.v_ref, bf16[768,2304]{1,0:T(8,128)(2,1)} %get-tuple-element.70.q_ref.k_ref.v_ref, bf16[768,2304]{1,0:T(8,128)(2,1)} %get-tuple-element.70.q_ref.k_ref.v_ref, ...), custom_call_target="tpu_custom_call" | custom-call | flops 9059696640 | bytes 9437184 | tf_op jit(solution)/shard_map/pallas_call | solution.py:791
  735.5 4.3 fusion.24
  743.1 5.6 convolution_convert_fusion.6
  759.4 6.1 fusion.20
  766.4 4.6 fusion.19
  771.7 124.9 %shard_map.409 = (f32[8,128]{1,0:T(8,128)}, f32[96,768]{1,0:T(8,128)}, f32[96,768]{1,0:T(8,128)}, f32[96,768]{1,0:T(8,128)}, f32[96,768]{1,0:T(8,128)}, /*index=5*/f32[48,1536]{1,0:T(8,128)}, f32[8,128]{1,0:T(8,128)}) custom-call(f32[4,2,2,8,128]{4,3,2,1,0:T(8,128)} %bitcast.204, bf16[4,2,2,96,768]{4,3,2,1,0:T(8,128)(2,1)} %bitcast.190, ...), custom_call_target="tpu_custom_call" | custom-call | tf_op jit(solution)/shard_map/pallas_call | solution.py:569
  (311 shorter events, 126.8 us)
Async XLA Ops:
  7.2 661.2 %reduce-scatter.10.cloned.1.call-start = ((), (), s32[]{:S(2)}) async-start(), calls=%async_computation.7 | async-start | bytes 2949120 | tf_op jit(solution)/shard_map/reduce_scatter | solution.py:613
  391.0 247.2 %collective-permute-start = (f32[384,1536]{1,0:T(8,128)}, f32[384,1536]{1,0:T(8,128)}, u32[]{:S(2)}, u32[]{:S(2)}) collective-permute-start(f32[384,1536]{1,0:T(8,128)} %fusion.42), channel_id=1, source_target_pairs={{0,1},{1,0},{2,3},{3,2},{4,5},{5,4},{6,7},{7,6},{8,9},{9,8},{10,11... | collective-permute-start | bytes 7077896 | tf_op jit(solution)/shard_map/ppermute | solution.py:20
  395.7 208.0 %collective-permute-start.1 = (f32[384,1536]{1,0:T(8,128)}, f32[384,1536]{1,0:T(8,128)}, u32[]{:S(2)}, u32[]{:S(2)}) collective-permute-start(f32[384,1536]{1,0:T(8,128)} %fusion.39), channel_id=1, source_target_pairs={{0,1},{1,0},{2,3},{3,2},{4,5},{5,4},{6,7},{7,6},{8,9},{9,8},{10,11... | collective-permute-start | bytes 7077896 | tf_op jit(solution)/shard_map/ppermute | solution.py:20
  411.9 54.3 %collective-permute-start.15 = (bf16[4,192,1536]{2,1,0:T(8,128)(2,1)}, bf16[4,192,1536]{2,1,0:T(8,128)(2,1)S(1)}, u32[]{:S(2)}, u32[]{:S(2)}) collective-permute-start(bf16[4,192,1536]{2,1,0:T(8,128)(2,1)} %dynamic-slice_bitcast_fusion.2), channel_id=1, source_target_pairs={{0,4},{4,0},{1,5},{5,1},{2,6},{6,2},{3,7},{7,3},{8,12},{12,8},{9,1... | collective-permute-start | bytes 7077896 | tf_op jit(solution)/shard_map/ppermute | solution.py:20
  427.1 88.8 %collective-permute-start.17 = (bf16[4,192,1536]{2,1,0:T(8,128)(2,1)}, bf16[4,192,1536]{2,1,0:T(8,128)(2,1)}, u32[]{:S(2)}, u32[]{:S(2)}) collective-permute-start(bf16[4,192,1536]{2,1,0:T(8,128)(2,1)} %dynamic-slice_bitcast_fusion.1), channel_id=1, source_target_pairs={{0,4},{4,0},{1,5},{5,1},{2,6},{6,2},{3,7},{7,3},{8,12},{12,8},{9,1... | collective-permute-start | bytes 7077896 | tf_op jit(solution)/shard_map/ppermute | solution.py:20
  436.8 100.9 %collective-permute-start.3 = (f32[384,1536]{1,0:T(8,128)}, f32[384,1536]{1,0:T(8,128)}, u32[]{:S(2)}, u32[]{:S(2)}) collective-permute-start(f32[384,1536]{1,0:T(8,128)} %convolution_add_fusion.3), channel_id=1, source_target_pairs={{0,1},{1,0},{2,3},{3,2},{4,5},{5,4},{6,7},{7,6},{8,9},{9,8},{10,11... | collective-permute-start | bytes 7077896 | tf_op jit(solution)/shard_map/ppermute | solution.py:20
  466.2 54.5 %collective-permute-start.4 = (f32[384,1536]{1,0:T(8,128)}, f32[384,1536]{1,0:T(8,128)}, u32[]{:S(2)}, u32[]{:S(2)}) collective-permute-start(f32[384,1536]{1,0:T(8,128)} %convolution_add_fusion.1), channel_id=1, source_target_pairs={{0,1},{1,0},{2,3},{3,2},{4,5},{5,4},{6,7},{7,6},{8,9},{9,8},{10,11... | collective-permute-start | bytes 7077896 | tf_op jit(solution)/shard_map/ppermute | solution.py:20
  468.3 202.3 %reduce-scatter.12.cloned.1.call-start = ((), (), s32[]{:S(2)}) async-start(), calls=%async_computation.8 | async-start | bytes 2949120 | tf_op jit(solution)/shard_map/reduce_scatter | solution.py:613
  516.0 52.6 %collective-permute-start.19 = (bf16[4,192,1536]{2,1,0:T(8,128)(2,1)}, bf16[4,192,1536]{2,1,0:T(8,128)(2,1)}, u32[]{:S(2)}, u32[]{:S(2)}) collective-permute-start(bf16[4,192,1536]{2,1,0:T(8,128)(2,1)} %dynamic-slice_bitcast_fusion), channel_id=1, source_target_pairs={{0,4},{4,0},{1,5},{5,1},{2,6},{6,2},{3,7},{7,3},{8,12},{12,8},{9,1... | collective-permute-start | bytes 7077896 | tf_op jit(solution)/shard_map/ppermute | solution.py:20
  520.2 163.5 %reduce-scatter.14.cloned.1.call-start = ((), (), s32[]{:S(2)}) async-start(), calls=%async_computation.9 | async-start | bytes 2949120 | tf_op jit(solution)/shard_map/reduce_scatter | solution.py:613
  528.0 27.1 %collective-permute-start.5 = (bf16[384,1536]{1,0:T(8,128)(2,1)}, bf16[384,1536]{1,0:T(8,128)(2,1)}, u32[]{:S(2)}, u32[]{:S(2)}) collective-permute-start(bf16[384,1536]{1,0:T(8,128)(2,1)} %fusion.13), channel_id=1, source_target_pairs={{0,2},{2,0},{1,3},{3,1},{4,6},{6,4},{5,7},{7,5},{8,10},{10,8},{9,1... | collective-permute-start | bytes 3538952 | tf_op jit(solution)/shard_map/ppermute | solution.py:20
  530.4 42.2 %copy-start.41 = (f32[384]{0:T(512)}, f32[384]{0:T(512)S(1)}, u32[]{:S(2)}) copy-start(f32[384]{0:T(512)S(1)} %broadcast_multiply_fusion.5) | copy-start | bytes 4612
  565.5 10.6 %collective-permute-start.6 = (bf16[384,1536]{1,0:T(8,128)(2,1)S(1)}, bf16[384,1536]{1,0:T(8,128)(2,1)S(1)}, u32[]{:S(2)}, u32[]{:S(2)}) collective-permute-start(bf16[384,1536]{1,0:T(8,128)(2,1)S(1)} %get-tuple-element.109), channel_id=1, source_target_pairs={{0,1},{1,0},{2,3},{3,2},{4,5},{5,4},{6,7},{7,6},{8,9},{9,8},{10,11... | collective-permute-start | bytes 3538952 | tf_op jit(solution)/shard_map/ppermute | solution.py:20
  572.4 167.5 %reduce-scatter.8.cloned.1.call-start = ((), (), s32[]{:S(2)}) async-start(), calls=%async_computation.6 | async-start | bytes 737280 | tf_op jit(solution)/shard_map/reduce_scatter | solution.py:605
  579.3 31.2 %collective-permute-start.13 = (bf16[8,96,768]{2,1,0:T(8,128)(2,1)}, bf16[8,96,768]{2,1,0:T(8,128)(2,1)}, u32[]{:S(2)}, u32[]{:S(2)}) collective-permute-start(bf16[8,96,768]{2,1,0:T(8,128)(2,1)} %dynamic-slice_bitcast_fusion.3), channel_id=1, source_target_pairs={{0,2},{2,0},{1,3},{3,1},{4,6},{6,4},{5,7},{7,5},{8,10},{10,8},{9,1... | collective-permute-start | bytes 3538952 | tf_op jit(solution)/shard_map/ppermute | solution.py:20
  603.1 29.4 %collective-permute-start.11 = (bf16[8,96,768]{2,1,0:T(8,128)(2,1)S(1)}, bf16[8,96,768]{2,1,0:T(8,128)(2,1)}, u32[]{:S(2)}, u32[]{:S(2)}) collective-permute-start(bf16[8,96,768]{2,1,0:T(8,128)(2,1)S(1)} %dynamic-slice_bitcast_fusion.4), channel_id=1, source_target_pairs={{0,2},{2,0},{1,3},{3,1},{4,6},{6,4},{5,7},{7,5},{8,10},{10,8},{9,1... | collective-permute-start | bytes 3538952 | tf_op jit(solution)/shard_map/ppermute | solution.py:20
  608.8 47.5 %collective-permute-start.2 = (bf16[384,1536]{1,0:T(8,128)(2,1)}, bf16[384,1536]{1,0:T(8,128)(2,1)}, u32[]{:S(2)}, u32[]{:S(2)}) collective-permute-start(bf16[384,1536]{1,0:T(8,128)(2,1)} %fusion.15), channel_id=1, source_target_pairs={{0,2},{2,0},{1,3},{3,1},{4,6},{6,4},{5,7},{7,5},{8,10},{10,8},{9,1... | collective-permute-start | bytes 3538952 | tf_op jit(solution)/shard_map/ppermute | solution.py:20
  612.6 24.1 %collective-permute-start.14 = (bf16[4,96,768]{2,1,0:T(8,128)(2,1)S(1)}, bf16[4,96,768]{2,1,0:T(8,128)(2,1)S(1)}, u32[]{:S(2)}, u32[]{:S(2)}) collective-permute-start(bf16[4,96,768]{2,1,0:T(8,128)(2,1)S(1)} %dynamic-slice_bitcast_fusion.5), channel_id=1, source_target_pairs={{0,4},{4,0},{1,5},{5,1},{2,6},{6,2},{3,7},{7,3},{8,12},{12,8},{9,1... | collective-permute-start | bytes 1769480 | tf_op jit(solution)/shard_map/ppermute | solution.py:20
  615.8 58.0 %collective-permute-start.7 = (f32[384,1536]{1,0:T(8,128)}, f32[384,1536]{1,0:T(8,128)}, u32[]{:S(2)}, u32[]{:S(2)}) collective-permute-start(f32[384,1536]{1,0:T(8,128)} %fusion.50), channel_id=1, source_target_pairs={{0,1},{1,0},{2,3},{3,2},{4,5},{5,4},{6,7},{7,6},{8,9},{9,8},{10,11... | collective-permute-start | bytes 7077896 | tf_op jit(solution)/shard_map/ppermute | solution.py:20
  636.0 30.1 %collective-permute-start.12 = (bf16[4,96,768]{2,1,0:T(8,128)(2,1)}, bf16[4,96,768]{2,1,0:T(8,128)(2,1)}, u32[]{:S(2)}, u32[]{:S(2)}) collective-permute-start(bf16[4,96,768]{2,1,0:T(8,128)(2,1)} %dynamic-slice_bitcast_fusion.6), channel_id=1, source_target_pairs={{0,4},{4,0},{1,5},{5,1},{2,6},{6,2},{3,7},{7,3},{8,12},{12,8},{9,1... | collective-permute-start | bytes 1769480 | tf_op jit(solution)/shard_map/ppermute | solution.py:20
  637.7 103.7 %reduce-scatter.6.cloned.1.call-start = ((), (), s32[]{:S(2)}) async-start(), calls=%async_computation.5 | async-start | bytes 737280 | tf_op jit(solution)/shard_map/reduce_scatter | solution.py:605
  670.1 15.2 %collective-permute-start.16 = (bf16[96,1536]{1,0:T(8,128)(2,1)}, bf16[96,1536]{1,0:T(8,128)(2,1)}, u32[]{:S(2)}, u32[]{:S(2)}) collective-permute-start(bf16[96,1536]{1,0:T(8,128)(2,1)} %dynamic-slice_bitcast_fusion.9), channel_id=1, source_target_pairs={{0,2},{2,0},{1,3},{3,1},{4,6},{6,4},{5,7},{7,5},{8,10},{10,8},{9,1... | collective-permute-start | bytes 884744 | tf_op jit(solution)/shard_map/ppermute | solution.py:20
  672.3 15.2 %collective-permute-start.18 = (bf16[96,1536]{1,0:T(8,128)(2,1)}, bf16[96,1536]{1,0:T(8,128)(2,1)}, u32[]{:S(2)}, u32[]{:S(2)}) collective-permute-start(bf16[96,1536]{1,0:T(8,128)(2,1)} %dynamic-slice_bitcast_fusion.8), channel_id=1, source_target_pairs={{0,2},{2,0},{1,3},{3,1},{4,6},{6,4},{5,7},{7,5},{8,10},{10,8},{9,1... | collective-permute-start | bytes 884744 | tf_op jit(solution)/shard_map/ppermute | solution.py:20
  683.7 11.6 %collective-permute-start.8 = (bf16[384,1536]{1,0:T(8,128)(2,1)S(1)}, bf16[384,1536]{1,0:T(8,128)(2,1)S(1)}, u32[]{:S(2)}, u32[]{:S(2)}) collective-permute-start(bf16[384,1536]{1,0:T(8,128)(2,1)S(1)} %get-tuple-element.107), channel_id=1, source_target_pairs={{0,1},{1,0},{2,3},{3,2},{4,5},{5,4},{6,7},{7,6},{8,9},{9,8},{10,11... | collective-permute-start | bytes 3538952 | tf_op jit(solution)/shard_map/ppermute | solution.py:20
  684.7 9.5 %collective-permute-start.20 = (bf16[96,1536]{1,0:T(8,128)(2,1)S(1)}, bf16[96,1536]{1,0:T(8,128)(2,1)S(1)}, u32[]{:S(2)}, u32[]{:S(2)}) collective-permute-start(bf16[96,1536]{1,0:T(8,128)(2,1)S(1)} %dynamic-slice_bitcast_fusion.7), channel_id=1, source_target_pairs={{0,2},{2,0},{1,3},{3,1},{4,6},{6,4},{5,7},{7,5},{8,10},{10,8},{9,1... | collective-permute-start | bytes 884744 | tf_op jit(solution)/shard_map/ppermute | solution.py:20
  695.4 40.1 %slice-start.6 = ((s8[7077888]{0:T(1024)(128)(4,1)}), s8[4194304]{0:T(1024)(128)(4,1)S(1)}, s32[]{:S(2)}) async-start(s8[7077888]{0:T(1024)(128)(4,1)} %bitcast.217), calls=%async_computation.16 | async-start | bytes 8388608
  739.8 19.3 %collective-permute-start.9 = (f32[384,1536]{1,0:T(8,128)}, f32[384,1536]{1,0:T(8,128)}, u32[]{:S(2)}, u32[]{:S(2)}) collective-permute-start(f32[384,1536]{1,0:T(8,128)} %fusion.24), channel_id=1, source_target_pairs={{0,1},{1,0},{2,3},{3,2},{4,5},{5,4},{6,7},{7,6},{8,9},{9,8},{10,11... | collective-permute-start | bytes 7077896 | tf_op jit(solution)/shard_map/ppermute | solution.py:20
  765.9 5.1 collective-permute-start.10
  771.7 126.3 %copy-start.34 = (bf16[48,768]{1,0:T(8,128)(2,1)S(1)}, bf16[48,768]{1,0:T(8,128)(2,1)}, u32[]{:S(2)}) copy-start(bf16[48,768]{1,0:T(8,128)(2,1)} %refs_6_.1) | copy-start | bytes 221188
  771.7 127.0 %copy-start.31 = (bf16[96,768]{1,0:T(8,128)(2,1)S(1)}, bf16[96,768]{1,0:T(8,128)(2,1)}, u32[]{:S(2)}) copy-start(bf16[96,768]{1,0:T(8,128)(2,1)} %refs_1_.1) | copy-start | bytes 442372
  771.7 127.0 %copy-start.32 = (bf16[96,768]{1,0:T(8,128)(2,1)S(1)}, bf16[96,768]{1,0:T(8,128)(2,1)}, u32[]{:S(2)}) copy-start(bf16[96,768]{1,0:T(8,128)(2,1)} %refs_2_.1) | copy-start | bytes 442372
  771.7 127.0 %copy-start.33 = (bf16[96,768]{1,0:T(8,128)(2,1)S(1)}, bf16[96,768]{1,0:T(8,128)(2,1)}, u32[]{:S(2)}) copy-start(bf16[96,768]{1,0:T(8,128)(2,1)} %refs_5_.1) | copy-start | bytes 442372
  (67 other events, 649.1 us)
Sparse Core Ops, SparseCore 0:
  468.4 46.3 reduce-scatter.9
  520.3 47.2 reduce-scatter.11
  572.5 46.2 reduce-scatter.13
  637.8 20.8 reduce-scatter.7
  668.5 20.3 reduce-scatter.5

commit v6 on v5

--- a/solution.py
+++ b/solution.py
@@ -593,28 +593,46 @@
     return lax.dot_general(left, right, (((0,), (0,)), ((), ())), preferred_element_type=F32)
 
 
-def reduce_full(left, right, zs):
-    held = tn(left, right).astype(BF).reshape(zs * 2, 2, -1, right.shape[1])
-    at = lax.axis_index("x")
-    got = swap(pick(held, 1 - at, 1), "x")
-    held = (pick(held, at, 1).astype(F32) + got.astype(F32)).astype(BF)
-    held = held.reshape(zs, 2, -1, right.shape[1])
-    at = lax.axis_index("y")
-    got = swap(pick(held, 1 - at, 1), "y")
-    held = (pick(held, at, 1).astype(F32) + got.astype(F32)).astype(BF)
-    return lax.psum_scatter(held, "z", scatter_dimension=0, tiled=False)
-
-
-def reduce_pair(left, right, zs):
-    held = tn(left, right).astype(BF).reshape(zs, 2, -1, right.shape[1])
-    at = lax.axis_index("y")
-    got = swap(pick(held, 1 - at, 1), "y")
-    held = (pick(held, at, 1).astype(F32) + got.astype(F32)).astype(BF)
-    held = lax.psum_scatter(held, "z", scatter_dimension=0, tiled=False)
-    held = held.reshape(2, -1, right.shape[1])
-    at = lax.axis_index("x")
-    got = swap(pick(held, 1 - at, 0), "x")
-    return pick(held, at, 0), got
+def after(value, *others):
+    return lax.optimization_barrier((value, others))[0]
+
+
+class FullSum:
+    def __init__(self, left, right, zs):
+        self.zs = zs
+        held = tn(left, right).astype(BF)
+        self.held = held.reshape(2 * zs, 2, -1, held.shape[1])
+        self.x, self.y = lax.axis_index("x"), lax.axis_index("y")
+        self.got = swap(pick(self.held, 1 - self.x, 1), "x")
+
+    def second(self, *others):
+        got = after(self.got, others)
+        held = pick(self.held, self.x, 1).astype(F32) + got.astype(F32)
+        self.held = held.astype(BF).reshape(self.zs, 2, -1, held.shape[-1])
+        self.got = swap(pick(self.held, 1 - self.y, 1), "y")
+
+    def third(self, *others):
+        got = after(self.got, others)
+        held = pick(self.held, self.y, 1).astype(F32) + got.astype(F32)
+        return lax.psum_scatter(held.astype(BF), "z", scatter_dimension=0, tiled=False)
+
+
+class PairSum:
+    def __init__(self, left, right, zs):
+        held = tn(left, right).astype(BF)
+        self.held = held.reshape(zs, 2, -1, held.shape[1])
+        self.y = lax.axis_index("y")
+        self.got = swap(pick(self.held, 1 - self.y, 1), "y")
+
+    def second(self, *others):
+        got = after(self.got, others)
+        held = pick(self.held, self.y, 1).astype(F32) + got.astype(F32)
+        held = lax.psum_scatter(held.astype(BF), "z", scatter_dimension=0, tiled=False)
+        self.held = held.reshape(2, -1, held.shape[-1])
+
+    def third(self):
+        at = lax.axis_index("x")
+        return pick(self.held, at, 0), swap(pick(self.held, 1 - at, 0), "x")
 
 
 def norm_forward(stream, gain_vec, bias_vec):
@@ -854,16 +872,16 @@
 
 
 PLAN = (
-    100, 700, 0, 1000, 2000, 2001, 800, 1100, 2100, 2101, 3000, 2010, 2011, 3001, 1700, 600,
-    2110, 2111, 3100, 2020, 2021, 1800, 3101, 3010, 3011, 2700, 2701, 200, 2120, 2121, 3020,
-    3021, 300, 400, 3110, 3111, 2710, 2711, 500, 2200, 2201, 1600, 5800, 2720, 2721, 2300, 2301,
-    2400, 2401, 2210, 2211, 3120, 3121, 2220, 2221, 2310, 2311, 2500, 2501, 2410, 2411, 1200,
-    4000, 2320, 2321, 2600, 2601, 2420, 2421, 1300, 1400, 3200, 3201, 4100, -1, 4700, -1, -1,
-    1500, 3300, 3301, -1, -1, 2800, 2801, -1, 3400, 3401, -1, -1, 2510, 2511, 3210, 3211, -1,
-    -1, 3220, 3221, -1, 3310, 3311, -1, -1, 2610, 2611, -1, 3410, 3411, 3320, 3321, -1, -1,
-    3420, 3421, 3500, 3501, 4200, -1, -1, 2810, 2811, -1, -1, -1, -1, 4300, 2620, 2621, 4400,
-    -1, -1, 2520, 2521, -1, -1, -1, -1, -1, -1, -1, -1, -1, 3510, 3511, -1, 4600, -1, -1, 3520,
-    3521, 4500, -1, -1, -1, -1, -1, 2820, 2821, -1,
+    100, 0, 1000, 2000, 2001, 1100, 2100, 2101, 3000, 2010, 2011, 3001, 800, 2110, 2111, 3100,
+    2020, 2021, 400, 700, 3101, 2120, 2121, 3010, 3011, 3020, 3021, 2400, 2401, 600, 200, 2410,
+    2411, 2420, 2421, 3110, 3111, 2200, 2201, 1400, 3120, 3121, 2210, 2211, 3400, 1800, 3401,
+    2220, 2221, 3410, 3411, 500, 1200, 2800, 2801, 3420, 3421, 3200, 3201, 1700, 3210, 3211,
+    3220, 3221, 2500, 2501, 2810, 2811, 300, 4000, 2820, 2821, 1500, 2510, 2511, 2520, 2521,
+    2300, 2301, 1600, 2310, 2311, 2320, 2321, 2600, 2601, 5700, 4100, -1, -1, -1, 2610, 2611,
+    -1, -1, 3500, 3501, 4800, -1, -1, 3510, 3511, -1, 1300, -1, 3520, 3521, -1, 4400, -1, -1,
+    -1, 4200, 2700, 2701, 3300, 3301, -1, 3310, 3311, -1, 3320, 3321, -1, 2620, 2621, -1, -1,
+    -1, -1, -1, -1, -1, 4500, 2710, 2711, 4300, -1, -1, -1, 4600, -1, -1, -1, -1, -1, -1, -1,
+    -1, -1, -1, 2720, 2721, -1, -1, -1, -1, -1, -1,
 )
 
 
@@ -872,21 +890,6 @@
     centred = stream - average
     inverse = lax.rsqrt(jnp.mean(centred * centred, axis=-1, keepdims=True) + EPSILON)
     return centred * inverse * gain_vec + bias_vec
-
-
-def attend_pair(query, keys, values, bias, tile):
-    outs_all, peaks = [], [None, None]
-    for start in range(0, tile[0], tile[1]):
-        rows = query(start, tile[1]) * BF(HEAD_DIM ** (-0.5))
-        outs = []
-        for which in range(2):
-            one = jnp.where(head_lanes(rows.shape, which), rows, jnp.zeros_like(rows))
-            out, top = attend_tile(one, keys, values, bias)
-            outs.append(out)
-            top = jnp.max(top, axis=0, keepdims=True)
-            peaks[which] = top if peaks[which] is None else jnp.maximum(peaks[which], top)
-        outs_all.append((start, jnp.where(head_lanes(outs[0].shape, 0), outs[0], outs[1])))
-    return outs_all, peaks
 
 
 def forward_kernel(zs, *refs):
@@ -910,8 +913,8 @@
     (
         x_all, normed_self, taken, mixed_self, stream_cross, normed_cross,
         query_cross, taken_cross, mixed_cross, stream_feed, normed_feed,
-        part_send, part_got, part_send2, part_got2, vectors,
-    ) = take(16)
+        part_send, part_got, vectors, crest,
+    ) = take(15)
     lanes = Lanes(send_sems, recv_sems, local_sems, zs)
     z, y, x = lanes.z, lanes.y, lanes.x
     t = lax.axis_index("tensor")
@@ -946,17 +949,13 @@
         across(cot_hbm, cot_out.at[2]),
         mate(cot_out.at[2], cot_out.at[3]),
     ]
-    feed_moves = [
-        mate(normed_feed.at[0], normed_feed.at[1]),
-        across(normed_feed.at[0], normed_feed.at[2]),
-        mate(normed_feed.at[2], normed_feed.at[3]),
-    ]
+    feed_moves = [mate(normed_feed.at[0], normed_feed.at[1])]
     mate_self = mate(part_send, part_got)
     mate_normed = mate(normed_cross.at[0], normed_cross.at[1])
-    mate_cross = mate(part_send2, part_got2)
+    mate_cross = mate(part_send, part_got)
     gathers = [Gather(lanes, whole) for whole in wholes]
     quarters = [
-        PairGather(lanes, quarters_in[i], quarter_outs[i], i == 2) for i in range(3)
+        PairGather(lanes, quarters_in[i], quarter_outs[i], i == 1) for i in range(3)
     ]
     loads = [
         local(whole, held)
@@ -980,7 +979,7 @@
     chunk = width // zs
     total = 2 * rows
     step = total // 3 if total % 3 == 0 and (total // 3) % 16 == 0 else total
-    tops, ready = [], set()
+    ready = set()
 
     def vec(i):
         return vectors[i : i + 1, :]
@@ -988,40 +987,63 @@
     def need(*groups):
         assert ready.issuperset(groups)
 
-    def tiles():
-        return [slice(start, start + tile) for start in range(0, rows, tile)]
+    def over(count, size, body):
+        @pl.loop(0, count // size)
+        def _(i):
+            body(pl.ds(pl.multiple_of(i * size, size), size), i)
 
     def attend_all(query_ref, keys_at, values_at, kv_ref, bias_ref, mixed_ref):
+        lane = lax.broadcasted_iota(jnp.int32, (8, wide), 1)
         for j in range(pairs):
-            lanes_at = j * wide
-            bits, peaks = attend_pair(
-                lambda start, count: query_ref[start : start + count, lanes_at : lanes_at + wide],
-                kv_ref[:, keys_at + lanes_at : keys_at + lanes_at + wide],
-                kv_ref[:, values_at + lanes_at : values_at + lanes_at + wide],
-                bias_ref[...],
-                (total, step),
-            )
-            for start, bit in bits:
-                mixed_ref[start : start + step, lanes_at : lanes_at + wide] = bit.astype(BF)
-            tops.append(peaks)
+            at = slice(j * wide, (j + 1) * wide)
+            keys_in = slice(keys_at + j * wide, keys_at + (j + 1) * wide)
+            values_in = slice(values_at + j * wide, values_at + (j + 1) * wide)
+
+            def body(part, _):
+                query = query_ref[part, at] * BF(HEAD_DIM ** (-0.5))
+                outs = []
+                for which in range(2):
+                    mine = head_lanes(query.shape, which)
+                    one = jnp.where(mine, query, jnp.zeros_like(query))
+                    out, top = attend_tile(
+                        one, kv_ref[:, keys_in], kv_ref[:, values_in], bias_ref[...]
+                    )
+                    outs.append(out)
+                    top = jnp.broadcast_to(jnp.max(top, axis=0, keepdims=True), lane.shape)
+                    best = jnp.where(lane == 2 * j + which, top, NEGATIVE)
+                    crest[...] = jnp.maximum(crest[...], best)
+                made = jnp.where(head_lanes(outs[0].shape, 0), outs[0], outs[1])
+                mixed_ref[part, at] = made.astype(BF)
+
+            over(total, step, body)
             yield
-
-    def out_rows(mixed_ref, first, weight, zz):
-        columns_here = weight[zz].reshape(-1, inner)
-        return nt(mixed_ref[first : first + rows, :], columns_here)
 
     def out_project(mixed_ref, weight, move, send, got, base, target):
         for zz in range(zs):
-            send[:, zz * chunk : (zz + 1) * chunk] = out_rows(mixed_ref, rows, weight, zz)
+            cols = slice(zz * chunk, (zz + 1) * chunk)
+
+            def body(part, i):
+                left = mixed_ref[pl.ds(pl.multiple_of(rows + i * tile, tile), tile), :]
+                send[part, cols] = nt(left, weight[zz].reshape(-1, inner)).astype(BF)
+
+            over(rows, tile, body)
         move.start()
         yield
         for zz in range(zs):
-            part = slice(zz * chunk, (zz + 1) * chunk)
-            target[:, part] = out_rows(mixed_ref, 0, weight, zz) + base(part)
+            cols = slice(zz * chunk, (zz + 1) * chunk)
+
+            def body(part, _):
+                made = nt(mixed_ref[part, :], weight[zz].reshape(-1, inner))
+                target[part, cols] = made + base(part, cols)
+
+            over(rows, tile, body)
             yield
         move.arrived()
-        for part in tiles():
-            target[part, :] = target[part, :] + got[part, :]
+
+        def body(part, _):
+            target[part, :] = target[part, :] + got[part, :].astype(F32)
+
+        over(rows, tile, body)
 
     def compute():
         need(0, 1)
@@ -1029,21 +1051,30 @@
         mate_inputs.arrived()
         loads[0].wait()
         vectors[...] = jnp.transpose(w_vec[...].reshape(width, w_vec.shape[-1]))
+        crest[...] = jnp.full(crest.shape, NEGATIVE, F32)
         for side in range(2):
-            for part in tiles():
+
+            def body(part, i):
                 made = normalise(x_all[side, part, :].astype(F32), vec(0), vec(1))
-                at = side * rows + part.start
-                normed_self[at : at + tile, :] = made.astype(BF)
+                at = pl.multiple_of(side * rows + i * tile, tile)
+                normed_self[pl.ds(at, tile), :] = made.astype(BF)
+
+            over(rows, tile, body)
         saves[0].start()
         loads[1].wait()
         yield
         for start in range(0, columns, block):
-            made = nn(normed_self[...], w_in[..., start : start + block].reshape(width, block))
-            for at in range(0, block, wide):
-                piece = made[:, at : at + wide]
-                if start + at < 2 * inner:
-                    piece = turn(piece, cos_ref[...], sa_ref[...], sb_ref[...], 1.0)
-                taken[:, start + at : start + at + wide] = piece.astype(BF)
+
+            def body(part, _):
+                weight = w_in[..., start : start + block].reshape(width, block)
+                made = nn(normed_self[part, :], weight)
+                for at in range(0, block, wide):
+                    piece = made[:, at : at + wide]
+                    if start + at < 2 * inner:
+                        piece = turn(piece, cos_ref[part, :], sa_ref[part, :], sb_ref[part, :], 1.0)
+                    taken[part, start + at : start + at + wide] = piece.astype(BF)
+
+            over(total, step, body)
             yield
         saves[1].start()
         yield from attend_all(taken, inner, 2 * inner, taken, self_bias, mixed_self)
@@ -1052,12 +1083,15 @@
         loads[2].wait()
         yield from out_project(
             mixed_self, w_so, mate_self, part_send, part_got,
-            lambda part: x_all[0, :, part].astype(F32), stream_cross,
+            lambda part, cols: x_all[0, part, cols].astype(F32), stream_cross,
         )
         saves[3].start()
-        for part in tiles():
+
+        def second_norm(part, _):
             made = normalise(stream_cross[part, :], vec(2), vec(3))
             normed_cross[0, part, :] = made.astype(BF)
+
+        over(rows, tile, second_norm)
         mate_normed.start()
         yield
         need(4)
@@ -1076,24 +1110,32 @@
                 mate_normed.arrived()
                 saves[4].start()
             for start in range(0, inner, block):
-                weight = w_cq[..., start : start + block].reshape(width, block)
-                made = nn(normed_cross[side], weight).astype(BF)
-                query_cross[side * rows : (side + 1) * rows, start : start + block] = made
+
+                def body(part, i):
+                    weight = w_cq[..., start : start + block].reshape(width, block)
+                    made = nn(normed_cross[side, part, :], weight).astype(BF)
+                    at = pl.multiple_of(side * rows + i * tile, tile)
+                    query_cross[pl.ds(at, tile), start : start + block] = made
+
+                over(rows, tile, body)
                 yield
         saves[5].start()
         yield from attend_all(query_cross, 0, inner, taken_cross, cross_bias, mixed_cross)
         saves[7].start()
         need(5)
         loads[5].wait()
+        mate_self.sent()
         yield from out_project(
-            mixed_cross, w_co, mate_cross, part_send2, part_got2,
-            lambda part: stream_cross[:, part], stream_feed,
+            mixed_cross, w_co, mate_cross, part_send, part_got,
+            lambda part, cols: stream_cross[part, cols], stream_feed,
         )
         saves[8].start()
-        for part in tiles():
+
+        def third_norm(part, _):
             made = normalise(stream_feed[part, :], vec(4), vec(5))
             normed_feed[0, part, :] = made.astype(BF)
-        feed_moves[1].start()
+
+        over(rows, tile, third_norm)
         feed_moves[0].start()
 
     items = gathers + quarters
@@ -1116,27 +1158,18 @@
     cot_moves[2].start()
     for _ in work:
         pass
-    lane = lax.broadcasted_iota(jnp.int32, peak_out.shape, 1)
-    crest = jnp.full(peak_out.shape, NEGATIVE, F32)
-    for i, peaks in enumerate(tops):
-        for which in range(2):
-            head = (i % pairs) * 2 + which
-            crest = jnp.where(lane == head, jnp.maximum(crest, peaks[which]), crest)
-    peak_out[...] = crest
-    feed_moves[1].arrived()
-    feed_moves[2].start()
+    peak_out[...] = crest[...]
     for i, item in enumerate(items):
         if i not in ready:
             item.landed()
     feed_moves[0].arrived()
-    feed_moves[2].arrived()
     saves[9].start()
     cot_moves[0].arrived()
     cot_moves[2].arrived()
     own_cot.wait()
     for item in gathers + quarters:
         item.sent()
-    for move in [mate_inputs, mate_self, mate_normed, mate_cross] + cot_moves + feed_moves:
+    for move in [mate_inputs, mate_normed, mate_cross] + cot_moves + feed_moves:
         move.sent()
     for save in saves:
         save.wait()
@@ -1165,18 +1198,18 @@
         jax.ShapeDtypeStruct((tokens, 2 * inner), BF),
         jax.ShapeDtypeStruct((seq_len, inner), BF),
         jax.ShapeDtypeStruct((rows, width), F32),
-        jax.ShapeDtypeStruct((4, rows, width), BF),
+        jax.ShapeDtypeStruct((2, rows, width), BF),
     ]
     cot_out = jax.ShapeDtypeStruct((4, rows, width), BF)
     peak = jax.ShapeDtypeStruct((8, 2 * HEAD_DIM), F32)
-    moves = 6 * (3 + 8 * (zs - 1)) + 3 * (2 + 4 * (zs - 1)) + 10
+    moves = 6 * (3 + 8 * (zs - 1)) + 3 * (2 + 4 * (zs - 1)) + 8
     hbm = pl.BlockSpec(memory_space=pltpu.HBM)
     vmem = pl.BlockSpec(memory_space=pltpu.VMEM)
     held = [pltpu.VMEM(shape.shape, shape.dtype) for shape in spread[:6]]
     held += [pltpu.VMEM((2, rows, width), BF)]
     held += [pltpu.VMEM(shape.shape, shape.dtype) for shape in results]
-    held += [pltpu.VMEM((rows, width), F32)] * 4
-    held += [pltpu.VMEM((shards[0].shape[1], width), F32)]
+    held += [pltpu.VMEM((rows, width), BF)] * 2
+    held += [pltpu.VMEM((shards[0].shape[1], width), F32), pltpu.VMEM(peak.shape, F32)]
     flops = 2 * seq_len * inner * (7 * width + 4 * seq_len) // 1
     made = pl.pallas_call(
         functools.partial(forward_kernel, zs),
@@ -1328,7 +1361,7 @@
         ) = made
         gate_full, up_full, down_t = spread[6:]
         normed_cross = normed_cross.reshape(seq_len, width)
-        normed_feed, cot_group = (v.reshape(-1, width) for v in (normed_feed, cot_group))
+        near_feed, cot_group = (v.reshape(-1, width) for v in (normed_feed, cot_group))
     else:
         vectors = jnp.stack(vector_list).astype(F32)
         vectors = jnp.pad(vectors, ((0, 2), (0, 128 - shard_rows)))
@@ -1370,7 +1403,7 @@
         )
         stream_feed = stream_cross + spread_pair(mixed_cross, cross_out_t)
         normed, _, _ = norm_forward(stream_feed, norms[4], norms[5])
-        normed_feed = group_rows(normed.astype(BF))
+        near_feed = pair_rows(normed.astype(BF))
         crest = jnp.pad(
             jnp.maximum(peak_self, peak_cross)[None], ((0, 7), (0, 128 - heads_here))
         )
@@ -1380,45 +1413,74 @@
     )
     unit_cross, inverse_cross = unit_rows_of(stream_cross)
     unit_feed, inverse_feed = unit_rows_of(stream_feed)
-    gate_pre = nn(normed_feed, gate_full)
-    upward = nn(normed_feed, up_full)
-    sigmoid_gate = jax.nn.sigmoid(gate_pre)
-    hidden = (gate_pre * sigmoid_gate * upward).astype(BF)
-    result = (stream_feed + spread_group(Product([(hidden, down_t)], True))).astype(BF)
-
-    down_keep, down_got = reduce_pair(cot_group, hidden, zs)
-    grad_hidden = nn(cot_group, down_t)
-    grad_gate = grad_hidden * upward * sigmoid_gate * (1.0 + gate_pre * (1.0 - sigmoid_gate))
-    grad_upward = grad_hidden * gate_pre * sigmoid_gate
-    grad_gate = grad_gate.astype(BF)
-    grad_upward = grad_upward.astype(BF)
-    grad_normed = spread_group(Product([(grad_gate, gate_full), (grad_upward, up_full)], True))
-    gate_keep, gate_got = reduce_pair(normed_feed, grad_gate, zs)
-    up_keep, up_got = reduce_pair(normed_feed, grad_upward, zs)
+    far_feed = pair_rows(swap(near_feed[:rows], "x"))
+
+    def feed_half(normed, cot_rows):
+        gate_pre = nn(normed, gate_full)
+        upward = nn(normed, up_full)
+        sigmoid_gate = jax.nn.sigmoid(gate_pre)
+        hidden = (gate_pre * sigmoid_gate * upward).astype(BF)
+        grad_hidden = nn(cot_rows, down_t)
+        grad_gate = grad_hidden * upward * sigmoid_gate * (1.0 + gate_pre * (1.0 - sigmoid_gate))
+        grad_upward = grad_hidden * gate_pre * sigmoid_gate
+        return hidden, grad_gate.astype(BF), grad_upward.astype(BF)
+
+    def feed_back(grad_gate, grad_upward):
+        return nt(grad_gate, gate_full) + nt(grad_upward, up_full)
+
+    hidden_near, gate_near, up_near = feed_half(near_feed, cot_group[:seq_len])
+    far_feed, gate_near, up_near, hidden_near = lax.optimization_barrier(
+        (far_feed, gate_near, up_near, hidden_near)
+    )
+    hidden_far, gate_far, up_far = feed_half(far_feed, cot_group[seq_len:])
+    far_sum = feed_back(gate_far[:rows], up_far[:rows]) + swap(
+        feed_back(gate_far[rows:], up_far[rows:]), "tensor"
+    )
+    far_sum = far_sum.astype(BF)
+    got_far = swap(far_sum, "x")
+    normed_feed = jnp.concatenate([near_feed, far_feed], axis=0)
+    hidden = jnp.concatenate([hidden_near, hidden_far], axis=0)
+    grad_gate = jnp.concatenate([gate_near, gate_far], axis=0)
+    grad_upward = jnp.concatenate([up_near, up_far], axis=0)
+    down_pair = PairSum(after(cot_group, far_sum), hidden, zs)
+    gate_pair = PairSum(after(normed_feed, far_sum), grad_gate, zs)
+    grad_normed = feed_back(gate_near[:rows], up_near[:rows]) + swap(
+        feed_back(gate_near[rows:], up_near[rows:]), "tensor"
+    )
+    grad_normed, got_far = after((grad_normed, got_far), gate_pair.got, down_pair.got)
+    grad_normed = grad_normed + got_far.astype(F32)
     stream_part, grad_feed_gain, grad_feed_bias = norm_backward(
         grad_normed, unit_feed, inverse_feed, norms[4]
     )
     grad_stream = cotangent.astype(F32) + stream_part
     grad_full = pair_rows(grad_stream.astype(BF))
-    sum_cross_output = reduce_full(grad_full, mixed_cross, zs).astype(F32)
+    up_pair = PairSum(after(normed_feed, grad_full), grad_upward, zs)
+    down_pair.second(grad_full)
+    cross_output_sum = FullSum(grad_full, mixed_cross, zs)
     grad_mixed = nn(grad_full, cross_out_t).astype(BF)
     grad_query, grad_keys, grad_values = attend_back(
         query_cross, taken_cross, taken_cross, grad_mixed, cross_bias_row[:, None], (0, 0, pairs), None
     )
+    gate_pair.second(grad_query)
     grad_normed = spread_pair(grad_query, cross_in)
-    sum_cross_query = reduce_full(normed_cross, grad_query, zs).astype(F32)
+    cross_query_sum = FullSum(normed_cross, grad_query, zs)
     part_memory = tn(memory, jnp.concatenate([grad_keys, grad_values], axis=1))
     stream_part, grad_cross_gain, grad_cross_bias = norm_backward(
         grad_normed, unit_cross, inverse_cross, norms[2]
     )
     grad_stream = grad_stream + stream_part
     grad_full = pair_rows(grad_stream.astype(BF))
+    up_pair.second(grad_full)
     part_self_output = tn(grad_full, mixed_self)
     grad_mixed = nn(grad_full, self_out_t).astype(BF)
+    cross_output_sum.second(grad_mixed)
+    cross_query_sum.second(grad_mixed)
     grad_parts = attend_back(
         taken, taken, taken, grad_mixed, self_bias_row[:, None], (0, pairs, 2 * pairs), turns
     )
     grad_in = jnp.concatenate(grad_parts, axis=1)
+    sum_cross_output = cross_output_sum.third(grad_in).astype(F32)
+    sum_cross_query = cross_query_sum.third(grad_in).astype(F32)
     part_query, part_key, part_value = (tn(normed_self, part) for part in grad_parts)
     grad_normed = spread_pair(grad_in, in_weight)
     unit_self, inverse_self = unit_rows_of(stream)
@@ -1464,6 +1526,11 @@
     peaks = crest[0, :heads_here]
     factor = jnp.sqrt(threshold[0] / jnp.maximum(peaks, threshold[0]))
     columns = jnp.repeat(factor, HEAD_DIM)[None, :]
+    result = stream_feed + spread_group(Product([(hidden, down_t)], True))
+    result = result.astype(BF)
+    down_keep, down_got = down_pair.third()
+    gate_keep, gate_got = gate_pair.third()
+    up_keep, up_got = up_pair.third()
 
     def side_by_side(kept, got):
         low = jnp.where(x_at == 0, kept, got).astype(F32)

time: 916 us -> 941 us (1.027)
  waiting for transfers between devices: 99.3 us -> 138 us
  matrix products: 193 us -> 173 us
  Pallas kernels: 503 us -> 488 us
    ppermute x21 -> x23, waiting for transfers between devices: 99.2 us -> 138 us  [swap(): return lax.ppermute(value, axis, [(0, 1), (1, 0)])]
    pallas_call x1, Pallas kernels: 325 us -> 308 us  [forward(): pl.pallas_call(functools.partial(forward_kernel, zs), out_shape=spread +...]
    dot_general x16, matrix products: 86.7 us -> 74.7 us  [nt(): lax.dot_general(left, right, (((1,), (1,)), ((), ())), preferred_element_...]
    dot_general x5 -> x8, matrix products: 48 us -> 48.9 us  [nn(): lax.dot_general(left, right, (((1,), (0,)), ((), ())), preferred_element_...]
  transfers between devices with their start and end apart: 26 -> 28, of which waited for: 7 -> 10; matrix products, arithmetic and copies ran while one was open for 22% -> 23% of each run, Pallas kernels for 6% -> 19%
where the time goes in v6:
time: 941 us; the launch traced here: 937 us
  Pallas kernels  488 us (52%)
  matrix products  173 us (18%)
  waiting for transfers between devices  138 us (15%)
  other arithmetic  52.7 us (6%)
  local copies, waits for them, and re-layouts  51.7 us (5%)
  between operations  16.5 us (2%)
  starting transfers between devices  16.3 us (2%)
    pallas_call x1, Pallas kernels, forward(): pl.pallas_call(functools.partial(forward_kernel, zs), out_shape=spread +...  308 us
    ppermute x23, waiting for transfers between devices, swap(): return lax.ppermute(value, axis, [(0, 1), (1, 0)])  138 us
    pallas_call x1, Pallas kernels, scatter_all(): pl.pallas_call(functools.partial(scatter_kernel, zs, orders), out_shape=[...  127 us
    dot_general x16, matrix products, nt(): lax.dot_general(left, right, (((1,), (1,)), ((), ())), preferred_element_...  74.7 us
    pallas_call x2, Pallas kernels, attend_back(): pl.pallas_call(functools.partial(attend_back_kernel, turns is not None),...  52.9 us
    dot_general x10, matrix products, tn(): lax.dot_general(left, right, (((0,), (0,)), ((), ())), preferred_element_...  49.9 us
    dot_general x8, matrix products, nn(): lax.dot_general(left, right, (((1,), (0,)), ((), ())), preferred_element_...  48.9 us
  transfers between devices with their start and end apart: 28, of which 10 were waited for; matrix products, arithmetic and copies ran while one was open for 23% of the time, Pallas kernels for 19%

profile of v6, /device:TPU:0, one launch (start us, length us, event | category | flops | bytes accessed | tf_op | source)
XLA Modules:
  0.0 937.0 jit_solution(7698289675865810886)
XLA Ops:
  18.1 308.3 %shard_map.406 = (f32[4,2,2,96,128]{4,3,2,1,0:T(8,128)}, bf16[4,2,2,96,2304]{4,3,2,1,0:T(8,128)(2,1)}, bf16[4,2,2,96,768]{4,3,2,1,0:T(8,128)(2,1)}, bf16[4,2,2,9...) custom-call(f32[96,128]{1,0:T(8,128)} %pad_convert_fusion.refs_0_, ...), custom_call_target="tpu_custom_call" | custom-call | flops 16307453952 | bytes 100000000 | tf_op jit(solution)/shard_map/pallas_call | solution.py:1214
  328.5 6.5 fusion.74
  340.6 15.7 %collective-permute-done = bf16[384,1536]{1,0:T(8,128)(2,1)S(1)} collective-permute-done((bf16[384,1536]{1,0:T(8,128)(2,1)S(1)}, bf16[384,1536]{1,0:T(8,128)(2,1)S(1)}, u32[]{:S(2)}, u32[]{:S(2)}) %collective-permute-start) | collective-permute-done | bytes 1179680 | tf_op jit(solution)/shard_map/ppermute | solution.py:20
  356.6 7.5 multiply_convert_fusion.3
  364.2 9.0 fusion.76
  374.8 7.9 fusion.75
  382.7 9.2 multiply_convert_fusion
  408.2 5.6 fusion.21
  413.8 8.3 convolution_convert_fusion.2
  427.1 8.3 convolution_convert_fusion.1
  442.6 4.9 fusion.50
  451.3 19.3 %collective-permute-done.7 = bf16[384,1536]{1,0:T(8,128)(2,1)S(1)} collective-permute-done((bf16[384,1536]{1,0:T(8,128)(2,1)S(1)}, bf16[384,1536]{1,0:T(8,128)(2,1)S(1)}, u32[]{:S(2)}, u32[]{:S(2)}) %collective-permute-start.7) | collective-permute-done | bytes 1179680 | tf_op jit(solution)/shard_map/ppermute | solution.py:20
  470.6 9.5 %collective-permute-done.8 = bf16[4,192,1536]{2,1,0:T(8,128)(2,1)} collective-permute-done((bf16[4,192,1536]{2,1,0:T(8,128)(2,1)}, bf16[4,192,1536]{2,1,0:T(8,128)(2,1)}, u32[]{:S(2)}, u32[]{:S(2)}) %collective-permute-start.8) | collective-permute-done | bytes 2359328 | tf_op jit(solution)/shard_map/ppermute | solution.py:20
  480.1 49.9 %collective-permute-done.9 = bf16[4,192,1536]{2,1,0:T(8,128)(2,1)} collective-permute-done((bf16[4,192,1536]{2,1,0:T(8,128)(2,1)}, bf16[4,192,1536]{2,1,0:T(8,128)(2,1)}, u32[]{:S(2)}, u32[]{:S(2)}) %collective-permute-start.9) | collective-permute-done | bytes 2359328 | tf_op jit(solution)/shard_map/ppermute | solution.py:20
  538.3 6.3 fusion.41
  546.8 16.5 %shard_map.407 = (bf16[768,768]{1,0:T(8,128)(2,1)S(1)}, bf16[256,768]{1,0:T(8,128)(2,1)S(1)}, bf16[256,768]{1,0:T(8,128)(2,1)S(1)}) custom-call(bf16[768,768]{1,0:T(8,128)(2,1)S(1)} %copy-done.6, bf16[256,1536]{1,0:T(8,128)(2,1)S(1)} %copy-done.7, bf16[256,1536]{1,0:T(8,128)(2,1)S(1)} %copy-done.7, bf16[768,768]{1,0:T(8,128)(2,1)S(1)} %convolution_convert_fusion.11.g_ref, ...), custom_call_target="tpu_custom_call" | custom-call | flops 3019898880 | bytes 6291456 | tf_op jit(solution)/shard_map/pallas_call | solution.py:809
  573.9 6.0 fusion.52
  583.0 6.3 fusion.23
  604.8 4.8 multiply_reduce_fusion.1
  613.4 8.2 convolution_convert_fusion
  629.5 14.2 %collective-permute-done.15 = bf16[8,96,768]{2,1,0:T(8,128)(2,1)} collective-permute-done((bf16[8,96,768]{2,1,0:T(8,128)(2,1)}, bf16[8,96,768]{2,1,0:T(8,128)(2,1)}, u32[]{:S(2)}, u32[]{:S(2)}) %collective-permute-start.15) | collective-permute-done | bytes 1179680 | tf_op jit(solution)/shard_map/ppermute | solution.py:20
  647.0 36.4 %shard_map.408 = (bf16[768,768]{1,0:T(8,128)(2,1)S(1)}, bf16[768,768]{1,0:T(8,128)(2,1)S(1)}, bf16[768,768]{1,0:T(8,128)(2,1)S(1)}) custom-call(bf16[768,2304]{1,0:T(8,128)(2,1)} %get-tuple-element.94.q_ref.k_ref.v_ref, bf16[768,2304]{1,0:T(8,128)(2,1)} %get-tuple-element.94.q_ref.k_ref.v_ref, bf16[768,2304]{1,0:T(8,128)(2,1)} %get-tuple-element.94.q_ref.k_ref.v_ref, ...), custom_call_target="tpu_custom_call" | custom-call | flops 9059696640 | bytes 9437184 | tf_op jit(solution)/shard_map/pallas_call | solution.py:809
  683.7 7.2 collective-permute-done.16
  696.7 11.7 %collective-permute-done.18 = bf16[4,96,768]{2,1,0:T(8,128)(2,1)S(1)} collective-permute-done((bf16[4,96,768]{2,1,0:T(8,128)(2,1)S(1)}, bf16[4,96,768]{2,1,0:T(8,128)(2,1)S(1)}, u32[]{:S(2)}, u32[]{:S(2)}) %collective-permute-start.18) | collective-permute-done | bytes 589856 | tf_op jit(solution)/shard_map/ppermute | solution.py:20
  709.6 7.5 fusion.22
  723.6 4.4 fusion.10
  728.0 5.4 convolution_convert_fusion.9
  740.3 4.3 fusion.32
  746.8 5.1 convolution_convert_fusion.6
  756.3 5.8 collective-permute-done.22
  766.6 9.7 %fusion.28 = (f32[1536]{0:T(1024)}, f32[384]{0:T(512)}, f32[384]{0:T(512)}, f32[1536]{0:T(1024)}, f32[384,1536]{1,0:T(8,128)}) fusion(bf16[384,1536]{1,0:T(8,128)(2,1)S(1)} %copy-done.11, f32[384]{0:T(512)} %add_rsqrt_fusion, f32[384]{0:T(512)} %copy-done.48, f32[1536]{0:T(1024)} %get-tuple-element.134, f32[384,1536]{1,0:T(8,128)} %collective-permute-done.13, ...), kind=kOutput, calls=%fused_computation.60 | convolution fusion | flops 2724392960 | bytes 14773248 | tf_op jit(solution)/shard_map/dot_general | solution.py:589
  786.4 127.2 %shard_map.409 = (f32[8,128]{1,0:T(8,128)}, f32[96,768]{1,0:T(8,128)}, f32[96,768]{1,0:T(8,128)}, f32[96,768]{1,0:T(8,128)}, f32[96,768]{1,0:T(8,128)}, /*index=5*/f32[48,1536]{1,0:T(8,128)}, f32[8,128]{1,0:T(8,128)}) custom-call(f32[4,2,2,8,128]{4,3,2,1,0:T(8,128)} %bitcast.221, bf16[4,2,2,96,768]{4,3,2,1,0:T(8,128)(2,1)} %bitcast.204, ...), custom_call_target="tpu_custom_call" | custom-call | tf_op jit(solution)/shard_map/pallas_call | solution.py:569
  (385 shorter events, 163.5 us)
Async XLA Ops:
  7.2 737.5 %reduce-scatter.10.cloned.1.call-start = ((), (), s32[]{:S(2)}) async-start(), calls=%async_computation.7 | async-start | bytes 2949120 | tf_op jit(solution)/shard_map/reduce_scatter | solution.py:630
  327.9 28.5 %collective-permute-start = (bf16[384,1536]{1,0:T(8,128)(2,1)S(1)}, bf16[384,1536]{1,0:T(8,128)(2,1)S(1)}, u32[]{:S(2)}, u32[]{:S(2)}) collective-permute-start(bf16[384,1536]{1,0:T(8,128)(2,1)S(1)} %slice_bitcast_fusion), channel_id=1, source_target_pairs={{0,2},{2,0},{1,3},{3,1},{4,6},{6,4},{5,7},{7,5},{8,10},{10,8},{9,1... | collective-permute-start | bytes 3538952 | tf_op jit(solution)/shard_map/ppermute | solution.py:20
  356.4 16.8 %collective-permute-start.1 = (bf16[384,1536]{1,0:T(8,128)(2,1)S(1)}, bf16[384,1536]{1,0:T(8,128)(2,1)}, u32[]{:S(2)}, u32[]{:S(2)}) collective-permute-start(bf16[384,1536]{1,0:T(8,128)(2,1)S(1)} %collective-permute-done), channel_id=1, source_target_pairs={{0,1},{1,0},{2,3},{3,2},{4,5},{5,4},{6,7},{7,6},{8,9},{9,8},{10,11... | collective-permute-start | bytes 3538952 | tf_op jit(solution)/shard_map/ppermute | solution.py:20
  396.0 9.8 %collective-permute-start.6 = (f32[384,1536]{1,0:T(8,128)S(1)}, f32[384,1536]{1,0:T(8,128)S(1)}, u32[]{:S(2)}, u32[]{:S(2)}) collective-permute-start(f32[384,1536]{1,0:T(8,128)S(1)} %convolution_add_fusion.1), channel_id=1, source_target_pairs={{0,1},{1,0},{2,3},{3,2},{4,5},{5,4},{6,7},{7,6},{8,9},{9,8},{10,11... | collective-permute-start | bytes 7077896 | tf_op jit(solution)/shard_map/ppermute | solution.py:20
  401.8 45.7 %collective-permute-start.5 = (f32[384,1536]{1,0:T(8,128)}, f32[384,1536]{1,0:T(8,128)}, u32[]{:S(2)}, u32[]{:S(2)}) collective-permute-start(f32[384,1536]{1,0:T(8,128)} %convolution_add_fusion.3), channel_id=1, source_target_pairs={{0,1},{1,0},{2,3},{3,2},{4,5},{5,4},{6,7},{7,6},{8,9},{9,8},{10,11... | collective-permute-start | bytes 7077896 | tf_op jit(solution)/shard_map/ppermute | solution.py:20
  425.7 54.4 %collective-permute-start.8 = (bf16[4,192,1536]{2,1,0:T(8,128)(2,1)}, bf16[4,192,1536]{2,1,0:T(8,128)(2,1)}, u32[]{:S(2)}, u32[]{:S(2)}) collective-permute-start(bf16[4,192,1536]{2,1,0:T(8,128)(2,1)} %dynamic-slice_bitcast_fusion.2), channel_id=1, source_target_pairs={{0,4},{4,0},{1,5},{5,1},{2,6},{6,2},{3,7},{7,3},{8,12},{12,8},{9,1... | collective-permute-start | bytes 7077896 | tf_op jit(solution)/shard_map/ppermute | solution.py:20
  438.5 91.5 %collective-permute-start.9 = (bf16[4,192,1536]{2,1,0:T(8,128)(2,1)}, bf16[4,192,1536]{2,1,0:T(8,128)(2,1)}, u32[]{:S(2)}, u32[]{:S(2)}) collective-permute-start(bf16[4,192,1536]{2,1,0:T(8,128)(2,1)} %dynamic-slice_bitcast_fusion.1), channel_id=1, source_target_pairs={{0,4},{4,0},{1,5},{5,1},{2,6},{6,2},{3,7},{7,3},{8,12},{12,8},{9,1... | collective-permute-start | bytes 7077896 | tf_op jit(solution)/shard_map/ppermute | solution.py:20
  442.6 28.0 %collective-permute-start.7 = (bf16[384,1536]{1,0:T(8,128)(2,1)S(1)}, bf16[384,1536]{1,0:T(8,128)(2,1)S(1)}, u32[]{:S(2)}, u32[]{:S(2)}) collective-permute-start(bf16[384,1536]{1,0:T(8,128)(2,1)S(1)} %copy-done.60), channel_id=1, source_target_pairs={{0,2},{2,0},{1,3},{3,1},{4,6},{6,4},{5,7},{7,5},{8,10},{10,8},{9,1... | collective-permute-start | bytes 3538952 | tf_op jit(solution)/shard_map/ppermute | solution.py:20
  533.8 11.0 %collective-permute-start.10 = (bf16[384,1536]{1,0:T(8,128)(2,1)S(1)}, bf16[384,1536]{1,0:T(8,128)(2,1)S(1)}, u32[]{:S(2)}, u32[]{:S(2)}) collective-permute-start(bf16[384,1536]{1,0:T(8,128)(2,1)S(1)} %get-tuple-element.141), channel_id=1, source_target_pairs={{0,1},{1,0},{2,3},{3,2},{4,5},{5,4},{6,7},{7,6},{8,9},{9,8},{10,11... | collective-permute-start | bytes 3538952 | tf_op jit(solution)/shard_map/ppermute | solution.py:20
  544.7 38.4 %collective-permute-start.3 = (f32[384,1536]{1,0:T(8,128)}, f32[384,1536]{1,0:T(8,128)}, u32[]{:S(2)}, u32[]{:S(2)}) collective-permute-start(f32[384,1536]{1,0:T(8,128)} %fusion.41), channel_id=1, source_target_pairs={{0,1},{1,0},{2,3},{3,2},{4,5},{5,4},{6,7},{7,6},{8,9},{9,8},{10,11... | collective-permute-start | bytes 7077896 | tf_op jit(solution)/shard_map/ppermute | solution.py:20
  568.6 183.3 %reduce-scatter.14.cloned.1.call-start = ((), (), s32[]{:S(2)}) async-start(), calls=%async_computation.9 | async-start | bytes 2949120 | tf_op jit(solution)/shard_map/reduce_scatter | solution.py:630
  579.9 129.7 %collective-permute-start.2 = (f32[384,1536]{1,0:T(8,128)}, f32[384,1536]{1,0:T(8,128)}, u32[]{:S(2)}, u32[]{:S(2)}) collective-permute-start(f32[384,1536]{1,0:T(8,128)} %fusion.52), channel_id=1, source_target_pairs={{0,1},{1,0},{2,3},{3,2},{4,5},{5,4},{6,7},{7,6},{8,9},{9,8},{10,11... | collective-permute-start | bytes 7077896 | tf_op jit(solution)/shard_map/ppermute | solution.py:20
  582.9 21.9 %collective-permute-start.11 = (f32[384,1536]{1,0:T(8,128)}, f32[384,1536]{1,0:T(8,128)}, u32[]{:S(2)}, u32[]{:S(2)}) collective-permute-start(f32[384,1536]{1,0:T(8,128)} %fusion.58), channel_id=1, source_target_pairs={{0,1},{1,0},{2,3},{3,2},{4,5},{5,4},{6,7},{7,6},{8,9},{9,8},{10,11... | collective-permute-start | bytes 7077896 | tf_op jit(solution)/shard_map/ppermute | solution.py:20
  589.3 120.3 %collective-permute-start.4 = (bf16[384,1536]{1,0:T(8,128)(2,1)}, bf16[384,1536]{1,0:T(8,128)(2,1)}, u32[]{:S(2)}, u32[]{:S(2)}) collective-permute-start(bf16[384,1536]{1,0:T(8,128)(2,1)} %fusion.23), channel_id=1, source_target_pairs={{0,2},{2,0},{1,3},{3,1},{4,6},{6,4},{5,7},{7,5},{8,10},{10,8},{9,1... | collective-permute-start | bytes 3538952 | tf_op jit(solution)/shard_map/ppermute | solution.py:20
  593.4 50.3 %collective-permute-start.15 = (bf16[8,96,768]{2,1,0:T(8,128)(2,1)}, bf16[8,96,768]{2,1,0:T(8,128)(2,1)}, u32[]{:S(2)}, u32[]{:S(2)}) collective-permute-start(bf16[8,96,768]{2,1,0:T(8,128)(2,1)} %dynamic-slice_bitcast_fusion.4), channel_id=1, source_target_pairs={{0,2},{2,0},{1,3},{3,1},{4,6},{6,4},{5,7},{7,5},{8,10},{10,8},{9,1... | collective-permute-start | bytes 3538952 | tf_op jit(solution)/shard_map/ppermute | solution.py:20
  599.9 83.6 %collective-permute-start.17 = (bf16[8,96,768]{2,1,0:T(8,128)(2,1)}, bf16[8,96,768]{2,1,0:T(8,128)(2,1)}, u32[]{:S(2)}, u32[]{:S(2)}) collective-permute-start(bf16[8,96,768]{2,1,0:T(8,128)(2,1)} %dynamic-slice_bitcast_fusion.3), channel_id=1, source_target_pairs={{0,2},{2,0},{1,3},{3,1},{4,6},{6,4},{5,7},{7,5},{8,10},{10,8},{9,1... | collective-permute-start | bytes 3538952 | tf_op jit(solution)/shard_map/ppermute | solution.py:20
  604.7 158.6 %reduce-scatter.6.cloned.1.call-start = ((), (), s32[]{:S(2)}) async-start(), calls=%async_computation.5 | async-start | bytes 737280 | tf_op jit(solution)/shard_map/reduce_scatter | solution.py:617
  611.9 13.0 %collective-permute-start.12 = (bf16[384,1536]{1,0:T(8,128)(2,1)S(1)}, bf16[384,1536]{1,0:T(8,128)(2,1)S(1)}, u32[]{:S(2)}, u32[]{:S(2)}) collective-permute-start(bf16[384,1536]{1,0:T(8,128)(2,1)S(1)} %get-tuple-element.139), channel_id=1, source_target_pairs={{0,1},{1,0},{2,3},{3,2},{4,5},{5,4},{6,7},{7,6},{8,9},{9,8},{10,11... | collective-permute-start | bytes 3538952 | tf_op jit(solution)/shard_map/ppermute | solution.py:20
  624.9 98.7 %collective-permute-start.20 = (bf16[4,192,1536]{2,1,0:T(8,128)(2,1)}, bf16[4,192,1536]{2,1,0:T(8,128)(2,1)}, u32[]{:S(2)}, u32[]{:S(2)}) collective-permute-start(bf16[4,192,1536]{2,1,0:T(8,128)(2,1)} %dynamic-slice_bitcast_fusion), channel_id=1, source_target_pairs={{0,4},{4,0},{1,5},{5,1},{2,6},{6,2},{3,7},{7,3},{8,12},{12,8},{9,1... | collective-permute-start | bytes 7077896 | tf_op jit(solution)/shard_map/ppermute | solution.py:20
  645.4 45.5 %collective-permute-start.16 = (bf16[4,96,768]{2,1,0:T(8,128)(2,1)S(1)}, bf16[4,96,768]{2,1,0:T(8,128)(2,1)S(1)}, u32[]{:S(2)}, u32[]{:S(2)}) collective-permute-start(bf16[4,96,768]{2,1,0:T(8,128)(2,1)S(1)} %dynamic-slice_bitcast_fusion.6), channel_id=1, source_target_pairs={{0,4},{4,0},{1,5},{5,1},{2,6},{6,2},{3,7},{7,3},{8,12},{12,8},{9,1... | collective-permute-start | bytes 1769480 | tf_op jit(solution)/shard_map/ppermute | solution.py:20
  691.8 73.1 %reduce-scatter.8.cloned.1.call-start = ((), (), s32[]{:S(2)}) async-start(), calls=%async_computation.6 | async-start | bytes 737280 | tf_op jit(solution)/shard_map/reduce_scatter | solution.py:617
  694.0 14.4 %collective-permute-start.18 = (bf16[4,96,768]{2,1,0:T(8,128)(2,1)S(1)}, bf16[4,96,768]{2,1,0:T(8,128)(2,1)S(1)}, u32[]{:S(2)}, u32[]{:S(2)}) collective-permute-start(bf16[4,96,768]{2,1,0:T(8,128)(2,1)S(1)} %dynamic-slice_bitcast_fusion.5), channel_id=1, source_target_pairs={{0,4},{4,0},{1,5},{5,1},{2,6},{6,2},{3,7},{7,3},{8,12},{12,8},{9,1... | collective-permute-start | bytes 1769480 | tf_op jit(solution)/shard_map/ppermute | solution.py:20
  709.4 208.0 %reduce-scatter.12.cloned.1.call-start = ((), (), s32[]{:S(2)}) async-start(), calls=%async_computation.8 | async-start | bytes 2949120 | tf_op jit(solution)/shard_map/reduce_scatter | solution.py:630
  744.7 21.9 %collective-permute-start.13 = (f32[384,1536]{1,0:T(8,128)}, f32[384,1536]{1,0:T(8,128)}, u32[]{:S(2)}, u32[]{:S(2)}) collective-permute-start(f32[384,1536]{1,0:T(8,128)} %fusion.32), channel_id=1, source_target_pairs={{0,1},{1,0},{2,3},{3,2},{4,5},{5,4},{6,7},{7,6},{8,9},{9,8},{10,11... | collective-permute-start | bytes 7077896 | tf_op jit(solution)/shard_map/ppermute | solution.py:20
  745.6 9.5 %collective-permute-start.19 = (bf16[96,1536]{1,0:T(8,128)(2,1)S(1)}, bf16[96,1536]{1,0:T(8,128)(2,1)S(1)}, u32[]{:S(2)}, u32[]{:S(2)}) collective-permute-start(bf16[96,1536]{1,0:T(8,128)(2,1)S(1)} %dynamic-slice_bitcast_fusion.9), channel_id=1, source_target_pairs={{0,2},{2,0},{1,3},{3,1},{4,6},{6,4},{5,7},{7,5},{8,10},{10,8},{9,1... | collective-permute-start | bytes 884744 | tf_op jit(solution)/shard_map/ppermute | solution.py:20
  752.9 9.2 collective-permute-start.22
  780.5 5.3 collective-permute-start.14
  786.4 128.6 %copy-start.41 = (bf16[48,768]{1,0:T(8,128)(2,1)S(1)}, bf16[48,768]{1,0:T(8,128)(2,1)}, u32[]{:S(2)}) copy-start(bf16[48,768]{1,0:T(8,128)(2,1)} %refs_6_.1) | copy-start | bytes 221188
  786.4 134.6 %copy-start.38 = (bf16[96,768]{1,0:T(8,128)(2,1)S(1)}, bf16[96,768]{1,0:T(8,128)(2,1)}, u32[]{:S(2)}) copy-start(bf16[96,768]{1,0:T(8,128)(2,1)} %refs_1_.1) | copy-start | bytes 442372
  786.4 134.6 %copy-start.39 = (bf16[96,768]{1,0:T(8,128)(2,1)S(1)}, bf16[96,768]{1,0:T(8,128)(2,1)}, u32[]{:S(2)}) copy-start(bf16[96,768]{1,0:T(8,128)(2,1)} %refs_2_.1) | copy-start | bytes 442372
  786.4 134.6 %copy-start.40 = (bf16[96,768]{1,0:T(8,128)(2,1)S(1)}, bf16[96,768]{1,0:T(8,128)(2,1)}, u32[]{:S(2)}) copy-start(bf16[96,768]{1,0:T(8,128)(2,1)} %refs_5_.1) | copy-start | bytes 442372
  918.4 6.8 collective-permute-start.21
  (99 other events, 692.0 us)
Sparse Core Ops, SparseCore 0:
  568.7 47.4 reduce-scatter.9
  618.5 47.5 reduce-scatter.13
  692.0 21.8 reduce-scatter.5
  716.0 20.2 reduce-scatter.7
  738.5 46.4 reduce-scatter.11

commit v7 on v6

--- a/solution.py
+++ b/solution.py
@@ -872,16 +872,16 @@
 
 
 PLAN = (
-    100, 0, 1000, 2000, 2001, 1100, 2100, 2101, 3000, 2010, 2011, 3001, 800, 2110, 2111, 3100,
-    2020, 2021, 400, 700, 3101, 2120, 2121, 3010, 3011, 3020, 3021, 2400, 2401, 600, 200, 2410,
-    2411, 2420, 2421, 3110, 3111, 2200, 2201, 1400, 3120, 3121, 2210, 2211, 3400, 1800, 3401,
-    2220, 2221, 3410, 3411, 500, 1200, 2800, 2801, 3420, 3421, 3200, 3201, 1700, 3210, 3211,
-    3220, 3221, 2500, 2501, 2810, 2811, 300, 4000, 2820, 2821, 1500, 2510, 2511, 2520, 2521,
-    2300, 2301, 1600, 2310, 2311, 2320, 2321, 2600, 2601, 5700, 4100, -1, -1, -1, 2610, 2611,
-    -1, -1, 3500, 3501, 4800, -1, -1, 3510, 3511, -1, 1300, -1, 3520, 3521, -1, 4400, -1, -1,
-    -1, 4200, 2700, 2701, 3300, 3301, -1, 3310, 3311, -1, 3320, 3321, -1, 2620, 2621, -1, -1,
-    -1, -1, -1, -1, -1, 4500, 2710, 2711, 4300, -1, -1, -1, 4600, -1, -1, -1, -1, -1, -1, -1,
-    -1, -1, -1, 2720, 2721, -1, -1, -1, -1, -1, -1,
+    0, 100, 200, 800, 300, 700, 400, 2000, 2100, 2101, 2010, 1700, 1100, 2001, 2110, 2111, 600,
+    3010, 1400, 1800, 2210, 500, 2120, 3100, 3101, 2121, 2200, 2201, 2211, 2011, 2701, 2410,
+    3001, 3121, 2020, 2400, 2700, 2711, 2720, 2710, 2220, 3110, 1600, 3120, 5800, 3111, 2021,
+    3000, 3021, 3020, 1000, 2221, 2401, 4100, 3011, 1500, 2301, 2721, 2411, 2500, 3410, 4000,
+    -1, 2300, 2501, -1, -1, 1200, 3221, -1, 2600, 3220, -1, -1, 2311, 3401, 2321, -1, -1, 3210,
+    3201, 1300, 3211, -1, 2801, -1, 2511, 3200, -1, 2421, 2510, 2420, -1, 3500, -1, 3301, 2310,
+    3321, 3421, 2520, -1, 2610, 2601, -1, 3300, -1, 3411, 3400, 2800, 4200, 3511, -1, -1, 3310,
+    3420, 2521, -1, 2320, 3311, -1, 3510, -1, 2620, -1, 3320, 4400, 2611, -1, 4300, -1, 3520,
+    -1, 3521, -1, -1, 3501, 2811, -1, -1, 2810, -1, -1, -1, -1, -1, -1, 2621, 4500, -1, -1,
+    4700, -1, -1, -1, -1, -1, 2821, 2820, 4600,
 )
 
 
@@ -955,7 +955,7 @@
     mate_cross = mate(part_send, part_got)
     gathers = [Gather(lanes, whole) for whole in wholes]
     quarters = [
-        PairGather(lanes, quarters_in[i], quarter_outs[i], i == 1) for i in range(3)
+        PairGather(lanes, quarters_in[i], quarter_outs[i], i == 2) for i in range(3)
     ]
     loads = [
         local(whole, held)
@@ -1413,7 +1413,7 @@
     )
     unit_cross, inverse_cross = unit_rows_of(stream_cross)
     unit_feed, inverse_feed = unit_rows_of(stream_feed)
-    far_feed = pair_rows(swap(near_feed[:rows], "x"))
+    far_own = swap(near_feed[:rows], "x")
 
     def feed_half(normed, cot_rows):
         gate_pre = nn(normed, gate_full)
@@ -1429,9 +1429,10 @@
         return nt(grad_gate, gate_full) + nt(grad_upward, up_full)
 
     hidden_near, gate_near, up_near = feed_half(near_feed, cot_group[:seq_len])
-    far_feed, gate_near, up_near, hidden_near = lax.optimization_barrier(
-        (far_feed, gate_near, up_near, hidden_near)
-    )
+    far_own, hidden_near, gate_near, up_near = lax.optimization_barrier(
+        (far_own, hidden_near, gate_near, up_near)
+    )
+    far_feed = pair_rows(far_own)
     hidden_far, gate_far, up_far = feed_half(far_feed, cot_group[seq_len:])
     far_sum = feed_back(gate_far[:rows], up_far[:rows]) + swap(
         feed_back(gate_far[rows:], up_far[rows:]), "tensor"
@@ -1447,7 +1448,7 @@
     grad_normed = feed_back(gate_near[:rows], up_near[:rows]) + swap(
         feed_back(gate_near[rows:], up_near[rows:]), "tensor"
     )
-    grad_normed, got_far = after((grad_normed, got_far), gate_pair.got, down_pair.got)
+    got_far = after(got_far, grad_normed, gate_pair.held, down_pair.held)
     grad_normed = grad_normed + got_far.astype(F32)
     stream_part, grad_feed_gain, grad_feed_bias = norm_backward(
         grad_normed, unit_feed, inverse_feed, norms[4]
@@ -1473,15 +1474,17 @@
     up_pair.second(grad_full)
     part_self_output = tn(grad_full, mixed_self)
     grad_mixed = nn(grad_full, self_out_t).astype(BF)
-    cross_output_sum.second(grad_mixed)
-    cross_query_sum.second(grad_mixed)
     grad_parts = attend_back(
         taken, taken, taken, grad_mixed, self_bias_row[:, None], (0, pairs, 2 * pairs), turns
     )
     grad_in = jnp.concatenate(grad_parts, axis=1)
-    sum_cross_output = cross_output_sum.third(grad_in).astype(F32)
-    sum_cross_query = cross_query_sum.third(grad_in).astype(F32)
-    part_query, part_key, part_value = (tn(normed_self, part) for part in grad_parts)
+    cross_output_sum.second(grad_in)
+    cross_query_sum.second(grad_in)
+    part_query, part_key, part_value = (
+        tn(normed_self, part).astype(BF) for part in grad_parts
+    )
+    sum_cross_output = cross_output_sum.third(part_query, part_key).astype(F32)
+    sum_cross_query = cross_query_sum.third(part_query, part_key).astype(F32)
     grad_normed = spread_pair(grad_in, in_weight)
     unit_self, inverse_self = unit_rows_of(stream)
     stream_part, grad_self_gain, grad_self_bias = norm_backward(

time: 941 us -> 873 us (0.928)
  waiting for transfers between devices: 138 us -> 71.4 us
    ppermute x23, waiting for transfers between devices: 138 us -> 71.3 us  [swap(): return lax.ppermute(value, axis, [(0, 1), (1, 0)])]
  transfers between devices with their start and end apart: 28 -> 28, of which waited for: 10 -> 8; matrix products, arithmetic and copies ran while one was open for 23% -> 28% of each run, Pallas kernels for 19% -> 21%
where the time goes in v7:
time: 873 us; the launch traced here: 868 us
  Pallas kernels  487 us (56%)
  matrix products  181 us (21%)
  waiting for transfers between devices  71.4 us (8%)
  other arithmetic  50.9 us (6%)
  local copies, waits for them, and re-layouts  44.8 us (5%)
  starting transfers between devices  16.9 us (2%)
  between operations  16.6 us (2%)
    pallas_call x1, Pallas kernels, forward(): pl.pallas_call(functools.partial(forward_kernel, zs), out_shape=spread +...  307 us
    pallas_call x1, Pallas kernels, scatter_all(): pl.pallas_call(functools.partial(scatter_kernel, zs, orders), out_shape=[...  127 us
    dot_general x16, matrix products, nt(): lax.dot_general(left, right, (((1,), (1,)), ((), ())), preferred_element_...  77.1 us
    ppermute x23, waiting for transfers between devices, swap(): return lax.ppermute(value, axis, [(0, 1), (1, 0)])  71.3 us
    dot_general x8, matrix products, nn(): lax.dot_general(left, right, (((1,), (0,)), ((), ())), preferred_element_...  53.6 us
    pallas_call x2, Pallas kernels, attend_back(): pl.pallas_call(functools.partial(attend_back_kernel, turns is not None),...  53.1 us
    dot_general x10, matrix products, tn(): lax.dot_general(left, right, (((0,), (0,)), ((), ())), preferred_element_...  50.5 us
  transfers between devices with their start and end apart: 28, of which 8 were waited for; matrix products, arithmetic and copies ran while one was open for 28% of the time, Pallas kernels for 21%

profile of v7, /device:TPU:0, one launch (start us, length us, event | category | flops | bytes accessed | tf_op | source)
XLA Modules:
  0.0 868.2 jit_solution(8619103056877185358)
XLA Ops:
  16.9 306.9 %shard_map.406 = (f32[4,2,2,96,128]{4,3,2,1,0:T(8,128)}, bf16[4,2,2,96,2304]{4,3,2,1,0:T(8,128)(2,1)}, bf16[4,2,2,96,768]{4,3,2,1,0:T(8,128)(2,1)}, bf16[4,2,2,9...) custom-call(f32[96,128]{1,0:T(8,128)} %pad_convert_fusion.refs_0_, ...), custom_call_target="tpu_custom_call" | custom-call | flops 16307453952 | bytes 100000000 | tf_op jit(solution)/shard_map/pallas_call | solution.py:1214
  326.9 7.9 fusion.74
  334.8 5.6 fusion.73
  349.9 11.2 %multiply_convert_fusion.3 = (bf16[768,1536]{1,0:T(8,128)(2,1)}, bf16[768,1536]{1,0:T(8,128)(2,1)}, bf16[768,1536]{1,0:T(8,128)(2,1)}) fusion(f32[768,1536]{1,0:T(8,128)} %fusion.73, f32[768,1536]{1,0:T(8,128)} %fusion.74, bf16[768,1536]{1,0:T(8,128)(2,1)S(1)} %bitcast.207, bf16[1536,1536]{1,0:T(8,128)(2,1)} %bitcast.234), kind=kOutput, calls=%fused_computation.23 | convolution fusion | flops 3642753024 | bytes 23592960 | tf_op jit(solution)/shard_map/dot_general | solution.py:585
  362.2 9.2 %fusion.76 = f32[768,1536]{1,0:T(8,128)} fusion(bf16[768,1536]{1,0:T(8,128)(2,1)} %bitcast.206, bf16[1536,1536]{1,0:T(8,128)(2,1)} %bitcast.235), kind=kOutput, calls=%fused_computation.196 | convolution fusion | flops 3623878656 | bytes 11796480 | tf_op jit(solution)/shard_map/dot_general | solution.py:585
  371.8 4.5 fusion.46
  380.1 5.5 fusion.75
  385.6 9.3 %multiply_convert_fusion = (bf16[768,1536]{1,0:T(8,128)(2,1)S(1)}, bf16[768,1536]{1,0:T(8,128)(2,1)S(1)}, bf16[768,1536]{1,0:T(8,128)(2,1)}) fusion(f32[768,1536]{1,0:T(8,128)} %fusion.76, f32[768,1536]{1,0:T(8,128)} %fusion.75, bf16[768,1536]{1,0:T(8,128)(2,1)S(1)} %constant_dynamic-update-slice_fusion, bf16[1536,1536]{1,0:T(8,128)(2,1)S(1)} %bitcast.259), kind=kOutput, calls=%fused_computation.19 | convolution fusion | flops 3642753024 | bytes 23592960 | tf_op jit(solution)/shard_map/dot_general | solution.py:585
  406.3 6.1 pad_maximum_fusion
  412.4 6.9 fusion.14
  424.9 8.3 convolution_convert_fusion.1
  435.5 9.2 %convolution_convert_fusion.2 = bf16[1536,1536]{1,0:T(8,128)(2,1)} fusion(bf16[1536,1536]{1,0:T(8,128)(2,1)S(1)} %pad_maximum_fusion, bf16[768,1536]{1,0:T(8,128)(2,1)S(1)} %copy-done.73, bf16[768,1536]{1,0:T(8,128)(2,1)S(1)} %copy-done.65), kind=kOutput, calls=%fused_computation.2 | convolution fusion | flops 7259553792 | bytes 14155776 | tf_op jit(solution)/shard_map/dot_general | solution.py:593
  444.8 6.6 collective-permute-done.7
  460.0 26.4 %collective-permute-done.21 = bf16[4,192,1536]{2,1,0:T(8,128)(2,1)S(1)} collective-permute-done((bf16[4,192,1536]{2,1,0:T(8,128)(2,1)S(1)}, bf16[4,192,1536]{2,1,0:T(8,128)(2,1)S(1)}, u32[]{:S(2)}, u32[]{:S(2)}) %collective-permute-start.21) | collective-permute-done | bytes 2359328 | tf_op jit(solution)/shard_map/ppermute | solution.py:20
  488.8 6.1 fusion.52
  500.6 16.4 %shard_map.407 = (bf16[768,768]{1,0:T(8,128)(2,1)S(1)}, bf16[256,768]{1,0:T(8,128)(2,1)S(1)}, bf16[256,768]{1,0:T(8,128)(2,1)S(1)}) custom-call(bf16[768,768]{1,0:T(8,128)(2,1)S(1)} %copy-done.3, bf16[256,1536]{1,0:T(8,128)(2,1)S(1)} %copy-done.4, bf16[256,1536]{1,0:T(8,128)(2,1)S(1)} %copy-done.4, bf16[768,768]{1,0:T(8,128)(2,1)S(1)} %convolution_convert_fusion.11.g_ref, ...), custom_call_target="tpu_custom_call" | custom-call | flops 3019898880 | bytes 6291456 | tf_op jit(solution)/shard_map/pallas_call | solution.py:809
  516.9 4.3 fusion.58
  521.4 4.8 fusion.23
  526.8 9.2 %convolution_convert_fusion = bf16[1536,1536]{1,0:T(8,128)(2,1)S(1)} fusion(bf16[1536,1536]{1,0:T(8,128)(2,1)S(1)} %bitcast.193, bf16[768,1536]{1,0:T(8,128)(2,1)S(1)} %copy-done.62, bf16[768,1536]{1,0:T(8,128)(2,1)} %get-tuple-element.81), kind=kOutput, calls=%fused_computation | convolution fusion | flops 7259553792 | bytes 14155776 | tf_op jit(solution)/shard_map/dot_general | solution.py:593
  540.6 10.5 %collective-permute-done.17 = bf16[4,192,1536]{2,1,0:T(8,128)(2,1)S(1)} collective-permute-done((bf16[4,192,1536]{2,1,0:T(8,128)(2,1)S(1)}, bf16[4,192,1536]{2,1,0:T(8,128)(2,1)S(1)}, u32[]{:S(2)}, u32[]{:S(2)}) %collective-permute-start.17) | collective-permute-done | bytes 2359328 | tf_op jit(solution)/shard_map/ppermute | solution.py:20
  553.4 5.4 multiply_reduce_fusion.1
  573.0 36.8 %shard_map.408 = (bf16[768,768]{1,0:T(8,128)(2,1)S(1)}, bf16[768,768]{1,0:T(8,128)(2,1)S(1)}, bf16[768,768]{1,0:T(8,128)(2,1)S(1)}) custom-call(bf16[768,2304]{1,0:T(8,128)(2,1)} %get-tuple-element.92.q_ref.k_ref.v_ref, bf16[768,2304]{1,0:T(8,128)(2,1)} %get-tuple-element.92.q_ref.k_ref.v_ref, bf16[768,2304]{1,0:T(8,128)(2,1)} %get-tuple-element.92.q_ref.k_ref.v_ref, ...), custom_call_target="tpu_custom_call" | custom-call | flops 9059696640 | bytes 9437184 | tf_op jit(solution)/shard_map/pallas_call | solution.py:809
  620.7 7.2 collective-permute-done.16
  633.5 12.3 %collective-permute-done.14 = bf16[4,96,768]{2,1,0:T(8,128)(2,1)S(1)} collective-permute-done((bf16[4,96,768]{2,1,0:T(8,128)(2,1)S(1)}, bf16[4,96,768]{2,1,0:T(8,128)(2,1)S(1)}, u32[]{:S(2)}, u32[]{:S(2)}) %collective-permute-start.14) | collective-permute-done | bytes 589856 | tf_op jit(solution)/shard_map/ppermute | solution.py:20
  647.1 7.5 fusion.22
  659.0 4.4 fusion.10
  663.4 5.3 convolution_convert_fusion.7
  668.7 7.5 fusion.32
  678.3 5.2 convolution_convert_fusion.6
  689.7 4.1 collective-permute-done.18
  698.3 9.7 %fusion.28 = (f32[1536]{0:T(1024)}, f32[384]{0:T(512)}, f32[384]{0:T(512)}, f32[1536]{0:T(1024)}, f32[384,1536]{1,0:T(8,128)}) fusion(bf16[384,1536]{1,0:T(8,128)(2,1)S(1)} %copy-done.8, f32[384]{0:T(512)} %add_rsqrt_fusion, f32[384]{0:T(512)} %copy-done.40, f32[1536]{0:T(1024)} %get-tuple-element.132, f32[384,1536]{1,0:T(8,128)} %collective-permute-done.11, ...), kind=kOutput, calls=%fused_computation.60 | convolution fusion | flops 2724392960 | bytes 14773248 | tf_op jit(solution)/shard_map/dot_general | solution.py:589
  718.3 126.6 %shard_map.409 = (f32[8,128]{1,0:T(8,128)}, f32[96,768]{1,0:T(8,128)}, f32[96,768]{1,0:T(8,128)}, f32[96,768]{1,0:T(8,128)}, f32[96,768]{1,0:T(8,128)}, /*index=5*/f32[48,1536]{1,0:T(8,128)}, f32[8,128]{1,0:T(8,128)}) custom-call(f32[4,2,2,8,128]{4,3,2,1,0:T(8,128)} %bitcast.219, bf16[4,2,2,96,768]{4,3,2,1,0:T(8,128)(2,1)} %bitcast.203, ...), custom_call_target="tpu_custom_call" | custom-call | tf_op jit(solution)/shard_map/pallas_call | solution.py:569
  (366 shorter events, 144.9 us)
Async XLA Ops:
  7.2 669.0 %reduce-scatter.14.cloned.1.call-start = ((), (), s32[]{:S(2)}) async-start(), calls=%async_computation.9 | async-start | bytes 2949120 | tf_op jit(solution)/shard_map/reduce_scatter | solution.py:630
  326.4 45.0 %collective-permute-start = (bf16[384,1536]{1,0:T(8,128)(2,1)}, bf16[384,1536]{1,0:T(8,128)(2,1)}, u32[]{:S(2)}, u32[]{:S(2)}) collective-permute-start(bf16[384,1536]{1,0:T(8,128)(2,1)} %slice_bitcast_fusion), channel_id=1, source_target_pairs={{0,2},{2,0},{1,3},{3,1},{4,6},{6,4},{5,7},{7,5},{8,10},{10,8},{9,1... | collective-permute-start | bytes 3538952 | tf_op jit(solution)/shard_map/ppermute | solution.py:20
  371.4 8.6 collective-permute-start.2
  378.4 34.0 %collective-permute-start.5 = (f32[384,1536]{1,0:T(8,128)S(1)}, f32[384,1536]{1,0:T(8,128)S(1)}, u32[]{:S(2)}, u32[]{:S(2)}) collective-permute-start(f32[384,1536]{1,0:T(8,128)S(1)} %convolution_add_fusion.3), channel_id=1, source_target_pairs={{0,1},{1,0},{2,3},{3,2},{4,5},{5,4},{6,7},{7,6},{8,9},{9,8},{10,11... | collective-permute-start | bytes 7077896 | tf_op jit(solution)/shard_map/ppermute | solution.py:20
  399.0 20.3 %collective-permute-start.6 = (f32[384,1536]{1,0:T(8,128)S(1)}, f32[384,1536]{1,0:T(8,128)S(1)}, u32[]{:S(2)}, u32[]{:S(2)}) collective-permute-start(f32[384,1536]{1,0:T(8,128)S(1)} %convolution_add_fusion.1), channel_id=1, source_target_pairs={{0,1},{1,0},{2,3},{3,2},{4,5},{5,4},{6,7},{7,6},{8,9},{9,8},{10,11... | collective-permute-start | bytes 7077896 | tf_op jit(solution)/shard_map/ppermute | solution.py:20
  423.3 28.1 %collective-permute-start.7 = (bf16[384,1536]{1,0:T(8,128)(2,1)S(1)}, bf16[384,1536]{1,0:T(8,128)(2,1)S(1)}, u32[]{:S(2)}, u32[]{:S(2)}) collective-permute-start(bf16[384,1536]{1,0:T(8,128)(2,1)S(1)} %fusion.21), channel_id=1, source_target_pairs={{0,2},{2,0},{1,3},{3,1},{4,6},{6,4},{5,7},{7,5},{8,10},{10,8},{9,1... | collective-permute-start | bytes 3538952 | tf_op jit(solution)/shard_map/ppermute | solution.py:20
  433.3 53.1 %collective-permute-start.21 = (bf16[4,192,1536]{2,1,0:T(8,128)(2,1)S(1)}, bf16[4,192,1536]{2,1,0:T(8,128)(2,1)S(1)}, u32[]{:S(2)}, u32[]{:S(2)}) collective-permute-start(bf16[4,192,1536]{2,1,0:T(8,128)(2,1)S(1)} %dynamic-slice_bitcast_fusion), channel_id=1, source_target_pairs={{0,4},{4,0},{1,5},{5,1},{2,6},{6,2},{3,7},{7,3},{8,12},{12,8},{9,1... | collective-permute-start | bytes 7077896 | tf_op jit(solution)/shard_map/ppermute | solution.py:20
  455.2 4.8 collective-permute-start.8
  459.7 61.7 %collective-permute-start.3 = (f32[384,1536]{1,0:T(8,128)}, f32[384,1536]{1,0:T(8,128)}, u32[]{:S(2)}, u32[]{:S(2)}) collective-permute-start(f32[384,1536]{1,0:T(8,128)} %fusion.41), channel_id=1, source_target_pairs={{0,1},{1,0},{2,3},{3,2},{4,5},{5,4},{6,7},{7,6},{8,9},{9,8},{10,11... | collective-permute-start | bytes 7077896 | tf_op jit(solution)/shard_map/ppermute | solution.py:20
  488.6 195.0 %reduce-scatter.10.cloned.1.call-start = ((), (), s32[]{:S(2)}) async-start(), calls=%async_computation.7 | async-start | bytes 2949120 | tf_op jit(solution)/shard_map/reduce_scatter | solution.py:630
  494.9 152.1 %collective-permute-start.1 = (f32[384,1536]{1,0:T(8,128)}, f32[384,1536]{1,0:T(8,128)}, u32[]{:S(2)}, u32[]{:S(2)}) collective-permute-start(f32[384,1536]{1,0:T(8,128)} %fusion.52), channel_id=1, source_target_pairs={{0,1},{1,0},{2,3},{3,2},{4,5},{5,4},{6,7},{7,6},{8,9},{9,8},{10,11... | collective-permute-start | bytes 7077896 | tf_op jit(solution)/shard_map/ppermute | solution.py:20
  496.9 54.1 %collective-permute-start.17 = (bf16[4,192,1536]{2,1,0:T(8,128)(2,1)S(1)}, bf16[4,192,1536]{2,1,0:T(8,128)(2,1)S(1)}, u32[]{:S(2)}, u32[]{:S(2)}) collective-permute-start(bf16[4,192,1536]{2,1,0:T(8,128)(2,1)S(1)} %dynamic-slice_bitcast_fusion.2), channel_id=1, source_target_pairs={{0,4},{4,0},{1,5},{5,1},{2,6},{6,2},{3,7},{7,3},{8,12},{12,8},{9,1... | collective-permute-start | bytes 7077896 | tf_op jit(solution)/shard_map/ppermute | solution.py:20
  521.3 32.1 %collective-permute-start.9 = (f32[384,1536]{1,0:T(8,128)}, f32[384,1536]{1,0:T(8,128)}, u32[]{:S(2)}, u32[]{:S(2)}) collective-permute-start(f32[384,1536]{1,0:T(8,128)} %fusion.58), channel_id=1, source_target_pairs={{0,1},{1,0},{2,3},{3,2},{4,5},{5,4},{6,7},{7,6},{8,9},{9,8},{10,11... | collective-permute-start | bytes 7077896 | tf_op jit(solution)/shard_map/ppermute | solution.py:20
  526.2 120.8 %collective-permute-start.4 = (bf16[384,1536]{1,0:T(8,128)(2,1)}, bf16[384,1536]{1,0:T(8,128)(2,1)}, u32[]{:S(2)}, u32[]{:S(2)}) collective-permute-start(bf16[384,1536]{1,0:T(8,128)(2,1)} %fusion.23), channel_id=1, source_target_pairs={{0,2},{2,0},{1,3},{3,1},{4,6},{6,4},{5,7},{7,5},{8,10},{10,8},{9,1... | collective-permute-start | bytes 3538952 | tf_op jit(solution)/shard_map/ppermute | solution.py:20
  539.7 117.9 %collective-permute-start.19 = (bf16[4,192,1536]{2,1,0:T(8,128)(2,1)}, bf16[4,192,1536]{2,1,0:T(8,128)(2,1)}, u32[]{:S(2)}, u32[]{:S(2)}) collective-permute-start(bf16[4,192,1536]{2,1,0:T(8,128)(2,1)} %dynamic-slice_bitcast_fusion.1), channel_id=1, source_target_pairs={{0,4},{4,0},{1,5},{5,1},{2,6},{6,2},{3,7},{7,3},{8,12},{12,8},{9,1... | collective-permute-start | bytes 7077896 | tf_op jit(solution)/shard_map/ppermute | solution.py:20
  553.1 141.9 %reduce-scatter.8.cloned.1.call-start = ((), (), s32[]{:S(2)}) async-start(), calls=%async_computation.6 | async-start | bytes 737280 | tf_op jit(solution)/shard_map/reduce_scatter | solution.py:617
  561.1 6.1 collective-permute-start.10
  563.4 48.4 %collective-permute-start.15 = (bf16[8,96,768]{2,1,0:T(8,128)(2,1)S(1)}, bf16[8,96,768]{2,1,0:T(8,128)(2,1)S(1)}, u32[]{:S(2)}, u32[]{:S(2)}) collective-permute-start(bf16[8,96,768]{2,1,0:T(8,128)(2,1)S(1)} %dynamic-slice_bitcast_fusion.3), channel_id=1, source_target_pairs={{0,2},{2,0},{1,3},{3,1},{4,6},{6,4},{5,7},{7,5},{8,10},{10,8},{9,1... | collective-permute-start | bytes 3538952 | tf_op jit(solution)/shard_map/ppermute | solution.py:20
  567.2 50.0 %collective-permute-start.13 = (bf16[8,96,768]{2,1,0:T(8,128)(2,1)S(1)}, bf16[8,96,768]{2,1,0:T(8,128)(2,1)S(1)}, u32[]{:S(2)}, u32[]{:S(2)}) collective-permute-start(bf16[8,96,768]{2,1,0:T(8,128)(2,1)S(1)} %dynamic-slice_bitcast_fusion.4), channel_id=1, source_target_pairs={{0,2},{2,0},{1,3},{3,1},{4,6},{6,4},{5,7},{7,5},{8,10},{10,8},{9,1... | collective-permute-start | bytes 3538952 | tf_op jit(solution)/shard_map/ppermute | solution.py:20
  612.2 15.6 %collective-permute-start.16 = (bf16[4,96,768]{2,1,0:T(8,128)(2,1)S(1)}, bf16[4,96,768]{2,1,0:T(8,128)(2,1)S(1)}, u32[]{:S(2)}, u32[]{:S(2)}) collective-permute-start(bf16[4,96,768]{2,1,0:T(8,128)(2,1)S(1)} %dynamic-slice_bitcast_fusion.5), channel_id=1, source_target_pairs={{0,4},{4,0},{1,5},{5,1},{2,6},{6,2},{3,7},{7,3},{8,12},{12,8},{9,1... | collective-permute-start | bytes 1769480 | tf_op jit(solution)/shard_map/ppermute | solution.py:20
  628.9 67.8 %reduce-scatter.6.cloned.1.call-start = ((), (), s32[]{:S(2)}) async-start(), calls=%async_computation.5 | async-start | bytes 737280 | tf_op jit(solution)/shard_map/reduce_scatter | solution.py:617
  631.0 14.8 %collective-permute-start.14 = (bf16[4,96,768]{2,1,0:T(8,128)(2,1)S(1)}, bf16[4,96,768]{2,1,0:T(8,128)(2,1)S(1)}, u32[]{:S(2)}, u32[]{:S(2)}) collective-permute-start(bf16[4,96,768]{2,1,0:T(8,128)(2,1)S(1)} %dynamic-slice_bitcast_fusion.6), channel_id=1, source_target_pairs={{0,4},{4,0},{1,5},{5,1},{2,6},{6,2},{3,7},{7,3},{8,12},{12,8},{9,1... | collective-permute-start | bytes 1769480 | tf_op jit(solution)/shard_map/ppermute | solution.py:20
  646.8 201.8 %reduce-scatter.12.cloned.1.call-start = ((), (), s32[]{:S(2)}) async-start(), calls=%async_computation.8 | async-start | bytes 2949120 | tf_op jit(solution)/shard_map/reduce_scatter | solution.py:630
  676.2 22.1 %collective-permute-start.11 = (f32[384,1536]{1,0:T(8,128)}, f32[384,1536]{1,0:T(8,128)}, u32[]{:S(2)}, u32[]{:S(2)}) collective-permute-start(f32[384,1536]{1,0:T(8,128)} %fusion.32), channel_id=1, source_target_pairs={{0,1},{1,0},{2,3},{3,2},{4,5},{5,4},{6,7},{7,6},{8,9},{9,8},{10,11... | collective-permute-start | bytes 7077896 | tf_op jit(solution)/shard_map/ppermute | solution.py:20
  677.9 9.7 %collective-permute-start.22 = (bf16[96,1536]{1,0:T(8,128)(2,1)}, bf16[96,1536]{1,0:T(8,128)(2,1)}, u32[]{:S(2)}, u32[]{:S(2)}) collective-permute-start(bf16[96,1536]{1,0:T(8,128)(2,1)} %dynamic-slice_bitcast_fusion.7), channel_id=1, source_target_pairs={{0,2},{2,0},{1,3},{3,1},{4,6},{6,4},{5,7},{7,5},{8,10},{10,8},{9,1... | collective-permute-start | bytes 884744 | tf_op jit(solution)/shard_map/ppermute | solution.py:20
  684.6 9.2 %collective-permute-start.18 = (bf16[96,1536]{1,0:T(8,128)(2,1)S(1)}, bf16[96,1536]{1,0:T(8,128)(2,1)S(1)}, u32[]{:S(2)}, u32[]{:S(2)}) collective-permute-start(bf16[96,1536]{1,0:T(8,128)(2,1)S(1)} %dynamic-slice_bitcast_fusion.9), channel_id=1, source_target_pairs={{0,2},{2,0},{1,3},{3,1},{4,6},{6,4},{5,7},{7,5},{8,10},{10,8},{9,1... | collective-permute-start | bytes 884744 | tf_op jit(solution)/shard_map/ppermute | solution.py:20
  712.2 5.5 collective-permute-start.12
  718.3 127.9 %copy-start.38 = (bf16[48,768]{1,0:T(8,128)(2,1)S(1)}, bf16[48,768]{1,0:T(8,128)(2,1)}, u32[]{:S(2)}) copy-start(bf16[48,768]{1,0:T(8,128)(2,1)} %refs_6_.1) | copy-start | bytes 221188
  718.3 134.3 %copy-start.35 = (bf16[96,768]{1,0:T(8,128)(2,1)S(1)}, bf16[96,768]{1,0:T(8,128)(2,1)}, u32[]{:S(2)}) copy-start(bf16[96,768]{1,0:T(8,128)(2,1)} %refs_1_.1) | copy-start | bytes 442372
  718.3 134.3 %copy-start.36 = (bf16[96,768]{1,0:T(8,128)(2,1)S(1)}, bf16[96,768]{1,0:T(8,128)(2,1)}, u32[]{:S(2)}) copy-start(bf16[96,768]{1,0:T(8,128)(2,1)} %refs_2_.1) | copy-start | bytes 442372
  718.3 134.3 %copy-start.37 = (bf16[96,768]{1,0:T(8,128)(2,1)S(1)}, bf16[96,768]{1,0:T(8,128)(2,1)}, u32[]{:S(2)}) copy-start(bf16[96,768]{1,0:T(8,128)(2,1)} %refs_5_.1) | copy-start | bytes 442372
  849.6 6.8 collective-permute-start.20
  (90 other events, 587.4 us)
Sparse Core Ops, SparseCore 0:
  488.7 45.3 reduce-scatter.13
  553.2 45.3 reduce-scatter.9
  629.0 19.5 reduce-scatter.7
  651.3 20.2 reduce-scatter.5
  673.7 46.4 reduce-scatter.11

commit v8 on v7

--- a/solution.py
+++ b/solution.py
@@ -622,7 +622,8 @@
         held = tn(left, right).astype(BF)
         self.held = held.reshape(zs, 2, -1, held.shape[1])
         self.y = lax.axis_index("y")
-        self.got = swap(pick(self.held, 1 - self.y, 1), "y")
+        self.sent = pick(self.held, 1 - self.y, 1)
+        self.got = swap(self.sent, "y")
 
     def second(self, *others):
         got = after(self.got, others)
@@ -872,16 +873,13 @@
 
 
 PLAN = (
-    0, 100, 200, 800, 300, 700, 400, 2000, 2100, 2101, 2010, 1700, 1100, 2001, 2110, 2111, 600,
-    3010, 1400, 1800, 2210, 500, 2120, 3100, 3101, 2121, 2200, 2201, 2211, 2011, 2701, 2410,
-    3001, 3121, 2020, 2400, 2700, 2711, 2720, 2710, 2220, 3110, 1600, 3120, 5800, 3111, 2021,
-    3000, 3021, 3020, 1000, 2221, 2401, 4100, 3011, 1500, 2301, 2721, 2411, 2500, 3410, 4000,
-    -1, 2300, 2501, -1, -1, 1200, 3221, -1, 2600, 3220, -1, -1, 2311, 3401, 2321, -1, -1, 3210,
-    3201, 1300, 3211, -1, 2801, -1, 2511, 3200, -1, 2421, 2510, 2420, -1, 3500, -1, 3301, 2310,
-    3321, 3421, 2520, -1, 2610, 2601, -1, 3300, -1, 3411, 3400, 2800, 4200, 3511, -1, -1, 3310,
-    3420, 2521, -1, 2320, 3311, -1, 3510, -1, 2620, -1, 3320, 4400, 2611, -1, 4300, -1, 3520,
-    -1, 3521, -1, -1, 3501, 2811, -1, -1, 2810, -1, -1, -1, -1, -1, -1, 2621, 4500, -1, -1,
-    4700, -1, -1, -1, -1, -1, 2821, 2820, 4600,
+    0, 100, 300, 400, 500, 200, 2000, 1100, 2020, 2010, 2001, 3010, 1000, 1300, 3000, 2011,
+    2101, 3011, 1500, 3001, 2220, 2021, 3021, 2100, 2200, 2300, 2110, 2201, 3020, 2210, 1400,
+    2111, 2121, 2221, 2120, 2211, 3101, 2301, 5500, 4000, -1, -1, 2400, 3201, 2310, 3110, -1,
+    1200, 3111, 3120, -1, -1, -1, 2401, 2410, 2311, 3100, 3200, -1, -1, -1, 3121, -1, -1, -1,
+    -1, 2411, 3221, -1, 2421, 2501, 3211, 2500, 2320, -1, -1, 3210, 3220, 4100, 2420, 6000, -1,
+    -1, -1, -1, -1, -1, 2510, 2511, 4200, -1, -1, -1, -1, -1, -1, 2321, -1, -1, -1, -1, -1, -1,
+    -1, -1, -1, -1, -1, -1, -1, -1, 2521, 7000, 2520,
 )
 
 
@@ -903,13 +901,13 @@
     shards = take(9)
     quarters_in = take(3)
     inputs_hbm, cot_hbm, cos_ref, sa_ref, sb_ref, self_bias, cross_bias, memory = take(8)
-    wholes = take(6)
+    wholes = take(3)
     quarter_outs = take(3)
-    outs = take(10)
+    outs = take(15)
     cot_out = take(1)[0]
     peak_out = take(1)[0]
     send_sems, recv_sems, local_sems = take(3)
-    w_vec, w_in, w_so, w_cq, w_kv, w_co = take(6)
+    w_in, w_a, w_b = take(3)
     (
         x_all, normed_self, taken, mixed_self, stream_cross, normed_cross,
         query_cross, taken_cross, mixed_cross, stream_feed, normed_feed,
@@ -924,13 +922,24 @@
     def local(source, target):
         return pltpu.make_async_copy(source, target, lanes.local())
 
-    pieces, at = [], 0
-    for count, whole in zip((1, 3, 1, 1, 2, 1), wholes):
-        columns = whole.shape[-1] // count
-        for i in range(count):
-            target = whole.at[z, y, x, :, pl.ds(i * columns, columns)]
-            pieces.append(local(shards[at], target))
-            at += 1
+    rows_here, inner = shards[1].shape
+    rows_kv = shards[6].shape[0]
+
+    def spot(whole, row, count, column, wide_):
+        return whole.at[z, y, x, pl.ds(row, count), pl.ds(column, wide_)]
+
+    places = [
+        spot(wholes[0], 0, rows_here, 3 * inner, shards[0].shape[1]),
+        spot(wholes[0], 0, rows_here, 0, inner),
+        spot(wholes[0], 0, rows_here, inner, inner),
+        spot(wholes[0], 0, rows_here, 2 * inner, inner),
+        spot(wholes[1], 0, rows_here, 0, inner),
+        spot(wholes[1], 0, rows_here, inner, inner),
+        spot(wholes[2], 0, rows_kv, 0, inner),
+        spot(wholes[2], rows_kv, rows_kv, 0, inner),
+        spot(wholes[2], 0, rows_here, inner, inner),
+    ]
+    pieces = [local(shard, place) for shard, place in zip(shards, places)]
     own_inputs = local(inputs_hbm, x_all.at[0])
     own_cot = local(cot_hbm, cot_out.at[0])
     for piece in pieces + [own_inputs, own_cot]:
@@ -959,11 +968,16 @@
     ]
     loads = [
         local(whole, held)
-        for whole, held in zip(wholes, (w_vec, w_in, w_so, w_cq, w_kv, w_co))
+        for whole, held in zip(wholes, (w_in, w_a, w_b))
     ]
     results = (
         normed_self, taken, mixed_self, stream_cross, normed_cross,
         query_cross, taken_cross, mixed_cross, stream_feed, normed_feed,
+        w_in.at[:, :, :, :, pl.ds(0, 3 * inner)],
+        w_a.at[:, :, :, :, pl.ds(0, inner)],
+        w_a.at[:, :, :, :, pl.ds(inner, inner)],
+        w_b.at[:, :, :, :, pl.ds(inner, inner)],
+        vectors,
     )
     saves = [local(held, out) for held, out in zip(results, outs)]
 
@@ -971,8 +985,7 @@
     cot_moves[0].start()
     for piece in pieces:
         piece.wait()
-    columns = w_in.shape[-1]
-    inner = columns // 3
+    columns = 3 * inner
     pairs = inner // wide
     block = 2 * wide
     tile = 128 if rows % 128 == 0 else rows
@@ -1024,7 +1037,7 @@
 
             def body(part, i):
                 left = mixed_ref[pl.ds(pl.multiple_of(rows + i * tile, tile), tile), :]
-                send[part, cols] = nt(left, weight[zz].reshape(-1, inner)).astype(BF)
+                send[part, cols] = nt(left, weight(zz)).astype(BF)
 
             over(rows, tile, body)
         move.start()
@@ -1033,7 +1046,7 @@
             cols = slice(zz * chunk, (zz + 1) * chunk)
 
             def body(part, _):
-                made = nt(mixed_ref[part, :], weight[zz].reshape(-1, inner))
+                made = nt(mixed_ref[part, :], weight(zz))
                 target[part, cols] = made + base(part, cols)
 
             over(rows, tile, body)
@@ -1046,11 +1059,14 @@
         over(rows, tile, body)
 
     def compute():
-        need(0, 1)
+        need(0)
         own_inputs.wait()
         mate_inputs.arrived()
         loads[0].wait()
-        vectors[...] = jnp.transpose(w_vec[...].reshape(width, w_vec.shape[-1]))
+        tail = w_in[..., columns : w_in.shape[-1]].reshape(width, w_in.shape[-1] - columns)
+        vectors[...] = jnp.transpose(tail.astype(F32))
+        saves[10].start()
+        saves[14].start()
         crest[...] = jnp.full(crest.shape, NEGATIVE, F32)
         for side in range(2):
 
@@ -1061,7 +1077,6 @@
 
             over(rows, tile, body)
         saves[0].start()
-        loads[1].wait()
         yield
         for start in range(0, columns, block):
 
@@ -1079,10 +1094,12 @@
         saves[1].start()
         yield from attend_all(taken, inner, 2 * inner, taken, self_bias, mixed_self)
         saves[2].start()
-        need(2)
-        loads[2].wait()
+        need(1)
+        loads[1].wait()
+        saves[11].start()
+        saves[12].start()
         yield from out_project(
-            mixed_self, w_so, mate_self, part_send, part_got,
+            mixed_self, lambda zz: w_a[zz, :, :, :, 0:inner].reshape(-1, inner), mate_self, part_send, part_got,
             lambda part, cols: x_all[0, part, cols].astype(F32), stream_cross,
         )
         saves[3].start()
@@ -1094,16 +1111,18 @@
         over(rows, tile, second_norm)
         mate_normed.start()
         yield
-        need(4)
-        loads[4].wait()
+        need(2)
+        loads[2].wait()
+        saves[13].start()
         depth = memory.shape[1]
-        for start in range(0, 2 * inner, block):
-            weight = w_kv[..., start : start + block].reshape(depth, block)
-            taken_cross[:, start : start + block] = nn(memory[...], weight).astype(BF)
+        for side in range(2):
+            for start in range(0, inner, block):
+                part = slice(side * rows_kv, (side + 1) * rows_kv)
+                weight = w_b[:, :, :, part, start : start + block].reshape(depth, block)
+                at = side * inner + start
+                taken_cross[:, at : at + block] = nn(memory[...], weight).astype(BF)
         saves[6].start()
         yield
-        need(3)
-        loads[3].wait()
         yield
         for side in range(2):
             if side == 1:
@@ -1112,7 +1131,7 @@
             for start in range(0, inner, block):
 
                 def body(part, i):
-                    weight = w_cq[..., start : start + block].reshape(width, block)
+                    weight = w_a[..., inner + start : inner + start + block].reshape(width, block)
                     made = nn(normed_cross[side, part, :], weight).astype(BF)
                     at = pl.multiple_of(side * rows + i * tile, tile)
                     query_cross[pl.ds(at, tile), start : start + block] = made
@@ -1122,11 +1141,9 @@
         saves[5].start()
         yield from attend_all(query_cross, 0, inner, taken_cross, cross_bias, mixed_cross)
         saves[7].start()
-        need(5)
-        loads[5].wait()
         mate_self.sent()
         yield from out_project(
-            mixed_cross, w_co, mate_cross, part_send, part_got,
+            mixed_cross, lambda zz: w_b[zz, :, :, :, inner : 2 * inner].reshape(-1, inner), mate_cross, part_send, part_got,
             lambda part, cols: stream_cross[part, cols], stream_feed,
         )
         saves[8].start()
@@ -1146,16 +1163,19 @@
             next(work, None)
             continue
         kind, which, k, side = entry // 1000, entry // 100 % 10, entry // 10 % 10, entry % 10
+        if kind == 6:
+            cot_moves[1].start()
+            continue
+        if kind == 7:
+            cot_moves[1].arrived()
+            cot_moves[2].start()
+            continue
         item = items[which]
         getattr(item, names[kind])(*((k, side) if kind in (2, 3) else ()))
-        if kind == 0 and which == 4:
-            cot_moves[1].start()
         if kind == 4:
             ready.add(which)
-            if which < 6:
+            if which < 3:
                 loads[which].start()
-    cot_moves[1].arrived()
-    cot_moves[2].start()
     for _ in work:
         pass
     peak_out[...] = crest[...]
@@ -1180,10 +1200,9 @@
     seq_len, inner = 2 * rows, shards[1].shape[1]
     tokens = memory.shape[0]
     spread = []
-    groups = ([shards[0]], shards[1:4], [shards[4]], [shards[5]], shards[6:8], [shards[8]])
-    for group in groups:
-        columns = sum(shard.shape[1] for shard in group)
-        spread.append(jax.ShapeDtypeStruct((zs, 2, 2, group[0].shape[0], columns), group[0].dtype))
+    count = shards[1].shape[0]
+    for columns in (3 * inner + shards[0].shape[1], 2 * inner, 2 * inner):
+        spread.append(jax.ShapeDtypeStruct((zs, 2, 2, count, columns), BF))
     for shard in quarters:
         spread.append(
             jax.ShapeDtypeStruct((zs, 2, 2, shard.shape[0], shard.shape[1] // 2), shard.dtype)
@@ -1200,12 +1219,17 @@
         jax.ShapeDtypeStruct((rows, width), F32),
         jax.ShapeDtypeStruct((2, rows, width), BF),
     ]
+    saved = [
+        jax.ShapeDtypeStruct((zs, 2, 2, count, columns), BF)
+        for columns in (3 * inner, inner, inner, inner)
+    ]
+    saved.append(jax.ShapeDtypeStruct((shards[0].shape[1], width), F32))
     cot_out = jax.ShapeDtypeStruct((4, rows, width), BF)
     peak = jax.ShapeDtypeStruct((8, 2 * HEAD_DIM), F32)
-    moves = 6 * (3 + 8 * (zs - 1)) + 3 * (2 + 4 * (zs - 1)) + 8
+    moves = 3 * (3 + 8 * (zs - 1)) + 3 * (2 + 4 * (zs - 1)) + 8
     hbm = pl.BlockSpec(memory_space=pltpu.HBM)
     vmem = pl.BlockSpec(memory_space=pltpu.VMEM)
-    held = [pltpu.VMEM(shape.shape, shape.dtype) for shape in spread[:6]]
+    held = [pltpu.VMEM(shape.shape, shape.dtype) for shape in spread[:3]]
     held += [pltpu.VMEM((2, rows, width), BF)]
     held += [pltpu.VMEM(shape.shape, shape.dtype) for shape in results]
     held += [pltpu.VMEM((rows, width), BF)] * 2
@@ -1213,13 +1237,13 @@
     flops = 2 * seq_len * inner * (7 * width + 4 * seq_len) // 1
     made = pl.pallas_call(
         functools.partial(forward_kernel, zs),
-        out_shape=spread + results + [cot_out, peak],
+        out_shape=spread + results + saved + [cot_out, peak],
         in_specs=[hbm] * 14 + [vmem] * 6,
-        out_specs=[hbm] * 20 + [vmem],
+        out_specs=[hbm] * 22 + [vmem],
         scratch_shapes=[
             pltpu.SemaphoreType.DMA((moves,)),
             pltpu.SemaphoreType.DMA((moves,)),
-            pltpu.SemaphoreType.DMA((9 + 2 + 3 + 6 + 10,)),
+            pltpu.SemaphoreType.DMA((9 + 2 + 3 + 3 + 15,)),
         ]
         + held,
         compiler_params=pltpu.CompilerParams(
@@ -1227,7 +1251,7 @@
         ),
         cost_estimate=pl.CostEstimate(flops=flops, bytes_accessed=10**8, transcendentals=10**7),
     )(*shards, *quarters, inputs, cotangent, *turns, self_bias, cross_bias, memory)
-    return made[:9], made[9:19], made[19], made[20]
+    return made[3:6], made[6:16], made[16:21], made[21], made[22]
 
 
 def pair_rows(own):
@@ -1323,8 +1347,8 @@
     pairs = inner // (2 * HEAD_DIM)
 
     if shard_rows % 32 == 0:
-        vectors = jnp.pad(jnp.stack(vector_list, axis=1).astype(F32), ((0, 0), (0, 122)))
-        spread, made, cot_group, crest = forward(
+        vectors = jnp.pad(jnp.stack(vector_list, axis=1), ((0, 0), (0, 122)))
+        spread, made, saved, cot_group, crest = forward(
             [
                 vectors,
                 self_query,
@@ -1345,8 +1369,7 @@
             memory,
             zs,
         )
-        norms, in_weight, self_out_t, cross_in, memory_weight, cross_out_t = spread[:6]
-        norms = norms.reshape(width, -1).T
+        in_weight, self_out_t, cross_in, cross_out_t, norms = saved
         (
             normed_self,
             taken,
@@ -1359,7 +1382,7 @@
             stream_feed,
             normed_feed,
         ) = made
-        gate_full, up_full, down_t = spread[6:]
+        gate_full, up_full, down_t = spread
         normed_cross = normed_cross.reshape(seq_len, width)
         near_feed, cot_group = (v.reshape(-1, width) for v in (normed_feed, cot_group))
     else:
@@ -1448,7 +1471,7 @@
     grad_normed = feed_back(gate_near[:rows], up_near[:rows]) + swap(
         feed_back(gate_near[rows:], up_near[rows:]), "tensor"
     )
-    got_far = after(got_far, grad_normed, gate_pair.held, down_pair.held)
+    got_far = after(got_far, grad_normed, gate_pair.sent, down_pair.sent)
     grad_normed = grad_normed + got_far.astype(F32)
     stream_part, grad_feed_gain, grad_feed_bias = norm_backward(
         grad_normed, unit_feed, inverse_feed, norms[4]
@@ -1456,13 +1479,12 @@
     grad_stream = cotangent.astype(F32) + stream_part
     grad_full = pair_rows(grad_stream.astype(BF))
     up_pair = PairSum(after(normed_feed, grad_full), grad_upward, zs)
-    down_pair.second(grad_full)
     cross_output_sum = FullSum(grad_full, mixed_cross, zs)
     grad_mixed = nn(grad_full, cross_out_t).astype(BF)
     grad_query, grad_keys, grad_values = attend_back(
         query_cross, taken_cross, taken_cross, grad_mixed, cross_bias_row[:, None], (0, 0, pairs), None
     )
-    gate_pair.second(grad_query)
+    down_pair.second(grad_query)
     grad_normed = spread_pair(grad_query, cross_in)
     cross_query_sum = FullSum(normed_cross, grad_query, zs)
     part_memory = tn(memory, jnp.concatenate([grad_keys, grad_values], axis=1))
@@ -1471,21 +1493,21 @@
     )
     grad_stream = grad_stream + stream_part
     grad_full = pair_rows(grad_stream.astype(BF))
-    up_pair.second(grad_full)
+    gate_pair.second(grad_full)
     part_self_output = tn(grad_full, mixed_self)
     grad_mixed = nn(grad_full, self_out_t).astype(BF)
     grad_parts = attend_back(
         taken, taken, taken, grad_mixed, self_bias_row[:, None], (0, pairs, 2 * pairs), turns
     )
     grad_in = jnp.concatenate(grad_parts, axis=1)
+    up_pair.second(grad_in)
     cross_output_sum.second(grad_in)
     cross_query_sum.second(grad_in)
-    part_query, part_key, part_value = (
-        tn(normed_self, part).astype(BF) for part in grad_parts
-    )
-    sum_cross_output = cross_output_sum.third(part_query, part_key).astype(F32)
-    sum_cross_query = cross_query_sum.third(part_query, part_key).astype(F32)
+    part_in = tn(normed_self, grad_in[:, : 2 * inner]).astype(BF)
+    part_value = tn(normed_self, grad_parts[2]).astype(BF)
     grad_normed = spread_pair(grad_in, in_weight)
+    sum_cross_output = cross_output_sum.third(grad_normed).astype(F32)
+    sum_cross_query = cross_query_sum.third(grad_normed).astype(F32)
     unit_self, inverse_self = unit_rows_of(stream)
     stream_part, grad_self_gain, grad_self_bias = norm_backward(
         grad_normed, unit_self, inverse_self, norms[0]
@@ -1510,20 +1532,17 @@
     def blocks(part):
         return part.astype(BF).reshape(zs, 2, 2, -1, part.shape[1])
 
-    (vector_sums, sum_query, sum_key, sum_value, sum_self_output, sum_memory, crest) = (
-        scatter_all(
-            [
-                vector_sums,
-                blocks(part_query),
-                blocks(part_key),
-                blocks(part_value),
-                blocks(part_self_output),
-                blocks(part_memory),
-            ],
-            ["x", "x", "y", "x", "y", "z"],
-            crest,
-            zs,
-        )
+    vector_sums, sum_in, sum_value, sum_self_output, sum_memory, crest = scatter_all(
+        [
+            vector_sums,
+            blocks(part_in),
+            blocks(part_value),
+            blocks(part_self_output),
+            blocks(part_memory),
+        ],
+        ["z", "x", "y", "y", "z"],
+        crest,
+        zs,
     )
     vector_sums = vector_sums[:, :shard_rows]
     peaks = crest[0, :heads_here]
@@ -1548,8 +1567,8 @@
         grad_stream,
         vector_sums[0],
         vector_sums[1],
-        sum_query,
-        sum_key,
+        sum_in[:, :inner],
+        sum_in[:, inner:],
         sum_value,
         sum_self_output.T,
         vector_sums[2],

time: 873 us -> 847 us (0.970)
  waiting for transfers between devices: 71.4 us -> 43.8 us
  Pallas kernels: 487 us -> 475 us
    ppermute x23, waiting for transfers between devices: 71.3 us -> 43.8 us  [swap(): return lax.ppermute(value, axis, [(0, 1), (1, 0)])]
    pallas_call x1, Pallas kernels: 307 us -> 285 us  [forward(): pl.pallas_call(functools.partial(forward_kernel, zs), out_shape=spread +...]
    pallas_call x1, Pallas kernels: 127 us -> 137 us  [scatter_all(): pl.pallas_call(functools.partial(scatter_kernel, zs, orders), out_shape=[...]
    dot_general x10 -> x9, matrix products: 50.5 us -> 46.5 us  [tn(): lax.dot_general(left, right, (((0,), (0,)), ((), ())), preferred_element_...]
  transfers between devices with their start and end apart: 28 -> 28, of which waited for: 8 -> 7; matrix products, arithmetic and copies ran while one was open for 28% -> 31% of each run, Pallas kernels for 21% -> 23%
where the time goes in v8:
time: 847 us; the launch traced here: 842 us
  Pallas kernels  475 us (56%)
  matrix products  182 us (21%)
  other arithmetic  59.6 us (7%)
  local copies, waits for them, and re-layouts  49.4 us (6%)
  waiting for transfers between devices  43.8 us (5%)
  between operations  16.7 us (2%)
  starting transfers between devices  16.4 us (2%)
    pallas_call x1, Pallas kernels, forward(): pl.pallas_call(functools.partial(forward_kernel, zs), out_shape=spread +...  285 us
    pallas_call x1, Pallas kernels, scatter_all(): pl.pallas_call(functools.partial(scatter_kernel, zs, orders), out_shape=[...  137 us
    dot_general x16, matrix products, nt(): lax.dot_general(left, right, (((1,), (1,)), ((), ())), preferred_element_...  79.2 us
    dot_general x8, matrix products, nn(): lax.dot_general(left, right, (((1,), (0,)), ((), ())), preferred_element_...  56 us
    pallas_call x2, Pallas kernels, attend_back(): pl.pallas_call(functools.partial(attend_back_kernel, turns is not None),...  53.1 us
    dot_general x9, matrix products, tn(): lax.dot_general(left, right, (((0,), (0,)), ((), ())), preferred_element_...  46.5 us
    ppermute x23, waiting for transfers between devices, swap(): return lax.ppermute(value, axis, [(0, 1), (1, 0)])  43.8 us
  transfers between devices with their start and end apart: 28, of which 7 were waited for; matrix products, arithmetic and copies ran while one was open for 31% of the time, Pallas kernels for 23%

profile of v8, /device:TPU:0, one launch (start us, length us, event | category | flops | bytes accessed | tf_op | source)
XLA Modules:
  0.0 842.5 jit_solution(4052305853195516735)
XLA Ops:
  16.9 284.7 %shard_map.406 = (bf16[4,2,2,96,2432]{4,3,2,1,0:T(8,128)(2,1)}, bf16[4,2,2,96,1536]{4,3,2,1,0:T(8,128)(2,1)}, bf16[4,2,2,96,1536]{4,3,2,1,0:T(8,128)(2,1)}, bf16...) custom-call(bf16[96,128]{1,0:T(8,128)(2,1)} %pad.16.refs_0_, ...), custom_call_target="tpu_custom_call" | custom-call | flops 16307453952 | bytes 100000000 | tf_op jit(solution)/shard_map/pallas_call | solution.py:1238
  305.9 7.9 fusion.79
  313.8 5.6 fusion.78
  328.4 11.3 %multiply_convert_fusion.3 = (bf16[768,1536]{1,0:T(8,128)(2,1)}, bf16[768,1536]{1,0:T(8,128)(2,1)}, bf16[768,1536]{1,0:T(8,128)(2,1)}) fusion(f32[768,1536]{1,0:T(8,128)} %fusion.78, f32[768,1536]{1,0:T(8,128)} %fusion.79, bf16[768,1536]{1,0:T(8,128)(2,1)S(1)} %bitcast.200, bf16[1536,1536]{1,0:T(8,128)(2,1)} %bitcast.225), kind=kOutput, calls=%fused_computation.24 | convolution fusion | flops 3642753024 | bytes 23592960 | tf_op jit(solution)/shard_map/dot_general | solution.py:585
  340.9 9.2 %fusion.81 = f32[768,1536]{1,0:T(8,128)} fusion(bf16[768,1536]{1,0:T(8,128)(2,1)} %bitcast.199, bf16[1536,1536]{1,0:T(8,128)(2,1)} %bitcast.226), kind=kOutput, calls=%fused_computation.199 | convolution fusion | flops 3623878656 | bytes 11796480 | tf_op jit(solution)/shard_map/dot_general | solution.py:585
  351.2 4.9 fusion.49
  359.8 5.5 fusion.80
  365.3 9.3 %multiply_convert_fusion = (bf16[768,1536]{1,0:T(8,128)(2,1)S(1)}, bf16[768,1536]{1,0:T(8,128)(2,1)S(1)}, bf16[768,1536]{1,0:T(8,128)(2,1)}) fusion(f32[768,1536]{1,0:T(8,128)} %fusion.81, f32[768,1536]{1,0:T(8,128)} %fusion.80, bf16[768,1536]{1,0:T(8,128)(2,1)S(1)} %constant_dynamic-update-slice_fusion, bf16[1536,1536]{1,0:T(8,128)(2,1)S(1)} %bitcast.248), kind=kOutput, calls=%fused_computation.20 | convolution fusion | flops 3642753024 | bytes 23592960 | tf_op jit(solution)/shard_map/dot_general | solution.py:585
  386.4 6.1 pad_maximum_fusion
  392.5 7.2 fusion.14
  399.8 5.3 fusion.21
  405.7 8.1 convolution_convert_fusion.2
  415.5 9.5 %convolution_convert_fusion.3 = bf16[1536,1536]{1,0:T(8,128)(2,1)S(1)} fusion(bf16[1536,1536]{1,0:T(8,128)(2,1)S(1)} %pad_maximum_fusion, bf16[768,1536]{1,0:T(8,128)(2,1)} %copy-done.74, bf16[768,1536]{1,0:T(8,128)(2,1)S(1)} %copy-done.67), kind=kOutput, calls=%fused_computation.3 | convolution fusion | flops 7259553792 | bytes 14155776 | tf_op jit(solution)/shard_map/dot_general | solution.py:593
  428.0 5.1 collective-permute-done.7
  444.8 16.3 %shard_map.407 = (bf16[768,768]{1,0:T(8,128)(2,1)S(1)}, bf16[256,768]{1,0:T(8,128)(2,1)S(1)}, bf16[256,768]{1,0:T(8,128)(2,1)S(1)}) custom-call(bf16[768,768]{1,0:T(8,128)(2,1)S(1)} %copy-done.4, bf16[256,1536]{1,0:T(8,128)(2,1)S(1)} %copy-done.5, bf16[256,1536]{1,0:T(8,128)(2,1)S(1)} %copy-done.5, bf16[768,768]{1,0:T(8,128)(2,1)S(1)} %convolution_convert_fusion.10.g_ref, ...), custom_call_target="tpu_custom_call" | custom-call | flops 3019898880 | bytes 6291456 | tf_op jit(solution)/shard_map/pallas_call | solution.py:810
  461.2 5.8 collective-permute-done.21
  469.3 6.3 fusion.55
  476.2 6.5 fusion.23
  487.4 7.8 convolution_convert_fusion.1
  499.4 11.3 %collective-permute-done.4 = bf16[384,1536]{1,0:T(8,128)(2,1)} collective-permute-done((bf16[384,1536]{1,0:T(8,128)(2,1)}, bf16[384,1536]{1,0:T(8,128)(2,1)}, u32[]{:S(2)}, u32[]{:S(2)}) %collective-permute-start.4) | collective-permute-done | bytes 1179680 | tf_op jit(solution)/shard_map/ppermute | solution.py:20
  510.7 7.5 fusion.22
  518.2 11.8 %collective-permute-done.17 = bf16[4,192,1536]{2,1,0:T(8,128)(2,1)} collective-permute-done((bf16[4,192,1536]{2,1,0:T(8,128)(2,1)}, bf16[4,192,1536]{2,1,0:T(8,128)(2,1)}, u32[]{:S(2)}, u32[]{:S(2)}) %collective-permute-start.17) | collective-permute-done | bytes 2359328 | tf_op jit(solution)/shard_map/ppermute | solution.py:20
  530.0 4.5 fusion.11
  534.8 4.8 multiply_reduce_fusion.1
  555.5 5.2 convolution_convert_fusion.9.g_ref
  560.7 36.8 %shard_map.408 = (bf16[768,768]{1,0:T(8,128)(2,1)S(1)}, bf16[768,768]{1,0:T(8,128)(2,1)S(1)}, bf16[768,768]{1,0:T(8,128)(2,1)S(1)}) custom-call(bf16[768,2304]{1,0:T(8,128)(2,1)} %get-tuple-element.91.q_ref.k_ref.v_ref, bf16[768,2304]{1,0:T(8,128)(2,1)} %get-tuple-element.91.q_ref.k_ref.v_ref, bf16[768,2304]{1,0:T(8,128)(2,1)} %get-tuple-element.91.q_ref.k_ref.v_ref, ...), custom_call_target="tpu_custom_call" | custom-call | flops 9059696640 | bytes 9437184 | tf_op jit(solution)/shard_map/pallas_call | solution.py:810
  608.3 8.0 fusion.35
  621.7 5.9 convolution_convert_fusion
  632.5 5.2 convolution_convert_fusion.7
  641.3 6.3 collective-permute-done.18
  649.5 9.7 %fusion.28 = (f32[1536]{0:T(1024)}, f32[384]{0:T(512)}, f32[384]{0:T(512)}, f32[1536]{0:T(1024)}, f32[384,1536]{1,0:T(8,128)}) fusion(bf16[384,1536]{1,0:T(8,128)(2,1)S(1)} %copy-done.10, f32[384]{0:T(512)S(1)} %copy-done.47, f32[384]{0:T(512)S(1)} %copy-done.45, f32[1536]{0:T(1024)S(1)} %copy-done.42, f32[384,1536]{1,0:T(8,128)} %collective-permute-done.11, ...), kind=kOutput, calls=%fused_computation.59 | convolution fusion | flops 2724392960 | bytes 14770176 | tf_op jit(solution)/shard_map/dot_general | solution.py:589
  679.2 137.1 %shard_map.409 = (f32[8,128]{1,0:T(8,128)}, f32[96,1536]{1,0:T(8,128)}, f32[96,768]{1,0:T(8,128)}, f32[96,768]{1,0:T(8,128)}, f32[48,1536]{1,0:T(8,128)}, /*index=5*/f32[8,128]{1,0:T(8,128)}) custom-call(f32[4,2,2,8,128]{4,3,2,1,0:T(8,128)} %bitcast.210, bf16[4,2,2,96,1536]{4,3,2,1,0:T(8,128)(2,1)} %bitcast.186, bf16[4,2,2,96,768]{4,3,2,1,0:T(8,128)(2,1)} %bitcast.197, ...), custom_call_target="tpu_custom_call" | custom-call | tf_op jit(solution)/shard_map/pallas_call | solution.py:569
  (362 shorter events, 149.3 us)
Async XLA Ops:
  7.2 623.9 %reduce-scatter.14.cloned.1.call-start = ((), (), s32[]{:S(2)}) async-start(), calls=%async_computation.9 | async-start | bytes 2949120 | tf_op jit(solution)/shard_map/reduce_scatter | solution.py:631
  304.1 45.9 %collective-permute-start = (bf16[384,1536]{1,0:T(8,128)(2,1)}, bf16[384,1536]{1,0:T(8,128)(2,1)}, u32[]{:S(2)}, u32[]{:S(2)}) collective-permute-start(bf16[384,1536]{1,0:T(8,128)(2,1)} %slice_bitcast_fusion), channel_id=1, source_target_pairs={{0,2},{2,0},{1,3},{3,1},{4,6},{6,4},{5,7},{7,5},{8,10},{10,8},{9,1... | collective-permute-start | bytes 3538952 | tf_op jit(solution)/shard_map/ppermute | solution.py:20
  350.1 9.6 %collective-permute-start.2 = (bf16[384,1536]{1,0:T(8,128)(2,1)}, bf16[384,1536]{1,0:T(8,128)(2,1)S(1)}, u32[]{:S(2)}, u32[]{:S(2)}) collective-permute-start(bf16[384,1536]{1,0:T(8,128)(2,1)} %collective-permute-done), channel_id=1, source_target_pairs={{0,1},{1,0},{2,3},{3,2},{4,5},{5,4},{6,7},{7,6},{8,9},{9,8},{10,11... | collective-permute-start | bytes 3538952 | tf_op jit(solution)/shard_map/ppermute | solution.py:20
  358.3 34.2 %collective-permute-start.5 = (f32[384,1536]{1,0:T(8,128)S(1)}, f32[384,1536]{1,0:T(8,128)S(1)}, u32[]{:S(2)}, u32[]{:S(2)}) collective-permute-start(f32[384,1536]{1,0:T(8,128)S(1)} %convolution_add_fusion.3), channel_id=1, source_target_pairs={{0,1},{1,0},{2,3},{3,2},{4,5},{5,4},{6,7},{7,6},{8,9},{9,8},{10,11... | collective-permute-start | bytes 7077896 | tf_op jit(solution)/shard_map/ppermute | solution.py:20
  378.9 20.9 %collective-permute-start.6 = (f32[384,1536]{1,0:T(8,128)S(1)}, f32[384,1536]{1,0:T(8,128)S(1)}, u32[]{:S(2)}, u32[]{:S(2)}) collective-permute-start(f32[384,1536]{1,0:T(8,128)S(1)} %convolution_add_fusion.1), channel_id=1, source_target_pairs={{0,1},{1,0},{2,3},{3,2},{4,5},{5,4},{6,7},{7,6},{8,9},{9,8},{10,11... | collective-permute-start | bytes 7077896 | tf_op jit(solution)/shard_map/ppermute | solution.py:20
  405.1 28.0 %collective-permute-start.7 = (bf16[384,1536]{1,0:T(8,128)(2,1)S(1)}, bf16[384,1536]{1,0:T(8,128)(2,1)S(1)}, u32[]{:S(2)}, u32[]{:S(2)}) collective-permute-start(bf16[384,1536]{1,0:T(8,128)(2,1)S(1)} %fusion.21), channel_id=1, source_target_pairs={{0,2},{2,0},{1,3},{3,1},{4,6},{6,4},{5,7},{7,5},{8,10},{10,8},{9,1... | collective-permute-start | bytes 3538952 | tf_op jit(solution)/shard_map/ppermute | solution.py:20
  414.0 53.0 %collective-permute-start.21 = (bf16[4,192,1536]{2,1,0:T(8,128)(2,1)S(1)}, bf16[4,192,1536]{2,1,0:T(8,128)(2,1)S(1)}, u32[]{:S(2)}, u32[]{:S(2)}) collective-permute-start(bf16[4,192,1536]{2,1,0:T(8,128)(2,1)S(1)} %dynamic-slice_bitcast_fusion.1), channel_id=1, source_target_pairs={{0,4},{4,0},{1,5},{5,1},{2,6},{6,2},{3,7},{7,3},{8,12},{12,8},{9,1... | collective-permute-start | bytes 7077896 | tf_op jit(solution)/shard_map/ppermute | solution.py:20
  437.0 5.8 collective-permute-start.8
  441.3 34.8 %collective-permute-start.3 = (f32[384,1536]{1,0:T(8,128)}, f32[384,1536]{1,0:T(8,128)}, u32[]{:S(2)}, u32[]{:S(2)}) collective-permute-start(f32[384,1536]{1,0:T(8,128)} %fusion.44), channel_id=1, source_target_pairs={{0,1},{1,0},{2,3},{3,2},{4,5},{5,4},{6,7},{7,6},{8,9},{9,8},{10,11... | collective-permute-start | bytes 7077896 | tf_op jit(solution)/shard_map/ppermute | solution.py:20
  469.0 168.7 %reduce-scatter.10.cloned.1.call-start = ((), (), s32[]{:S(2)}) async-start(), calls=%async_computation.7 | async-start | bytes 2949120 | tf_op jit(solution)/shard_map/reduce_scatter | solution.py:631
  475.6 23.9 %collective-permute-start.1 = (f32[384,1536]{1,0:T(8,128)}, f32[384,1536]{1,0:T(8,128)}, u32[]{:S(2)}, u32[]{:S(2)}) collective-permute-start(f32[384,1536]{1,0:T(8,128)} %fusion.55), channel_id=1, source_target_pairs={{0,1},{1,0},{2,3},{3,2},{4,5},{5,4},{6,7},{7,6},{8,9},{9,8},{10,11... | collective-permute-start | bytes 7077896 | tf_op jit(solution)/shard_map/ppermute | solution.py:20
  475.6 54.4 %collective-permute-start.17 = (bf16[4,192,1536]{2,1,0:T(8,128)(2,1)}, bf16[4,192,1536]{2,1,0:T(8,128)(2,1)}, u32[]{:S(2)}, u32[]{:S(2)}) collective-permute-start(bf16[4,192,1536]{2,1,0:T(8,128)(2,1)} %dynamic-slice_bitcast_fusion.2), channel_id=1, source_target_pairs={{0,4},{4,0},{1,5},{5,1},{2,6},{6,2},{3,7},{7,3},{8,12},{12,8},{9,1... | collective-permute-start | bytes 7077896 | tf_op jit(solution)/shard_map/ppermute | solution.py:20
  482.6 28.1 %collective-permute-start.4 = (bf16[384,1536]{1,0:T(8,128)(2,1)}, bf16[384,1536]{1,0:T(8,128)(2,1)}, u32[]{:S(2)}, u32[]{:S(2)}) collective-permute-start(bf16[384,1536]{1,0:T(8,128)(2,1)} %fusion.23), channel_id=1, source_target_pairs={{0,2},{2,0},{1,3},{3,1},{4,6},{6,4},{5,7},{7,5},{8,10},{10,8},{9,1... | collective-permute-start | bytes 3538952 | tf_op jit(solution)/shard_map/ppermute | solution.py:20
  486.9 47.9 %collective-permute-start.9 = (f32[384,1536]{1,0:T(8,128)}, f32[384,1536]{1,0:T(8,128)}, u32[]{:S(2)}, u32[]{:S(2)}) collective-permute-start(f32[384,1536]{1,0:T(8,128)} %fusion.61), channel_id=1, source_target_pairs={{0,1},{1,0},{2,3},{3,2},{4,5},{5,4},{6,7},{7,6},{8,9},{9,8},{10,11... | collective-permute-start | bytes 7077896 | tf_op jit(solution)/shard_map/ppermute | solution.py:20
  498.2 99.7 %collective-permute-start.19 = (bf16[4,192,1536]{2,1,0:T(8,128)(2,1)}, bf16[4,192,1536]{2,1,0:T(8,128)(2,1)}, u32[]{:S(2)}, u32[]{:S(2)}) collective-permute-start(bf16[4,192,1536]{2,1,0:T(8,128)(2,1)} %dynamic-slice_bitcast_fusion), channel_id=1, source_target_pairs={{0,4},{4,0},{1,5},{5,1},{2,6},{6,2},{3,7},{7,3},{8,12},{12,8},{9,1... | collective-permute-start | bytes 7077896 | tf_op jit(solution)/shard_map/ppermute | solution.py:20
  534.5 289.8 %reduce-scatter.12.cloned.1.call-start = ((), (), s32[]{:S(2)}) async-start(), calls=%async_computation.8 | async-start | bytes 2949120 | tf_op jit(solution)/shard_map/reduce_scatter | solution.py:631
  541.9 13.6 %collective-permute-start.10 = (bf16[384,1536]{1,0:T(8,128)(2,1)S(1)}, bf16[384,1536]{1,0:T(8,128)(2,1)}, u32[]{:S(2)}, u32[]{:S(2)}) collective-permute-start(bf16[384,1536]{1,0:T(8,128)(2,1)S(1)} %get-tuple-element.135), channel_id=1, source_target_pairs={{0,1},{1,0},{2,3},{3,2},{4,5},{5,4},{6,7},{7,6},{8,9},{9,8},{10,11... | collective-permute-start | bytes 3538952 | tf_op jit(solution)/shard_map/ppermute | solution.py:20
  545.4 52.4 %collective-permute-start.15 = (bf16[8,96,768]{2,1,0:T(8,128)(2,1)}, bf16[8,96,768]{2,1,0:T(8,128)(2,1)}, u32[]{:S(2)}, u32[]{:S(2)}) collective-permute-start(bf16[8,96,768]{2,1,0:T(8,128)(2,1)} %dynamic-slice_bitcast_fusion.3), channel_id=1, source_target_pairs={{0,2},{2,0},{1,3},{3,1},{4,6},{6,4},{5,7},{7,5},{8,10},{10,8},{9,1... | collective-permute-start | bytes 3538952 | tf_op jit(solution)/shard_map/ppermute | solution.py:20
  550.4 65.9 %collective-permute-start.13 = (bf16[8,96,768]{2,1,0:T(8,128)(2,1)}, bf16[8,96,768]{2,1,0:T(8,128)(2,1)}, u32[]{:S(2)}, u32[]{:S(2)}) collective-permute-start(bf16[8,96,768]{2,1,0:T(8,128)(2,1)} %dynamic-slice_bitcast_fusion.4), channel_id=1, source_target_pairs={{0,2},{2,0},{1,3},{3,1},{4,6},{6,4},{5,7},{7,5},{8,10},{10,8},{9,1... | collective-permute-start | bytes 3538952 | tf_op jit(solution)/shard_map/ppermute | solution.py:20
  604.0 55.2 %collective-permute-start.16 = (bf16[4,96,768]{2,1,0:T(8,128)(2,1)}, bf16[4,96,768]{2,1,0:T(8,128)(2,1)}, u32[]{:S(2)}, u32[]{:S(2)}) collective-permute-start(bf16[4,96,768]{2,1,0:T(8,128)(2,1)} %dynamic-slice_bitcast_fusion.5), channel_id=1, source_target_pairs={{0,4},{4,0},{1,5},{5,1},{2,6},{6,2},{3,7},{7,3},{8,12},{12,8},{9,1... | collective-permute-start | bytes 1769480 | tf_op jit(solution)/shard_map/ppermute | solution.py:20
  608.2 217.9 %reduce-scatter.8.cloned.1.call-start = ((), (), s32[]{:S(2)}) async-start(), calls=%async_computation.6 | async-start | bytes 737280 | tf_op jit(solution)/shard_map/reduce_scatter | solution.py:617
  616.3 33.2 %collective-permute-start.11 = (f32[384,1536]{1,0:T(8,128)}, f32[384,1536]{1,0:T(8,128)}, u32[]{:S(2)}, u32[]{:S(2)}) collective-permute-start(f32[384,1536]{1,0:T(8,128)} %fusion.35), channel_id=1, source_target_pairs={{0,1},{1,0},{2,3},{3,2},{4,5},{5,4},{6,7},{7,6},{8,9},{9,8},{10,11... | collective-permute-start | bytes 7077896 | tf_op jit(solution)/shard_map/ppermute | solution.py:20
  620.1 44.7 %collective-permute-start.14 = (bf16[4,96,768]{2,1,0:T(8,128)(2,1)}, bf16[4,96,768]{2,1,0:T(8,128)(2,1)}, u32[]{:S(2)}, u32[]{:S(2)}) collective-permute-start(bf16[4,96,768]{2,1,0:T(8,128)(2,1)} %dynamic-slice_bitcast_fusion.6), channel_id=1, source_target_pairs={{0,4},{4,0},{1,5},{5,1},{2,6},{6,2},{3,7},{7,3},{8,12},{12,8},{9,1... | collective-permute-start | bytes 1769480 | tf_op jit(solution)/shard_map/ppermute | solution.py:20
  632.1 9.2 %collective-permute-start.22 = (bf16[96,1536]{1,0:T(8,128)(2,1)S(1)}, bf16[96,1536]{1,0:T(8,128)(2,1)S(1)}, u32[]{:S(2)}, u32[]{:S(2)}) collective-permute-start(bf16[96,1536]{1,0:T(8,128)(2,1)S(1)} %dynamic-slice_bitcast_fusion.7), channel_id=1, source_target_pairs={{0,2},{2,0},{1,3},{3,1},{4,6},{6,4},{5,7},{7,5},{8,10},{10,8},{9,1... | collective-permute-start | bytes 884744 | tf_op jit(solution)/shard_map/ppermute | solution.py:20
  638.8 8.8 %collective-permute-start.18 = (bf16[96,1536]{1,0:T(8,128)(2,1)S(1)}, bf16[96,1536]{1,0:T(8,128)(2,1)S(1)}, u32[]{:S(2)}, u32[]{:S(2)}) collective-permute-start(bf16[96,1536]{1,0:T(8,128)(2,1)S(1)} %dynamic-slice_bitcast_fusion.9), channel_id=1, source_target_pairs={{0,2},{2,0},{1,3},{3,1},{4,6},{6,4},{5,7},{7,5},{8,10},{10,8},{9,1... | collective-permute-start | bytes 884744 | tf_op jit(solution)/shard_map/ppermute | solution.py:20
  661.2 166.6 %reduce-scatter.6.cloned.1.call-start = ((), (), s32[]{:S(2)}) async-start(), calls=%async_computation.5 | async-start | bytes 737280 | tf_op jit(solution)/shard_map/reduce_scatter | solution.py:617
  668.9 8.8 %collective-permute-start.12 = (f32[6,16,96]{2,0,1:T(8,128)}, f32[6,16,96]{2,0,1:T(8,128)}, u32[]{:S(2)}, u32[]{:S(2)}) collective-permute-start(f32[6,16,96]{2,0,1:T(8,128)} %stack.55), channel_id=1, source_target_pairs={{0,1},{1,0},{2,3},{3,2},{4,5},{5,4},{6,7},{7,6},{8,9},{9,8},{10,11... | collective-permute-start | bytes 110600 | tf_op jit(solution)/shard_map/ppermute | solution.py:20
  679.2 140.1 %copy-start.41 = (bf16[48,768]{1,0:T(8,128)(2,1)S(1)}, bf16[48,768]{1,0:T(8,128)(2,1)}, u32[]{:S(2)}) copy-start(bf16[48,768]{1,0:T(8,128)(2,1)} %refs_6_.1) | copy-start | bytes 221188
  679.2 144.2 %copy-start.38 = (bf16[96,768]{1,0:T(8,128)(2,1)S(1)}, bf16[96,768]{1,0:T(8,128)(2,1)}, u32[]{:S(2)}) copy-start(bf16[96,768]{1,0:T(8,128)(2,1)} %refs_1_.1) | copy-start | bytes 442372
  679.2 144.2 %copy-start.39 = (bf16[96,768]{1,0:T(8,128)(2,1)S(1)}, bf16[96,768]{1,0:T(8,128)(2,1)}, u32[]{:S(2)}) copy-start(bf16[96,768]{1,0:T(8,128)(2,1)} %refs_2_.1) | copy-start | bytes 442372
  679.2 144.2 %copy-start.40 = (bf16[96,768]{1,0:T(8,128)(2,1)S(1)}, bf16[96,768]{1,0:T(8,128)(2,1)}, u32[]{:S(2)}) copy-start(bf16[96,768]{1,0:T(8,128)(2,1)} %refs_5_.1) | copy-start | bytes 442372
  825.4 6.8 collective-permute-start.20
  (90 other events, 695.0 us)
Sparse Core Ops, SparseCore 0:
  469.2 48.9 reduce-scatter.13
  534.6 48.9 reduce-scatter.9
  608.4 50.4 reduce-scatter.11
  661.4 23.1 reduce-scatter.7
  687.3 27.3 reduce-scatter.5

commit v9 on v8

--- a/solution.py
+++ b/solution.py
@@ -509,22 +509,123 @@
             move.sent()
 
 
-def scatter_kernel(zs, orders, *refs):
+class LastNorm:
+    def __init__(self, lanes, given, held, out, local_sems):
+        grad_hbm, weight_hbm, self.inputs, self.stream, self.gain, self.others = given
+        (
+            self.grad, self.weight, self.send, self.got, self.normed,
+            self.rows8, self.got8, self.tall, self.blocks,
+        ) = held
+        self.out, self.zs = out, lanes.zs
+        mate = {"tensor": 1 - lax.axis_index("tensor")}
+        self.loads = [
+            pltpu.make_async_copy(grad_hbm, self.grad, local_sems.at[0]),
+            pltpu.make_async_copy(weight_hbm, self.weight, local_sems.at[1]),
+        ]
+        self.mate_part = Move(lanes.copy(self.send, self.got, mate), None, None)
+        self.mate_rows = Move(lanes.copy(self.rows8, self.got8, mate), None, None)
+
+    def pieces(self):
+        rows, width = self.out.shape
+        tile = 128 if rows % 128 == 0 else rows
+        chunk = width // self.zs
+
+        def over(body):
+            @pl.loop(0, rows // tile)
+            def _(i):
+                body(pl.multiple_of(i * tile, tile))
+
+        def part_of(first, zz):
+            weight = self.weight[zz].reshape(chunk, self.weight.shape[-1])
+            return nt(self.grad[pl.ds(first, tile), :], weight)
+
+        self.loads[0].wait()
+        self.loads[1].wait()
+        for zz in range(self.zs):
+            cols = slice(zz * chunk, (zz + 1) * chunk)
+
+            def body(at):
+                made = part_of(pl.multiple_of(rows + at, tile), zz)
+                self.send[pl.ds(at, tile), cols] = made.astype(BF)
+
+            over(body)
+            yield
+        self.mate_part.start()
+        for zz in range(self.zs):
+            cols = slice(zz * chunk, (zz + 1) * chunk)
+
+            def body(at):
+                self.normed[pl.ds(at, tile), cols] = part_of(at, zz)
+
+            over(body)
+            yield
+        self.mate_part.arrived()
+        self.rows8[...] = self.others[...]
+
+        def body(at):
+            part = pl.ds(at, tile)
+            incoming = self.normed[part, :] + self.got[part, :].astype(F32)
+            stream = self.inputs[part, :].astype(F32)
+            centred = stream - jnp.mean(stream, axis=-1, keepdims=True)
+            inverse = lax.rsqrt(jnp.mean(centred * centred, axis=-1, keepdims=True) + EPSILON)
+            unit = centred * inverse
+            scaled = incoming * self.gain[...]
+            slope = scaled - jnp.mean(scaled, axis=-1, keepdims=True)
+            slope = slope - unit * jnp.mean(scaled * unit, axis=-1, keepdims=True)
+            self.out[part, :] = self.stream[part, :] + inverse * slope
+            self.rows8[0:1, :] += jnp.sum(incoming * unit, axis=0, keepdims=True)
+            self.rows8[1:2, :] += jnp.sum(incoming, axis=0, keepdims=True)
+
+        over(body)
+        self.mate_rows.start()
+        self.tall[...] = jnp.zeros_like(self.tall)
+        yield
+        self.mate_rows.arrived()
+        self.tall[0:8, :] = self.rows8[...] + self.got8[...]
+        turned = jnp.transpose(self.tall[...]).astype(BF)
+        self.blocks[...] = turned.reshape(self.blocks.shape)
+        yield
+
+    def finish(self):
+        self.mate_part.sent()
+        self.mate_rows.sent()
+
+
+def scatter_kernel(zs, orders, fused, *refs):
+    refs = list(refs)
+
+    def take(number):
+        taken = refs[:number]
+        del refs[:number]
+        return taken
+
     count = len(orders)
-    parts, crest_in, refs = refs[:count], refs[count], refs[count + 1 :]
-    outs, crest_out, rest = refs[:count], refs[count], list(refs[count + 1 :])
-    send_sems, recv_sems = rest[:2]
-    rest = rest[2:]
+    parts = take(count - 1 if fused else count)
+    crest_in = take(1)[0]
+    given = take(6) if fused else None
+    outs = take(count)
+    crest_out = take(1)[0]
+    norm_out = take(1)[0] if fused else None
+    send_sems, recv_sems, local_sems = take(3)
     lanes = Lanes(send_sems, recv_sems, None, zs)
-    greet(zs)
+    norm = None
+    pieces = iter(())
+    if fused:
+        norm = LastNorm(lanes, given, take(9), norm_out, local_sems)
+        for load in norm.loads:
+            load.start()
+        parts = [norm.blocks] + parts
+        pieces = norm.pieces()
+    greet(zs, fused)
     full, zfirst = [], []
     for i, order in enumerate(orders):
-        held, rest = rest[:5], rest[5:]
+        held = take(5)
         if order == "z":
             zfirst.append(ScatterZ(lanes, parts[i], held, outs[i]))
         else:
             full.append(Scatter(lanes, parts[i], held, outs[i], order))
-    crest = Crest(lanes, crest_in, rest[0], crest_out)
+    late = [zfirst.pop(0)] if fused else []
+    crest = Crest(lanes, crest_in, take(1)[0], crest_out)
     crest.one.start()
     order = ends_first(zs)
     for i in range(zs + 3):
@@ -536,49 +637,89 @@
         if i < zs:
             for item in zfirst:
                 item.pass_on(order[i])
+        for _ in range((0, 4, 4, 1, 1)[i] if i < 5 else 0):
+            next(pieces, None)
         for item in full:
             if 2 <= i < zs + 2:
                 item.second(order[i - 2])
         if i == zs:
             for item in zfirst:
                 item.total()
+            for _ in pieces:
+                pass
+            for item in late:
+                for d in order:
+                    item.pass_on(d)
         for item in full:
             if 3 <= i:
                 item.third(order[i - 3])
+    for item in late:
+        item.total()
     crest.finish()
-    for item in zfirst:
+    for item in zfirst + late:
         item.after()
     for item in full:
         item.finish()
-    for item in zfirst:
+    for item in zfirst + late:
         item.finish()
-
-
-def scatter_all(parts, orders, crest, zs):
+    if fused:
+        norm.finish()
+
+
+def scatter_all(parts, orders, crest, zs, given=None):
     scratch, moves = [], 4
-    for part, order in zip(parts, orders):
-        block = part.shape[3:]
+    shapes_in = [(part.shape, part.dtype) for part in parts]
+    extra_in, extra_out = [], []
+    vmem = pl.BlockSpec(memory_space=pltpu.VMEM)
+    specs = [vmem] * (len(parts) + 1)
+    if given is not None:
+        grad, weight, inputs = given[:3]
+        rows, width = inputs.shape
+        blocks = (zs, 2, 2, weight.shape[3], 128)
+        shapes_in = [(blocks, BF)] + shapes_in
+        extra_in = list(given)
+        extra_out = [jax.ShapeDtypeStruct((rows, width), F32)]
+        hbm = pl.BlockSpec(memory_space=pltpu.HBM)
+        specs += [hbm, hbm] + [vmem] * 4
+        moves += 2
+        scratch += [
+            pltpu.VMEM(grad.shape, grad.dtype),
+            pltpu.VMEM(weight.shape, weight.dtype),
+            pltpu.VMEM((rows, width), BF),
+            pltpu.VMEM((rows, width), BF),
+            pltpu.VMEM((rows, width), F32),
+            pltpu.VMEM((8, width), F32),
+            pltpu.VMEM((8, width), F32),
+            pltpu.VMEM((128, width), F32),
+            pltpu.VMEM(blocks, BF),
+        ]
+    for (shape, dtype), order in zip(shapes_in, orders):
+        block = shape[3:]
         if order == "z":
             shapes = [(zs, 2, 2) + block] * 2 + [(2, 2) + block, (2,) + block, block]
             moves += 2 * zs + 2
         else:
             shapes = [(zs, 2) + block] + [(zs,) + block] * 4
             moves += 5 * zs
-        scratch += [pltpu.VMEM(shape, part.dtype) for shape in shapes]
-    vmem = pl.BlockSpec(memory_space=pltpu.VMEM)
+        scratch += [pltpu.VMEM(shape, dtype) for shape in shapes]
+    outs = [jax.ShapeDtypeStruct(shape[3:], F32) for shape, _ in shapes_in]
+    outs += [jax.ShapeDtypeStruct(crest.shape, F32)] + extra_out
     return pl.pallas_call(
-        functools.partial(scatter_kernel, zs, orders),
-        out_shape=[jax.ShapeDtypeStruct(part.shape[3:], F32) for part in parts]
-        + [jax.ShapeDtypeStruct(crest.shape, F32)],
-        in_specs=[vmem] * (len(parts) + 1),
-        out_specs=[vmem] * (len(parts) + 1),
-        scratch_shapes=[pltpu.SemaphoreType.DMA((moves,)), pltpu.SemaphoreType.DMA((moves,))]
+        functools.partial(scatter_kernel, zs, orders, given is not None),
+        out_shape=outs,
+        in_specs=specs,
+        out_specs=[vmem] * len(outs),
+        scratch_shapes=[
+            pltpu.SemaphoreType.DMA((moves,)),
+            pltpu.SemaphoreType.DMA((moves,)),
+            pltpu.SemaphoreType.DMA((2,)),
+        ]
         + scratch
         + [pltpu.VMEM((8,) + crest.shape, F32)],
         compiler_params=pltpu.CompilerParams(
-            collective_id=2, has_side_effects=True, vmem_limit_bytes=56 * 2**20
+            collective_id=2, has_side_effects=True, vmem_limit_bytes=62 * 2**20
         ),
-    )(*parts, crest)
+    )(*parts, crest, *extra_in)
 
 
 def nn(left, right):
@@ -603,7 +744,8 @@
         held = tn(left, right).astype(BF)
         self.held = held.reshape(2 * zs, 2, -1, held.shape[1])
         self.x, self.y = lax.axis_index("x"), lax.axis_index("y")
-        self.got = swap(pick(self.held, 1 - self.x, 1), "x")
+        self.sent = pick(self.held, 1 - self.x, 1)
+        self.got = swap(self.sent, "x")
 
     def second(self, *others):
         got = after(self.got, others)
@@ -1480,7 +1622,7 @@
     grad_full = pair_rows(grad_stream.astype(BF))
     up_pair = PairSum(after(normed_feed, grad_full), grad_upward, zs)
     cross_output_sum = FullSum(grad_full, mixed_cross, zs)
-    grad_mixed = nn(grad_full, cross_out_t).astype(BF)
+    grad_mixed = after(nn(grad_full, cross_out_t).astype(BF), cross_output_sum.sent)
     grad_query, grad_keys, grad_values = attend_back(
         query_cross, taken_cross, taken_cross, grad_mixed, cross_bias_row[:, None], (0, 0, pairs), None
     )
@@ -1494,57 +1636,85 @@
     grad_stream = grad_stream + stream_part
     grad_full = pair_rows(grad_stream.astype(BF))
     gate_pair.second(grad_full)
+    cross_output_sum.second(grad_full)
     part_self_output = tn(grad_full, mixed_self)
-    grad_mixed = nn(grad_full, self_out_t).astype(BF)
+    grad_mixed = after(nn(grad_full, self_out_t).astype(BF), cross_query_sum.sent)
     grad_parts = attend_back(
         taken, taken, taken, grad_mixed, self_bias_row[:, None], (0, pairs, 2 * pairs), turns
     )
     grad_in = jnp.concatenate(grad_parts, axis=1)
     up_pair.second(grad_in)
-    cross_output_sum.second(grad_in)
     cross_query_sum.second(grad_in)
+    sum_cross_output = cross_output_sum.third(grad_in).astype(F32)
     part_in = tn(normed_self, grad_in[:, : 2 * inner]).astype(BF)
     part_value = tn(normed_self, grad_parts[2]).astype(BF)
-    grad_normed = spread_pair(grad_in, in_weight)
-    sum_cross_output = cross_output_sum.third(grad_normed).astype(F32)
-    sum_cross_query = cross_query_sum.third(grad_normed).astype(F32)
-    unit_self, inverse_self = unit_rows_of(stream)
-    stream_part, grad_self_gain, grad_self_bias = norm_backward(
-        grad_normed, unit_self, inverse_self, norms[0]
-    )
-    grad_stream = grad_stream + stream_part
-
-    vector_sums = jnp.stack(
-        [
-            grad_self_gain,
-            grad_self_bias,
-            grad_cross_gain,
-            grad_cross_bias,
-            grad_feed_gain,
-            grad_feed_bias,
-        ]
-    ).reshape(6, -1, shard_rows)
-    vector_sums = vector_sums + swap(vector_sums, "tensor")
-    vector_sums = jnp.pad(
-        vector_sums.transpose(1, 0, 2), ((0, 0), (0, 2), (0, 128 - shard_rows))
-    ).reshape(zs, 2, 2, 8, 128)
-
+    sum_cross_query = cross_query_sum.third(part_value).astype(F32)
     def blocks(part):
         return part.astype(BF).reshape(zs, 2, 2, -1, part.shape[1])
 
-    vector_sums, sum_in, sum_value, sum_self_output, sum_memory, crest = scatter_all(
-        [
-            vector_sums,
-            blocks(part_in),
-            blocks(part_value),
-            blocks(part_self_output),
-            blocks(part_memory),
-        ],
-        ["z", "x", "y", "y", "z"],
-        crest,
-        zs,
-    )
-    vector_sums = vector_sums[:, :shard_rows]
+    if shard_rows % 32 == 0:
+        none = jnp.zeros_like(grad_feed_gain)
+        other_sums = jnp.stack(
+            [none, none, grad_cross_gain, grad_cross_bias, grad_feed_gain, grad_feed_bias, none, none]
+        )
+        vector_sums, sum_in, sum_value, sum_self_output, sum_memory, crest, grad_stream = (
+            scatter_all(
+                [
+                    blocks(part_in),
+                    blocks(part_value),
+                    blocks(part_self_output),
+                    blocks(part_memory),
+                ],
+                ["z", "x", "y", "y", "z"],
+                crest,
+                zs,
+                (
+                    grad_in,
+                    in_weight.reshape(zs, 2, 2, shard_rows, -1),
+                    inputs,
+                    grad_stream,
+                    norms[:1],
+                    other_sums,
+                ),
+            )
+        )
+        vector_sums = vector_sums.T
+    else:
+        grad_normed = spread_pair(grad_in, in_weight)
+        unit_self, inverse_self = unit_rows_of(stream)
+        stream_part, grad_self_gain, grad_self_bias = norm_backward(
+            grad_normed, unit_self, inverse_self, norms[0]
+        )
+        grad_stream = grad_stream + stream_part
+
+        vector_sums = jnp.stack(
+            [
+                grad_self_gain,
+                grad_self_bias,
+                grad_cross_gain,
+                grad_cross_bias,
+                grad_feed_gain,
+                grad_feed_bias,
+            ]
+        ).reshape(6, -1, shard_rows)
+        vector_sums = vector_sums + swap(vector_sums, "tensor")
+        vector_sums = jnp.pad(
+            vector_sums.transpose(1, 0, 2), ((0, 0), (0, 2), (0, 128 - shard_rows))
+        ).reshape(zs, 2, 2, 8, 128)
+
+        vector_sums, sum_in, sum_value, sum_self_output, sum_memory, crest = scatter_all(
+            [
+                vector_sums,
+                blocks(part_in),
+                blocks(part_value),
+                blocks(part_self_output),
+                blocks(part_memory),
+            ],
+            ["z", "x", "y", "y", "z"],
+            crest,
+            zs,
+        )
+        vector_sums = vector_sums[:, :shard_rows]
     peaks = crest[0, :heads_here]
     factor = jnp.sqrt(threshold[0] / jnp.maximum(peaks, threshold[0]))
     columns = jnp.repeat(factor, HEAD_DIM)[None, :]

time: 847 us -> 903 us (1.066)
  waiting for transfers between devices: 43.8 us -> 126 us
  other arithmetic: 59.6 us -> 40.3 us
  matrix products: 182 us -> 169 us
    ppermute x23 -> x21, waiting for transfers between devices: 43.8 us -> 126 us  [swap(): return lax.ppermute(value, axis, [(0, 1), (1, 0)])]
    dot_general x16 -> x14, matrix products: 79.2 us -> 66.3 us  [nt(): lax.dot_general(left, right, (((1,), (1,)), ((), ())), preferred_element_...]
  transfers between devices with their start and end apart: 28 -> 26, of which waited for: 7 -> 10; matrix products, arithmetic and copies ran while one was open for 31% -> 26% of each run, Pallas kernels for 23% -> 22%
where the time goes in v9:
time: 903 us; the launch traced here: 898 us
  Pallas kernels  478 us (53%)
  matrix products  169 us (19%)
  waiting for transfers between devices  126 us (14%)
  local copies, waits for them, and re-layouts  56 us (6%)
  other arithmetic  40.3 us (4%)
  between operations  16.5 us (2%)
  starting transfers between devices  12.4 us (1%)
    pallas_call x1, Pallas kernels, forward(): pl.pallas_call(functools.partial(forward_kernel, zs), out_shape=spread +...  285 us
    pallas_call x1, Pallas kernels, scatter_all(): pl.pallas_call(functools.partial(scatter_kernel, zs, orders, given is not...  140 us
    ppermute x21, waiting for transfers between devices, swap(): return lax.ppermute(value, axis, [(0, 1), (1, 0)])  126 us
    dot_general x14, matrix products, nt(): lax.dot_general(left, right, (((1,), (1,)), ((), ())), preferred_element_...  66.3 us
    dot_general x8, matrix products, nn(): lax.dot_general(left, right, (((1,), (0,)), ((), ())), preferred_element_...  55.1 us
    pallas_call x2, Pallas kernels, attend_back(): pl.pallas_call(functools.partial(attend_back_kernel, turns is not None),...  53.3 us
    dot_general x9, matrix products, tn(): lax.dot_general(left, right, (((0,), (0,)), ((), ())), preferred_element_...  47.2 us
  transfers between devices with their start and end apart: 26, of which 10 were waited for; matrix products, arithmetic and copies ran while one was open for 26% of the time, Pallas kernels for 22%

profile of v9, /device:TPU:0, one launch (start us, length us, event | category | flops | bytes accessed | tf_op | source)
XLA Modules:
  0.0 898.0 jit_solution(9076914655995988161)
XLA Ops:
  17.0 284.7 %shard_map.406 = (bf16[4,2,2,96,2432]{4,3,2,1,0:T(8,128)(2,1)}, bf16[4,2,2,96,1536]{4,3,2,1,0:T(8,128)(2,1)}, bf16[4,2,2,96,1536]{4,3,2,1,0:T(8,128)(2,1)}, bf16...) custom-call(bf16[96,128]{1,0:T(8,128)(2,1)} %pad.12.refs_0_, ...), custom_call_target="tpu_custom_call" | custom-call | flops 16307453952 | bytes 100000000 | tf_op jit(solution)/shard_map/pallas_call | solution.py:1380
  305.7 7.9 fusion.65
  313.6 5.6 fusion.64
  323.7 11.4 %multiply_convert_fusion.3 = (bf16[768,1536]{1,0:T(8,128)(2,1)}, bf16[768,1536]{1,0:T(8,128)(2,1)}, bf16[768,1536]{1,0:T(8,128)(2,1)}) fusion(f32[768,1536]{1,0:T(8,128)} %fusion.64, f32[768,1536]{1,0:T(8,128)} %fusion.65, bf16[768,1536]{1,0:T(8,128)(2,1)S(1)} %bitcast.181, bf16[1536,1536]{1,0:T(8,128)(2,1)} %bitcast.204), kind=kOutput, calls=%fused_computation.24 | convolution fusion | flops 3642753024 | bytes 23592960 | tf_op jit(solution)/shard_map/dot_general | solution.py:726
  337.8 9.2 %fusion.67 = f32[768,1536]{1,0:T(8,128)} fusion(bf16[768,1536]{1,0:T(8,128)(2,1)} %bitcast.179, bf16[1536,1536]{1,0:T(8,128)(2,1)} %bitcast.205), kind=kOutput, calls=%fused_computation.175 | convolution fusion | flops 3623878656 | bytes 11796480 | tf_op jit(solution)/shard_map/dot_general | solution.py:726
  348.3 4.9 fusion.35
  355.5 5.5 fusion.66
  361.0 10.6 %multiply_convert_fusion = (bf16[768,1536]{1,0:T(8,128)(2,1)S(1)}, bf16[768,1536]{1,0:T(8,128)(2,1)S(1)}, bf16[768,1536]{1,0:T(8,128)(2,1)}) fusion(f32[768,1536]{1,0:T(8,128)} %fusion.67, f32[768,1536]{1,0:T(8,128)} %fusion.66, bf16[768,1536]{1,0:T(8,128)(2,1)S(1)} %constant_dynamic-update-slice_fusion, bf16[1536,1536]{1,0:T(8,128)(2,1)} %bitcast.218), kind=kOutput, calls=%fused_computation.20 | convolution fusion | flops 3642753024 | bytes 23592960 | tf_op jit(solution)/shard_map/dot_general | solution.py:726
  371.7 6.1 fusion.25
  387.7 7.2 fusion.14
  399.4 9.3 %convolution_convert_fusion.2 = bf16[1536,1536]{1,0:T(8,128)(2,1)S(1)} fusion(bf16[1536,1536]{1,0:T(8,128)(2,1)S(1)} %bitcast.168, bf16[768,1536]{1,0:T(8,128)(2,1)} %get-tuple-element.148, bf16[768,1536]{1,0:T(8,128)(2,1)S(1)} %copy-done.64), kind=kOutput, calls=%fused_computation.2 | convolution fusion | flops 7259553792 | bytes 14155776 | tf_op jit(solution)/shard_map/dot_general | solution.py:734
  414.1 7.9 convolution_convert_fusion.3
  441.7 16.8 %shard_map.407 = (bf16[768,768]{1,0:T(8,128)(2,1)S(1)}, bf16[256,768]{1,0:T(8,128)(2,1)S(1)}, bf16[256,768]{1,0:T(8,128)(2,1)S(1)}) custom-call(bf16[768,768]{1,0:T(8,128)(2,1)S(1)} %copy-done.8, bf16[256,1536]{1,0:T(8,128)(2,1)S(1)} %copy-done.9, bf16[256,1536]{1,0:T(8,128)(2,1)S(1)} %copy-done.9, bf16[768,768]{1,0:T(8,128)(2,1)S(1)} %convolution_convert_fusion.10.g_ref, ...), custom_call_target="tpu_custom_call" | custom-call | flops 3019898880 | bytes 6291456 | tf_op jit(solution)/shard_map/pallas_call | solution.py:952
  469.8 15.6 %collective-permute-done.19 = bf16[4,192,1536]{2,1,0:T(8,128)(2,1)} collective-permute-done((bf16[4,192,1536]{2,1,0:T(8,128)(2,1)}, bf16[4,192,1536]{2,1,0:T(8,128)(2,1)}, u32[]{:S(2)}, u32[]{:S(2)}) %collective-permute-start.19) | collective-permute-done | bytes 2359328 | tf_op jit(solution)/shard_map/ppermute | solution.py:20
  485.4 4.4 fusion.9
  489.9 4.7 multiply_reduce_fusion.1
  498.6 8.0 convolution_convert_fusion.1
  513.6 20.7 %collective-permute-done.13 = bf16[8,96,768]{2,1,0:T(8,128)(2,1)S(1)} collective-permute-done((bf16[8,96,768]{2,1,0:T(8,128)(2,1)S(1)}, bf16[8,96,768]{2,1,0:T(8,128)(2,1)S(1)}, u32[]{:S(2)}, u32[]{:S(2)}) %collective-permute-start.13) | collective-permute-done | bytes 1179680 | tf_op jit(solution)/shard_map/ppermute | solution.py:20
  538.7 36.6 %shard_map.408 = (bf16[768,768]{1,0:T(8,128)(2,1)S(1)}, bf16[768,768]{1,0:T(8,128)(2,1)S(1)}, bf16[768,768]{1,0:T(8,128)(2,1)S(1)}) custom-call(bf16[768,2304]{1,0:T(8,128)(2,1)} %get-tuple-element.83.q_ref.k_ref.v_ref, bf16[768,2304]{1,0:T(8,128)(2,1)} %get-tuple-element.83.q_ref.k_ref.v_ref, bf16[768,2304]{1,0:T(8,128)(2,1)} %get-tuple-element.83.q_ref.k_ref.v_ref, ...), custom_call_target="tpu_custom_call" | custom-call | flops 9059696640 | bytes 9437184 | tf_op jit(solution)/shard_map/pallas_call | solution.py:952
  579.9 4.4 fusion.10
  584.7 6.5 fusion.30
  592.3 19.2 %collective-permute-done.11 = bf16[8,96,768]{2,1,0:T(8,128)(2,1)S(1)} collective-permute-done((bf16[8,96,768]{2,1,0:T(8,128)(2,1)}, bf16[8,96,768]{2,1,0:T(8,128)(2,1)S(1)}, u32[]{:S(2)}, u32[]{:S(2)}) %collective-permute-start.11) | collective-permute-done | bytes 1179680 | tf_op jit(solution)/shard_map/ppermute | solution.py:20
  612.8 5.8 fusion.41
  622.1 35.6 %collective-permute-done.12 = bf16[4,96,768]{2,1,0:T(8,128)(2,1)S(1)} collective-permute-done((bf16[4,96,768]{2,1,0:T(8,128)(2,1)S(1)}, bf16[4,96,768]{2,1,0:T(8,128)(2,1)S(1)}, u32[]{:S(2)}, u32[]{:S(2)}) %collective-permute-start.12) | collective-permute-done | bytes 589856 | tf_op jit(solution)/shard_map/ppermute | solution.py:20
  659.1 6.5 fusion.18
  667.7 4.4 fusion.11
  672.2 21.3 %collective-permute-done.4 = bf16[384,1536]{1,0:T(8,128)(2,1)S(1)} collective-permute-done((bf16[384,1536]{1,0:T(8,128)(2,1)}, bf16[384,1536]{1,0:T(8,128)(2,1)S(1)}, u32[]{:S(2)}, u32[]{:S(2)}) %collective-permute-start.4) | collective-permute-done | bytes 1179680 | tf_op jit(solution)/shard_map/ppermute | solution.py:20
  693.4 7.3 fusion.17
  706.8 5.2 convolution_convert_fusion.5
  712.1 5.7 convolution_convert_fusion
  717.8 139.8 %shard_map.409 = (f32[96,128]{1,0:T(8,128)}, f32[96,1536]{1,0:T(8,128)}, f32[96,768]{1,0:T(8,128)}, f32[96,768]{1,0:T(8,128)}, f32[48,1536]{1,0:T(8,128)}, /*index=5*/f32[8,128]{1,0:T(8,128)}, f32[384,1536]{1,0:T(8,128)}) custom-call(bf16[4,2,2,96,1536]{4,3,2,1,0:T(8,128)(2,1)} %bitcast.173, bf16[4,2,2,96,768]{4,3,2,1,0:T(8,128)(2,1)} %bitcast.178, ...), custom_call_target="tpu_custom_call" | custom-call | tf_op jit(solution)/shard_map/pallas_call | solution.py:707
  866.2 7.4 collective-permute-done.20
  (344 shorter events, 135.5 us)
Async XLA Ops:
  7.2 856.1 %reduce-scatter.14.cloned.1.call-start = ((), (), s32[]{:S(2)}) async-start(), calls=%async_computation.9 | async-start | bytes 2949120 | tf_op jit(solution)/shard_map/reduce_scatter | solution.py:773
  304.2 42.8 %collective-permute-start = (bf16[384,1536]{1,0:T(8,128)(2,1)}, bf16[384,1536]{1,0:T(8,128)(2,1)S(1)}, u32[]{:S(2)}, u32[]{:S(2)}) collective-permute-start(bf16[384,1536]{1,0:T(8,128)(2,1)} %slice_bitcast_fusion), channel_id=1, source_target_pairs={{0,2},{2,0},{1,3},{3,1},{4,6},{6,4},{5,7},{7,5},{8,10},{10,8},{9,1... | collective-permute-start | bytes 3538952 | tf_op jit(solution)/shard_map/ppermute | solution.py:20
  347.0 8.4 collective-permute-start.2
  355.3 32.4 %collective-permute-start.5 = (f32[384,1536]{1,0:T(8,128)S(1)}, f32[384,1536]{1,0:T(8,128)S(1)}, u32[]{:S(2)}, u32[]{:S(2)}) collective-permute-start(f32[384,1536]{1,0:T(8,128)S(1)} %convolution_add_fusion.3), channel_id=1, source_target_pairs={{0,1},{1,0},{2,3},{3,2},{4,5},{5,4},{6,7},{7,6},{8,9},{9,8},{10,11... | collective-permute-start | bytes 7077896 | tf_op jit(solution)/shard_map/ppermute | solution.py:20
  379.8 15.0 %collective-permute-start.6 = (f32[384,1536]{1,0:T(8,128)S(1)}, f32[384,1536]{1,0:T(8,128)S(1)}, u32[]{:S(2)}, u32[]{:S(2)}) collective-permute-start(f32[384,1536]{1,0:T(8,128)S(1)} %convolution_add_fusion.1), channel_id=1, source_target_pairs={{0,1},{1,0},{2,3},{3,2},{4,5},{5,4},{6,7},{7,6},{8,9},{9,8},{10,11... | collective-permute-start | bytes 7077896 | tf_op jit(solution)/shard_map/ppermute | solution.py:20
  398.8 28.0 %collective-permute-start.7 = (bf16[384,1536]{1,0:T(8,128)(2,1)S(1)}, bf16[384,1536]{1,0:T(8,128)(2,1)S(1)}, u32[]{:S(2)}, u32[]{:S(2)}) collective-permute-start(bf16[384,1536]{1,0:T(8,128)(2,1)S(1)} %fusion.16), channel_id=1, source_target_pairs={{0,2},{2,0},{1,3},{3,1},{4,6},{6,4},{5,7},{7,5},{8,10},{10,8},{9,1... | collective-permute-start | bytes 3538952 | tf_op jit(solution)/shard_map/ppermute | solution.py:20
  430.5 2.8 collective-permute-start.8
  431.4 54.0 %collective-permute-start.19 = (bf16[4,192,1536]{2,1,0:T(8,128)(2,1)}, bf16[4,192,1536]{2,1,0:T(8,128)(2,1)}, u32[]{:S(2)}, u32[]{:S(2)}) collective-permute-start(bf16[4,192,1536]{2,1,0:T(8,128)(2,1)} %dynamic-slice_bitcast_fusion.1), channel_id=1, source_target_pairs={{0,4},{4,0},{1,5},{5,1},{2,6},{6,2},{3,7},{7,3},{8,12},{12,8},{9,1... | collective-permute-start | bytes 7077896 | tf_op jit(solution)/shard_map/ppermute | solution.py:20
  461.1 28.8 %collective-permute-start.9 = (f32[384,1536]{1,0:T(8,128)}, f32[384,1536]{1,0:T(8,128)}, u32[]{:S(2)}, u32[]{:S(2)}) collective-permute-start(f32[384,1536]{1,0:T(8,128)} %fusion.47), channel_id=1, source_target_pairs={{0,1},{1,0},{2,3},{3,2},{4,5},{5,4},{6,7},{7,6},{8,9},{9,8},{10,11... | collective-permute-start | bytes 7077896 | tf_op jit(solution)/shard_map/ppermute | solution.py:20
  489.8 384.9 %reduce-scatter.8.cloned.1.call-start = ((), (), s32[]{:S(2)}) async-start(), calls=%async_computation.6 | async-start | bytes 737280 | tf_op jit(solution)/shard_map/reduce_scatter | solution.py:759
  496.9 37.4 %copy-start.28 = (bf16[384,1536]{1,0:T(8,128)(2,1)}, bf16[384,1536]{1,0:T(8,128)(2,1)S(1)}, u32[]{:S(2)}) copy-start(bf16[384,1536]{1,0:T(8,128)(2,1)S(1)} %get-tuple-element.142) | copy-start | bytes 3538948
  497.0 16.7 %collective-permute-start.10 = (bf16[384,1536]{1,0:T(8,128)(2,1)S(1)}, bf16[384,1536]{1,0:T(8,128)(2,1)S(1)}, u32[]{:S(2)}, u32[]{:S(2)}) collective-permute-start(bf16[384,1536]{1,0:T(8,128)(2,1)S(1)} %get-tuple-element.142), channel_id=1, source_target_pairs={{0,1},{1,0},{2,3},{3,2},{4,5},{5,4},{6,7},{7,6},{8,9},{9,8},{10,11... | collective-permute-start | bytes 3538952 | tf_op jit(solution)/shard_map/ppermute | solution.py:20
  506.6 27.7 %collective-permute-start.13 = (bf16[8,96,768]{2,1,0:T(8,128)(2,1)S(1)}, bf16[8,96,768]{2,1,0:T(8,128)(2,1)S(1)}, u32[]{:S(2)}, u32[]{:S(2)}) collective-permute-start(bf16[8,96,768]{2,1,0:T(8,128)(2,1)S(1)} %copy-done.26), channel_id=1, source_target_pairs={{0,2},{2,0},{1,3},{3,1},{4,6},{6,4},{5,7},{7,5},{8,10},{10,8},{9,1... | collective-permute-start | bytes 3538952 | tf_op jit(solution)/shard_map/ppermute | solution.py:20
  509.8 70.0 %collective-permute-start.17 = (bf16[4,192,1536]{2,1,0:T(8,128)(2,1)}, bf16[4,192,1536]{2,1,0:T(8,128)(2,1)}, u32[]{:S(2)}, u32[]{:S(2)}) collective-permute-start(bf16[4,192,1536]{2,1,0:T(8,128)(2,1)} %dynamic-slice_bitcast_fusion), channel_id=1, source_target_pairs={{0,4},{4,0},{1,5},{5,1},{2,6},{6,2},{3,7},{7,3},{8,12},{12,8},{9,1... | collective-permute-start | bytes 7077896 | tf_op jit(solution)/shard_map/ppermute | solution.py:20
  537.8 41.0 %collective-permute-start.14 = (bf16[4,96,768]{2,1,0:T(8,128)(2,1)S(1)}, bf16[4,96,768]{2,1,0:T(8,128)(2,1)S(1)}, u32[]{:S(2)}, u32[]{:S(2)}) collective-permute-start(bf16[4,96,768]{2,1,0:T(8,128)(2,1)S(1)} %dynamic-slice_bitcast_fusion.5), channel_id=1, source_target_pairs={{0,4},{4,0},{1,5},{5,1},{2,6},{6,2},{3,7},{7,3},{8,12},{12,8},{9,1... | collective-permute-start | bytes 1769480 | tf_op jit(solution)/shard_map/ppermute | solution.py:20
  579.8 296.6 %reduce-scatter.12.cloned.1.call-start = ((), (), s32[]{:S(2)}) async-start(), calls=%async_computation.8 | async-start | bytes 2949120 | tf_op jit(solution)/shard_map/reduce_scatter | solution.py:773
  584.3 293.2 %reduce-scatter.6.cloned.1.call-start = ((), (), s32[]{:S(2)}) async-start(), calls=%async_computation.5 | async-start | bytes 737280 | tf_op jit(solution)/shard_map/reduce_scatter | solution.py:759
  584.3 27.2 %copy-start.23 = (bf16[1536,768]{1,0:T(8,128)(2,1)S(1)}, bf16[1536,768]{1,0:T(8,128)(2,1)}, u32[]{:S(2)}) copy-start(bf16[1536,768]{1,0:T(8,128)(2,1)} %copy-done.22) | copy-start | bytes 7077892
  584.3 27.2 %collective-permute-start.11 = (bf16[8,96,768]{2,1,0:T(8,128)(2,1)}, bf16[8,96,768]{2,1,0:T(8,128)(2,1)S(1)}, u32[]{:S(2)}, u32[]{:S(2)}) collective-permute-start(bf16[8,96,768]{2,1,0:T(8,128)(2,1)} %dynamic-slice_bitcast_fusion.3), channel_id=1, source_target_pairs={{0,2},{2,0},{1,3},{3,1},{4,6},{6,4},{5,7},{7,5},{8,10},{10,8},{9,1... | collective-permute-start | bytes 3538952 | tf_op jit(solution)/shard_map/ppermute | solution.py:20
  591.2 67.9 %collective-permute-start.3 = (f32[384,1536]{1,0:T(8,128)}, f32[384,1536]{1,0:T(8,128)}, u32[]{:S(2)}, u32[]{:S(2)}) collective-permute-start(f32[384,1536]{1,0:T(8,128)} %fusion.30), channel_id=1, source_target_pairs={{0,1},{1,0},{2,3},{3,2},{4,5},{5,4},{6,7},{7,6},{8,9},{9,8},{10,11... | collective-permute-start | bytes 7077896 | tf_op jit(solution)/shard_map/ppermute | solution.py:20
  591.2 76.5 %collective-permute-start.15 = (bf16[4,192,1536]{2,1,0:T(8,128)(2,1)}, bf16[4,192,1536]{2,1,0:T(8,128)(2,1)}, u32[]{:S(2)}, u32[]{:S(2)}) collective-permute-start(bf16[4,192,1536]{2,1,0:T(8,128)(2,1)} %dynamic-slice_bitcast_fusion.2), channel_id=1, source_target_pairs={{0,4},{4,0},{1,5},{5,1},{2,6},{6,2},{3,7},{7,3},{8,12},{12,8},{9,1... | collective-permute-start | bytes 7077896 | tf_op jit(solution)/shard_map/ppermute | solution.py:20
  611.9 45.8 %collective-permute-start.12 = (bf16[4,96,768]{2,1,0:T(8,128)(2,1)S(1)}, bf16[4,96,768]{2,1,0:T(8,128)(2,1)S(1)}, u32[]{:S(2)}, u32[]{:S(2)}) collective-permute-start(bf16[4,96,768]{2,1,0:T(8,128)(2,1)S(1)} %dynamic-slice_bitcast_fusion.6), channel_id=1, source_target_pairs={{0,4},{4,0},{1,5},{5,1},{2,6},{6,2},{3,7},{7,3},{8,12},{12,8},{9,1... | collective-permute-start | bytes 1769480 | tf_op jit(solution)/shard_map/ppermute | solution.py:20
  618.6 53.5 %collective-permute-start.1 = (f32[384,1536]{1,0:T(8,128)}, f32[384,1536]{1,0:T(8,128)}, u32[]{:S(2)}, u32[]{:S(2)}) collective-permute-start(f32[384,1536]{1,0:T(8,128)} %fusion.41), channel_id=1, source_target_pairs={{0,1},{1,0},{2,3},{3,2},{4,5},{5,4},{6,7},{7,6},{8,9},{9,8},{10,11... | collective-permute-start | bytes 7077896 | tf_op jit(solution)/shard_map/ppermute | solution.py:20
  658.7 220.4 %reduce-scatter.10.cloned.1.call-start = ((), (), s32[]{:S(2)}) async-start(), calls=%async_computation.7 | async-start | bytes 2949120 | tf_op jit(solution)/shard_map/reduce_scatter | solution.py:773
  665.6 27.8 %collective-permute-start.4 = (bf16[384,1536]{1,0:T(8,128)(2,1)}, bf16[384,1536]{1,0:T(8,128)(2,1)S(1)}, u32[]{:S(2)}, u32[]{:S(2)}) collective-permute-start(bf16[384,1536]{1,0:T(8,128)(2,1)} %fusion.18), channel_id=1, source_target_pairs={{0,2},{2,0},{1,3},{3,1},{4,6},{6,4},{5,7},{7,5},{8,10},{10,8},{9,1... | collective-permute-start | bytes 3538952 | tf_op jit(solution)/shard_map/ppermute | solution.py:20
  672.1 29.8 %copy-start.1 = (bf16[256,768]{1,0:T(8,128)(2,1)S(1)}, bf16[256,768]{1,0:T(8,128)(2,1)}, u32[]{:S(2)}) copy-start(bf16[256,768]{1,0:T(8,128)(2,1)} %copy-done) | copy-start | bytes 1179652
  672.1 29.8 %copy-start.3 = (bf16[256,768]{1,0:T(8,128)(2,1)S(1)}, bf16[256,768]{1,0:T(8,128)(2,1)}, u32[]{:S(2)}) copy-start(bf16[256,768]{1,0:T(8,128)(2,1)} %copy-done.2) | copy-start | bytes 1179652
  672.1 29.8 %copy-start.31 = (bf16[1,130,768]{2,1,0:T(8,128)(2,1)S(1)}, bf16[1,130,768]{2,1,0:T(8,128)(2,1)}, u32[]{:S(2)}) copy-start(bf16[1,130,768]{2,1,0:T(8,128)(2,1)} %param.25) | copy-start | bytes 599044
  717.8 141.2 %copy-start.40 = (bf16[48,768]{1,0:T(8,128)(2,1)S(1)}, bf16[48,768]{1,0:T(8,128)(2,1)}, u32[]{:S(2)}) copy-start(bf16[48,768]{1,0:T(8,128)(2,1)} %refs_6_.1) | copy-start | bytes 221188
  864.3 9.2 %collective-permute-start.20 = (bf16[96,1536]{1,0:T(8,128)(2,1)S(1)}, bf16[96,1536]{1,0:T(8,128)(2,1)S(1)}, u32[]{:S(2)}, u32[]{:S(2)}) collective-permute-start(bf16[96,1536]{1,0:T(8,128)(2,1)S(1)} %dynamic-slice_bitcast_fusion.7), channel_id=1, source_target_pairs={{0,2},{2,0},{1,3},{3,1},{4,6},{6,4},{5,7},{7,5},{8,10},{10,8},{9,1... | collective-permute-start | bytes 884744 | tf_op jit(solution)/shard_map/ppermute | solution.py:20
  877.3 6.8 collective-permute-start.18
  880.2 7.1 collective-permute-start.16
  (87 other events, 505.8 us)
Sparse Core Ops, SparseCore 0:
  489.9 48.8 reduce-scatter.13
  579.9 23.4 reduce-scatter.7
  605.7 46.3 reduce-scatter.11
  658.8 23.4 reduce-scatter.5
  684.4 46.4 reduce-scatter.9

commit v10 on v9

--- a/solution.py
+++ b/solution.py
@@ -342,10 +342,10 @@
         for d in ends_first(zs):
             after, before = jnp.minimum(z + 1, zs - 1), jnp.maximum(z - 1, 0)
             self.right[d] = lanes.copies(
-                (part.at[d], from_left.at[d]), from_left.at[d], {"z": after}
+                (part(d), from_left.at[d]), from_left.at[d], {"z": after}
             )
             self.left[d] = lanes.copies(
-                (part.at[d], from_right.at[d]), from_right.at[d], {"z": before}
+                (part(d), from_right.at[d]), from_right.at[d], {"z": before}
             )
 
     def pass_on(self, d):
@@ -361,7 +361,7 @@
             @pl.when(sends & jnp.logical_not(edge))
             def _():
                 moves[1].wait_recv()
-                inbox[d] = plus(self.part[d], inbox[d]).astype(inbox.dtype)
+                inbox[d] = plus(self.part(d)[...], inbox[d]).astype(inbox.dtype)
                 moves[1].start()
 
     def total(self, sink):
@@ -369,7 +369,7 @@
 
             @pl.when(self.z == d)
             def _():
-                terms = [self.part[d]]
+                terms = [self.part(d)[...]]
                 if d > 0:
                     self.right[d][0].wait_recv()
                     terms.append(self.from_left[d])
@@ -387,11 +387,9 @@
 class Scatter:
     def __init__(self, lanes, part, held, out, first):
         zs, z, y, x = lanes.zs, lanes.z, lanes.y, lanes.x
-        got, near, from_left, from_right, ready = held
+        got, near, from_left, from_right = held
         second = "y" if first == "x" else "x"
-        self.lanes, self.part, self.got, self.near, self.ready, self.out = (
-            lanes, part, got, near, ready, out,
-        )
+        self.lanes, self.part, self.got, self.near, self.out = lanes, part, got, near, out
         f, s = (x, y) if first == "x" else (y, x)
         self.f, self.s = f, s
 
@@ -409,7 +407,7 @@
             self.two[zz] = Move(
                 lanes.copy(got.at[zz, 0], near.at[zz], {second: 1 - s}), None, None
             )
-        self.line = Line(lanes, ready, from_left, from_right)
+        self.line = Line(lanes, lambda d: got.at[d, 1], from_left, from_right)
 
     def begin(self, zz):
         for j in range(2):
@@ -425,7 +423,8 @@
         self.one[zz, 1].arrived()
         self.two[zz].arrived()
         mine = self.block(zz, self.f, self.s)
-        self.ready[zz] = plus(mine[...], self.got[zz, 1], self.near[zz]).astype(self.ready.dtype)
+        got = self.got
+        got[zz, 1] = plus(mine[...], got[zz, 1], self.near[zz]).astype(got.dtype)
         self.line.pass_on(zz)
 
     def finish(self):
@@ -440,7 +439,7 @@
         y, x = lanes.y, lanes.x
         from_left, from_right, held_z, near, last = held
         self.lanes, self.sum_z, self.near, self.last, self.out = lanes, held_z, near, last, out
-        self.line = Line(lanes, part, from_left, from_right)
+        self.line = Line(lanes, lambda d: part.at[d], from_left, from_right)
         self.two = Move(lanes.copy(held_z.at[1 - y], near, {"y": 1 - y}), None, None)
         self.three = Move(lanes.copy(near.at[1 - x], last, {"x": 1 - x}), None, None)
 
@@ -513,14 +512,16 @@
     def __init__(self, lanes, given, held, out, local_sems):
         grad_hbm, weight_hbm, self.inputs, self.stream, self.gain, self.others = given
         (
-            self.grad, self.weight, self.send, self.got, self.normed,
+            self.grad, self.weight, self.send, self.got,
             self.rows8, self.got8, self.tall, self.blocks,
         ) = held
         self.out, self.zs = out, lanes.zs
         mate = {"tensor": 1 - lax.axis_index("tensor")}
-        self.loads = [
-            pltpu.make_async_copy(grad_hbm, self.grad, local_sems.at[0]),
-            pltpu.make_async_copy(weight_hbm, self.weight, local_sems.at[1]),
+        self.loads = [pltpu.make_async_copy(grad_hbm, self.grad, local_sems.at[0])] + [
+            pltpu.make_async_copy(
+                weight_hbm.at[zz], self.weight.at[zz % 2], local_sems.at[1 + zz % 2]
+            )
+            for zz in range(lanes.zs)
         ]
         self.mate_part = Move(lanes.copy(self.send, self.got, mate), None, None)
         self.mate_rows = Move(lanes.copy(self.rows8, self.got8, mate), None, None)
@@ -536,35 +537,30 @@
                 body(pl.multiple_of(i * tile, tile))
 
         def part_of(first, zz):
-            weight = self.weight[zz].reshape(chunk, self.weight.shape[-1])
+            weight = self.weight[zz % 2].reshape(chunk, self.weight.shape[-1])
             return nt(self.grad[pl.ds(first, tile), :], weight)
 
         self.loads[0].wait()
-        self.loads[1].wait()
         for zz in range(self.zs):
             cols = slice(zz * chunk, (zz + 1) * chunk)
+            self.loads[1 + zz].wait()
 
             def body(at):
                 made = part_of(pl.multiple_of(rows + at, tile), zz)
                 self.send[pl.ds(at, tile), cols] = made.astype(BF)
+                self.out[pl.ds(at, tile), cols] = part_of(at, zz)
 
             over(body)
+            if zz + 2 < self.zs:
+                self.loads[3 + zz].start()
             yield
         self.mate_part.start()
-        for zz in range(self.zs):
-            cols = slice(zz * chunk, (zz + 1) * chunk)
-
-            def body(at):
-                self.normed[pl.ds(at, tile), cols] = part_of(at, zz)
-
-            over(body)
-            yield
         self.mate_part.arrived()
         self.rows8[...] = self.others[...]
 
         def body(at):
             part = pl.ds(at, tile)
-            incoming = self.normed[part, :] + self.got[part, :].astype(F32)
+            incoming = self.out[part, :] + self.got[part, :].astype(F32)
             stream = self.inputs[part, :].astype(F32)
             centred = stream - jnp.mean(stream, axis=-1, keepdims=True)
             inverse = lax.rsqrt(jnp.mean(centred * centred, axis=-1, keepdims=True) + EPSILON)
@@ -611,15 +607,15 @@
     norm = None
     pieces = iter(())
     if fused:
-        norm = LastNorm(lanes, given, take(9), norm_out, local_sems)
-        for load in norm.loads:
+        norm = LastNorm(lanes, given, take(8), norm_out, local_sems)
+        for load in norm.loads[:3]:
             load.start()
         parts = [norm.blocks] + parts
         pieces = norm.pieces()
     greet(zs, fused)
     full, zfirst = [], []
     for i, order in enumerate(orders):
-        held = take(5)
+        held = take(5 if order == "z" else 4)
         if order == "z":
             zfirst.append(ScatterZ(lanes, parts[i], held, outs[i]))
         else:
@@ -637,7 +633,7 @@
         if i < zs:
             for item in zfirst:
                 item.pass_on(order[i])
-        for _ in range((0, 4, 4, 1, 1)[i] if i < 5 else 0):
+        for _ in range((0, 2, 2, 1, 1)[i] if i < 5 else 0):
             next(pieces, None)
         for item in full:
             if 2 <= i < zs + 2:
@@ -684,10 +680,9 @@
         moves += 2
         scratch += [
             pltpu.VMEM(grad.shape, grad.dtype),
-            pltpu.VMEM(weight.shape, weight.dtype),
+            pltpu.VMEM((2,) + weight.shape[1:], weight.dtype),
             pltpu.VMEM((rows, width), BF),
             pltpu.VMEM((rows, width), BF),
-            pltpu.VMEM((rows, width), F32),
             pltpu.VMEM((8, width), F32),
             pltpu.VMEM((8, width), F32),
             pltpu.VMEM((128, width), F32),
@@ -699,7 +694,7 @@
             shapes = [(zs, 2, 2) + block] * 2 + [(2, 2) + block, (2,) + block, block]
             moves += 2 * zs + 2
         else:
-            shapes = [(zs, 2) + block] + [(zs,) + block] * 4
+            shapes = [(zs, 2) + block] + [(zs,) + block] * 3
             moves += 5 * zs
         scratch += [pltpu.VMEM(shape, dtype) for shape in shapes]
     outs = [jax.ShapeDtypeStruct(shape[3:], F32) for shape, _ in shapes_in]
@@ -712,7 +707,7 @@
         scratch_shapes=[
             pltpu.SemaphoreType.DMA((moves,)),
             pltpu.SemaphoreType.DMA((moves,)),
-            pltpu.SemaphoreType.DMA((2,)),
+            pltpu.SemaphoreType.DMA((3,)),
         ]
         + scratch
         + [pltpu.VMEM((8,) + crest.shape, F32)],
@@ -736,27 +731,6 @@
 
 def after(value, *others):
     return lax.optimization_barrier((value, others))[0]
-
-
-class FullSum:
-    def __init__(self, left, right, zs):
-        self.zs = zs
-        held = tn(left, right).astype(BF)
-        self.held = held.reshape(2 * zs, 2, -1, held.shape[1])
-        self.x, self.y = lax.axis_index("x"), lax.axis_index("y")
-        self.sent = pick(self.held, 1 - self.x, 1)
-        self.got = swap(self.sent, "x")
-
-    def second(self, *others):
-        got = after(self.got, others)
-        held = pick(self.held, self.x, 1).astype(F32) + got.astype(F32)
-        self.held = held.astype(BF).reshape(self.zs, 2, -1, held.shape[-1])
-        self.got = swap(pick(self.held, 1 - self.y, 1), "y")
-
-    def third(self, *others):
-        got = after(self.got, others)
-        held = pick(self.held, self.y, 1).astype(F32) + got.astype(F32)
-        return lax.psum_scatter(held.astype(BF), "z", scatter_dimension=0, tiled=False)
 
 
 class PairSum:
@@ -1621,14 +1595,14 @@
     grad_stream = cotangent.astype(F32) + stream_part
     grad_full = pair_rows(grad_stream.astype(BF))
     up_pair = PairSum(after(normed_feed, grad_full), grad_upward, zs)
-    cross_output_sum = FullSum(grad_full, mixed_cross, zs)
-    grad_mixed = after(nn(grad_full, cross_out_t).astype(BF), cross_output_sum.sent)
+    part_cross_output = tn(grad_full, mixed_cross).astype(BF)
+    grad_mixed = nn(grad_full, cross_out_t).astype(BF)
     grad_query, grad_keys, grad_values = attend_back(
         query_cross, taken_cross, taken_cross, grad_mixed, cross_bias_row[:, None], (0, 0, pairs), None
     )
     down_pair.second(grad_query)
     grad_normed = spread_pair(grad_query, cross_in)
-    cross_query_sum = FullSum(normed_cross, grad_query, zs)
+    part_cross_query = tn(normed_cross, grad_query).astype(BF)
     part_memory = tn(memory, jnp.concatenate([grad_keys, grad_values], axis=1))
     stream_part, grad_cross_gain, grad_cross_bias = norm_backward(
         grad_normed, unit_cross, inverse_cross, norms[2]
@@ -1636,19 +1610,15 @@
     grad_stream = grad_stream + stream_part
     grad_full = pair_rows(grad_stream.astype(BF))
     gate_pair.second(grad_full)
-    cross_output_sum.second(grad_full)
     part_self_output = tn(grad_full, mixed_self)
-    grad_mixed = after(nn(grad_full, self_out_t).astype(BF), cross_query_sum.sent)
+    grad_mixed = nn(grad_full, self_out_t).astype(BF)
     grad_parts = attend_back(
         taken, taken, taken, grad_mixed, self_bias_row[:, None], (0, pairs, 2 * pairs), turns
     )
     grad_in = jnp.concatenate(grad_parts, axis=1)
     up_pair.second(grad_in)
-    cross_query_sum.second(grad_in)
-    sum_cross_output = cross_output_sum.third(grad_in).astype(F32)
     part_in = tn(normed_self, grad_in[:, : 2 * inner]).astype(BF)
     part_value = tn(normed_self, grad_parts[2]).astype(BF)
-    sum_cross_query = cross_query_sum.third(part_value).astype(F32)
     def blocks(part):
         return part.astype(BF).reshape(zs, 2, 2, -1, part.shape[1])
 
@@ -1657,15 +1627,17 @@
         other_sums = jnp.stack(
             [none, none, grad_cross_gain, grad_cross_bias, grad_feed_gain, grad_feed_bias, none, none]
         )
-        vector_sums, sum_in, sum_value, sum_self_output, sum_memory, crest, grad_stream = (
+        vector_sums, sum_in, sum_value, sum_self_output, sum_cross_output, sum_cross_query, sum_memory, crest, grad_stream = (
             scatter_all(
                 [
                     blocks(part_in),
                     blocks(part_value),
                     blocks(part_self_output),
+                    blocks(part_cross_output),
+                    blocks(part_cross_query),
                     blocks(part_memory),
                 ],
-                ["z", "x", "y", "y", "z"],
+                ["z", "x", "y", "y", "x", "y", "z"],
                 crest,
                 zs,
                 (
@@ -1702,15 +1674,17 @@
             vector_sums.transpose(1, 0, 2), ((0, 0), (0, 2), (0, 128 - shard_rows))
         ).reshape(zs, 2, 2, 8, 128)
 
-        vector_sums, sum_in, sum_value, sum_self_output, sum_memory, crest = scatter_all(
+        vector_sums, sum_in, sum_value, sum_self_output, sum_cross_output, sum_cross_query, sum_memory, crest = scatter_all(
             [
                 vector_sums,
                 blocks(part_in),
                 blocks(part_value),
                 blocks(part_self_output),
+                blocks(part_cross_output),
+                blocks(part_cross_query),
                 blocks(part_memory),
             ],
-            ["z", "x", "y", "y", "z"],
+            ["z", "x", "y", "y", "x", "y", "z"],
             crest,
             zs,
         )

time: 903 us -> 851 us (0.942)
  waiting for transfers between devices: 126 us -> 55.5 us
  Pallas kernels: 478 us -> 518 us
    ppermute x21 -> x17, waiting for transfers between devices: 126 us -> 55.5 us  [swap(): return lax.ppermute(value, axis, [(0, 1), (1, 0)])]
    pallas_call x1, Pallas kernels: 140 us -> 181 us  [scatter_all(): pl.pallas_call(functools.partial(scatter_kernel, zs, orders, given is not...]
    dot_general x14, matrix products: 66.3 us -> 56.5 us  [nt(): lax.dot_general(left, right, (((1,), (1,)), ((), ())), preferred_element_...]
  transfers between devices with their start and end apart: 26 -> 20, of which waited for: 10 -> 6; matrix products, arithmetic and copies ran while one was open for 26% -> 25% of each run, Pallas kernels for 22% -> 28%
where the time goes in v10:
time: 851 us; the launch traced here: 846 us
  Pallas kernels  518 us (61%)
  matrix products  165 us (19%)
  waiting for transfers between devices  55.5 us (7%)
  local copies, waits for them, and re-layouts  47.1 us (6%)
  other arithmetic  32.2 us (4%)
  between operations  16.5 us (2%)
  starting transfers between devices  12.4 us (1%)
    pallas_call x1, Pallas kernels, forward(): pl.pallas_call(functools.partial(forward_kernel, zs), out_shape=spread +...  285 us
    pallas_call x1, Pallas kernels, scatter_all(): pl.pallas_call(functools.partial(scatter_kernel, zs, orders, given is not...  181 us
    dot_general x8, matrix products, nn(): lax.dot_general(left, right, (((1,), (0,)), ((), ())), preferred_element_...  58.9 us
    dot_general x14, matrix products, nt(): lax.dot_general(left, right, (((1,), (1,)), ((), ())), preferred_element_...  56.5 us
    ppermute x17, waiting for transfers between devices, swap(): return lax.ppermute(value, axis, [(0, 1), (1, 0)])  55.5 us
    pallas_call x2, Pallas kernels, attend_back(): pl.pallas_call(functools.partial(attend_back_kernel, turns is not None),...  52.9 us
    dot_general x9, matrix products, tn(): lax.dot_general(left, right, (((0,), (0,)), ((), ())), preferred_element_...  49.2 us
  transfers between devices with their start and end apart: 20, of which 6 were waited for; matrix products, arithmetic and copies ran while one was open for 25% of the time, Pallas kernels for 28%

profile of v10, /device:TPU:0, one launch (start us, length us, event | category | flops | bytes accessed | tf_op | source)
XLA Modules:
  0.0 846.5 jit_solution(14817255051752406666)
XLA Ops:
  16.9 284.7 %shard_map.406 = (bf16[4,2,2,96,2432]{4,3,2,1,0:T(8,128)(2,1)}, bf16[4,2,2,96,1536]{4,3,2,1,0:T(8,128)(2,1)}, bf16[4,2,2,96,1536]{4,3,2,1,0:T(8,128)(2,1)}, bf16...) custom-call(bf16[96,128]{1,0:T(8,128)(2,1)} %pad.12.refs_0_, ...), custom_call_target="tpu_custom_call" | custom-call | flops 16307453952 | bytes 100000000 | tf_op jit(solution)/shard_map/pallas_call | solution.py:1354
  305.6 7.9 fusion.61
  313.6 5.6 fusion.60
  323.6 11.2 %multiply_convert_fusion.3 = (bf16[768,1536]{1,0:T(8,128)(2,1)}, bf16[768,1536]{1,0:T(8,128)(2,1)}, bf16[768,1536]{1,0:T(8,128)(2,1)}) fusion(f32[768,1536]{1,0:T(8,128)} %fusion.60, f32[768,1536]{1,0:T(8,128)} %fusion.61, bf16[768,1536]{1,0:T(8,128)(2,1)S(1)} %bitcast.146, bf16[1536,1536]{1,0:T(8,128)(2,1)} %bitcast.170), kind=kOutput, calls=%fused_computation.24 | convolution fusion | flops 3642753024 | bytes 23592960 | tf_op jit(solution)/shard_map/dot_general | solution.py:721
  337.5 9.2 %fusion.63 = f32[768,1536]{1,0:T(8,128)} fusion(bf16[768,1536]{1,0:T(8,128)(2,1)} %bitcast.145, bf16[1536,1536]{1,0:T(8,128)(2,1)} %bitcast.171), kind=kOutput, calls=%fused_computation.161 | convolution fusion | flops 3623878656 | bytes 11796480 | tf_op jit(solution)/shard_map/dot_general | solution.py:721
  347.9 4.9 fusion.31
  355.2 5.4 fusion.62
  360.6 10.0 %multiply_convert_fusion = (bf16[768,1536]{1,0:T(8,128)(2,1)}, bf16[768,1536]{1,0:T(8,128)(2,1)S(1)}, bf16[768,1536]{1,0:T(8,128)(2,1)}) fusion(f32[768,1536]{1,0:T(8,128)} %fusion.63, f32[768,1536]{1,0:T(8,128)} %fusion.62, bf16[768,1536]{1,0:T(8,128)(2,1)S(1)} %constant_dynamic-update-slice_fusion, bf16[1536,1536]{1,0:T(8,128)(2,1)S(1)} %bitcast.195), kind=kOutput, calls=%fused_computation.20 | convolution fusion | flops 3642753024 | bytes 23592960 | tf_op jit(solution)/shard_map/dot_general | solution.py:721
  383.0 7.2 fusion.14
  390.2 3.9 fusion.16
  394.7 9.3 %convolution_convert_fusion.2 = bf16[1536,1536]{1,0:T(8,128)(2,1)S(1)} fusion(bf16[1536,1536]{1,0:T(8,128)(2,1)S(1)} %bitcast.140, bf16[768,1536]{1,0:T(8,128)(2,1)} %get-tuple-element.140, bf16[768,1536]{1,0:T(8,128)(2,1)S(1)} %copy-done.50), kind=kOutput, calls=%fused_computation.2 | convolution fusion | flops 7259553792 | bytes 14155776 | tf_op jit(solution)/shard_map/dot_general | solution.py:729
  408.9 7.9 convolution_convert_fusion.3
  431.0 4.1 convolution_convert_fusion.10.g_ref
  435.2 16.3 %shard_map.407 = (bf16[768,768]{1,0:T(8,128)(2,1)S(1)}, bf16[256,768]{1,0:T(8,128)(2,1)S(1)}, bf16[256,768]{1,0:T(8,128)(2,1)S(1)}) custom-call(bf16[768,768]{1,0:T(8,128)(2,1)S(1)} %copy-done.4, bf16[256,1536]{1,0:T(8,128)(2,1)S(1)} %copy-done.5, bf16[256,1536]{1,0:T(8,128)(2,1)S(1)} %copy-done.5, bf16[768,768]{1,0:T(8,128)(2,1)S(1)} %convolution_convert_fusion.10.g_ref, ...), custom_call_target="tpu_custom_call" | custom-call | flops 3019898880 | bytes 6291456 | tf_op jit(solution)/shard_map/pallas_call | solution.py:926
  451.5 9.3 %collective-permute-done.15 = bf16[4,192,1536]{2,1,0:T(8,128)(2,1)} collective-permute-done((bf16[4,192,1536]{2,1,0:T(8,128)(2,1)}, bf16[4,192,1536]{2,1,0:T(8,128)(2,1)}, u32[]{:S(2)}, u32[]{:S(2)}) %collective-permute-start.15) | collective-permute-done | bytes 2359328 | tf_op jit(solution)/shard_map/ppermute | solution.py:20
  460.8 4.4 fusion.9
  468.2 4.9 fusion.28
  473.2 5.9 fusion.37
  482.7 7.9 convolution_convert_fusion.1
  495.8 4.3 fusion.18
  501.7 32.1 %collective-permute-done.11 = bf16[4,192,1536]{2,1,0:T(8,128)(2,1)S(1)} collective-permute-done((bf16[4,192,1536]{2,1,0:T(8,128)(2,1)S(1)}, bf16[4,192,1536]{2,1,0:T(8,128)(2,1)S(1)}, u32[]{:S(2)}, u32[]{:S(2)}) %collective-permute-start.11) | collective-permute-done | bytes 2359328 | tf_op jit(solution)/shard_map/ppermute | solution.py:20
  536.5 4.8 multiply_reduce_fusion.1
  545.4 5.2 fusion.17
  550.7 3.5 convolution_convert_fusion.6
  560.7 5.5 convolution_convert_fusion.9.g_ref
  566.2 36.5 %shard_map.408 = (bf16[768,768]{1,0:T(8,128)(2,1)S(1)}, bf16[768,768]{1,0:T(8,128)(2,1)S(1)}, bf16[768,768]{1,0:T(8,128)(2,1)S(1)}) custom-call(bf16[768,2304]{1,0:T(8,128)(2,1)} %get-tuple-element.79.q_ref.k_ref.v_ref, bf16[768,2304]{1,0:T(8,128)(2,1)} %get-tuple-element.79.q_ref.k_ref.v_ref, bf16[768,2304]{1,0:T(8,128)(2,1)} %get-tuple-element.79.q_ref.k_ref.v_ref, ...), custom_call_target="tpu_custom_call" | custom-call | flops 9059696640 | bytes 9437184 | tf_op jit(solution)/shard_map/pallas_call | solution.py:926
  606.2 3.7 fusion.10
  610.0 5.6 convolution_convert_fusion.7
  619.0 5.9 convolution_convert_fusion
  624.9 180.7 %shard_map.409 = (f32[96,128]{1,0:T(8,128)}, f32[96,1536]{1,0:T(8,128)}, f32[96,768]{1,0:T(8,128)}, f32[96,768]{1,0:T(8,128)}, f32[96,768]{1,0:T(8,128)}, /*inde...) custom-call(bf16[4,2,2,96,1536]{4,3,2,1,0:T(8,128)(2,1)} %bitcast.123, ...), custom_call_target="tpu_custom_call" | custom-call | tf_op jit(solution)/shard_map/pallas_call | solution.py:702
  817.2 3.6 collective-permute-done.16
  829.5 4.7 collective-permute-done.14
  (311 shorter events, 114.1 us)
Async XLA Ops:
  7.2 805.0 %reduce-scatter.8.cloned.1.call-start = ((), (), s32[]{:S(2)}) async-start(), calls=%async_computation.5 | async-start | bytes 2949120 | tf_op jit(solution)/shard_map/reduce_scatter | solution.py:747
  304.1 42.5 %collective-permute-start = (bf16[384,1536]{1,0:T(8,128)(2,1)}, bf16[384,1536]{1,0:T(8,128)(2,1)S(1)}, u32[]{:S(2)}, u32[]{:S(2)}) collective-permute-start(bf16[384,1536]{1,0:T(8,128)(2,1)} %slice_bitcast_fusion), channel_id=1, source_target_pairs={{0,2},{2,0},{1,3},{3,1},{4,6},{6,4},{5,7},{7,5},{8,10},{10,8},{9,1... | collective-permute-start | bytes 3538952 | tf_op jit(solution)/shard_map/ppermute | solution.py:20
  305.6 13.5 %slice-start.6 = ((s8[4718592]{0:T(1024)(128)(4,1)}), s8[4194304]{0:T(1024)(128)(4,1)S(1)}, s32[]{:S(2)}) async-start(s8[4718592]{0:T(1024)(128)(4,1)} %bitcast.136), calls=%async_computation.12 | async-start | bytes 8388608
  346.7 8.3 collective-permute-start.2
  354.9 28.1 %collective-permute-start.5 = (f32[384,1536]{1,0:T(8,128)S(1)}, f32[384,1536]{1,0:T(8,128)S(1)}, u32[]{:S(2)}, u32[]{:S(2)}) collective-permute-start(f32[384,1536]{1,0:T(8,128)S(1)} %convolution_add_fusion.3), channel_id=1, source_target_pairs={{0,1},{1,0},{2,3},{3,2},{4,5},{5,4},{6,7},{7,6},{8,9},{9,8},{10,11... | collective-permute-start | bytes 7077896 | tf_op jit(solution)/shard_map/ppermute | solution.py:20
  375.2 15.0 %collective-permute-start.6 = (f32[384,1536]{1,0:T(8,128)S(1)}, f32[384,1536]{1,0:T(8,128)S(1)}, u32[]{:S(2)}, u32[]{:S(2)}) collective-permute-start(f32[384,1536]{1,0:T(8,128)S(1)} %convolution_add_fusion.1), channel_id=1, source_target_pairs={{0,1},{1,0},{2,3},{3,2},{4,5},{5,4},{6,7},{7,6},{8,9},{9,8},{10,11... | collective-permute-start | bytes 7077896 | tf_op jit(solution)/shard_map/ppermute | solution.py:20
  382.9 25.1 %copy-start.15 = (bf16[1536,1536]{1,0:T(8,128)(2,1)}, bf16[1536,1536]{1,0:T(8,128)(2,1)S(1)}, u32[]{:S(2)}) copy-start(bf16[1536,1536]{1,0:T(8,128)(2,1)S(1)} %pad_maximum_fusion) | copy-start | bytes 14155780
  394.1 28.0 %collective-permute-start.7 = (bf16[384,1536]{1,0:T(8,128)(2,1)S(1)}, bf16[384,1536]{1,0:T(8,128)(2,1)S(1)}, u32[]{:S(2)}, u32[]{:S(2)}) collective-permute-start(bf16[384,1536]{1,0:T(8,128)(2,1)S(1)} %fusion.16), channel_id=1, source_target_pairs={{0,2},{2,0},{1,3},{3,1},{4,6},{6,4},{5,7},{7,5},{8,10},{10,8},{9,1... | collective-permute-start | bytes 3538952 | tf_op jit(solution)/shard_map/ppermute | solution.py:20
  407.6 53.2 %collective-permute-start.15 = (bf16[4,192,1536]{2,1,0:T(8,128)(2,1)}, bf16[4,192,1536]{2,1,0:T(8,128)(2,1)}, u32[]{:S(2)}, u32[]{:S(2)}) collective-permute-start(bf16[4,192,1536]{2,1,0:T(8,128)(2,1)} %dynamic-slice_bitcast_fusion.1), channel_id=1, source_target_pairs={{0,4},{4,0},{1,5},{5,1},{2,6},{6,2},{3,7},{7,3},{8,12},{12,8},{9,1... | collective-permute-start | bytes 7077896 | tf_op jit(solution)/shard_map/ppermute | solution.py:20
  425.8 5.2 collective-permute-start.8
  465.2 349.8 %reduce-scatter.4.cloned.1.call-start = ((), (), s32[]{:S(2)}) async-start(), calls=%async_computation.3 | async-start | bytes 2949120 | tf_op jit(solution)/shard_map/reduce_scatter | solution.py:747
  468.2 14.5 %slice-start.4 = ((s8[4718592]{0:T(1024)(128)(4,1)}), s8[4194304]{0:T(1024)(128)(4,1)S(1)}, s32[]{:S(2)}) async-start(s8[4718592]{0:T(1024)(128)(4,1)} %bitcast.134), calls=%async_computation.10 | async-start | bytes 8388608
  473.1 22.7 %collective-permute-start.3 = (f32[384,1536]{1,0:T(8,128)S(1)}, f32[384,1536]{1,0:T(8,128)S(1)}, u32[]{:S(2)}, u32[]{:S(2)}) collective-permute-start(f32[384,1536]{1,0:T(8,128)S(1)} %fusion.28), channel_id=1, source_target_pairs={{0,1},{1,0},{2,3},{3,2},{4,5},{5,4},{6,7},{7,6},{8,9},{9,8},{10,11... | collective-permute-start | bytes 7077896 | tf_op jit(solution)/shard_map/ppermute | solution.py:20
  479.1 65.0 %collective-permute-start.1 = (f32[384,1536]{1,0:T(8,128)}, f32[384,1536]{1,0:T(8,128)}, u32[]{:S(2)}, u32[]{:S(2)}) collective-permute-start(f32[384,1536]{1,0:T(8,128)} %fusion.37), channel_id=1, source_target_pairs={{0,1},{1,0},{2,3},{3,2},{4,5},{5,4},{6,7},{7,6},{8,9},{9,8},{10,11... | collective-permute-start | bytes 7077896 | tf_op jit(solution)/shard_map/ppermute | solution.py:20
  479.6 54.1 %collective-permute-start.11 = (bf16[4,192,1536]{2,1,0:T(8,128)(2,1)S(1)}, bf16[4,192,1536]{2,1,0:T(8,128)(2,1)S(1)}, u32[]{:S(2)}, u32[]{:S(2)}) collective-permute-start(bf16[4,192,1536]{2,1,0:T(8,128)(2,1)S(1)} %copy-done.16), channel_id=1, source_target_pairs={{0,4},{4,0},{1,5},{5,1},{2,6},{6,2},{3,7},{7,3},{8,12},{12,8},{9,1... | collective-permute-start | bytes 7077896 | tf_op jit(solution)/shard_map/ppermute | solution.py:20
  480.2 15.6 %slice-start.10 = ((s8[4718592]{0:T(1024)(128)(4,1)}), s8[4194304]{0:T(1024)(128)(4,1)S(1)}, s32[]{:S(2)}) async-start(s8[4718592]{0:T(1024)(128)(4,1)} %bitcast.174), calls=%async_computation.16 | async-start | bytes 8388608
  482.7 53.6 %collective-permute-start.9 = (f32[384,1536]{1,0:T(8,128)}, f32[384,1536]{1,0:T(8,128)}, u32[]{:S(2)}, u32[]{:S(2)}) collective-permute-start(f32[384,1536]{1,0:T(8,128)} %fusion.43), channel_id=1, source_target_pairs={{0,1},{1,0},{2,3},{3,2},{4,5},{5,4},{6,7},{7,6},{8,9},{9,8},{10,11... | collective-permute-start | bytes 7077896 | tf_op jit(solution)/shard_map/ppermute | solution.py:20
  492.8 40.9 %slice-start = ((s8[4718592]{0:T(1024)(128)(4,1)}), s8[4194304]{0:T(1024)(128)(4,1)S(1)}, s32[]{:S(2)}) async-start(s8[4718592]{0:T(1024)(128)(4,1)} %bitcast.125), calls=%async_computation.6 | async-start | bytes 8388608
  494.4 39.4 %slice-start.1 = ((s8[4718592]{0:T(1024)(128)(4,1)}), s8[524288]{0:T(1024)(128)(4,1)S(1)}, s32[]{:S(2)}) async-start(s8[4718592]{0:T(1024)(128)(4,1)} %bitcast.125), calls=%async_computation.7 | async-start | bytes 1048576
  494.4 111.9 %collective-permute-start.13 = (bf16[4,192,1536]{2,1,0:T(8,128)(2,1)}, bf16[4,192,1536]{2,1,0:T(8,128)(2,1)}, u32[]{:S(2)}, u32[]{:S(2)}) collective-permute-start(bf16[4,192,1536]{2,1,0:T(8,128)(2,1)} %dynamic-slice_bitcast_fusion), channel_id=1, source_target_pairs={{0,4},{4,0},{1,5},{5,1},{2,6},{6,2},{3,7},{7,3},{8,12},{12,8},{9,1... | collective-permute-start | bytes 7077896 | tf_op jit(solution)/shard_map/ppermute | solution.py:20
  500.1 44.0 %collective-permute-start.4 = (bf16[384,1536]{1,0:T(8,128)(2,1)}, bf16[384,1536]{1,0:T(8,128)(2,1)}, u32[]{:S(2)}, u32[]{:S(2)}) collective-permute-start(bf16[384,1536]{1,0:T(8,128)(2,1)} %fusion.18), channel_id=1, source_target_pairs={{0,2},{2,0},{1,3},{3,1},{4,6},{6,4},{5,7},{7,5},{8,10},{10,8},{9,1... | collective-permute-start | bytes 3538952 | tf_op jit(solution)/shard_map/ppermute | solution.py:20
  535.8 290.5 %reduce-scatter.6.cloned.1.call-start = ((), (), s32[]{:S(2)}) async-start(), calls=%async_computation.4 | async-start | bytes 2949120 | tf_op jit(solution)/shard_map/reduce_scatter | solution.py:747
  544.1 16.5 %collective-permute-start.10 = (bf16[384,1536]{1,0:T(8,128)(2,1)}, bf16[384,1536]{1,0:T(8,128)(2,1)}, u32[]{:S(2)}, u32[]{:S(2)}) collective-permute-start(bf16[384,1536]{1,0:T(8,128)(2,1)} %get-tuple-element.134), channel_id=1, source_target_pairs={{0,1},{1,0},{2,3},{3,2},{4,5},{5,4},{6,7},{7,6},{8,9},{9,8},{10,11... | collective-permute-start | bytes 3538952 | tf_op jit(solution)/shard_map/ppermute | solution.py:20
  560.6 45.6 %slice-start.2 = ((s8[4718592]{0:T(1024)(128)(4,1)}), s8[4194304]{0:T(1024)(128)(4,1)S(1)}, s32[]{:S(2)}) async-start(s8[4718592]{0:T(1024)(128)(4,1)} %bitcast.129), calls=%async_computation.8 | async-start | bytes 8388608
  566.2 40.0 %slice-start.3 = ((s8[4718592]{0:T(1024)(128)(4,1)}), s8[524288]{0:T(1024)(128)(4,1)S(1)}, s32[]{:S(2)}) async-start(s8[4718592]{0:T(1024)(128)(4,1)} %bitcast.129), calls=%async_computation.9 | async-start | bytes 1048576
  624.9 182.0 %copy-start.32 = (bf16[48,768]{1,0:T(8,128)(2,1)S(1)}, bf16[48,768]{1,0:T(8,128)(2,1)}, u32[]{:S(2)}) copy-start(bf16[48,768]{1,0:T(8,128)(2,1)} %refs_6_.1) | copy-start | bytes 221188
  624.9 186.3 %copy-start.29 = (bf16[96,768]{1,0:T(8,128)(2,1)S(1)}, bf16[96,768]{1,0:T(8,128)(2,1)}, u32[]{:S(2)}) copy-start(bf16[96,768]{1,0:T(8,128)(2,1)} %refs_1_.1) | copy-start | bytes 442372
  624.9 186.3 %copy-start.30 = (bf16[96,768]{1,0:T(8,128)(2,1)S(1)}, bf16[96,768]{1,0:T(8,128)(2,1)}, u32[]{:S(2)}) copy-start(bf16[96,768]{1,0:T(8,128)(2,1)} %refs_2_.1) | copy-start | bytes 442372
  624.9 186.3 %copy-start.31 = (bf16[96,768]{1,0:T(8,128)(2,1)S(1)}, bf16[96,768]{1,0:T(8,128)(2,1)}, u32[]{:S(2)}) copy-start(bf16[96,768]{1,0:T(8,128)(2,1)} %refs_5_.1) | copy-start | bytes 442372
  813.2 7.6 collective-permute-start.16
  816.0 10.2 %collective-permute-start.12 = (bf16[96,1536]{1,0:T(8,128)(2,1)S(1)}, bf16[96,1536]{1,0:T(8,128)(2,1)S(1)}, u32[]{:S(2)}, u32[]{:S(2)}) collective-permute-start(bf16[96,1536]{1,0:T(8,128)(2,1)S(1)} %dynamic-slice_bitcast_fusion.5), channel_id=1, source_target_pairs={{0,2},{2,0},{1,3},{3,1},{4,6},{6,4},{5,7},{7,5},{8,10},{10,8},{9,1... | collective-permute-start | bytes 884744 | tf_op jit(solution)/shard_map/ppermute | solution.py:20
  827.4 6.8 collective-permute-start.14
  (74 other events, 362.8 us)
Sparse Core Ops, SparseCore 0:
  465.4 48.9 reduce-scatter.7
  536.0 49.1 reduce-scatter.3
  610.1 68.5 reduce-scatter.5

commit v11 on v10

--- a/solution.py
+++ b/solution.py
@@ -624,7 +624,7 @@
     crest = Crest(lanes, crest_in, take(1)[0], crest_out)
     crest.one.start()
     order = ends_first(zs)
-    for i in range(zs + 3):
+    for i in range(zs + 4):
         for item in full:
             if i < zs:
                 item.begin(order[i])
@@ -647,8 +647,8 @@
                 for d in order:
                     item.pass_on(d)
         for item in full:
-            if 3 <= i:
-                item.third(order[i - 3])
+            if 4 <= i:
+                item.third(order[i - 4])
     for item in late:
         item.total()
     crest.finish()

time: 851 us -> 851 us (level)
  no operation moved by 1% of the time
where the time goes in v11:
time: 851 us; the launch traced here: 847 us
  Pallas kernels  519 us (61%)
  matrix products  165 us (19%)
  waiting for transfers between devices  55.3 us (6%)
  local copies, waits for them, and re-layouts  47.1 us (6%)
  other arithmetic  32.2 us (4%)
  between operations  16.5 us (2%)
  starting transfers between devices  12.6 us (1%)
    pallas_call x1, Pallas kernels, forward(): pl.pallas_call(functools.partial(forward_kernel, zs), out_shape=spread +...  285 us
    pallas_call x1, Pallas kernels, scatter_all(): pl.pallas_call(functools.partial(scatter_kernel, zs, orders, given is not...  181 us
    dot_general x8, matrix products, nn(): lax.dot_general(left, right, (((1,), (0,)), ((), ())), preferred_element_...  58.9 us
    dot_general x14, matrix products, nt(): lax.dot_general(left, right, (((1,), (1,)), ((), ())), preferred_element_...  56.5 us
    ppermute x17, waiting for transfers between devices, swap(): return lax.ppermute(value, axis, [(0, 1), (1, 0)])  55.2 us
    pallas_call x2, Pallas kernels, attend_back(): pl.pallas_call(functools.partial(attend_back_kernel, turns is not None),...  52.9 us
    dot_general x9, matrix products, tn(): lax.dot_general(left, right, (((0,), (0,)), ((), ())), preferred_element_...  49.2 us
  transfers between devices with their start and end apart: 20, of which 6 were waited for; matrix products, arithmetic and copies ran while one was open for 25% of the time, Pallas kernels for 28%

profile of v11, /device:TPU:0, one launch (start us, length us, event | category | flops | bytes accessed | tf_op | source)
XLA Modules:
  0.0 846.9 jit_solution(14055248738345457564)
XLA Ops:
  16.9 284.7 %shard_map.406 = (bf16[4,2,2,96,2432]{4,3,2,1,0:T(8,128)(2,1)}, bf16[4,2,2,96,1536]{4,3,2,1,0:T(8,128)(2,1)}, bf16[4,2,2,96,1536]{4,3,2,1,0:T(8,128)(2,1)}, bf16...) custom-call(bf16[96,128]{1,0:T(8,128)(2,1)} %pad.12.refs_0_, ...), custom_call_target="tpu_custom_call" | custom-call | flops 16307453952 | bytes 100000000 | tf_op jit(solution)/shard_map/pallas_call | solution.py:1354
  305.6 7.9 fusion.61
  313.6 5.6 fusion.60
  323.6 11.2 %multiply_convert_fusion.3 = (bf16[768,1536]{1,0:T(8,128)(2,1)}, bf16[768,1536]{1,0:T(8,128)(2,1)}, bf16[768,1536]{1,0:T(8,128)(2,1)}) fusion(f32[768,1536]{1,0:T(8,128)} %fusion.60, f32[768,1536]{1,0:T(8,128)} %fusion.61, bf16[768,1536]{1,0:T(8,128)(2,1)S(1)} %bitcast.146, bf16[1536,1536]{1,0:T(8,128)(2,1)} %bitcast.170), kind=kOutput, calls=%fused_computation.24 | convolution fusion | flops 3642753024 | bytes 23592960 | tf_op jit(solution)/shard_map/dot_general | solution.py:721
  337.5 9.2 %fusion.63 = f32[768,1536]{1,0:T(8,128)} fusion(bf16[768,1536]{1,0:T(8,128)(2,1)} %bitcast.145, bf16[1536,1536]{1,0:T(8,128)(2,1)} %bitcast.171), kind=kOutput, calls=%fused_computation.161 | convolution fusion | flops 3623878656 | bytes 11796480 | tf_op jit(solution)/shard_map/dot_general | solution.py:721
  347.9 4.9 fusion.31
  355.2 5.4 fusion.62
  360.6 10.0 %multiply_convert_fusion = (bf16[768,1536]{1,0:T(8,128)(2,1)}, bf16[768,1536]{1,0:T(8,128)(2,1)S(1)}, bf16[768,1536]{1,0:T(8,128)(2,1)}) fusion(f32[768,1536]{1,0:T(8,128)} %fusion.63, f32[768,1536]{1,0:T(8,128)} %fusion.62, bf16[768,1536]{1,0:T(8,128)(2,1)S(1)} %constant_dynamic-update-slice_fusion, bf16[1536,1536]{1,0:T(8,128)(2,1)S(1)} %bitcast.195), kind=kOutput, calls=%fused_computation.20 | convolution fusion | flops 3642753024 | bytes 23592960 | tf_op jit(solution)/shard_map/dot_general | solution.py:721
  383.0 7.2 fusion.14
  390.2 3.9 fusion.16
  394.7 9.3 %convolution_convert_fusion.2 = bf16[1536,1536]{1,0:T(8,128)(2,1)S(1)} fusion(bf16[1536,1536]{1,0:T(8,128)(2,1)S(1)} %bitcast.140, bf16[768,1536]{1,0:T(8,128)(2,1)} %get-tuple-element.140, bf16[768,1536]{1,0:T(8,128)(2,1)S(1)} %copy-done.50), kind=kOutput, calls=%fused_computation.2 | convolution fusion | flops 7259553792 | bytes 14155776 | tf_op jit(solution)/shard_map/dot_general | solution.py:729
  408.9 7.9 convolution_convert_fusion.3
  431.0 4.1 convolution_convert_fusion.10.g_ref
  435.2 16.3 %shard_map.407 = (bf16[768,768]{1,0:T(8,128)(2,1)S(1)}, bf16[256,768]{1,0:T(8,128)(2,1)S(1)}, bf16[256,768]{1,0:T(8,128)(2,1)S(1)}) custom-call(bf16[768,768]{1,0:T(8,128)(2,1)S(1)} %copy-done.4, bf16[256,1536]{1,0:T(8,128)(2,1)S(1)} %copy-done.5, bf16[256,1536]{1,0:T(8,128)(2,1)S(1)} %copy-done.5, bf16[768,768]{1,0:T(8,128)(2,1)S(1)} %convolution_convert_fusion.10.g_ref, ...), custom_call_target="tpu_custom_call" | custom-call | flops 3019898880 | bytes 6291456 | tf_op jit(solution)/shard_map/pallas_call | solution.py:926
  451.5 9.3 %collective-permute-done.15 = bf16[4,192,1536]{2,1,0:T(8,128)(2,1)} collective-permute-done((bf16[4,192,1536]{2,1,0:T(8,128)(2,1)}, bf16[4,192,1536]{2,1,0:T(8,128)(2,1)}, u32[]{:S(2)}, u32[]{:S(2)}) %collective-permute-start.15) | collective-permute-done | bytes 2359328 | tf_op jit(solution)/shard_map/ppermute | solution.py:20
  460.8 4.4 fusion.9
  468.2 4.9 fusion.28
  473.2 5.9 fusion.37
  482.7 7.9 convolution_convert_fusion.1
  495.8 4.3 fusion.18
  501.7 32.1 %collective-permute-done.11 = bf16[4,192,1536]{2,1,0:T(8,128)(2,1)S(1)} collective-permute-done((bf16[4,192,1536]{2,1,0:T(8,128)(2,1)S(1)}, bf16[4,192,1536]{2,1,0:T(8,128)(2,1)S(1)}, u32[]{:S(2)}, u32[]{:S(2)}) %collective-permute-start.11) | collective-permute-done | bytes 2359328 | tf_op jit(solution)/shard_map/ppermute | solution.py:20
  536.5 4.8 multiply_reduce_fusion.1
  545.4 5.2 fusion.17
  550.7 3.5 convolution_convert_fusion.6
  560.7 5.5 convolution_convert_fusion.9.g_ref
  566.2 36.5 %shard_map.408 = (bf16[768,768]{1,0:T(8,128)(2,1)S(1)}, bf16[768,768]{1,0:T(8,128)(2,1)S(1)}, bf16[768,768]{1,0:T(8,128)(2,1)S(1)}) custom-call(bf16[768,2304]{1,0:T(8,128)(2,1)} %get-tuple-element.79.q_ref.k_ref.v_ref, bf16[768,2304]{1,0:T(8,128)(2,1)} %get-tuple-element.79.q_ref.k_ref.v_ref, bf16[768,2304]{1,0:T(8,128)(2,1)} %get-tuple-element.79.q_ref.k_ref.v_ref, ...), custom_call_target="tpu_custom_call" | custom-call | flops 9059696640 | bytes 9437184 | tf_op jit(solution)/shard_map/pallas_call | solution.py:926
  606.2 3.7 fusion.10
  610.0 5.6 convolution_convert_fusion.7
  619.0 5.9 convolution_convert_fusion
  624.9 181.1 %shard_map.409 = (f32[96,128]{1,0:T(8,128)}, f32[96,1536]{1,0:T(8,128)}, f32[96,768]{1,0:T(8,128)}, f32[96,768]{1,0:T(8,128)}, f32[96,768]{1,0:T(8,128)}, /*inde...) custom-call(bf16[4,2,2,96,1536]{4,3,2,1,0:T(8,128)(2,1)} %bitcast.123, ...), custom_call_target="tpu_custom_call" | custom-call | tf_op jit(solution)/shard_map/pallas_call | solution.py:702
  817.7 3.6 collective-permute-done.16
  830.2 4.4 collective-permute-done.14
  (311 shorter events, 114.3 us)
Async XLA Ops:
  7.2 805.5 %reduce-scatter.8.cloned.1.call-start = ((), (), s32[]{:S(2)}) async-start(), calls=%async_computation.5 | async-start | bytes 2949120 | tf_op jit(solution)/shard_map/reduce_scatter | solution.py:747
  304.1 42.5 %collective-permute-start = (bf16[384,1536]{1,0:T(8,128)(2,1)}, bf16[384,1536]{1,0:T(8,128)(2,1)S(1)}, u32[]{:S(2)}, u32[]{:S(2)}) collective-permute-start(bf16[384,1536]{1,0:T(8,128)(2,1)} %slice_bitcast_fusion), channel_id=1, source_target_pairs={{0,2},{2,0},{1,3},{3,1},{4,6},{6,4},{5,7},{7,5},{8,10},{10,8},{9,1... | collective-permute-start | bytes 3538952 | tf_op jit(solution)/shard_map/ppermute | solution.py:20
  305.6 13.5 %slice-start.6 = ((s8[4718592]{0:T(1024)(128)(4,1)}), s8[4194304]{0:T(1024)(128)(4,1)S(1)}, s32[]{:S(2)}) async-start(s8[4718592]{0:T(1024)(128)(4,1)} %bitcast.136), calls=%async_computation.12 | async-start | bytes 8388608
  346.7 8.3 collective-permute-start.2
  354.9 28.1 %collective-permute-start.5 = (f32[384,1536]{1,0:T(8,128)S(1)}, f32[384,1536]{1,0:T(8,128)S(1)}, u32[]{:S(2)}, u32[]{:S(2)}) collective-permute-start(f32[384,1536]{1,0:T(8,128)S(1)} %convolution_add_fusion.3), channel_id=1, source_target_pairs={{0,1},{1,0},{2,3},{3,2},{4,5},{5,4},{6,7},{7,6},{8,9},{9,8},{10,11... | collective-permute-start | bytes 7077896 | tf_op jit(solution)/shard_map/ppermute | solution.py:20
  375.2 15.0 %collective-permute-start.6 = (f32[384,1536]{1,0:T(8,128)S(1)}, f32[384,1536]{1,0:T(8,128)S(1)}, u32[]{:S(2)}, u32[]{:S(2)}) collective-permute-start(f32[384,1536]{1,0:T(8,128)S(1)} %convolution_add_fusion.1), channel_id=1, source_target_pairs={{0,1},{1,0},{2,3},{3,2},{4,5},{5,4},{6,7},{7,6},{8,9},{9,8},{10,11... | collective-permute-start | bytes 7077896 | tf_op jit(solution)/shard_map/ppermute | solution.py:20
  382.9 25.1 %copy-start.15 = (bf16[1536,1536]{1,0:T(8,128)(2,1)}, bf16[1536,1536]{1,0:T(8,128)(2,1)S(1)}, u32[]{:S(2)}) copy-start(bf16[1536,1536]{1,0:T(8,128)(2,1)S(1)} %pad_maximum_fusion) | copy-start | bytes 14155780
  394.1 28.0 %collective-permute-start.7 = (bf16[384,1536]{1,0:T(8,128)(2,1)S(1)}, bf16[384,1536]{1,0:T(8,128)(2,1)S(1)}, u32[]{:S(2)}, u32[]{:S(2)}) collective-permute-start(bf16[384,1536]{1,0:T(8,128)(2,1)S(1)} %fusion.16), channel_id=1, source_target_pairs={{0,2},{2,0},{1,3},{3,1},{4,6},{6,4},{5,7},{7,5},{8,10},{10,8},{9,1... | collective-permute-start | bytes 3538952 | tf_op jit(solution)/shard_map/ppermute | solution.py:20
  407.6 53.2 %collective-permute-start.15 = (bf16[4,192,1536]{2,1,0:T(8,128)(2,1)}, bf16[4,192,1536]{2,1,0:T(8,128)(2,1)}, u32[]{:S(2)}, u32[]{:S(2)}) collective-permute-start(bf16[4,192,1536]{2,1,0:T(8,128)(2,1)} %dynamic-slice_bitcast_fusion.1), channel_id=1, source_target_pairs={{0,4},{4,0},{1,5},{5,1},{2,6},{6,2},{3,7},{7,3},{8,12},{12,8},{9,1... | collective-permute-start | bytes 7077896 | tf_op jit(solution)/shard_map/ppermute | solution.py:20
  425.8 5.2 collective-permute-start.8
  465.2 350.4 %reduce-scatter.4.cloned.1.call-start = ((), (), s32[]{:S(2)}) async-start(), calls=%async_computation.3 | async-start | bytes 2949120 | tf_op jit(solution)/shard_map/reduce_scatter | solution.py:747
  468.2 14.5 %slice-start.4 = ((s8[4718592]{0:T(1024)(128)(4,1)}), s8[4194304]{0:T(1024)(128)(4,1)S(1)}, s32[]{:S(2)}) async-start(s8[4718592]{0:T(1024)(128)(4,1)} %bitcast.134), calls=%async_computation.10 | async-start | bytes 8388608
  473.1 22.7 %collective-permute-start.3 = (f32[384,1536]{1,0:T(8,128)S(1)}, f32[384,1536]{1,0:T(8,128)S(1)}, u32[]{:S(2)}, u32[]{:S(2)}) collective-permute-start(f32[384,1536]{1,0:T(8,128)S(1)} %fusion.28), channel_id=1, source_target_pairs={{0,1},{1,0},{2,3},{3,2},{4,5},{5,4},{6,7},{7,6},{8,9},{9,8},{10,11... | collective-permute-start | bytes 7077896 | tf_op jit(solution)/shard_map/ppermute | solution.py:20
  479.1 65.0 %collective-permute-start.1 = (f32[384,1536]{1,0:T(8,128)}, f32[384,1536]{1,0:T(8,128)}, u32[]{:S(2)}, u32[]{:S(2)}) collective-permute-start(f32[384,1536]{1,0:T(8,128)} %fusion.37), channel_id=1, source_target_pairs={{0,1},{1,0},{2,3},{3,2},{4,5},{5,4},{6,7},{7,6},{8,9},{9,8},{10,11... | collective-permute-start | bytes 7077896 | tf_op jit(solution)/shard_map/ppermute | solution.py:20
  479.6 54.1 %collective-permute-start.11 = (bf16[4,192,1536]{2,1,0:T(8,128)(2,1)S(1)}, bf16[4,192,1536]{2,1,0:T(8,128)(2,1)S(1)}, u32[]{:S(2)}, u32[]{:S(2)}) collective-permute-start(bf16[4,192,1536]{2,1,0:T(8,128)(2,1)S(1)} %copy-done.16), channel_id=1, source_target_pairs={{0,4},{4,0},{1,5},{5,1},{2,6},{6,2},{3,7},{7,3},{8,12},{12,8},{9,1... | collective-permute-start | bytes 7077896 | tf_op jit(solution)/shard_map/ppermute | solution.py:20
  480.2 15.6 %slice-start.10 = ((s8[4718592]{0:T(1024)(128)(4,1)}), s8[4194304]{0:T(1024)(128)(4,1)S(1)}, s32[]{:S(2)}) async-start(s8[4718592]{0:T(1024)(128)(4,1)} %bitcast.174), calls=%async_computation.16 | async-start | bytes 8388608
  482.7 53.6 %collective-permute-start.9 = (f32[384,1536]{1,0:T(8,128)}, f32[384,1536]{1,0:T(8,128)}, u32[]{:S(2)}, u32[]{:S(2)}) collective-permute-start(f32[384,1536]{1,0:T(8,128)} %fusion.43), channel_id=1, source_target_pairs={{0,1},{1,0},{2,3},{3,2},{4,5},{5,4},{6,7},{7,6},{8,9},{9,8},{10,11... | collective-permute-start | bytes 7077896 | tf_op jit(solution)/shard_map/ppermute | solution.py:20
  492.8 40.9 %slice-start = ((s8[4718592]{0:T(1024)(128)(4,1)}), s8[4194304]{0:T(1024)(128)(4,1)S(1)}, s32[]{:S(2)}) async-start(s8[4718592]{0:T(1024)(128)(4,1)} %bitcast.125), calls=%async_computation.6 | async-start | bytes 8388608
  494.4 39.4 %slice-start.1 = ((s8[4718592]{0:T(1024)(128)(4,1)}), s8[524288]{0:T(1024)(128)(4,1)S(1)}, s32[]{:S(2)}) async-start(s8[4718592]{0:T(1024)(128)(4,1)} %bitcast.125), calls=%async_computation.7 | async-start | bytes 1048576
  494.4 111.9 %collective-permute-start.13 = (bf16[4,192,1536]{2,1,0:T(8,128)(2,1)}, bf16[4,192,1536]{2,1,0:T(8,128)(2,1)}, u32[]{:S(2)}, u32[]{:S(2)}) collective-permute-start(bf16[4,192,1536]{2,1,0:T(8,128)(2,1)} %dynamic-slice_bitcast_fusion), channel_id=1, source_target_pairs={{0,4},{4,0},{1,5},{5,1},{2,6},{6,2},{3,7},{7,3},{8,12},{12,8},{9,1... | collective-permute-start | bytes 7077896 | tf_op jit(solution)/shard_map/ppermute | solution.py:20
  500.1 44.0 %collective-permute-start.4 = (bf16[384,1536]{1,0:T(8,128)(2,1)}, bf16[384,1536]{1,0:T(8,128)(2,1)}, u32[]{:S(2)}, u32[]{:S(2)}) collective-permute-start(bf16[384,1536]{1,0:T(8,128)(2,1)} %fusion.18), channel_id=1, source_target_pairs={{0,2},{2,0},{1,3},{3,1},{4,6},{6,4},{5,7},{7,5},{8,10},{10,8},{9,1... | collective-permute-start | bytes 3538952 | tf_op jit(solution)/shard_map/ppermute | solution.py:20
  535.8 291.0 %reduce-scatter.6.cloned.1.call-start = ((), (), s32[]{:S(2)}) async-start(), calls=%async_computation.4 | async-start | bytes 2949120 | tf_op jit(solution)/shard_map/reduce_scatter | solution.py:747
  544.1 16.5 %collective-permute-start.10 = (bf16[384,1536]{1,0:T(8,128)(2,1)}, bf16[384,1536]{1,0:T(8,128)(2,1)}, u32[]{:S(2)}, u32[]{:S(2)}) collective-permute-start(bf16[384,1536]{1,0:T(8,128)(2,1)} %get-tuple-element.134), channel_id=1, source_target_pairs={{0,1},{1,0},{2,3},{3,2},{4,5},{5,4},{6,7},{7,6},{8,9},{9,8},{10,11... | collective-permute-start | bytes 3538952 | tf_op jit(solution)/shard_map/ppermute | solution.py:20
  560.6 45.6 %slice-start.2 = ((s8[4718592]{0:T(1024)(128)(4,1)}), s8[4194304]{0:T(1024)(128)(4,1)S(1)}, s32[]{:S(2)}) async-start(s8[4718592]{0:T(1024)(128)(4,1)} %bitcast.129), calls=%async_computation.8 | async-start | bytes 8388608
  566.2 40.0 %slice-start.3 = ((s8[4718592]{0:T(1024)(128)(4,1)}), s8[524288]{0:T(1024)(128)(4,1)S(1)}, s32[]{:S(2)}) async-start(s8[4718592]{0:T(1024)(128)(4,1)} %bitcast.129), calls=%async_computation.9 | async-start | bytes 1048576
  624.9 182.5 %copy-start.32 = (bf16[48,768]{1,0:T(8,128)(2,1)S(1)}, bf16[48,768]{1,0:T(8,128)(2,1)}, u32[]{:S(2)}) copy-start(bf16[48,768]{1,0:T(8,128)(2,1)} %refs_6_.1) | copy-start | bytes 221188
  624.9 186.8 %copy-start.29 = (bf16[96,768]{1,0:T(8,128)(2,1)S(1)}, bf16[96,768]{1,0:T(8,128)(2,1)}, u32[]{:S(2)}) copy-start(bf16[96,768]{1,0:T(8,128)(2,1)} %refs_1_.1) | copy-start | bytes 442372
  624.9 186.8 %copy-start.30 = (bf16[96,768]{1,0:T(8,128)(2,1)S(1)}, bf16[96,768]{1,0:T(8,128)(2,1)}, u32[]{:S(2)}) copy-start(bf16[96,768]{1,0:T(8,128)(2,1)} %refs_2_.1) | copy-start | bytes 442372
  624.9 186.8 %copy-start.31 = (bf16[96,768]{1,0:T(8,128)(2,1)S(1)}, bf16[96,768]{1,0:T(8,128)(2,1)}, u32[]{:S(2)}) copy-start(bf16[96,768]{1,0:T(8,128)(2,1)} %refs_5_.1) | copy-start | bytes 442372
  813.6 7.6 collective-permute-start.16
  816.7 10.0 %collective-permute-start.12 = (bf16[96,1536]{1,0:T(8,128)(2,1)S(1)}, bf16[96,1536]{1,0:T(8,128)(2,1)S(1)}, u32[]{:S(2)}, u32[]{:S(2)}) collective-permute-start(bf16[96,1536]{1,0:T(8,128)(2,1)S(1)} %dynamic-slice_bitcast_fusion.5), channel_id=1, source_target_pairs={{0,2},{2,0},{1,3},{3,1},{4,6},{6,4},{5,7},{7,5},{8,10},{10,8},{9,1... | collective-permute-start | bytes 884744 | tf_op jit(solution)/shard_map/ppermute | solution.py:20
  827.9 6.8 collective-permute-start.14
  (74 other events, 362.5 us)
Sparse Core Ops, SparseCore 0:
  465.4 48.9 reduce-scatter.7
  536.0 49.1 reduce-scatter.3
  610.1 68.5 reduce-scatter.5
